TPU v7x, 32 devices: a whole 2x2x4 slice. The times are simulated.
32 devices in a mesh: dp: 8 (over z, core), expert: 4 (over y, x).
Axes of the slice: x: 2, y: 2, z: 4, core: 2. Of those that a mesh axis runs over, the one named last changes fastest.
Arguments:
- inputs: bfloat16 [8, 1024, 1536], P('dp', 'expert'), may hold values from -6 to 6
- routes: int32 [2, 4, 8, 256, 8], P(None, 'expert', 'dp'), may hold values from 0 to 19, all different within a row; in each aligned block of 256 rows (0 to 255, 256 to 511, ..., all dimensions but the last counted through in order) at most 192 rows name the same one
- cotangent: bfloat16 [8, 1024, 1536], P('dp', 'expert'), may hold values from -6 to 6
- query_weight: bfloat16 [2, 1536, 1536], P(None, ('dp', 'expert')), may hold values from -0.15625 to 0.15625
- key_projection_weight: bfloat16 [2, 1536, 512], P(None, ('dp', 'expert')), may hold values from -0.15625 to 0.15625
- value_projection_weight: bfloat16 [2, 1536, 512], P(None, ('dp', 'expert')), may hold values from -0.15625 to 0.15625
- output_weight: bfloat16 [2, 1536, 1536], P(None, None, ('dp', 'expert')), may hold values from -0.625 to 0.625
- attention_gain: bfloat16 [2, 1536], P(None, ('dp', 'expert')), may hold values from 0.5 to 1.5
- expert_gain: bfloat16 [2, 1536], P(None, ('dp', 'expert')), may hold values from 0.5 to 1.5
- router_weight: bfloat16 [2, 1536, 20], P(None, ('dp', 'expert')), may hold values from -0.078125 to 0.078125
- gate_weight: bfloat16 [2, 20, 1536, 512], P(None, 'expert', 'dp'), may hold values from -0.15625 to 0.15625
- up_weight: bfloat16 [2, 20, 1536, 512], P(None, 'expert', 'dp'), may hold values from -0.15625 to 0.15625
- down_weight: bfloat16 [2, 20, 512, 1536], P(None, 'expert', None, 'dp'), may hold values from -0.75 to 0.75
Outputs:
- result: bfloat16 [8, 1024, 1536], P('dp', 'expert')
- grad_inputs: float32 [8, 1024, 1536], P('dp', 'expert')
- grad_query_weight: float32 [2, 1536, 1536], P(None, ('dp', 'expert'))
- grad_key_weight: float32 [2, 1536, 512], P(None, ('dp', 'expert'))
- grad_value_weight: float32 [2, 1536, 512], P(None, ('dp', 'expert'))
- grad_output_weight: float32 [2, 1536, 1536], P(None, None, ('dp', 'expert'))
- grad_attention_gain: float32 [2, 1536], P(None, ('dp', 'expert'))
- grad_expert_gain: float32 [2, 1536], P(None, ('dp', 'expert'))
- grad_router_weight: float32 [2, 1536, 20], P(None, ('dp', 'expert'))
- grad_gate_weight: float32 [2, 20, 1536, 512], P(None, 'expert', 'dp')
- grad_up_weight: float32 [2, 20, 1536, 512], P(None, 'expert', 'dp')
- grad_down_weight: float32 [2, 20, 512, 1536], P(None, 'expert', None, 'dp')
Inputs may be any that keep to these rules, and one draw needn't show every extreme that they name: `routes`: each row names 8 different experts. Over the 256 rows of one device of one layer (one block of positions, the sequences of one dp index), no expert is named more than 192 times, a bound that some block reaches.
All inputs are finite; a program needn't handle non-finite values.
Results may differ from a plain program's by a relative error of at most 0.03.
Values may be sent and summed in bfloat16 or wider, within the bound.
No kernel may reach another device: no remote copies, remote signals or barrier semaphores. Data moves between devices by JAX's collectives and lax.ppermute only.
A program may use at most 448 MiB of HBM per device.

v0:
```python
import math

import jax
import jax.numpy as jnp
from jax import lax
from jax.sharding import PartitionSpec as P

QUERY_HEADS = 24
KEY_VALUE_HEADS = 8
HEAD_SIZE = 64
LAYER_COUNT = 2


eps_norm = 1e-06
highest_precision = lax.Precision.HIGHEST


def rotary_tables(positions, half_dim):
    frequency = jnp.exp(-math.log(10000.0) * jnp.arange(half_dim, dtype=jnp.float32) / half_dim)
    angles = positions.astype(jnp.float32)[:, None] * frequency[None, :]
    return (jnp.cos(angles), jnp.sin(angles))


def rotate_features(values, cosine_table, sine_table):
    half_dim = values.shape[-1] // 2
    first_half = values[..., :half_dim]
    second_half = values[..., half_dim:]
    cos_part = cosine_table[:, None, :]
    sin_part = sine_table[:, None, :]
    return jnp.concatenate(
        [
            first_half * cos_part - second_half * sin_part,
            second_half * cos_part + first_half * sin_part,
        ],
        axis=-1,
    )


def norm_forward(values, gain_vec):
    inv_rms = lax.rsqrt(jnp.mean(values * values, axis=-1, keepdims=True) + eps_norm)
    return (values * inv_rms * gain_vec, inv_rms)


def norm_backward(values, inv_rms, gain_vec, upstream):
    scaled = upstream * gain_vec
    grad_gain = jnp.sum(upstream * values * inv_rms, axis=0)
    grad_values = inv_rms * (
        scaled - values * inv_rms * inv_rms * jnp.mean(scaled * values, axis=-1, keepdims=True)
    )
    return (grad_values, grad_gain)


def stack_member(layer_list, member):
    return jnp.stack([layer_parts[member] for layer_parts in layer_list], axis=0)


def body(
    inputs,
    routes,
    cotangent,
    query_weight,
    key_projection_weight,
    value_projection_weight,
    output_weight,
    attention_gain,
    expert_gain,
    router_weight,
    gate_weight,
    up_weight,
    down_weight,
):
    sequences_per_device, block_length, model_width = inputs.shape
    token_total = sequences_per_device * block_length
    top_k = routes.shape[-1]
    exp_dev = gate_weight.shape[1]
    groups = lax.axis_size("expert")
    expert_total = exp_dev * groups
    capacity = 15 * token_total * top_k // (8 * expert_total)
    query_head_group = QUERY_HEADS // KEY_VALUE_HEADS
    score_scale = HEAD_SIZE ** (-0.5)
    positions = lax.axis_index("expert") * block_length + jnp.arange(block_length, dtype=jnp.int32)
    cosine_table, sine_table = rotary_tables(positions, HEAD_SIZE // 2)
    causal = positions[:, None] >= jnp.arange(block_length * groups, dtype=jnp.int32)[None, :]
    expert_ids = jnp.arange(expert_total, dtype=jnp.int32)

    def scatter_rows(pair_rows, dest_row):
        empty_rows = jnp.zeros((expert_total * capacity, model_width), jnp.bfloat16)
        return (
            empty_rows.at[dest_row].set(pair_rows).reshape(groups, exp_dev, capacity, model_width)
        )

    def layer_forward(hidden, layer_index):
        token_routes = routes[layer_index].reshape(token_total, top_k)
        query_full, key_full, value_full, output_full, gain_one, gain_two, router_full = (
            lax.all_gather(query_weight[layer_index], ("dp", "expert"), axis=0, tiled=True),
            lax.all_gather(
                key_projection_weight[layer_index], ("dp", "expert"), axis=0, tiled=True
            ),
            lax.all_gather(
                value_projection_weight[layer_index], ("dp", "expert"), axis=0, tiled=True
            ),
            lax.all_gather(output_weight[layer_index], ("dp", "expert"), axis=1, tiled=True),
            lax.all_gather(attention_gain[layer_index], ("dp", "expert"), axis=0, tiled=True),
            lax.all_gather(expert_gain[layer_index], ("dp", "expert"), axis=0, tiled=True),
            lax.all_gather(router_weight[layer_index], ("dp", "expert"), axis=0, tiled=True),
        )
        gain_one = gain_one.astype(jnp.float32)
        gain_two = gain_two.astype(jnp.float32)
        first_normalized, inv_one = norm_forward(hidden, gain_one)
        first_normalized = first_normalized.astype(jnp.bfloat16)
        query_linear = jnp.dot(first_normalized, query_full, preferred_element_type=jnp.float32)
        key_linear = jnp.dot(first_normalized, key_full, preferred_element_type=jnp.float32)
        value_low = (
            jnp.dot(first_normalized, value_full, preferred_element_type=jnp.float32)
            .astype(jnp.bfloat16)
            .reshape(sequences_per_device, block_length, KEY_VALUE_HEADS, HEAD_SIZE)
        )
        query_rotated = rotate_features(
            query_linear.reshape(sequences_per_device, block_length, QUERY_HEADS, HEAD_SIZE),
            cosine_table,
            sine_table,
        ).astype(jnp.bfloat16)
        query_grouped = query_rotated.reshape(
            sequences_per_device, block_length, KEY_VALUE_HEADS, query_head_group, HEAD_SIZE
        )
        key_rot = rotate_features(
            key_linear.reshape(sequences_per_device, block_length, KEY_VALUE_HEADS, HEAD_SIZE),
            cosine_table,
            sine_table,
        ).astype(jnp.bfloat16)
        key_all, value_everything = (
            lax.all_gather(key_rot, "expert", axis=1, tiled=True),
            lax.all_gather(value_low, "expert", axis=1, tiled=True),
        )
        scores = (
            jnp.einsum(
                "sqhgd,skhd->shgqk", query_grouped, key_all, preferred_element_type=jnp.float32
            )
            * score_scale
        )
        masked = jnp.where(causal, scores, -1e30)
        row_max = jnp.max(masked, axis=-1, keepdims=True)
        exp_scores = jnp.exp(masked - row_max)
        row_total = jnp.sum(exp_scores, axis=-1, keepdims=True)
        log_total = row_max + jnp.log(row_total)
        prob_low = (exp_scores / row_total).astype(jnp.bfloat16)
        attended = jnp.einsum(
            "shgqk,skhd->sqhgd", prob_low, value_everything, preferred_element_type=jnp.float32
        )
        attended = attended.reshape(token_total, QUERY_HEADS * HEAD_SIZE).astype(jnp.bfloat16)
        middle = hidden + jnp.dot(attended, output_full, preferred_element_type=jnp.float32)
        normed_two, inv_two = norm_forward(middle, gain_two)
        normed_two = normed_two.astype(jnp.bfloat16)
        logits = jnp.dot(normed_two, router_full, preferred_element_type=jnp.float32)
        route_hot = (token_routes[:, :, None] == expert_ids[None, None, :]).astype(jnp.float32)
        chosen = jnp.einsum("tke,te->tk", route_hot, logits, precision=highest_precision)
        gate_share = jax.nn.softmax(chosen, axis=-1)
        flat_expert = token_routes.reshape(-1)
        pair_hot = (flat_expert[:, None] == expert_ids[None, :]).astype(jnp.int32)
        slot_rank = jnp.sum((jnp.cumsum(pair_hot, axis=0) - 1) * pair_hot, axis=1)
        dest_row = flat_expert * capacity + slot_rank
        arrived = lax.all_to_all(
            scatter_rows(jnp.repeat(normed_two, top_k, axis=0), dest_row),
            "expert",
            split_axis=0,
            concat_axis=0,
            tiled=True,
        )
        gate_full, up_full, down_full = (
            lax.all_gather(gate_weight[layer_index], "dp", axis=1, tiled=True),
            lax.all_gather(up_weight[layer_index], "dp", axis=1, tiled=True),
            lax.all_gather(down_weight[layer_index], "dp", axis=2, tiled=True),
        )
        gate_val = jnp.einsum(
            "sepd,edf->sepf", arrived, gate_full, preferred_element_type=jnp.float32
        )
        up_val = jnp.einsum("sepd,edf->sepf", arrived, up_full, preferred_element_type=jnp.float32)
        inner_act = (jax.nn.silu(gate_val) * up_val).astype(jnp.bfloat16)
        out_rows = jnp.einsum(
            "sepf,efd->sepd", inner_act, down_full, preferred_element_type=jnp.float32
        ).astype(jnp.bfloat16)
        returned = lax.all_to_all(out_rows, "expert", split_axis=0, concat_axis=0, tiled=True)
        picked = (
            returned.reshape(expert_total * capacity, model_width)[dest_row]
            .astype(jnp.float32)
            .reshape(token_total, top_k, model_width)
        )
        output = middle + jnp.sum(gate_share[:, :, None] * picked, axis=1)
        kept_state = (
            hidden,
            inv_one,
            first_normalized,
            query_grouped,
            key_all,
            value_everything,
            log_total,
            attended,
            middle,
            inv_two,
            normed_two,
            route_hot,
            gate_share,
            dest_row,
            picked,
            arrived,
            gate_val,
            up_val,
            inner_act,
            query_full,
            key_full,
            value_full,
            output_full,
            gain_one,
            gain_two,
            router_full,
            gate_full,
            up_full,
            down_full,
        )
        return (output, kept_state)

    hidden = inputs.astype(jnp.float32).reshape(token_total, model_width)
    layer_inputs = []
    kept_states = []
    for layer_index in range(LAYER_COUNT):
        layer_inputs.append(hidden)
        hidden, kept_state = layer_forward(hidden, layer_index)
        kept_states.append(kept_state)
    output = hidden.astype(jnp.bfloat16).reshape(sequences_per_device, block_length, model_width)
    grad_hidden = cotangent.astype(jnp.float32).reshape(token_total, model_width)
    attention_list = [None] * LAYER_COUNT
    expert_list = [None] * LAYER_COUNT
    for layer_index in range(LAYER_COUNT - 1, -1, -1):
        kept_state = layer_forward(layer_inputs[layer_index], layer_index)[1]
        (
            layer_hidden,
            layer_inv_one,
            layer_first_normalized,
            layer_query_grouped,
            layer_key_all,
            layer_value_everything,
            layer_log_total,
            layer_attended,
            layer_middle,
            layer_inv_two,
            layer_normed_two,
            layer_route_hot,
            layer_gate_share,
            layer_dest_row,
            layer_picked,
            layer_arrived,
            layer_gate_val,
            layer_up_val,
            layer_inner_act,
            layer_query_full,
            layer_key_full,
            layer_value_full,
            layer_output_full,
            layer_gain_one,
            layer_gain_two,
            layer_router_full,
            layer_gate_full,
            layer_up_full,
            layer_down_full,
        ) = kept_state
        grad_gates = jnp.sum(grad_hidden[:, None, :] * layer_picked, axis=-1)
        grad_pairs = (
            (layer_gate_share[:, :, None] * grad_hidden[:, None, :])
            .astype(jnp.bfloat16)
            .reshape(token_total * top_k, model_width)
        )
        grad_arrived = lax.all_to_all(
            scatter_rows(grad_pairs, layer_dest_row),
            "expert",
            split_axis=0,
            concat_axis=0,
            tiled=True,
        )
        grad_down = jnp.einsum(
            "sepf,sepd->efd", layer_inner_act, grad_arrived, preferred_element_type=jnp.float32
        )
        grad_inner = jnp.einsum(
            "sepd,efd->sepf", grad_arrived, layer_down_full, preferred_element_type=jnp.float32
        )
        sigmoid_val = jax.nn.sigmoid(layer_gate_val)
        grad_gate_val = (
            grad_inner * layer_up_val * sigmoid_val * (1.0 + layer_gate_val * (1.0 - sigmoid_val))
        ).astype(jnp.bfloat16)
        grad_up_val = (grad_inner * layer_gate_val * sigmoid_val).astype(jnp.bfloat16)
        grad_gate_w = jnp.einsum(
            "sepd,sepf->edf", layer_arrived, grad_gate_val, preferred_element_type=jnp.float32
        )
        grad_up_w = jnp.einsum(
            "sepd,sepf->edf", layer_arrived, grad_up_val, preferred_element_type=jnp.float32
        )
        grad_rows = jnp.einsum(
            "sepf,edf->sepd", grad_gate_val, layer_gate_full, preferred_element_type=jnp.float32
        )
        grad_rows = (
            grad_rows
            + jnp.einsum(
                "sepf,edf->sepd", grad_up_val, layer_up_full, preferred_element_type=jnp.float32
            )
        ).astype(jnp.bfloat16)
        grad_back = lax.all_to_all(grad_rows, "expert", split_axis=0, concat_axis=0, tiled=True)
        grad_normed_two = (
            grad_back.reshape(expert_total * capacity, model_width)[layer_dest_row]
            .astype(jnp.float32)
            .reshape(token_total, top_k, model_width)
            .sum(axis=1)
        )
        grad_chosen = layer_gate_share * (
            grad_gates - jnp.sum(layer_gate_share * grad_gates, axis=-1, keepdims=True)
        )
        grad_logits = jnp.einsum(
            "tk,tke->te", grad_chosen, layer_route_hot, precision=highest_precision
        ).astype(jnp.bfloat16)
        grad_router = jnp.dot(layer_normed_two.T, grad_logits, preferred_element_type=jnp.float32)
        grad_normed_two = grad_normed_two + jnp.dot(
            grad_logits, layer_router_full.T, preferred_element_type=jnp.float32
        )
        grad_norm_mid, grad_gain_two = norm_backward(
            layer_middle, layer_inv_two, layer_gain_two, grad_normed_two
        )
        grad_middle = grad_hidden + grad_norm_mid
        grad_branch = grad_middle.astype(jnp.bfloat16)
        grad_output_w = jnp.dot(layer_attended.T, grad_branch, preferred_element_type=jnp.float32)
        grad_attended = (
            jnp.dot(grad_branch, layer_output_full.T, preferred_element_type=jnp.float32)
            .astype(jnp.bfloat16)
            .reshape(
                sequences_per_device, block_length, KEY_VALUE_HEADS, query_head_group, HEAD_SIZE
            )
        )
        layer_scores = (
            jnp.einsum(
                "sqhgd,skhd->shgqk",
                layer_query_grouped,
                layer_key_all,
                preferred_element_type=jnp.float32,
            )
            * score_scale
        )
        softmax_probs = jnp.exp(jnp.where(causal, layer_scores, -1e30) - layer_log_total)
        grad_probs = jnp.einsum(
            "sqhgd,skhd->shgqk",
            grad_attended,
            layer_value_everything,
            preferred_element_type=jnp.float32,
        )
        grad_scores = (
            softmax_probs
            * (grad_probs - jnp.sum(softmax_probs * grad_probs, axis=-1, keepdims=True))
        ).astype(jnp.bfloat16)
        grad_query = (
            jnp.einsum(
                "shgqk,skhd->sqhgd", grad_scores, layer_key_all, preferred_element_type=jnp.float32
            )
            * score_scale
        )
        grad_key_all = (
            jnp.einsum(
                "shgqk,sqhgd->skhd",
                grad_scores,
                layer_query_grouped,
                preferred_element_type=jnp.float32,
            )
            * score_scale
        )
        grad_value_all = jnp.einsum(
            "shgqk,sqhgd->skhd",
            softmax_probs.astype(jnp.bfloat16),
            grad_attended,
            preferred_element_type=jnp.float32,
        )
        grad_key = lax.psum_scatter(
            grad_key_all.astype(jnp.bfloat16), "expert", scatter_dimension=1, tiled=True
        ).astype(jnp.float32)
        value_gradient = lax.psum_scatter(
            grad_value_all.astype(jnp.bfloat16), "expert", scatter_dimension=1, tiled=True
        )
        grad_query_lin = (
            rotate_features(
                grad_query.reshape(sequences_per_device, block_length, QUERY_HEADS, HEAD_SIZE),
                cosine_table,
                -sine_table,
            )
            .astype(jnp.bfloat16)
            .reshape(token_total, QUERY_HEADS * HEAD_SIZE)
        )
        grad_key_lin = (
            rotate_features(grad_key, cosine_table, -sine_table)
            .astype(jnp.bfloat16)
            .reshape(token_total, KEY_VALUE_HEADS * HEAD_SIZE)
        )
        value_gradient_reduced = value_gradient.reshape(token_total, KEY_VALUE_HEADS * HEAD_SIZE)
        grad_query_w = jnp.dot(
            layer_first_normalized.T, grad_query_lin, preferred_element_type=jnp.float32
        )
        grad_key_w = jnp.dot(
            layer_first_normalized.T, grad_key_lin, preferred_element_type=jnp.float32
        )
        grad_value_w = jnp.dot(
            layer_first_normalized.T, value_gradient_reduced, preferred_element_type=jnp.float32
        )
        grad_normed_one = jnp.dot(
            grad_query_lin, layer_query_full.T, preferred_element_type=jnp.float32
        )
        grad_normed_one = grad_normed_one + jnp.dot(
            grad_key_lin, layer_key_full.T, preferred_element_type=jnp.float32
        )
        grad_normed_one = grad_normed_one + jnp.dot(
            value_gradient_reduced, layer_value_full.T, preferred_element_type=jnp.float32
        )
        grad_norm_in, grad_gain_one = norm_backward(
            layer_hidden, layer_inv_one, layer_gain_one, grad_normed_one
        )
        attention_parts = (
            lax.psum_scatter(grad_query_w, ("dp", "expert"), scatter_dimension=0, tiled=True),
            lax.psum_scatter(grad_key_w, ("dp", "expert"), scatter_dimension=0, tiled=True),
            lax.psum_scatter(grad_value_w, ("dp", "expert"), scatter_dimension=0, tiled=True),
            lax.psum_scatter(grad_output_w, ("dp", "expert"), scatter_dimension=1, tiled=True),
            lax.psum_scatter(grad_gain_one, ("dp", "expert"), scatter_dimension=0, tiled=True),
            lax.psum_scatter(grad_gain_two, ("dp", "expert"), scatter_dimension=0, tiled=True),
            lax.psum_scatter(grad_router, ("dp", "expert"), scatter_dimension=0, tiled=True),
        )
        expert_parts = (
            lax.psum_scatter(
                grad_gate_w.astype(jnp.bfloat16), "dp", scatter_dimension=1, tiled=True
            ).astype(jnp.float32),
            lax.psum_scatter(
                grad_up_w.astype(jnp.bfloat16), "dp", scatter_dimension=1, tiled=True
            ).astype(jnp.float32),
            lax.psum_scatter(
                grad_down.astype(jnp.bfloat16), "dp", scatter_dimension=2, tiled=True
            ).astype(jnp.float32),
        )
        grad_hidden, attention_parts, expert_parts = (
            grad_middle + grad_norm_in,
            attention_parts,
            expert_parts,
        )
        attention_list[layer_index] = attention_parts
        expert_list[layer_index] = expert_parts
    return (
        output,
        grad_hidden.reshape(sequences_per_device, block_length, model_width),
        stack_member(attention_list, 0),
        stack_member(attention_list, 1),
        stack_member(attention_list, 2),
        stack_member(attention_list, 3),
        stack_member(attention_list, 4),
        stack_member(attention_list, 5),
        stack_member(attention_list, 6),
        stack_member(expert_list, 0),
        stack_member(expert_list, 1),
        stack_member(expert_list, 2),
    )


def solution(mesh):
    in_specs = (
        P("dp", "expert", None),
        P(None, "expert", "dp", None, None),
        P("dp", "expert", None),
        P(None, ("dp", "expert"), None),
        P(None, ("dp", "expert"), None),
        P(None, ("dp", "expert"), None),
        P(None, None, ("dp", "expert")),
        P(None, ("dp", "expert")),
        P(None, ("dp", "expert")),
        P(None, ("dp", "expert"), None),
        P(None, "expert", "dp", None),
        P(None, "expert", "dp", None),
        P(None, "expert", None, "dp"),
    )
    out_specs = (
        P("dp", "expert", None),
        P("dp", "expert", None),
        P(None, ("dp", "expert"), None),
        P(None, ("dp", "expert"), None),
        P(None, ("dp", "expert"), None),
        P(None, None, ("dp", "expert")),
        P(None, ("dp", "expert")),
        P(None, ("dp", "expert")),
        P(None, ("dp", "expert"), None),
        P(None, "expert", "dp", None),
        P(None, "expert", "dp", None),
        P(None, "expert", None, "dp"),
    )
    return jax.shard_map(body, mesh=mesh, in_specs=in_specs, out_specs=out_specs, check_vma=False)
```

profile of v0, /device:TPU:0, one launch (start us, length us, event | category | flops | bytes accessed | tf_op | source)
XLA Modules:
  0.0 3955.9 jit_solution(8001135118815653429)
XLA Ops:
  14.5 42.2 %all-reduce.9 = (bf16[1536]{0:T(1024)(128)(2,1)S(1)}, bf16[1536]{0:T(1024)(128)(2,1)S(1)}, bf16[1536]{0:T(1024)(128)(2,1)}, bf16[1536]{0:T(1024)(128)(2,1)}) all-reduce(bf16[1536]{0:T(1024)(128)(2,1)S(1)} %dynamic-update-slice, bf16[1536]{0:T(1024)(128)(2,1)S(1)} %dynamic-update-slice.1, ...), channel_id=2, replica_groups=mesh['dp'=8,'expert'=4] {'dp','expert'}, use_global_device_ids=true, to_apply=%add | all-reduce | flops 6144 | bytes 24576
  72.5 54.1 %all-gather.47.cloned.1.call-done = bf16[1,1536,512]{2,1,0:T(8,128)(2,1)} async-done(((bf16[1,48,512]{2,1,0:T(8,128)(2,1)}), bf16[1,1536,512]{2,1,0:T(8,128)(2,1)}) %all-gather.47.cloned.1.call-update) | async-done | bytes 1572880 | tf_op jit(solution)/shard_map/all_gather | solution.py:99
  147.4 45.2 %all-gather.51.cloned.1.call-done = bf16[1,1536,1536]{2,1,0:T(8,128)(2,1)} async-done(((bf16[1,48,1536]{2,1,0:T(8,128)(2,1)}), bf16[1,1536,1536]{2,1,0:T(8,128)(2,1)}) %all-gather.51.cloned.1.call-update) | async-done | bytes 4718608 | tf_op jit(solution)/shard_map/all_gather | solution.py:95
  259.0 56.0 %all-gather.53.cloned.1.call-done = bf16[1,1536,1536]{1,2,0:T(8,128)(2,1)} async-done(((bf16[1,1536,48]{1,2,0:T(8,128)(2,1)}), bf16[1,1536,1536]{1,2,0:T(8,128)(2,1)}) %all-gather.53.cloned.1.call-update) | async-done | bytes 4718608 | tf_op jit(solution)/shard_map/all_gather | solution.py:102
  344.0 49.3 %all-gather.55.cloned.1.call-done = bf16[1,5,1536,512]{3,2,1,0:T(8,128)(2,1)} async-done(((bf16[1,5,192,512]{3,2,1,0:T(8,128)(2,1)}), bf16[1,5,1536,512]{3,2,1,0:T(8,128)(2,1)}) %all-gather.55.cloned.1.call-update) | async-done | bytes 7864336 | tf_op jit(solution)/shard_map/all_gather | solution.py:170
  393.3 79.0 %all-to-all-done = bf16[4,5,192,1536]{3,2,1,0:T(8,128)(2,1)} async-done(((bf16[4,5,192,1536]{3,2,1,0:T(8,128)(2,1)}), bf16[4,5,192,1536]{3,2,1,0:T(8,128)(2,1)}, u32[]{:S(2)}, u32[]{:S(2)}) %all-to-all-start) | async-done | bytes 11796512 | tf_op jit(solution)/shard_map/all_to_all | solution.py:162
  501.9 47.7 %all-gather.59.cloned.1.call-done = bf16[1,5,512,1536]{2,3,1,0:T(8,128)(2,1)} async-done(((bf16[1,5,512,192]{2,3,1,0:T(8,128)(2,1)}), bf16[1,5,512,1536]{2,3,1,0:T(8,128)(2,1)}) %all-gather.59.cloned.1.call-update) | async-done | bytes 7864336 | tf_op jit(solution)/shard_map/all_gather | solution.py:172
  579.3 195.2 %all-gather.6 = bf16[1,1536,20]{2,0,1:T(2,128)(2,1)S(1)} all-gather(bf16[1,48,20]{2,0,1:T(2,128)(2,1)S(1)} %copy.188), channel_id=8, replica_groups=mesh['dp'=8,'expert'=4] {'dp','expert'}, dimensions={1}, use_global_device_ids=true | all-gather | bytes 63360 | tf_op jit(solution)/shard_map/all_gather | solution.py:105
  884.4 55.5 %all-gather.67.cloned.1.call-done = bf16[1,1536,1536]{1,2,0:T(8,128)(2,1)} async-done(((bf16[1,1536,48]{1,2,0:T(8,128)(2,1)}), bf16[1,1536,1536]{1,2,0:T(8,128)(2,1)}) %all-gather.67.cloned.1.call-update) | async-done | bytes 4718608 | tf_op jit(solution)/shard_map/all_gather | solution.py:102
  969.8 199.6 %all-gather.16 = bf16[1,1536,20]{2,0,1:T(2,128)(2,1)S(1)} all-gather(bf16[1,48,20]{2,0,1:T(2,128)(2,1)S(1)} %copy.189), channel_id=18, replica_groups=mesh['dp'=8,'expert'=4] {'dp','expert'}, dimensions={1}, use_global_device_ids=true | all-gather | bytes 63360 | tf_op jit(solution)/shard_map/all_gather | solution.py:105
  1225.0 96.3 %all-to-all-done.4 = bf16[4,5,192,1536]{3,2,1,0:T(8,128)(2,1)} async-done(((bf16[4,5,192,1536]{3,2,1,0:T(8,128)(2,1)}), bf16[4,5,192,1536]{3,2,1,0:T(8,128)(2,1)}, u32[]{:S(2)}, u32[]{:S(2)}) %all-to-all-start.4) | async-done | bytes 11796512 | tf_op jit(solution)/shard_map/all_to_all | solution.py:272
  1412.6 83.5 %all-to-all-done.3 = bf16[4,5,192,1536]{3,2,1,0:T(8,128)(2,1)} async-done(((bf16[4,5,192,1536]{3,2,1,0:T(8,128)(2,1)}), bf16[4,5,192,1536]{3,2,1,0:T(8,128)(2,1)}, u32[]{:S(2)}, u32[]{:S(2)}) %all-to-all-start.3) | async-done | bytes 11796512 | tf_op jit(solution)/shard_map/all_to_all | solution.py:182
  1539.7 91.9 %all-to-all-done.5 = bf16[4,5,192,1536]{3,2,1,0:T(8,128)(2,1)} async-done(((bf16[4,5,192,1536]{3,2,1,0:T(8,128)(2,1)}), bf16[4,5,192,1536]{3,2,1,0:T(8,128)(2,1)}, u32[]{:S(2)}, u32[]{:S(2)}) %all-to-all-start.5) | async-done | bytes 11796512 | tf_op jit(solution)/shard_map/all_to_all | solution.py:305
  1746.4 25.7 reduce-scatter.27.cloned.1.call-done
  1795.2 138.7 %all_to_all.44 = bf16[4,5,192,1536]{3,2,1,0:T(8,128)(2,1)} all-to-all(bf16[4,5,192,1536]{3,2,1,0:T(8,128)(2,1)} %bitcast.667), channel_id=1, replica_groups=mesh['dp'=8,'expert'=4] {'expert'}, dimensions={0} | all-to-all | bytes 23592960 | tf_op jit(solution)/shard_map/all_to_all | solution.py:272
  2006.5 121.8 %all-to-all-done.7 = bf16[4,5,192,1536]{3,2,1,0:T(8,128)(2,1)} async-done(((bf16[4,5,192,1536]{3,2,1,0:T(8,128)(2,1)}), bf16[4,5,192,1536]{3,2,1,0:T(8,128)(2,1)}, u32[]{:S(2)}, u32[]{:S(2)}) %all-to-all-start.7) | async-done | bytes 11796512 | tf_op jit(solution)/shard_map/all_to_all | solution.py:305
  2356.8 88.2 %reduce-scatter.61.cloned.1.call-done = f32[48,20]{1,0:T(8,128)} async-done(((f32[1536,20]{1,0:T(8,128)}), f32[48,20]{1,0:T(8,128)}) %reduce-scatter.61.cloned.1.call-update) | async-done | bytes 3856
  2453.1 40.5 %all-reduce.8 = (f32[1536]{0:T(1024)S(1)}, f32[1536]{0:T(1024)S(1)}, f32[1536]{0:T(1024)S(1)}, f32[1536]{0:T(1024)S(1)}) all-reduce(f32[1536]{0:T(1024)S(1)} %copy-done.82, f32[1536]{0:T(1024)S(1)} %get-tuple-element.56, f32[1536]{0:T(1024)S(1)} %copy-done.81, ...), channel_id=35, replica_groups=mesh['dp'=8,'expert'=4] {'dp','expert'}, use_global_device_ids=true, to_apply=%region_51.52.clone | all-reduce | flops 6144 | bytes 49152
  2497.9 53.7 %reduce-scatter.43.cloned.1.call-done = f32[48,512]{1,0:T(8,128)} async-done(((f32[1536,512]{1,0:T(8,128)}), f32[48,512]{1,0:T(8,128)}) %reduce-scatter.43.cloned.1.call-update) | async-done | bytes 98320 | tf_op jit(solution)/shard_map/reduce_scatter | solution.py:421
  2551.7 106.5 %reduce-scatter.41.cloned.1.call-done = f32[48,512]{1,0:T(8,128)} async-done(((f32[1536,512]{1,0:T(8,128)}), f32[48,512]{1,0:T(8,128)}) %reduce-scatter.41.cloned.1.call-update) | async-done | bytes 98320 | tf_op jit(solution)/shard_map/reduce_scatter | solution.py:421
  2659.8 104.8 %reduce-scatter.39.cloned.1.call-done = f32[48,512]{1,0:T(8,128)} async-done(((f32[1536,512]{1,0:T(8,128)}), f32[48,512]{1,0:T(8,128)}) %reduce-scatter.39.cloned.1.call-update) | async-done | bytes 98320 | tf_op jit(solution)/shard_map/reduce_scatter | solution.py:420
  2764.7 106.6 %reduce-scatter.37.cloned.1.call-done = f32[48,512]{1,0:T(8,128)} async-done(((f32[1536,512]{1,0:T(8,128)}), f32[48,512]{1,0:T(8,128)}) %reduce-scatter.37.cloned.1.call-update) | async-done | bytes 98320 | tf_op jit(solution)/shard_map/reduce_scatter | solution.py:420
  2872.9 84.3 %reduce-scatter.59.cloned.1.call-done = bf16[5,512,192]{1,2,0:T(8,128)(2,1)} async-done(((bf16[5,512,1536]{1,2,0:T(8,128)(2,1)}), bf16[5,512,192]{1,2,0:T(8,128)(2,1)}) %reduce-scatter.59.cloned.1.call-update) | async-done | bytes 983056 | tf_op jit(solution)/shard_map/reduce_scatter | solution.py:434
  2957.2 85.2 %reduce-scatter.57.cloned.1.call-done = bf16[5,512,192]{1,2,0:T(8,128)(2,1)} async-done(((bf16[5,512,1536]{1,2,0:T(8,128)(2,1)}), bf16[5,512,192]{1,2,0:T(8,128)(2,1)}) %reduce-scatter.57.cloned.1.call-update) | async-done | bytes 983056 | tf_op jit(solution)/shard_map/reduce_scatter | solution.py:434
  3046.1 81.7 %reduce-scatter.55.cloned.1.call-done = bf16[5,192,512]{2,1,0:T(8,128)(2,1)} async-done(((bf16[5,1536,512]{2,1,0:T(8,128)(2,1)}), bf16[5,192,512]{2,1,0:T(8,128)(2,1)}) %reduce-scatter.55.cloned.1.call-update) | async-done | bytes 983056 | tf_op jit(solution)/shard_map/reduce_scatter | solution.py:431
  3127.8 85.4 %reduce-scatter.53.cloned.1.call-done = bf16[5,192,512]{2,1,0:T(8,128)(2,1)} async-done(((bf16[5,1536,512]{2,1,0:T(8,128)(2,1)}), bf16[5,192,512]{2,1,0:T(8,128)(2,1)}) %reduce-scatter.53.cloned.1.call-update) | async-done | bytes 983056 | tf_op jit(solution)/shard_map/reduce_scatter | solution.py:431
  3216.9 81.5 %reduce-scatter.51.cloned.1.call-done = bf16[5,192,512]{2,1,0:T(8,128)(2,1)} async-done(((bf16[5,1536,512]{2,1,0:T(8,128)(2,1)}), bf16[5,192,512]{2,1,0:T(8,128)(2,1)}) %reduce-scatter.51.cloned.1.call-update) | async-done | bytes 983056 | tf_op jit(solution)/shard_map/reduce_scatter | solution.py:428
  3298.5 85.4 %reduce-scatter.49.cloned.1.call-done = bf16[5,192,512]{2,1,0:T(8,128)(2,1)} async-done(((bf16[5,1536,512]{2,1,0:T(8,128)(2,1)}), bf16[5,192,512]{2,1,0:T(8,128)(2,1)}) %reduce-scatter.49.cloned.1.call-update) | async-done | bytes 983056 | tf_op jit(solution)/shard_map/reduce_scatter | solution.py:428
  3387.5 136.9 %reduce-scatter.47.cloned.1.call-done = f32[1536,48]{0,1:T(8,128)} async-done(((f32[1536,1536]{0,1:T(8,128)}), f32[1536,48]{0,1:T(8,128)}) %reduce-scatter.47.cloned.1.call-update) | async-done | bytes 294928 | tf_op jit(solution)/shard_map/reduce_scatter | solution.py:422
  3524.4 140.9 %reduce-scatter.45.cloned.1.call-done = f32[1536,48]{0,1:T(8,128)} async-done(((f32[1536,1536]{0,1:T(8,128)}), f32[1536,48]{0,1:T(8,128)}) %reduce-scatter.45.cloned.1.call-update) | async-done | bytes 294928 | tf_op jit(solution)/shard_map/reduce_scatter | solution.py:422
  3667.2 139.0 %reduce-scatter.35.cloned.1.call-done = f32[48,1536]{1,0:T(8,128)} async-done(((f32[1536,1536]{1,0:T(8,128)}), f32[48,1536]{1,0:T(8,128)}) %reduce-scatter.35.cloned.1.call-update) | async-done | bytes 294928 | tf_op jit(solution)/shard_map/reduce_scatter | solution.py:419
  3806.2 141.0 %reduce-scatter.33.cloned.1.call-done = f32[48,1536]{1,0:T(8,128)} async-done(((f32[1536,1536]{1,0:T(8,128)}), f32[48,1536]{1,0:T(8,128)}) %reduce-scatter.33.cloned.1.call-update) | async-done | bytes 294928 | tf_op jit(solution)/shard_map/reduce_scatter | solution.py:419
  (533 shorter events, 996.0 us)
Async XLA Ops:
  10.3 182.3 %all-gather.51.cloned.1.call-start = ((), (), s32[]{:S(2)}) async-start(), calls=%async_computation.52 | async-start | bytes 4866048 | tf_op jit(solution)/shard_map/all_gather | solution.py:95
  12.1 207.4 %all-gather.41.cloned.1.call-start = ((), (), s32[]{:S(2)}) async-start(), calls=%async_computation.29 | async-start | bytes 1310720 | tf_op jit(solution)/shard_map/all_gather | solution.py:132
  129.4 185.6 %all-gather.53.cloned.1.call-start = ((), (), s32[]{:S(2)}) async-start(), calls=%async_computation.53 | async-start | bytes 4866048 | tf_op jit(solution)/shard_map/all_gather | solution.py:102
  130.2 263.0 %all-gather.55.cloned.1.call-start = ((), (), s32[]{:S(2)}) async-start(), calls=%async_computation.54 | async-start | bytes 8847360 | tf_op jit(solution)/shard_map/all_gather | solution.py:170
  133.2 353.2 %all-gather.57.cloned.1.call-start = ((), (), s32[]{:S(2)}) async-start(), calls=%async_computation.55 | async-start | bytes 8847360 | tf_op jit(solution)/shard_map/all_gather | solution.py:171
  136.2 413.4 %all-gather.59.cloned.1.call-start = ((), (), s32[]{:S(2)}) async-start(), calls=%async_computation.56 | async-start | bytes 8847360 | tf_op jit(solution)/shard_map/all_gather | solution.py:172
  342.7 465.1 %all-gather.63.cloned.1.call-start = ((), (), s32[]{:S(2)}) async-start(), calls=%async_computation.58 | async-start | bytes 1622016 | tf_op jit(solution)/shard_map/all_gather | solution.py:96
  343.3 467.9 %all-gather.61.cloned.1.call-start = ((), (), s32[]{:S(2)}) async-start(), calls=%async_computation.57 | async-start | bytes 1622016 | tf_op jit(solution)/shard_map/all_gather | solution.py:99
  572.0 205.1 %all-to-all-start.1 = ((bf16[4,5,192,1536]{3,2,1,0:T(8,128)(2,1)}), bf16[4,5,192,1536]{3,2,1,0:T(8,128)(2,1)}, u32[]{:S(2)}, u32[]{:S(2)}) async-start(bf16[4,5,192,1536]{3,2,1,0:T(8,128)(2,1)} %copy.104), calls=%async_computation.1 | async-start | bytes 23592960 | tf_op jit(solution)/shard_map/all_to_all | solution.py:182
  578.4 244.6 %all-gather.65.cloned.1.call-start = ((), (), s32[]{:S(2)}) async-start(), calls=%async_computation.59 | async-start | bytes 4866048 | tf_op jit(solution)/shard_map/all_gather | solution.py:95
  578.9 266.6 %all-gather.45.cloned.1.call-start = ((), (), s32[]{:S(2)}) async-start(), calls=%async_computation.31 | async-start | bytes 1310720 | tf_op jit(solution)/shard_map/all_gather | solution.py:132
  814.6 382.6 %all-gather.71.cloned.1.call-start = ((), (), s32[]{:S(2)}) async-start(), calls=%async_computation.62 | async-start | bytes 8847360 | tf_op jit(solution)/shard_map/all_gather | solution.py:171
  815.2 396.0 %all-gather.69.cloned.1.call-start = ((), (), s32[]{:S(2)}) async-start(), calls=%async_computation.61 | async-start | bytes 8847360 | tf_op jit(solution)/shard_map/all_gather | solution.py:170
  961.9 228.8 %all-to-all-start.2 = ((bf16[4,5,192,1536]{3,2,1,0:T(8,128)(2,1)}), bf16[4,5,192,1536]{3,2,1,0:T(8,128)(2,1)}, u32[]{:S(2)}, u32[]{:S(2)}) async-start(bf16[4,5,192,1536]{3,2,1,0:T(8,128)(2,1)} %bitcast.664), calls=%async_computation.2 | async-start | bytes 23592960 | tf_op jit(solution)/shard_map/all_to_all | solution.py:162
  968.3 256.7 %all-gather.73.cloned.1.call-start = ((), (), s32[]{:S(2)}) async-start(), calls=%async_computation.63 | async-start | bytes 8847360 | tf_op jit(solution)/shard_map/all_gather | solution.py:172
  1502.3 239.2 %reduce-scatter.25.cloned.1.call-start = ((), (), s32[]{:S(2)}) async-start(), calls=%async_computation.32 | async-start | bytes 1310720 | tf_op jit(solution)/shard_map/reduce_scatter | solution.py:376
  2000.8 222.2 %reduce-scatter.31.cloned.1.call-start = ((), (), s32[]{:S(2)}) async-start(), calls=%async_computation.35 | async-start | bytes 1310720 | tf_op jit(solution)/shard_map/reduce_scatter | solution.py:379
  2217.9 227.0 %reduce-scatter.61.cloned.1.call-start = ((), (), s32[]{:S(2)}) async-start(), calls=%async_computation.64 | async-start | bytes 811008
  2220.5 331.2 %reduce-scatter.43.cloned.1.call-start = ((), (), s32[]{:S(2)}) async-start(), calls=%async_computation.41 | async-start | bytes 3244032 | tf_op jit(solution)/shard_map/reduce_scatter | solution.py:421
  2222.9 435.3 %reduce-scatter.41.cloned.1.call-start = ((), (), s32[]{:S(2)}) async-start(), calls=%async_computation.40 | async-start | bytes 3244032 | tf_op jit(solution)/shard_map/reduce_scatter | solution.py:421
  2226.3 538.3 %reduce-scatter.39.cloned.1.call-start = ((), (), s32[]{:S(2)}) async-start(), calls=%async_computation.39 | async-start | bytes 3244032 | tf_op jit(solution)/shard_map/reduce_scatter | solution.py:420
  2228.8 642.5 %reduce-scatter.37.cloned.1.call-start = ((), (), s32[]{:S(2)}) async-start(), calls=%async_computation.38 | async-start | bytes 3244032 | tf_op jit(solution)/shard_map/reduce_scatter | solution.py:420
  2246.8 710.4 %reduce-scatter.59.cloned.1.call-start = ((), (), s32[]{:S(2)}) async-start(), calls=%async_computation.49 | async-start | bytes 8847360 | tf_op jit(solution)/shard_map/reduce_scatter | solution.py:434
  2259.1 783.3 %reduce-scatter.57.cloned.1.call-start = ((), (), s32[]{:S(2)}) async-start(), calls=%async_computation.48 | async-start | bytes 8847360 | tf_op jit(solution)/shard_map/reduce_scatter | solution.py:434
  2271.8 856.0 %reduce-scatter.55.cloned.1.call-start = ((), (), s32[]{:S(2)}) async-start(), calls=%async_computation.47 | async-start | bytes 8847360 | tf_op jit(solution)/shard_map/reduce_scatter | solution.py:431
  2284.2 929.1 %reduce-scatter.53.cloned.1.call-start = ((), (), s32[]{:S(2)}) async-start(), calls=%async_computation.46 | async-start | bytes 8847360 | tf_op jit(solution)/shard_map/reduce_scatter | solution.py:431
  2296.6 1001.9 %reduce-scatter.51.cloned.1.call-start = ((), (), s32[]{:S(2)}) async-start(), calls=%async_computation.45 | async-start | bytes 8847360 | tf_op jit(solution)/shard_map/reduce_scatter | solution.py:428
  2309.3 1074.6 %reduce-scatter.49.cloned.1.call-start = ((), (), s32[]{:S(2)}) async-start(), calls=%async_computation.44 | async-start | bytes 8847360 | tf_op jit(solution)/shard_map/reduce_scatter | solution.py:428
  2321.6 1202.8 %reduce-scatter.47.cloned.1.call-start = ((), (), s32[]{:S(2)}) async-start(), calls=%async_computation.43 | async-start | bytes 9732096 | tf_op jit(solution)/shard_map/reduce_scatter | solution.py:422
  2329.2 1336.1 %reduce-scatter.45.cloned.1.call-start = ((), (), s32[]{:S(2)}) async-start(), calls=%async_computation.42 | async-start | bytes 9732096 | tf_op jit(solution)/shard_map/reduce_scatter | solution.py:422
  2336.7 1469.5 %reduce-scatter.35.cloned.1.call-start = ((), (), s32[]{:S(2)}) async-start(), calls=%async_computation.37 | async-start | bytes 9732096 | tf_op jit(solution)/shard_map/reduce_scatter | solution.py:419
  2343.0 1604.3 %reduce-scatter.33.cloned.1.call-start = ((), (), s32[]{:S(2)}) async-start(), calls=%async_computation.36 | async-start | bytes 9732096 | tf_op jit(solution)/shard_map/reduce_scatter | solution.py:419
  (118 other events, 6466.3 us)
Sparse Core Ops, SparseCore 0:
  11.5 57.6 all-gather.48
  72.6 53.8 all-gather.46
  130.0 62.5 all-gather.50
  251.5 63.4 all-gather.52
  317.2 75.9 all-gather.54
  395.5 76.2 all-gather.56
  473.3 76.2 all-gather.58
  552.3 106.1 all-gather.62
  661.4 91.2 all-gather.60
  756.0 62.2 all-gather.64
  876.3 63.4 all-gather.66
  941.9 76.2 all-gather.70
  1020.2 76.2 all-gather.68
  1098.0 79.1 all-gather.72
  1707.0 34.3 reduce-scatter.24
  2171.4 27.9 reduce-scatter.30
  2248.4 96.2 reduce-scatter.62
  2349.7 95.2 reduce-scatter.60
  2450.4 101.2 reduce-scatter.42
  2557.0 101.2 reduce-scatter.40
  2663.5 101.1 reduce-scatter.38
  2770.1 101.1 reduce-scatter.36
  2873.6 83.5 reduce-scatter.58
  2959.4 83.0 reduce-scatter.56
  3044.8 83.0 reduce-scatter.54
  3130.2 83.0 reduce-scatter.52
  3215.4 83.0 reduce-scatter.50
  3300.8 83.0 reduce-scatter.48
  3389.8 134.6 reduce-scatter.46
  3530.2 135.1 reduce-scatter.44
  3671.1 135.0 reduce-scatter.34
  3812.1 135.0 reduce-scatter.32
  (6 shorter events, 157.7 us)
where the time goes:
time: 3960 us
  waiting for transfers between devices  2410 us (61%)
  blocking collectives  616 us (16%)
  matrix products  480 us (12%)
  local copies, waits for them, and re-layouts  205 us (5%)
  other arithmetic  182 us (5%)
  starting transfers between devices  47.4 us (1%)
    all_gather x2, blocking collectives, layer_forward(): lax.all_gather(router_weight[layer_index], ('dp', 'expert'), axis=0, tile...  395 us
    reduce_scatter x2, waiting for transfers between devices, body(): lax.psum_scatter(grad_query_w, ('dp', 'expert'), scatter_dimension=0, til...  280 us
    reduce_scatter x2, waiting for transfers between devices, body(): lax.psum_scatter(grad_output_w, ('dp', 'expert'), scatter_dimension=1, ti...  278 us
    all_to_all x2, waiting for transfers between devices, body(): lax.all_to_all(grad_rows, 'expert', split_axis=0, concat_axis=0, tiled=True)  214 us
    reduce_scatter x2, waiting for transfers between devices, body(): lax.psum_scatter(grad_key_w, ('dp', 'expert'), scatter_dimension=0, tiled...  211 us
    reduce_scatter x2, waiting for transfers between devices, body(): lax.psum_scatter(grad_down.astype(jnp.bfloat16), 'dp', scatter_dimension=...  170 us
    reduce_scatter x2, waiting for transfers between devices, body(): lax.psum_scatter(grad_up_w.astype(jnp.bfloat16), 'dp', scatter_dimension=...  167 us
    reduce_scatter x2, waiting for transfers between devices, body(): lax.psum_scatter(grad_gate_w.astype(jnp.bfloat16), 'dp', scatter_dimensio...  167 us
  transfers between devices with their start and end apart: 45, of which 34 were waited for; matrix products, arithmetic and copies ran while one was open for 15% of the time, Pallas kernels for 0%

commit v1 on v0

v1 whole, which is shorter than its diff:
```python
import math

import jax
import jax.numpy as jnp
from jax import lax
from jax.sharding import PartitionSpec as P

QUERY_HEADS = 24
KEY_VALUE_HEADS = 8
HEAD_SIZE = 64
LAYER_COUNT = 2


eps_norm = 1e-06
highest_precision = lax.Precision.HIGHEST


def rotary_tables(positions, half_dim):
    frequency = jnp.exp(-math.log(10000.0) * jnp.arange(half_dim, dtype=jnp.float32) / half_dim)
    angles = positions.astype(jnp.float32)[:, None] * frequency[None, :]
    return (jnp.cos(angles), jnp.sin(angles))


def rotate_features(values, cosine_table, sine_table):
    half_dim = values.shape[-1] // 2
    first_half = values[..., :half_dim]
    second_half = values[..., half_dim:]
    cos_part = cosine_table[:, None, :]
    sin_part = sine_table[:, None, :]
    return jnp.concatenate(
        [
            first_half * cos_part - second_half * sin_part,
            second_half * cos_part + first_half * sin_part,
        ],
        axis=-1,
    )


def norm_forward(values, gain_vec):
    inv_rms = lax.rsqrt(jnp.mean(values * values, axis=-1, keepdims=True) + eps_norm)
    return (values * inv_rms * gain_vec, inv_rms)


def norm_backward(values, inv_rms, gain_vec, upstream):
    scaled = upstream * gain_vec
    grad_gain = jnp.sum(upstream * values * inv_rms, axis=0)
    grad_values = inv_rms * (
        scaled - values * inv_rms * inv_rms * jnp.mean(scaled * values, axis=-1, keepdims=True)
    )
    return (grad_values, grad_gain)


def stack_member(layer_list, member):
    return jnp.stack([layer_parts[member] for layer_parts in layer_list], axis=0)


def exchange(blocks):
    return lax.all_to_all(blocks, "expert", split_axis=0, concat_axis=0, tiled=True)


def gather_rows(rows):
    groups = lax.axis_size("expert")
    blocks = exchange(jnp.broadcast_to(rows[None], (groups,) + rows.shape))
    return blocks.reshape((groups * rows.shape[0],) + rows.shape[1:])


def sum_rows(partial_rows):
    groups = lax.axis_size("expert")
    blocks = partial_rows.reshape((groups, -1) + partial_rows.shape[1:])
    return jnp.sum(exchange(blocks).astype(jnp.float32), axis=0)


def dot_f32(left, right, left_dims, right_dims):
    return lax.dot_general(
        left, right, ((left_dims, right_dims), ((), ())), preferred_element_type=jnp.float32
    )


def body(
    inputs,
    routes,
    cotangent,
    query_weight,
    key_projection_weight,
    value_projection_weight,
    output_weight,
    attention_gain,
    expert_gain,
    router_weight,
    gate_weight,
    up_weight,
    down_weight,
):
    sequences_per_device, block_length, model_width = inputs.shape
    token_total = sequences_per_device * block_length
    exp_dev = gate_weight.shape[1]
    groups = lax.axis_size("expert")
    expert_total = exp_dev * groups
    all_rows = token_total * groups
    query_width = query_weight.shape[2]
    key_width = key_projection_weight.shape[2]
    query_head_group = QUERY_HEADS // KEY_VALUE_HEADS
    score_scale = HEAD_SIZE ** (-0.5)
    my_group = lax.axis_index("expert")
    positions = my_group * block_length + jnp.arange(block_length, dtype=jnp.int32)
    cosine_table, sine_table = rotary_tables(positions, HEAD_SIZE // 2)
    causal = positions[:, None] >= jnp.arange(block_length * groups, dtype=jnp.int32)[None, :]
    expert_ids = jnp.arange(expert_total, dtype=jnp.int32)
    small_width = -(-(expert_total + 2) // 128) * 128
    gate_width = -(-(2 * expert_total) // 128) * 128
    edges = (
        query_width,
        query_width + key_width,
        query_width + 2 * key_width,
        query_width + 2 * key_width + model_width,
        query_width + 2 * key_width + model_width + expert_total,
        query_width + 2 * key_width + model_width + expert_total + 1,
    )

    def pack_attention(query_part, key_part, value_part, output_part, router_part, one, two):
        rows = query_part.shape[0]
        fill = jnp.zeros((rows, small_width - expert_total - 2), query_part.dtype)
        return jnp.concatenate(
            [
                query_part,
                key_part,
                value_part,
                output_part,
                router_part,
                one[:, None],
                two[:, None],
                fill,
            ],
            axis=1,
        )

    chosen_hot = jnp.any(
        routes.reshape(LAYER_COUNT, token_total, -1)[:, :, :, None] == expert_ids, axis=2
    )
    chosen_all = gather_rows(
        jnp.moveaxis(chosen_hot, 0, 1).reshape(token_total, -1).astype(jnp.bfloat16)
    ).reshape(all_rows, LAYER_COUNT, expert_total)

    packed = [
        lax.all_gather(
            pack_attention(
                query_weight[layer],
                key_projection_weight[layer],
                value_projection_weight[layer],
                output_weight[layer].T,
                router_weight[layer],
                attention_gain[layer],
                expert_gain[layer],
            ),
            ("dp", "expert"),
            axis=0,
            tiled=True,
        )
        for layer in range(LAYER_COUNT)
    ]
    gathered = [
        (
            lax.all_gather(gate_weight[layer], "dp", axis=1, tiled=True),
            lax.all_gather(up_weight[layer], "dp", axis=1, tiled=True),
            lax.all_gather(down_weight[layer], "dp", axis=2, tiled=True),
        )
        for layer in range(LAYER_COUNT)
    ]

    def shares_of(rows, router_full, hot):
        logits = jnp.dot(rows, router_full, preferred_element_type=jnp.float32)
        masked = jnp.where(hot, logits, -1e30)
        exps = jnp.where(hot, jnp.exp(masked - jnp.max(masked, axis=1, keepdims=True)), 0.0)
        return exps / jnp.sum(exps, axis=1, keepdims=True)

    def layer_forward(hidden, layer):
        full = packed[layer]
        qkv_full = full[:, : edges[2]]
        output_full = full[:, edges[2] : edges[3]]
        router_full = full[:, edges[3] : edges[4]]
        gain_one = full[:, edges[4]].astype(jnp.float32)
        gain_two = full[:, edges[5]].astype(jnp.float32)
        gate_full, up_full, down_full = gathered[layer]
        first_normalized, inv_one = norm_forward(hidden, gain_one)
        first_normalized = first_normalized.astype(jnp.bfloat16)
        linear = jnp.dot(first_normalized, qkv_full, preferred_element_type=jnp.float32)
        query_rotated = rotate_features(
            linear[:, : edges[0]].reshape(token_total, QUERY_HEADS, HEAD_SIZE),
            cosine_table,
            sine_table,
        ).astype(jnp.bfloat16)
        query_grouped = query_rotated.reshape(
            token_total, KEY_VALUE_HEADS, query_head_group, HEAD_SIZE
        )
        key_rot = rotate_features(
            linear[:, edges[0] : edges[1]].reshape(token_total, KEY_VALUE_HEADS, HEAD_SIZE),
            cosine_table,
            sine_table,
        ).astype(jnp.bfloat16)
        key_value = jnp.concatenate(
            [
                key_rot.reshape(token_total, key_width),
                linear[:, edges[1] :].astype(jnp.bfloat16),
            ],
            axis=1,
        )
        key_value_all = gather_rows(key_value).reshape(all_rows, 2, KEY_VALUE_HEADS, HEAD_SIZE)
        key_all, value_all = key_value_all[:, 0], key_value_all[:, 1]
        scores = (
            jnp.einsum("qhgd,khd->hgqk", query_grouped, key_all, preferred_element_type=jnp.float32)
            * score_scale
        )
        masked = jnp.where(causal, scores, -1e30)
        row_max = jnp.max(masked, axis=-1, keepdims=True)
        exp_scores = jnp.exp(masked - row_max)
        row_total = jnp.sum(exp_scores, axis=-1, keepdims=True)
        log_total = row_max + jnp.log(row_total)
        prob_low = (exp_scores / row_total).astype(jnp.bfloat16)
        attended = jnp.einsum(
            "hgqk,khd->qhgd", prob_low, value_all, preferred_element_type=jnp.float32
        )
        attended = attended.reshape(token_total, query_width).astype(jnp.bfloat16)
        middle = hidden + dot_f32(attended, output_full, (1,), (1,))
        normed_two, inv_two = norm_forward(middle, gain_two)
        normed_two = normed_two.astype(jnp.bfloat16)
        arrived = gather_rows(normed_two)
        share_all = shares_of(arrived, router_full, chosen_all[:, layer] > 0)
        share_own = shares_of(normed_two, router_full, chosen_hot[layer])
        share_local = lax.dynamic_slice_in_dim(share_all, my_group * exp_dev, exp_dev, axis=1)
        gate_val = jnp.einsum("td,edf->tef", arrived, gate_full, preferred_element_type=jnp.float32)
        up_val = jnp.einsum("td,edf->tef", arrived, up_full, preferred_element_type=jnp.float32)
        scaled_act = (jax.nn.silu(gate_val) * up_val * share_local[:, :, None]).astype(jnp.bfloat16)
        out_rows = jnp.einsum(
            "tef,efd->td", scaled_act, down_full, preferred_element_type=jnp.float32
        ).astype(jnp.bfloat16)
        output = middle + sum_rows(out_rows)
        kept_state = (
            hidden,
            inv_one,
            first_normalized,
            query_grouped,
            key_all,
            value_all,
            log_total,
            attended,
            middle,
            inv_two,
            normed_two,
            share_own,
            share_local,
            arrived,
            gate_val.astype(jnp.bfloat16),
            up_val.astype(jnp.bfloat16),
            scaled_act,
            qkv_full,
            output_full,
            gain_one,
            gain_two,
            router_full,
            gate_full,
            up_full,
            down_full,
        )
        return (output, kept_state)

    hidden = inputs.astype(jnp.float32).reshape(token_total, model_width)
    kept_states = []
    for layer in range(LAYER_COUNT):
        hidden, kept_state = layer_forward(hidden, layer)
        kept_states.append(kept_state)
    output = hidden.astype(jnp.bfloat16).reshape(sequences_per_device, block_length, model_width)
    grad_hidden = cotangent.astype(jnp.float32).reshape(token_total, model_width)
    attention_list = [None] * LAYER_COUNT
    expert_list = [None] * LAYER_COUNT
    for layer in range(LAYER_COUNT - 1, -1, -1):
        (
            layer_hidden,
            inv_one,
            first_normalized,
            query_grouped,
            key_all,
            value_all,
            log_total,
            attended,
            middle,
            inv_two,
            normed_two,
            share_own,
            share_local,
            arrived,
            gate_low,
            up_low,
            scaled_act,
            qkv_full,
            output_full,
            gain_one,
            gain_two,
            router_full,
            gate_full,
            up_full,
            down_full,
        ) = kept_states[layer]
        grad_all = gather_rows(grad_hidden.astype(jnp.bfloat16))
        grad_down = jnp.einsum(
            "tef,td->efd", scaled_act, grad_all, preferred_element_type=jnp.float32
        ).astype(jnp.bfloat16)
        grad_scaled = jnp.einsum(
            "td,efd->tef", grad_all, down_full, preferred_element_type=jnp.float32
        )
        gate_val = gate_low.astype(jnp.float32)
        up_val = up_low.astype(jnp.float32)
        sigmoid_val = jax.nn.sigmoid(gate_val)
        silu_val = gate_val * sigmoid_val
        grad_gates = jnp.sum(grad_scaled * silu_val * up_val, axis=2)
        grad_inner = grad_scaled * share_local[:, :, None]
        grad_gate_val = (
            grad_inner * up_val * sigmoid_val * (1.0 + gate_val * (1.0 - sigmoid_val))
        ).astype(jnp.bfloat16)
        grad_up_val = (grad_inner * silu_val).astype(jnp.bfloat16)
        grad_gate_w = jnp.einsum(
            "td,tef->edf", arrived, grad_gate_val, preferred_element_type=jnp.float32
        ).astype(jnp.bfloat16)
        grad_up_w = jnp.einsum(
            "td,tef->edf", arrived, grad_up_val, preferred_element_type=jnp.float32
        ).astype(jnp.bfloat16)
        grad_rows = jnp.einsum(
            "tef,edf->td", grad_gate_val, gate_full, preferred_element_type=jnp.float32
        ) + jnp.einsum("tef,edf->td", grad_up_val, up_full, preferred_element_type=jnp.float32)
        gates_high = grad_gates.astype(jnp.bfloat16)
        gates_low = (grad_gates - gates_high.astype(jnp.float32)).astype(jnp.bfloat16)
        gate_columns = jnp.zeros((all_rows, gate_width), jnp.bfloat16)
        gate_columns = lax.dynamic_update_slice_in_dim(
            gate_columns, gates_high, my_group * exp_dev, axis=1
        )
        gate_columns = lax.dynamic_update_slice_in_dim(
            gate_columns, gates_low, expert_total + my_group * exp_dev, axis=1
        )
        back = sum_rows(
            jnp.concatenate([grad_rows.astype(jnp.bfloat16), gate_columns], axis=1)
        )
        grad_gates_own = (
            back[:, model_width : model_width + expert_total]
            + back[:, model_width + expert_total : model_width + 2 * expert_total]
        )
        grad_logits = (
            share_own
            * (grad_gates_own - jnp.sum(share_own * grad_gates_own, axis=-1, keepdims=True))
        ).astype(jnp.bfloat16)
        grad_router = dot_f32(normed_two, grad_logits, (0,), (0,))
        grad_normed_two = back[:, :model_width] + dot_f32(grad_logits, router_full, (1,), (1,))
        grad_norm_mid, grad_gain_two = norm_backward(middle, inv_two, gain_two, grad_normed_two)
        grad_middle = grad_hidden + grad_norm_mid
        grad_branch = grad_middle.astype(jnp.bfloat16)
        grad_output_w = dot_f32(grad_branch, attended, (0,), (0,))
        grad_attended = (
            dot_f32(grad_branch, output_full, (1,), (0,))
            .astype(jnp.bfloat16)
            .reshape(token_total, KEY_VALUE_HEADS, query_head_group, HEAD_SIZE)
        )
        layer_scores = (
            jnp.einsum("qhgd,khd->hgqk", query_grouped, key_all, preferred_element_type=jnp.float32)
            * score_scale
        )
        softmax_probs = jnp.exp(jnp.where(causal, layer_scores, -1e30) - log_total)
        grad_probs = jnp.einsum(
            "qhgd,khd->hgqk", grad_attended, value_all, preferred_element_type=jnp.float32
        )
        grad_scores = (
            softmax_probs
            * (grad_probs - jnp.sum(softmax_probs * grad_probs, axis=-1, keepdims=True))
        ).astype(jnp.bfloat16)
        grad_query = (
            jnp.einsum("hgqk,khd->qhgd", grad_scores, key_all, preferred_element_type=jnp.float32)
            * score_scale
        )
        grad_key_all = (
            jnp.einsum(
                "hgqk,qhgd->khd", grad_scores, query_grouped, preferred_element_type=jnp.float32
            )
            * score_scale
        )
        grad_value_all = jnp.einsum(
            "hgqk,qhgd->khd",
            softmax_probs.astype(jnp.bfloat16),
            grad_attended,
            preferred_element_type=jnp.float32,
        )
        grad_kv = sum_rows(
            jnp.concatenate(
                [
                    grad_key_all.reshape(all_rows, key_width).astype(jnp.bfloat16),
                    grad_value_all.reshape(all_rows, key_width).astype(jnp.bfloat16),
                ],
                axis=1,
            )
        )
        grad_query_lin = (
            rotate_features(
                grad_query.reshape(token_total, QUERY_HEADS, HEAD_SIZE), cosine_table, -sine_table
            )
            .astype(jnp.bfloat16)
            .reshape(token_total, query_width)
        )
        grad_key_lin = (
            rotate_features(
                grad_kv[:, :key_width].reshape(token_total, KEY_VALUE_HEADS, HEAD_SIZE),
                cosine_table,
                -sine_table,
            )
            .astype(jnp.bfloat16)
            .reshape(token_total, key_width)
        )
        grad_linear = jnp.concatenate(
            [grad_query_lin, grad_key_lin, grad_kv[:, key_width:].astype(jnp.bfloat16)], axis=1
        )
        grad_qkv_w = dot_f32(first_normalized, grad_linear, (0,), (0,))
        grad_normed_one = dot_f32(grad_linear, qkv_full, (1,), (1,))
        grad_norm_in, grad_gain_one = norm_backward(
            layer_hidden, inv_one, gain_one, grad_normed_one
        )
        fill = jnp.zeros((model_width, small_width - expert_total - 2), jnp.bfloat16)
        small_part = jnp.concatenate(
            [
                grad_router.astype(jnp.bfloat16),
                grad_gain_one[:, None].astype(jnp.bfloat16),
                grad_gain_two[:, None].astype(jnp.bfloat16),
                fill,
            ],
            axis=1,
        )
        attention_list[layer] = lax.psum_scatter(
            jnp.concatenate(
                [
                    grad_qkv_w.astype(jnp.bfloat16),
                    grad_output_w.astype(jnp.bfloat16),
                    small_part,
                ],
                axis=1,
            ),
            ("dp", "expert"),
            scatter_dimension=0,
            tiled=True,
        ).astype(jnp.float32)
        expert_list[layer] = (
            lax.psum_scatter(grad_gate_w, "dp", scatter_dimension=1, tiled=True),
            lax.psum_scatter(grad_up_w, "dp", scatter_dimension=1, tiled=True),
            lax.psum_scatter(grad_down, "dp", scatter_dimension=2, tiled=True),
        )
        grad_hidden = grad_middle + grad_norm_in
    stacked = jnp.stack(attention_list)
    return (
        output,
        grad_hidden.reshape(sequences_per_device, block_length, model_width),
        stacked[:, :, : edges[0]],
        stacked[:, :, edges[0] : edges[1]],
        stacked[:, :, edges[1] : edges[2]],
        jnp.swapaxes(stacked[:, :, edges[2] : edges[3]], 1, 2),
        stacked[:, :, edges[4]],
        stacked[:, :, edges[5]],
        stacked[:, :, edges[3] : edges[4]],
        stack_member(expert_list, 0).astype(jnp.float32),
        stack_member(expert_list, 1).astype(jnp.float32),
        stack_member(expert_list, 2).astype(jnp.float32),
    )


def solution(mesh):
    in_specs = (
        P("dp", "expert", None),
        P(None, "expert", "dp", None, None),
        P("dp", "expert", None),
        P(None, ("dp", "expert"), None),
        P(None, ("dp", "expert"), None),
        P(None, ("dp", "expert"), None),
        P(None, None, ("dp", "expert")),
        P(None, ("dp", "expert")),
        P(None, ("dp", "expert")),
        P(None, ("dp", "expert"), None),
        P(None, "expert", "dp", None),
        P(None, "expert", "dp", None),
        P(None, "expert", None, "dp"),
    )
    out_specs = (
        P("dp", "expert", None),
        P("dp", "expert", None),
        P(None, ("dp", "expert"), None),
        P(None, ("dp", "expert"), None),
        P(None, ("dp", "expert"), None),
        P(None, None, ("dp", "expert")),
        P(None, ("dp", "expert")),
        P(None, ("dp", "expert")),
        P(None, ("dp", "expert"), None),
        P(None, "expert", "dp", None),
        P(None, "expert", "dp", None),
        P(None, "expert", None, "dp"),
    )
    return jax.shard_map(body, mesh=mesh, in_specs=in_specs, out_specs=out_specs, check_vma=False)
```

time: 3960 us -> 1780 us (0.45)
  waiting for transfers between devices: 2410 us -> 742 us
  blocking collectives: 616 us -> 78.4 us
  local copies, waits for them, and re-layouts: 205 us -> 286 us
  other arithmetic: 182 us -> 119 us
    reduce_scatter x18 -> x4, waiting for transfers between devices: 1480 us -> 292 us  [the longest x2 292 us: body(): lax.psum_scatter(jnp.concatenate([grad_qkv_w.astype(jnp.bfloat16), grad_o...]
    all_gather x2 -> x0, blocking collectives: 395 us -> none  [layer_forward(): lax.all_gather(router_weight[layer_index], ('dp', 'expert'), axis=0, tile...]
    all_to_all x7 -> x11, waiting for transfers between devices: 472 us -> 142 us  [exchange(): lax.all_to_all(blocks, 'expert', split_axis=0, concat_axis=0, tiled=True)]
    unnamed x229 -> x215, local copies, waits for them, and re-layouts: 23.5 us -> 165 us
    unnamed x40 -> x20, waiting for transfers between devices: 92.2 us -> 1.63 us
    unnamed x2 -> x0, blocking collectives: 82.7 us -> none
    gather x4 -> x0, local copies, waits for them, and re-layouts: 77.5 us -> none  [the longest x2 38.9 us: body(): grad_back.reshape(expert_total * capacity, model_width)[layer_dest_row]]
    all_to_all x1 -> x2, blocking collectives: 139 us -> 78.4 us  [exchange(): lax.all_to_all(blocks, 'expert', split_axis=0, concat_axis=0, tiled=True)]
  transfers between devices with their start and end apart: 45 -> 27, of which waited for: 34 -> 16; matrix products, arithmetic and copies ran while one was open for 15% -> 44% of each run, Pallas kernels for 0% -> 0%
where the time goes in v1:
time: 1780 us; the launch traced here: 1770 us
  waiting for transfers between devices  742 us (42%)
  matrix products  477 us (27%)
  local copies, waits for them, and re-layouts  286 us (16%)
  other arithmetic  119 us (7%)
  blocking collectives  78.4 us (4%)
  starting transfers between devices  51.5 us (3%)
    reduce_scatter x2, waiting for transfers between devices, body(): lax.psum_scatter(jnp.concatenate([grad_qkv_w.astype(jnp.bfloat16), grad_o...  292 us
    all_gather x2, waiting for transfers between devices, body(): lax.all_gather(pack_attention(query_weight[layer], key_projection_weight[...  182 us
    unnamed x215, local copies, waits for them, and re-layouts  165 us
    all_to_all x11, waiting for transfers between devices, exchange(): lax.all_to_all(blocks, 'expert', split_axis=0, concat_axis=0, tiled=True)  142 us
    all_gather x2, waiting for transfers between devices, body(): lax.all_gather(down_weight[layer], 'dp', axis=2, tiled=True)  119 us
    all_to_all x2, blocking collectives, exchange(): lax.all_to_all(blocks, 'expert', split_axis=0, concat_axis=0, tiled=True)  78.4 us
    dot_general x14, matrix products, dot_f32(): lax.dot_general(left, right, ((left_dims, right_dims), ((), ())), preferr...  56.9 us
    all_to_all x11, starting transfers between devices, exchange(): lax.all_to_all(blocks, 'expert', split_axis=0, concat_axis=0, tiled=True)  50.3 us
  transfers between devices with their start and end apart: 27, of which 16 were waited for; matrix products, arithmetic and copies ran while one was open for 44% of the time, Pallas kernels for 0%

profile of v1, /device:TPU:0, one launch (start us, length us, event | category | flops | bytes accessed | tf_op | source)
XLA Modules:
  0.0 1769.2 jit_solution(14729369324557074277)
XLA Ops:
  24.3 89.5 %all-gather.15.cloned.1.call-done = bf16[1536,4224]{1,0:T(8,128)(2,1)} async-done(((bf16[48,4224]{1,0:T(8,128)(2,1)}), bf16[1536,4224]{1,0:T(8,128)(2,1)}) %all-gather.15.cloned.1.call-update) | async-done | bytes 12976144 | tf_op jit(solution)/shard_map/all_gather | solution.py:145
  137.5 16.4 all-to-all-done
  213.8 34.3 %all-to-all-done.1 = bf16[4,256,1536]{2,1,0:T(8,128)(2,1)} async-done(((bf16[4,256,1536]{2,1,0:T(8,128)(2,1)}), bf16[4,256,1536]{2,1,0:T(8,128)(2,1)}, u32[]{:S(2)}, u32[]{:S(2)}) %all-to-all-start.1) | async-done | bytes 3145760 | tf_op jit(solution)/shard_map/all_to_all | solution.py:58
  251.3 14.0 fusion.58
  270.1 17.5 multiply_convert_fusion.3
  287.6 60.2 %all-gather.23.cloned.1.call-done = bf16[1,5,512,1536]{2,3,1,0:T(8,128)(2,1)} async-done(((bf16[1,5,512,192]{2,3,1,0:T(8,128)(2,1)}), bf16[1,5,512,1536]{2,3,1,0:T(8,128)(2,1)}) %all-gather.23.cloned.1.call-update) | async-done | bytes 7864336 | tf_op jit(solution)/shard_map/all_gather | solution.py:165
  347.8 13.6 bitcast_convert_fusion.1
  366.1 92.6 %all-gather.17.cloned.1.call-done = bf16[1536,4224]{1,0:T(8,128)(2,1)} async-done(((bf16[48,4224]{1,0:T(8,128)(2,1)}), bf16[1536,4224]{1,0:T(8,128)(2,1)}) %all-gather.17.cloned.1.call-update) | async-done | bytes 12976144 | tf_op jit(solution)/shard_map/all_gather | solution.py:145
  484.8 19.2 %all-to-all-done.4 = bf16[4,256,1024]{1,2,0:T(8,128)(2,1)} async-done(((bf16[4,256,1024]{1,2,0:T(8,128)(2,1)}), bf16[4,256,1024]{1,2,0:T(8,128)(2,1)}, u32[]{:S(2)}, u32[]{:S(2)}) %all-to-all-start.4) | async-done | bytes 2097184 | tf_op jit(solution)/shard_map/all_to_all | solution.py:58
  553.3 38.8 %all_to_all.65 = bf16[4,256,1536]{2,1,0:T(8,128)(2,1)S(1)} all-to-all(bf16[4,256,1536]{2,1,0:T(8,128)(2,1)S(1)} %broadcast_in_dim.54), channel_id=1, replica_groups=mesh['dp'=8,'expert'=4] {'expert'}, dimensions={0} | all-to-all | bytes 6291456 | tf_op jit(solution)/shard_map/all_to_all | solution.py:58
  633.3 58.9 %all-gather.29.cloned.1.call-done = bf16[1,5,512,1536]{2,3,1,0:T(8,128)(2,1)} async-done(((bf16[1,5,512,192]{2,3,1,0:T(8,128)(2,1)}), bf16[1,5,512,1536]{2,3,1,0:T(8,128)(2,1)}) %all-gather.29.cloned.1.call-update) | async-done | bytes 7864336 | tf_op jit(solution)/shard_map/all_gather | solution.py:165
  692.2 25.9 %fusion.20 = (bf16[1024,5,512]{0,2,1:T(8,128)(2,1)}, f32[1024,5]{0,1:T(8,128)S(1)}, bf16[1024,5,512]{0,2,1:T(8,128)(2,1)}, bf16[1024,5,512]{0,2,1:T(8,128)(2,1)S(1)}) fusion(f32[1024,5]{0,1:T(8,128)S(1)} %dynamic-slice_divide_fusion, f32[1024,5,512]{0,2,1:T(8,128)} %fusion.42, f32[1024,5,512]{0,2,1:T(8,128)} %fusion.46, ...), kind=kOutput, calls=%fused_computation.42 | convolution fusion | flops 8126458880 | bytes 47751168 | tf_op jit(solution)/shard_map/td,efd->tef/dot_general | solution.py:307
  730.9 15.8 copy.410
  760.8 13.5 bitcast_convert_fusion
  836.6 15.7 copy.406
  882.3 21.4 %fusion.3 = (f32[8,3,256]{2,1,0:T(4,128)S(1)}, f32[8,1024,256,3]{2,1,3,0:T(8,128)}) fusion(f32[8,3,256]{2,1,0:T(4,128)S(1)} %log_add_fusion.1, f32[8,1024,256,3]{2,1,3,0:T(8,128)} %get-tuple-element.161, pred[256,1024]{0,1:T(8,128)(4,1)S(1)} %copy-done.3, bf16[256,8,3,64]{0,3,2,1:T(8,128)(2,1)S(1)} %bitcast.483, bf16[1024,2,8,64]{0,3,2,1:T(8,128)(2,1)S(1)} %copy-done.17), kind=kOutput, calls=%fused_computation.7 | convolution fusion | flops 836757504 | bytes 52486144 | tf_op jit(solution)/shard_map/qhgd,khd->hgqk/dot_general | solution.py:365
  903.7 17.5 fusion.5
  962.6 16.6 all-to-all-done.9
  989.0 39.6 %all_to_all.66 = bf16[4,256,1536]{2,1,0:T(8,128)(2,1)} all-to-all(bf16[4,256,1536]{2,1,0:T(8,128)(2,1)S(1)} %broadcast_in_dim.58), channel_id=1, replica_groups=mesh['dp'=8,'expert'=4] {'expert'}, dimensions={0} | all-to-all | bytes 6291456 | tf_op jit(solution)/shard_map/all_to_all | solution.py:58
  1028.6 22.7 %fusion.24 = (bf16[1024,5,512]{0,2,1:T(8,128)(2,1)}, f32[1024,5]{0,1:T(8,128)}, bf16[1024,5,512]{0,2,1:T(8,128)(2,1)}) fusion(f32[1024,5]{0,1:T(8,128)S(1)} %copy-done.82, bf16[1024,5,512]{0,2,1:T(8,128)(2,1)} %get-tuple-element.159, f32[1024,5,512]{0,2,1:T(8,128)} %fusion.58, bf16[1024,1536,1]{1,0,2:T(8,128)(2,1)} %bitcast.476, ...), kind=kOutput, calls=%fused_computation.46 | convolution fusion | flops 8105487360 | bytes 37265408 | tf_op jit(solution)/shard_map/td,efd->tef/dot_general | solution.py:307
  1064.7 16.1 copy.408
  1093.8 13.5 convert_bitcast_fusion.3
  1107.3 15.8 copy.404
  1136.1 13.7 convolution_convert_fusion.4
  1149.9 13.5 convolution_convert_fusion.5
  1179.3 19.8 %concatenate.103 = bf16[1536,4224]{1,0:T(8,128)(2,1)} concatenate(bf16[1536,2560]{1,0:T(8,128)(2,1)} %convolution_convert_fusion, bf16[1536,1536]{1,0:T(8,128)(2,1)} %convolution_convert_fusion.2, bf16[1536,20]{1,0:T(8,128)(2,1)S(1)} %copy.350, bf16[1536,1]{1,0:T(8,128)(2,1)S(1)} %convert_element_type.538, bf16[1536,1]{1,0:T(8,128)(2,1)S(1)} %copy-done.46, ...), dimensions={1} | concatenate | bytes 25952256 | tf_op jit(solution)/shard_map/concatenate | solution.py:432
  1237.2 35.9 %all-to-all-done.11 = bf16[4,256,1664]{2,1,0:T(8,128)(2,1)} async-done(((bf16[4,256,1664]{2,1,0:T(8,128)(2,1)}), bf16[4,256,1664]{2,1,0:T(8,128)(2,1)}, u32[]{:S(2)}, u32[]{:S(2)}) %all-to-all-start.11) | async-done | bytes 3407904 | tf_op jit(solution)/shard_map/all_to_all | solution.py:58
  1285.8 21.3 %fusion = (f32[8,3,256]{2,1,0:T(4,128)S(1)}, f32[8,1024,256,3]{2,1,3,0:T(8,128)}) fusion(f32[8,3,256]{2,1,0:T(4,128)S(1)} %log_add_fusion, f32[8,1024,256,3]{2,1,3,0:T(8,128)} %get-tuple-element.153, pred[256,1024]{0,1:T(8,128)(4,1)S(1)} %copy-done.4, bf16[256,8,3,64]{0,3,2,1:T(8,128)(2,1)S(1)} %bitcast.481, bf16[1024,2,8,64]{0,3,2,1:T(8,128)(2,1)S(1)} %copy-done.14), kind=kOutput, calls=%fused_computation.2 | convolution fusion | flops 836757504 | bytes 52486144 | tf_op jit(solution)/shard_map/qhgd,khd->hgqk/dot_general | solution.py:365
  1307.1 17.5 fusion.2
  1399.0 19.8 %concatenate.102 = bf16[1536,4224]{1,0:T(8,128)(2,1)} concatenate(bf16[1536,2560]{1,0:T(8,128)(2,1)} %convolution_convert_fusion.1, bf16[1536,1536]{1,0:T(8,128)(2,1)} %convolution_convert_fusion.3, bf16[1536,20]{1,0:T(8,128)(2,1)} %copy.346, bf16[1536,1]{1,0:T(8,128)(2,1)} %convert_element_type.536, bf16[1536,1]{1,0:T(8,128)(2,1)} %convert_element_type.537, ...), dimensions={1} | concatenate | bytes 25952256 | tf_op jit(solution)/shard_map/concatenate | solution.py:432
  1463.3 129.9 %reduce-scatter.19.cloned.1.call-done = bf16[48,4224]{1,0:T(8,128)(2,1)} async-done(((bf16[1536,4224]{1,0:T(8,128)(2,1)}), bf16[48,4224]{1,0:T(8,128)(2,1)}) %reduce-scatter.19.cloned.1.call-update) | async-done | bytes 405520 | tf_op jit(solution)/shard_map/reduce_scatter | solution.py:431
  1593.2 162.3 %reduce-scatter.17.cloned.1.call-done = bf16[48,4224]{1,0:T(8,128)(2,1)} async-done(((bf16[1536,4224]{1,0:T(8,128)(2,1)}), bf16[48,4224]{1,0:T(8,128)(2,1)}) %reduce-scatter.17.cloned.1.call-update) | async-done | bytes 405520 | tf_op jit(solution)/shard_map/reduce_scatter | solution.py:431
  (462 shorter events, 630.4 us)
Async XLA Ops:
  7.2 106.6 %all-gather.15.cloned.1.call-start = ((), (), s32[]{:S(2)}) async-start(), calls=%async_computation.21 | async-start | bytes 13381632 | tf_op jit(solution)/shard_map/all_gather | solution.py:145
  13.7 237.5 %all-gather.19.cloned.1.call-start = ((), (), s32[]{:S(2)}) async-start(), calls=%async_computation.27 | async-start | bytes 8847360 | tf_op jit(solution)/shard_map/all_gather | solution.py:163
  16.7 253.4 %all-gather.21.cloned.1.call-start = ((), (), s32[]{:S(2)}) async-start(), calls=%async_computation.28 | async-start | bytes 8847360 | tf_op jit(solution)/shard_map/all_gather | solution.py:164
  18.3 329.5 %all-gather.23.cloned.1.call-start = ((), (), s32[]{:S(2)}) async-start(), calls=%async_computation.29 | async-start | bytes 8847360 | tf_op jit(solution)/shard_map/all_gather | solution.py:165
  21.3 437.4 %all-gather.17.cloned.1.call-start = ((), (), s32[]{:S(2)}) async-start(), calls=%async_computation.22 | async-start | bytes 13381632 | tf_op jit(solution)/shard_map/all_gather | solution.py:145
  22.6 578.2 %all-gather.25.cloned.1.call-start = ((), (), s32[]{:S(2)}) async-start(), calls=%async_computation.30 | async-start | bytes 8847360 | tf_op jit(solution)/shard_map/all_gather | solution.py:163
  23.5 97.5 %copy-start.85 = (f32[256]{0:T(256)}, f32[256]{0:T(256)S(1)}, u32[]{:S(2)}) copy-start(f32[256]{0:T(256)S(1)} %add_rsqrt_fusion.3) | copy-start | bytes 3076
  24.3 98.5 %copy-start.39 = (f32[256,32]{0,1:T(8,128)}, f32[256,32]{0,1:T(8,128)S(1)}, u32[]{:S(2)}) copy-start(f32[256,32]{0,1:T(8,128)S(1)} %get-tuple-element.147) | copy-start | bytes 98308
  24.3 98.5 %copy-start.56 = (f32[256,32]{0,1:T(8,128)}, f32[256,32]{0,1:T(8,128)S(1)}, u32[]{:S(2)}) copy-start(f32[256,32]{0,1:T(8,128)S(1)} %get-tuple-element.146) | copy-start | bytes 98308
  124.8 29.2 %all-to-all-start = ((bf16[4,256,1024]{1,2,0:T(8,128)(2,1)}), bf16[4,256,1024]{1,2,0:T(8,128)(2,1)S(1)}, u32[]{:S(2)}, u32[]{:S(2)}) async-start(bf16[4,256,1024]{1,2,0:T(8,128)(2,1)} %broadcast_in_dim.46), calls=%async_computation | async-start | bytes 4194304 | tf_op jit(solution)/shard_map/all_to_all | solution.py:58
  129.3 406.7 %copy-start.2 = (pred[256,1024]{0,1:T(8,128)(4,1)}, pred[256,1024]{0,1:T(8,128)(4,1)S(1)}, u32[]{:S(2)}) copy-start(pred[256,1024]{0,1:T(8,128)(4,1)S(1)} %iota_compare_fusion) | copy-start | bytes 786436
  155.3 49.9 %all-to-all-start.2 = ((bf16[4,256,40]{1,2,0:T(8,128)(2,1)}), bf16[4,256,40]{1,2,0:T(8,128)(2,1)}, u32[]{:S(2)}, u32[]{:S(2)}) async-start(bf16[4,256,40]{1,2,0:T(8,128)(2,1)} %broadcast_in_dim.50), calls=%async_computation.2 | async-start | bytes 163840 | tf_op jit(solution)/shard_map/all_to_all | solution.py:58
  205.0 258.0 %copy-start.5 = (f32[256,1536]{1,0:T(8,128)}, f32[256,1536]{1,0:T(8,128)S(1)}, u32[]{:S(2)}) copy-start(f32[256,1536]{1,0:T(8,128)S(1)} %get-tuple-element.155) | copy-start | bytes 4718596
  207.4 40.7 %all-to-all-start.1 = ((bf16[4,256,1536]{2,1,0:T(8,128)(2,1)}), bf16[4,256,1536]{2,1,0:T(8,128)(2,1)}, u32[]{:S(2)}, u32[]{:S(2)}) async-start(bf16[4,256,1536]{2,1,0:T(8,128)(2,1)} %broadcast_in_dim.49), calls=%async_computation.1 | async-start | bytes 6291456 | tf_op jit(solution)/shard_map/all_to_all | solution.py:58
  212.1 402.2 %all-gather.27.cloned.1.call-start = ((), (), s32[]{:S(2)}) async-start(), calls=%async_computation.31 | async-start | bytes 8847360 | tf_op jit(solution)/shard_map/all_gather | solution.py:164
  361.4 99.0 %all-to-all-start.3 = ((bf16[4,256,1536]{2,1,0:T(8,128)(2,1)}), bf16[4,256,1536]{2,1,0:T(8,128)(2,1)}, u32[]{:S(2)}, u32[]{:S(2)}) async-start(bf16[4,256,1536]{2,1,0:T(8,128)(2,1)} %bitcast.479), calls=%async_computation.3 | async-start | bytes 6291456 | tf_op jit(solution)/shard_map/all_to_all | solution.py:58
  473.9 30.1 %all-to-all-start.4 = ((bf16[4,256,1024]{1,2,0:T(8,128)(2,1)}), bf16[4,256,1024]{1,2,0:T(8,128)(2,1)}, u32[]{:S(2)}, u32[]{:S(2)}) async-start(bf16[4,256,1024]{1,2,0:T(8,128)(2,1)} %broadcast_in_dim.53), calls=%async_computation.4 | async-start | bytes 4194304 | tf_op jit(solution)/shard_map/all_to_all | solution.py:58
  478.3 213.8 %all-gather.29.cloned.1.call-start = ((), (), s32[]{:S(2)}) async-start(), calls=%async_computation.32 | async-start | bytes 8847360 | tf_op jit(solution)/shard_map/all_gather | solution.py:165
  594.0 39.3 %all-to-all-start.7 = ((bf16[4,256,1536]{2,1,0:T(8,128)(2,1)}), bf16[4,256,1536]{2,1,0:T(8,128)(2,1)}, u32[]{:S(2)}, u32[]{:S(2)}) async-start(bf16[4,256,1536]{2,1,0:T(8,128)(2,1)} %broadcast_in_dim.55), calls=%async_computation.7 | async-start | bytes 6291456 | tf_op jit(solution)/shard_map/all_to_all | solution.py:58
  598.7 823.2 %reduce-scatter.31.cloned.1.call-start = ((), (), s32[]{:S(2)}) async-start(), calls=%async_computation.36 | async-start | bytes 8847360
  774.3 41.8 %all-to-all-start.6 = ((bf16[4,256,1536]{2,1,0:T(8,128)(2,1)}), bf16[4,256,1536]{2,1,0:T(8,128)(2,1)}, u32[]{:S(2)}, u32[]{:S(2)}) async-start(bf16[4,256,1536]{2,1,0:T(8,128)(2,1)} %bitcast.478), calls=%async_computation.6 | async-start | bytes 6291456 | tf_op jit(solution)/shard_map/all_to_all | solution.py:58
  816.2 51.8 %all-to-all-start.8 = ((bf16[4,256,1664]{2,1,0:T(8,128)(2,1)}), bf16[4,256,1664]{2,1,0:T(8,128)(2,1)}, u32[]{:S(2)}, u32[]{:S(2)}) async-start(bf16[4,256,1664]{2,1,0:T(8,128)(2,1)} %bitcast.74), calls=%async_computation.8 | async-start | bytes 6815744 | tf_op jit(solution)/shard_map/all_to_all | solution.py:58
  820.9 605.5 %reduce-scatter.27.cloned.1.call-start = ((), (), s32[]{:S(2)}) async-start(), calls=%async_computation.34 | async-start | bytes 8847360
  950.0 29.1 %all-to-all-start.9 = ((bf16[4,256,1024]{1,2,0:T(8,128)(2,1)}), bf16[4,256,1024]{1,2,0:T(8,128)(2,1)}, u32[]{:S(2)}, u32[]{:S(2)}) async-start(bf16[4,256,1024]{1,2,0:T(8,128)(2,1)} %pad_maximum_fusion.2), calls=%async_computation.9 | async-start | bytes 4194304 | tf_op jit(solution)/shard_map/all_to_all | solution.py:58
  954.5 475.6 %reduce-scatter.29.cloned.1.call-start = ((), (), s32[]{:S(2)}) async-start(), calls=%async_computation.35 | async-start | bytes 8847360
  1093.8 351.1 %reduce-scatter.25.cloned.1.call-start = ((), (), s32[]{:S(2)}) async-start(), calls=%async_computation.33 | async-start | bytes 8847360
  1136.1 323.4 %reduce-scatter.23.cloned.1.call-start = ((), (), s32[]{:S(2)}) async-start(), calls=%async_computation.26 | async-start | bytes 8847360 | tf_op jit(solution)/shard_map/reduce_scatter | solution.py:447
  1149.8 309.7 %reduce-scatter.21.cloned.1.call-start = ((), (), s32[]{:S(2)}) async-start(), calls=%async_computation.25 | async-start | bytes 8847360 | tf_op jit(solution)/shard_map/reduce_scatter | solution.py:447
  1163.5 429.7 %reduce-scatter.19.cloned.1.call-start = ((), (), s32[]{:S(2)}) async-start(), calls=%async_computation.24 | async-start | bytes 13381632 | tf_op jit(solution)/shard_map/reduce_scatter | solution.py:431
  1230.0 43.1 %all-to-all-start.11 = ((bf16[4,256,1664]{2,1,0:T(8,128)(2,1)}), bf16[4,256,1664]{2,1,0:T(8,128)(2,1)}, u32[]{:S(2)}, u32[]{:S(2)}) async-start(bf16[4,256,1664]{2,1,0:T(8,128)(2,1)} %bitcast.98), calls=%async_computation.11 | async-start | bytes 6815744 | tf_op jit(solution)/shard_map/all_to_all | solution.py:58
  1353.8 29.5 %all-to-all-start.12 = ((bf16[4,256,1024]{1,2,0:T(8,128)(2,1)}), bf16[4,256,1024]{1,2,0:T(8,128)(2,1)}, u32[]{:S(2)}, u32[]{:S(2)}) async-start(bf16[4,256,1024]{1,2,0:T(8,128)(2,1)} %pad_maximum_fusion.3), calls=%async_computation.12 | async-start | bytes 4194304 | tf_op jit(solution)/shard_map/all_to_all | solution.py:58
  1358.2 397.3 %reduce-scatter.17.cloned.1.call-start = ((), (), s32[]{:S(2)}) async-start(), calls=%async_computation.23 | async-start | bytes 13381632 | tf_op jit(solution)/shard_map/reduce_scatter | solution.py:431
  (92 other events, 1326.5 us)
Sparse Core Ops, SparseCore 0:
  13.9 99.8 all-gather.14
  116.0 76.2 all-gather.18
  193.8 76.2 all-gather.20
  271.6 76.2 all-gather.22
  351.1 107.5 all-gather.16
  460.2 76.2 all-gather.24
  538.1 76.2 all-gather.26
  615.9 76.2 all-gather.28
  759.8 83.0 reduce-scatter.30
  865.4 83.4 reduce-scatter.26
  1093.9 81.6 reduce-scatter.28
  1177.8 83.0 reduce-scatter.24
  1263.2 82.9 reduce-scatter.22
  1348.4 83.0 reduce-scatter.20
  1437.3 155.8 reduce-scatter.18
  1599.1 156.3 reduce-scatter.16

commit v2 on v1

--- a/solution.py
+++ b/solution.py
@@ -68,6 +68,58 @@
     groups = lax.axis_size("expert")
     blocks = partial_rows.reshape((groups, -1) + partial_rows.shape[1:])
     return jnp.sum(exchange(blocks).astype(jnp.float32), axis=0)
+
+
+def same_core():
+    members = range(lax.axis_size("dp"))
+    return [[i for i in members if i % 2 == core] for core in range(2)]
+
+
+def swap_cores(values):
+    return lax.ppermute(values, "dp", [(i, i ^ 1) for i in range(lax.axis_size("dp"))])
+
+
+def exchange_chips(blocks):
+    return lax.all_to_all(
+        blocks, "dp", split_axis=0, concat_axis=0, axis_index_groups=same_core(), tiled=True
+    )
+
+
+def gather_staged(shard):
+    chips = lax.axis_size("dp") // 2
+    groups = lax.axis_size("expert")
+    rows, width = shard.shape
+    chip_rows = exchange_chips(jnp.broadcast_to(shard[None], (chips, rows, width)))
+    own = exchange(jnp.broadcast_to(chip_rows[None], (groups, chips, rows, width)))
+    other = swap_cores(own)
+    first = lax.axis_index("dp") % 2 == 0
+    both = jnp.stack([jnp.where(first, own, other), jnp.where(first, other, own)])
+    return both.transpose(2, 0, 1, 3, 4).reshape(-1, width)
+
+
+def core_major(columns):
+    chips = lax.axis_size("dp") // 2
+    groups = lax.axis_size("expert")
+    split = columns.reshape(columns.shape[0], chips, 2, groups, -1)
+    halves = split.transpose(2, 0, 3, 1, 4).reshape(2, columns.shape[0], -1)
+    core = lax.axis_index("dp") % 2
+    mine = lax.dynamic_index_in_dim(halves, core, 0, keepdims=False)
+    theirs = lax.dynamic_index_in_dim(halves, 1 - core, 0, keepdims=False)
+    return jnp.concatenate([mine, swap_cores(theirs)], axis=0)
+
+
+def both_cores(rows):
+    return jnp.concatenate([rows, swap_cores(rows)], axis=0)
+
+
+def scatter_staged(partial):
+    chips = lax.axis_size("dp") // 2
+    groups = lax.axis_size("expert")
+    width = partial.shape[1]
+    blocks = exchange(partial.reshape(groups, -1, width))
+    chip_blocks = jnp.sum(blocks.astype(jnp.float32), axis=0).astype(jnp.bfloat16)
+    arrived = exchange_chips(chip_blocks.reshape(chips, -1, width))
+    return jnp.sum(arrived.astype(jnp.float32), axis=0)
 
 
 def dot_f32(left, right, left_dims, right_dims):
@@ -141,31 +193,38 @@
         jnp.moveaxis(chosen_hot, 0, 1).reshape(token_total, -1).astype(jnp.bfloat16)
     ).reshape(all_rows, LAYER_COUNT, expert_total)
 
-    packed = [
-        lax.all_gather(
-            pack_attention(
-                query_weight[layer],
-                key_projection_weight[layer],
-                value_projection_weight[layer],
-                output_weight[layer].T,
-                router_weight[layer],
-                attention_gain[layer],
-                expert_gain[layer],
-            ),
-            ("dp", "expert"),
-            axis=0,
-            tiled=True,
+    shards = [
+        pack_attention(
+            query_weight[layer],
+            key_projection_weight[layer],
+            value_projection_weight[layer],
+            output_weight[layer].T,
+            router_weight[layer],
+            attention_gain[layer],
+            expert_gain[layer],
         )
         for layer in range(LAYER_COUNT)
     ]
+    packed = [lax.all_gather(shards[0], ("dp", "expert"), axis=0, tiled=True)]
+    packed += [gather_staged(shard) for shard in shards[1:]]
+    ff_width = gate_weight.shape[3]
+    hidden_width = exp_dev * ff_width
     gathered = [
-        (
-            lax.all_gather(gate_weight[layer], "dp", axis=1, tiled=True),
-            lax.all_gather(up_weight[layer], "dp", axis=1, tiled=True),
-            lax.all_gather(down_weight[layer], "dp", axis=2, tiled=True),
+        tuple(
+            lax.all_gather(rows.reshape(-1, hidden_width), "dp", axis=0, tiled=True)
+            for rows in (
+                gate_weight[layer].transpose(1, 0, 2),
+                up_weight[layer].transpose(1, 0, 2),
+                down_weight[layer].transpose(2, 0, 1),
+            )
         )
         for layer in range(LAYER_COUNT)
     ]
+
+    def spread(columns):
+        return jnp.broadcast_to(
+            columns[:, :, None], columns.shape + (ff_width,)
+        ).reshape(columns.shape[0], hidden_width)
 
     def shares_of(rows, router_full, hot):
         logits = jnp.dot(rows, router_full, preferred_element_type=jnp.float32)
@@ -227,12 +286,10 @@
         share_all = shares_of(arrived, router_full, chosen_all[:, layer] > 0)
         share_own = shares_of(normed_two, router_full, chosen_hot[layer])
         share_local = lax.dynamic_slice_in_dim(share_all, my_group * exp_dev, exp_dev, axis=1)
-        gate_val = jnp.einsum("td,edf->tef", arrived, gate_full, preferred_element_type=jnp.float32)
-        up_val = jnp.einsum("td,edf->tef", arrived, up_full, preferred_element_type=jnp.float32)
-        scaled_act = (jax.nn.silu(gate_val) * up_val * share_local[:, :, None]).astype(jnp.bfloat16)
-        out_rows = jnp.einsum(
-            "tef,efd->td", scaled_act, down_full, preferred_element_type=jnp.float32
-        ).astype(jnp.bfloat16)
+        gate_val = jnp.dot(arrived, gate_full, preferred_element_type=jnp.float32)
+        up_val = jnp.dot(arrived, up_full, preferred_element_type=jnp.float32)
+        scaled_act = (jax.nn.silu(gate_val) * up_val * spread(share_local)).astype(jnp.bfloat16)
+        out_rows = dot_f32(scaled_act, down_full, (1,), (1,)).astype(jnp.bfloat16)
         output = middle + sum_rows(out_rows)
         kept_state = (
             hidden,
@@ -301,31 +358,31 @@
             down_full,
         ) = kept_states[layer]
         grad_all = gather_rows(grad_hidden.astype(jnp.bfloat16))
-        grad_down = jnp.einsum(
-            "tef,td->efd", scaled_act, grad_all, preferred_element_type=jnp.float32
-        ).astype(jnp.bfloat16)
-        grad_scaled = jnp.einsum(
-            "td,efd->tef", grad_all, down_full, preferred_element_type=jnp.float32
-        )
+        grad_down = dot_f32(grad_all, scaled_act, (0,), (0,)).astype(jnp.bfloat16)
+        grad_all, grad_down = lax.optimization_barrier((grad_all, grad_down))
+        expert_parts = [lax.psum_scatter(grad_down, "dp", scatter_dimension=0, tiled=True)]
+        grad_scaled = jnp.dot(grad_all, down_full, preferred_element_type=jnp.float32)
         gate_val = gate_low.astype(jnp.float32)
         up_val = up_low.astype(jnp.float32)
         sigmoid_val = jax.nn.sigmoid(gate_val)
         silu_val = gate_val * sigmoid_val
-        grad_gates = jnp.sum(grad_scaled * silu_val * up_val, axis=2)
-        grad_inner = grad_scaled * share_local[:, :, None]
+        grad_gates = jnp.sum(
+            (grad_scaled * silu_val * up_val).reshape(all_rows, exp_dev, ff_width), axis=2
+        )
+        grad_inner = grad_scaled * spread(share_local)
         grad_gate_val = (
             grad_inner * up_val * sigmoid_val * (1.0 + gate_val * (1.0 - sigmoid_val))
         ).astype(jnp.bfloat16)
         grad_up_val = (grad_inner * silu_val).astype(jnp.bfloat16)
-        grad_gate_w = jnp.einsum(
-            "td,tef->edf", arrived, grad_gate_val, preferred_element_type=jnp.float32
+        grad_rows = (
+            dot_f32(grad_gate_val, gate_full, (1,), (1,))
+            + dot_f32(grad_up_val, up_full, (1,), (1,))
         ).astype(jnp.bfloat16)
-        grad_up_w = jnp.einsum(
-            "td,tef->edf", arrived, grad_up_val, preferred_element_type=jnp.float32
-        ).astype(jnp.bfloat16)
-        grad_rows = jnp.einsum(
-            "tef,edf->td", grad_gate_val, gate_full, preferred_element_type=jnp.float32
-        ) + jnp.einsum("tef,edf->td", grad_up_val, up_full, preferred_element_type=jnp.float32)
+        grad_rows, grad_gate_val, grad_up_val = lax.optimization_barrier(
+            (grad_rows, grad_gate_val, grad_up_val)
+        )
+        grad_gate_w = dot_f32(arrived, grad_gate_val, (0,), (0,)).astype(jnp.bfloat16)
+        grad_up_w = dot_f32(arrived, grad_up_val, (0,), (0,)).astype(jnp.bfloat16)
         gates_high = grad_gates.astype(jnp.bfloat16)
         gates_low = (grad_gates - gates_high.astype(jnp.float32)).astype(jnp.bfloat16)
         gate_columns = jnp.zeros((all_rows, gate_width), jnp.bfloat16)
@@ -336,8 +393,13 @@
             gate_columns, gates_low, expert_total + my_group * exp_dev, axis=1
         )
         back = sum_rows(
-            jnp.concatenate([grad_rows.astype(jnp.bfloat16), gate_columns], axis=1)
-        )
+            jnp.concatenate([grad_rows, gate_columns], axis=1)
+        )
+        back, grad_gate_w, grad_up_w = lax.optimization_barrier((back, grad_gate_w, grad_up_w))
+        expert_parts += [
+            lax.psum_scatter(grad_gate_w, "dp", scatter_dimension=0, tiled=True),
+            lax.psum_scatter(grad_up_w, "dp", scatter_dimension=0, tiled=True),
+        ]
         grad_gates_own = (
             back[:, model_width : model_width + expert_total]
             + back[:, model_width + expert_total : model_width + 2 * expert_total]
@@ -351,7 +413,7 @@
         grad_norm_mid, grad_gain_two = norm_backward(middle, inv_two, gain_two, grad_normed_two)
         grad_middle = grad_hidden + grad_norm_mid
         grad_branch = grad_middle.astype(jnp.bfloat16)
-        grad_output_w = dot_f32(grad_branch, attended, (0,), (0,))
+        grad_output_w = dot_f32(core_major(grad_branch), both_cores(attended), (0,), (0,))
         grad_attended = (
             dot_f32(grad_branch, output_full, (1,), (0,))
             .astype(jnp.bfloat16)
@@ -410,11 +472,15 @@
             .astype(jnp.bfloat16)
             .reshape(token_total, key_width)
         )
-        grad_linear = jnp.concatenate(
-            [grad_query_lin, grad_key_lin, grad_kv[:, key_width:].astype(jnp.bfloat16)], axis=1
-        )
-        grad_qkv_w = dot_f32(first_normalized, grad_linear, (0,), (0,))
-        grad_normed_one = dot_f32(grad_linear, qkv_full, (1,), (1,))
+        grad_kv_lin = jnp.concatenate(
+            [grad_key_lin, grad_kv[:, key_width:].astype(jnp.bfloat16)], axis=1
+        )
+        normed_split = core_major(first_normalized)
+        grad_query_w = dot_f32(normed_split, both_cores(grad_query_lin), (0,), (0,))
+        grad_kv_w = dot_f32(normed_split, both_cores(grad_kv_lin), (0,), (0,))
+        grad_normed_one = dot_f32(grad_query_lin, qkv_full[:, : edges[0]], (1,), (1,)) + dot_f32(
+            grad_kv_lin, qkv_full[:, edges[0] :], (1,), (1,)
+        )
         grad_norm_in, grad_gain_one = norm_backward(
             layer_hidden, inv_one, gain_one, grad_normed_one
         )
@@ -428,39 +494,39 @@
             ],
             axis=1,
         )
-        attention_list[layer] = lax.psum_scatter(
-            jnp.concatenate(
-                [
-                    grad_qkv_w.astype(jnp.bfloat16),
-                    grad_output_w.astype(jnp.bfloat16),
-                    small_part,
-                ],
-                axis=1,
+        small_split = core_major(small_part.T).reshape(2, small_width, -1)
+        small_half = jnp.sum(small_split.astype(jnp.float32), axis=0).T
+        attention_list[layer] = (
+            scatter_staged(grad_query_w.astype(jnp.bfloat16)),
+            scatter_staged(grad_output_w.astype(jnp.bfloat16)),
+            scatter_staged(
+                jnp.concatenate([grad_kv_w, small_half], axis=1).astype(jnp.bfloat16)
             ),
-            ("dp", "expert"),
-            scatter_dimension=0,
-            tiled=True,
-        ).astype(jnp.float32)
-        expert_list[layer] = (
-            lax.psum_scatter(grad_gate_w, "dp", scatter_dimension=1, tiled=True),
-            lax.psum_scatter(grad_up_w, "dp", scatter_dimension=1, tiled=True),
-            lax.psum_scatter(grad_down, "dp", scatter_dimension=2, tiled=True),
-        )
+        )
+        expert_list[layer] = [
+            part.reshape(-1, exp_dev, ff_width) for part in expert_parts
+        ]
         grad_hidden = grad_middle + grad_norm_in
-    stacked = jnp.stack(attention_list)
+    query_grads, output_grads, other_grads = (
+        stack_member(attention_list, member) for member in range(3)
+    )
+    down_grads, gate_grads, up_grads = (
+        stack_member(expert_list, member).astype(jnp.float32) for member in range(3)
+    )
+    small_grads = other_grads[:, :, 2 * key_width :]
     return (
         output,
         grad_hidden.reshape(sequences_per_device, block_length, model_width),
-        stacked[:, :, : edges[0]],
-        stacked[:, :, edges[0] : edges[1]],
-        stacked[:, :, edges[1] : edges[2]],
-        jnp.swapaxes(stacked[:, :, edges[2] : edges[3]], 1, 2),
-        stacked[:, :, edges[4]],
-        stacked[:, :, edges[5]],
-        stacked[:, :, edges[3] : edges[4]],
-        stack_member(expert_list, 0).astype(jnp.float32),
-        stack_member(expert_list, 1).astype(jnp.float32),
-        stack_member(expert_list, 2).astype(jnp.float32),
+        query_grads,
+        other_grads[:, :, :key_width],
+        other_grads[:, :, key_width : 2 * key_width],
+        jnp.swapaxes(output_grads, 1, 2),
+        small_grads[:, :, expert_total],
+        small_grads[:, :, expert_total + 1],
+        small_grads[:, :, :expert_total],
+        gate_grads.transpose(0, 2, 1, 3),
+        up_grads.transpose(0, 2, 1, 3),
+        down_grads.transpose(0, 2, 3, 1),
     )
 
 

time: 1780 us -> 1580 us (0.89)
  waiting for transfers between devices: 742 us -> 439 us
  starting transfers between devices: 51.5 us -> 114 us
  other arithmetic: 119 us -> 181 us
  local copies, waits for them, and re-layouts: 286 us -> 251 us
    reduce_scatter x4 -> x5, waiting for transfers between devices: 292 us -> 0.05 us  [the longest x2 0.02 us: body(): lax.psum_scatter(grad_up_w, 'dp', scatter_dimension=0, tiled=True)]
    all_gather x8 -> x7, waiting for transfers between devices: 306 us -> 83.7 us  [the longest x1 83.7 us: body(): packed = [lax.all_gather(shards[0], ('dp', 'expert'), axis=0, tiled=True)]]
    dot_general x14 -> x30, matrix products: 56.9 us -> 214 us  [dot_f32(): lax.dot_general(left, right, ((left_dims, right_dims), ((), ())), preferr...]
    dot_general x18 -> x6, matrix products: 261 us -> 116 us  [the longest x2 51.9 us: body(): jnp.dot(grad_all, down_full, preferred_element_type=jnp.float32)]
    all_to_all x11 -> x18, waiting for transfers between devices: 142 us -> 267 us  [exchange(): lax.all_to_all(blocks, 'expert', split_axis=0, concat_axis=0, tiled=True)]
    unnamed x215 -> x248, local copies, waits for them, and re-layouts: 165 us -> 52.1 us
    all_to_all x0 -> x7, waiting for transfers between devices: none -> 81.8 us  [exchange_chips(): lax.all_to_all(blocks, 'dp', split_axis=0, concat_axis=0, axis_index_grou...]
    concatenate x2 -> x1, local copies, waits for them, and re-layouts: 39.6 us -> 0.59 us  [body(): jnp.concatenate([grad_router.astype(jnp.bfloat16), grad_gain_one[:, None]...]
  transfers between devices with their start and end apart: 27 -> 51, of which waited for: 16 -> 27; matrix products, arithmetic and copies ran while one was open for 44% -> 56% of each run, Pallas kernels for 0% -> 0%
where the time goes in v2:
time: 1580 us; the launch traced here: 1570 us
  matrix products  490 us (31%)
  waiting for transfers between devices  439 us (28%)
  local copies, waits for them, and re-layouts  251 us (16%)
  other arithmetic  181 us (11%)
  starting transfers between devices  114 us (7%)
  blocking collectives  78 us (5%)
  between operations  16.7 us (1%)
    all_to_all x18, waiting for transfers between devices, exchange(): lax.all_to_all(blocks, 'expert', split_axis=0, concat_axis=0, tiled=True)  267 us
    dot_general x30, matrix products, dot_f32(): lax.dot_general(left, right, ((left_dims, right_dims), ((), ())), preferr...  214 us
    all_gather x1, waiting for transfers between devices, body(): packed = [lax.all_gather(shards[0], ('dp', 'expert'), axis=0, tiled=True)]  83.7 us
    all_to_all x7, waiting for transfers between devices, exchange_chips(): lax.all_to_all(blocks, 'dp', split_axis=0, concat_axis=0, axis_index_grou...  81.8 us
    all_to_all x18, starting transfers between devices, exchange(): lax.all_to_all(blocks, 'expert', split_axis=0, concat_axis=0, tiled=True)  78.9 us
    all_to_all x2, blocking collectives, exchange(): lax.all_to_all(blocks, 'expert', split_axis=0, concat_axis=0, tiled=True)  78 us
    unnamed x248, local copies, waits for them, and re-layouts  52.1 us
    dot_general x2, matrix products, body(): jnp.dot(grad_all, down_full, preferred_element_type=jnp.float32)  51.9 us
  transfers between devices with their start and end apart: 51, of which 27 were waited for; matrix products, arithmetic and copies ran while one was open for 56% of the time, Pallas kernels for 0%

profile of v2, /device:TPU:0, one launch (start us, length us, event | category | flops | bytes accessed | tf_op | source)
XLA Modules:
  0.0 1569.6 jit_solution(6079566799819685426)
XLA Ops:
  31.2 83.7 %all-gather.8.cloned.1.call-done = bf16[1536,4224]{1,0:T(8,128)(2,1)} async-done(((bf16[48,4224]{1,0:T(8,128)(2,1)}), bf16[1536,4224]{1,0:T(8,128)(2,1)}) %all-gather.8.cloned.1.call-update) | async-done | bytes 12976144 | tf_op jit(solution)/shard_map/all_gather | solution.py:208
  137.0 18.2 %all-to-all-done = bf16[4,256,1024]{1,2,0:T(8,128)(2,1)S(1)} async-done(((bf16[4,256,1024]{1,2,0:T(8,128)(2,1)}), bf16[4,256,1024]{1,2,0:T(8,128)(2,1)S(1)}, u32[]{:S(2)}, u32[]{:S(2)}) %all-to-all-start) | async-done | bytes 2097184 | tf_op jit(solution)/shard_map/all_to_all | solution.py:58
  198.5 44.2 %all-to-all-done.4 = bf16[4,48,4224]{2,1,0:T(8,128)(2,1)} async-done(((bf16[4,48,4224]{2,1,0:T(8,128)(2,1)}), bf16[4,48,4224]{2,1,0:T(8,128)(2,1)}, u32[]{:S(2)}, u32[]{:S(2)}) %all-to-all-start.4) | async-done | bytes 1622048 | tf_op jit(solution)/shard_map/all_to_all | solution.py:83
  269.3 55.1 %all-to-all-done.5 = bf16[4,4,48,4224]{3,2,1,0:T(8,128)(2,1)} async-done(((bf16[4,4,48,4224]{3,2,1,0:T(8,128)(2,1)}), bf16[4,4,48,4224]{3,2,1,0:T(8,128)(2,1)}, u32[]{:S(2)}, u32[]{:S(2)}) %all-to-all-start.5) | async-done | bytes 6488096 | tf_op jit(solution)/shard_map/all_to_all | solution.py:58
  341.5 25.1 %all-to-all-done.1 = bf16[4,256,1536]{2,1,0:T(8,128)(2,1)} async-done(((bf16[4,256,1536]{2,1,0:T(8,128)(2,1)}), bf16[4,256,1536]{2,1,0:T(8,128)(2,1)}, u32[]{:S(2)}, u32[]{:S(2)}) %all-to-all-start.1) | async-done | bytes 3145760 | tf_op jit(solution)/shard_map/all_to_all | solution.py:58
  386.7 14.0 fusion.186
  400.7 19.4 %multiply_convert_fusion.3 = (bf16[1024,2560]{1,0:T(8,128)(2,1)}, bf16[1024,2560]{1,0:T(8,128)(2,1)}) fusion(f32[1024,2560]{1,0:T(8,128)} %copy.395, f32[1024,2560]{1,0:T(8,128)} %fusion.186, bf16[1024,1536]{1,0:T(8,128)(2,1)} %bitcast.23, bf16[1536,2560]{1,0:T(8,128)(2,1)} %all-gather.12.cloned.1.call-done), kind=kOutput, calls=%fused_computation.62 | convolution fusion | flops 8074035200 | bytes 42467328 | tf_op jit(solution)/shard_map/dot_general | solution.py:290
  420.1 13.5 convolution_convert_fusion.7
  450.5 23.2 %all-to-all-done.3 = bf16[4,256,1536]{2,1,0:T(8,128)(2,1)} async-done(((bf16[4,256,1536]{2,1,0:T(8,128)(2,1)}), bf16[4,256,1536]{2,1,0:T(8,128)(2,1)}, u32[]{:S(2)}, u32[]{:S(2)}) %all-to-all-start.3) | async-done | bytes 3145760 | tf_op jit(solution)/shard_map/all_to_all | solution.py:58
  511.1 12.9 all-to-all-done.6
  569.8 39.2 %all_to_all.135 = bf16[4,256,1536]{2,1,0:T(8,128)(2,1)S(1)} all-to-all(bf16[4,256,1536]{2,1,0:T(8,128)(2,1)S(1)} %broadcast_in_dim.65), channel_id=1, replica_groups=mesh['dp'=8,'expert'=4] {'expert'}, dimensions={0} | all-to-all | bytes 6291456 | tf_op jit(solution)/shard_map/all_to_all | solution.py:58
  634.8 12.9 fusion.187
  647.7 18.0 %multiply_convert_fusion.2 = (bf16[1024,2560]{1,0:T(8,128)(2,1)}, bf16[1024,2560]{1,0:T(8,128)(2,1)}) fusion(f32[1024,2560]{1,0:T(8,128)} %copy.416, f32[1024,2560]{1,0:T(8,128)} %fusion.187, bf16[1024,1536]{1,0:T(8,128)(2,1)S(1)} %bitcast.509, bf16[1536,2560]{1,0:T(8,128)(2,1)} %all-gather.18.cloned.1.call-done), kind=kOutput, calls=%fused_computation.61 | convolution fusion | flops 8074035200 | bytes 42467328 | tf_op jit(solution)/shard_map/dot_general | solution.py:290
  665.7 13.6 fusion.32
  689.9 25.7 %multiply_convert_fusion.1 = (bf16[1024,2560]{1,0:T(8,128)(2,1)}, bf16[1024,2560]{1,0:T(8,128)(2,1)}, f32[1024,2560]{1,0:T(8,128)}) fusion(f32[1024,2560]{1,0:T(8,128)} %copy.416, f32[1024,2560]{1,0:T(8,128)} %fusion.187, bf16[1024,2560]{1,0:T(8,128)(2,1)} %get-tuple-element.225, bf16[1024,1536]{1,0:T(8,128)(2,1)} %bitcast.81, ...), kind=kOutput, calls=%fused_computation.60 | convolution fusion | flops 8102871040 | bytes 58195968 | tf_op jit(solution)/shard_map/dot_general | solution.py:364
  770.5 13.7 convolution_convert_fusion.4
  784.2 13.5 convolution_convert_fusion.3
  812.0 13.6 convolution_convert_fusion.6
  844.5 12.6 fusion.107
  862.2 21.1 %fusion.3 = (f32[8,3,256]{2,1,0:T(4,128)S(1)}, f32[8,1024,256,3]{2,1,3,0:T(8,128)}) fusion(f32[8,3,256]{2,1,0:T(4,128)S(1)} %log_add_fusion.1, f32[8,1024,256,3]{2,1,3,0:T(8,128)} %get-tuple-element.219, pred[256,1024]{0,1:T(8,128)(4,1)S(1)} %copy-done.2, bf16[256,8,3,64]{0,3,2,1:T(8,128)(2,1)S(1)} %bitcast.558, bf16[1024,2,8,64]{0,3,2,1:T(8,128)(2,1)S(1)} %copy-done.12), kind=kOutput, calls=%fused_computation.7 | convolution fusion | flops 836757504 | bytes 52486144 | tf_op jit(solution)/shard_map/qhgd,khd->hgqk/dot_general | solution.py:427
  883.2 18.0 %fusion.5 = bf16[8,3,256,1024]{2,3,1,0:T(8,128)(2,1)S(1)} fusion(f32[8,1024,256,3]{2,1,3,0:T(8,128)} %get-tuple-element.230, f32[8,3,256]{2,1,0:T(4,128)S(1)} %get-tuple-element.229, f32[8,3,256]{2,1,0:T(4,128)S(1)} %log_add_fusion.1, f32[8,1024,256,3]{2,1,3,0:T(8,128)} %get-tuple-element.219, pred[256,1024]{0,1:T(8,128)(4,1)S(1)} %copy-done.2), kind=kLoop, calls=%fused_computation.9 | loop fusion | flops 37748736 | bytes 63225856 | tf_op jit(solution)/shard_map/convert_element_type | solution.py:433
  932.3 12.5 all-to-all-done.11
  958.2 38.8 %all_to_all.136 = bf16[4,256,1536]{2,1,0:T(8,128)(2,1)S(1)} all-to-all(bf16[4,256,1536]{2,1,0:T(8,128)(2,1)S(1)} %broadcast_in_dim.70), channel_id=1, replica_groups=mesh['dp'=8,'expert'=4] {'expert'}, dimensions={0} | all-to-all | bytes 6291456 | tf_op jit(solution)/shard_map/all_to_all | solution.py:58
  1007.3 26.1 %multiply_convert_fusion = (bf16[1024,2560]{1,0:T(8,128)(2,1)}, bf16[1024,2560]{1,0:T(8,128)(2,1)}, f32[1024,2560]{1,0:T(8,128)}) fusion(f32[1024,2560]{1,0:T(8,128)} %copy.395, f32[1024,2560]{1,0:T(8,128)} %fusion.186, bf16[1024,2560]{1,0:T(8,128)(2,1)} %get-tuple-element.217, bf16[1024,1536]{1,0:T(8,128)(2,1)S(1)} %bitcast.547, ...), kind=kOutput, calls=%fused_computation.59 | convolution fusion | flops 8102871040 | bytes 58195968 | tf_op jit(solution)/shard_map/dot_general | solution.py:364
  1089.3 13.5 convolution_convert_fusion.1
  1102.8 13.6 convolution_convert_fusion
  1147.1 19.5 %all-to-all-done.25 = bf16[4,192,1536]{2,1,0:T(8,128)(2,1)S(1)} async-done(((bf16[4,192,1536]{2,1,0:T(8,128)(2,1)}), bf16[4,192,1536]{2,1,0:T(8,128)(2,1)S(1)}, u32[]{:S(2)}, u32[]{:S(2)}) %all-to-all-start.25) | async-done | bytes 2359328 | tf_op jit(solution)/shard_map/all_to_all | solution.py:58
  1177.2 21.9 %all-to-all-done.17 = bf16[4,192,1536]{2,1,0:T(8,128)(2,1)} async-done(((bf16[4,192,1536]{2,1,0:T(8,128)(2,1)}), bf16[4,192,1536]{2,1,0:T(8,128)(2,1)}, u32[]{:S(2)}, u32[]{:S(2)}) %all-to-all-start.17) | async-done | bytes 2359328 | tf_op jit(solution)/shard_map/all_to_all | solution.py:58
  1217.6 21.0 %fusion = (f32[8,3,256]{2,1,0:T(4,128)S(1)}, f32[8,1024,256,3]{2,1,3,0:T(8,128)}) fusion(f32[8,3,256]{2,1,0:T(4,128)S(1)} %log_add_fusion, f32[8,1024,256,3]{2,1,3,0:T(8,128)} %get-tuple-element.211, pred[256,1024]{0,1:T(8,128)(4,1)S(1)} %copy-done.3, bf16[256,8,3,64]{0,3,2,1:T(8,128)(2,1)S(1)} %bitcast.555, bf16[1024,2,8,64]{0,3,2,1:T(8,128)(2,1)S(1)} %copy-done.10), kind=kOutput, calls=%fused_computation.2 | convolution fusion | flops 836757504 | bytes 52486144 | tf_op jit(solution)/shard_map/qhgd,khd->hgqk/dot_general | solution.py:427
  1238.7 22.5 %fusion.2 = bf16[8,3,256,1024]{2,3,1,0:T(8,128)(2,1)} fusion(f32[8,1024,256,3]{2,1,3,0:T(8,128)} %get-tuple-element.236, f32[8,3,256]{2,1,0:T(4,128)S(1)} %get-tuple-element.235, f32[8,3,256]{2,1,0:T(4,128)S(1)} %log_add_fusion, f32[8,1024,256,3]{2,1,3,0:T(8,128)} %get-tuple-element.211, pred[256,1024]{0,1:T(8,128)(4,1)S(1)} %copy-done.3), kind=kLoop, calls=%fused_computation.4 | loop fusion | flops 37748736 | bytes 63225856 | tf_op jit(solution)/shard_map/convert_element_type | solution.py:433
  1261.2 12.5 fusion.110
  1448.7 19.6 %all-to-all-done.19 = bf16[4,192,1152]{2,1,0:T(8,128)(2,1)} async-done(((bf16[4,192,1152]{2,1,0:T(8,128)(2,1)}), bf16[4,192,1152]{2,1,0:T(8,128)(2,1)}, u32[]{:S(2)}, u32[]{:S(2)}) %all-to-all-start.19) | async-done | bytes 1769504 | tf_op jit(solution)/shard_map/all_to_all | solution.py:58
  (616 shorter events, 820.0 us)
Async XLA Ops:
  7.2 107.7 %all-gather.8.cloned.1.call-start = ((), (), s32[]{:S(2)}) async-start(), calls=%async_computation.33 | async-start | bytes 13381632 | tf_op jit(solution)/shard_map/all_gather | solution.py:208
  14.9 371.8 %all-gather.10.cloned.1.call-start = ((), (), s32[]{:S(2)}) async-start(), calls=%async_computation.34 | async-start | bytes 8847360 | tf_op jit(solution)/shard_map/all_gather | solution.py:214
  18.6 382.1 %all-gather.12.cloned.1.call-start = ((), (), s32[]{:S(2)}) async-start(), calls=%async_computation.35 | async-start | bytes 8847360 | tf_op jit(solution)/shard_map/all_gather | solution.py:214
  23.4 396.7 %all-gather.14.cloned.1.call-start = ((), (), s32[]{:S(2)}) async-start(), calls=%async_computation.36 | async-start | bytes 8847360 | tf_op jit(solution)/shard_map/all_gather | solution.py:214
  28.1 606.7 %all-gather.16.cloned.1.call-start = ((), (), s32[]{:S(2)}) async-start(), calls=%async_computation.37 | async-start | bytes 8847360 | tf_op jit(solution)/shard_map/all_gather | solution.py:214
  126.0 29.3 %all-to-all-start = ((bf16[4,256,1024]{1,2,0:T(8,128)(2,1)}), bf16[4,256,1024]{1,2,0:T(8,128)(2,1)S(1)}, u32[]{:S(2)}, u32[]{:S(2)}) async-start(bf16[4,256,1024]{1,2,0:T(8,128)(2,1)} %broadcast_in_dim.54), calls=%async_computation | async-start | bytes 4194304 | tf_op jit(solution)/shard_map/all_to_all | solution.py:58
  171.0 71.8 %all-to-all-start.4 = ((bf16[4,48,4224]{2,1,0:T(8,128)(2,1)}), bf16[4,48,4224]{2,1,0:T(8,128)(2,1)}, u32[]{:S(2)}, u32[]{:S(2)}) async-start(bf16[4,48,4224]{2,1,0:T(8,128)(2,1)} %broadcast_in_dim.62), calls=%async_computation.4 | async-start | bytes 3244032 | tf_op jit(solution)/shard_map/all_to_all | solution.py:83
  247.5 76.9 %all-to-all-start.5 = ((bf16[4,4,48,4224]{3,2,1,0:T(8,128)(2,1)}), bf16[4,4,48,4224]{3,2,1,0:T(8,128)(2,1)}, u32[]{:S(2)}, u32[]{:S(2)}) async-start(bf16[4,4,48,4224]{3,2,1,0:T(8,128)(2,1)} %broadcast_in_dim.63), calls=%async_computation.5 | async-start | bytes 12976128 | tf_op jit(solution)/shard_map/all_to_all | solution.py:58
  326.3 40.4 %all-to-all-start.1 = ((bf16[4,256,1536]{2,1,0:T(8,128)(2,1)}), bf16[4,256,1536]{2,1,0:T(8,128)(2,1)}, u32[]{:S(2)}, u32[]{:S(2)}) async-start(bf16[4,256,1536]{2,1,0:T(8,128)(2,1)} %broadcast_in_dim.57), calls=%async_computation.1 | async-start | bytes 6291456 | tf_op jit(solution)/shard_map/all_to_all | solution.py:58
  331.0 316.7 %all-gather.18.cloned.1.call-start = ((), (), s32[]{:S(2)}) async-start(), calls=%async_computation.38 | async-start | bytes 8847360 | tf_op jit(solution)/shard_map/all_gather | solution.py:214
  341.5 96.7 %collective-permute-start = (bf16[4,4,48,4224]{3,2,0,1:T(8,128)(2,1)}, bf16[4,4,48,4224]{3,2,0,1:T(8,128)(2,1)}, u32[]{:S(2)}, u32[]{:S(2)}) collective-permute-start(bf16[4,4,48,4224]{3,2,0,1:T(8,128)(2,1)} %copy.403), channel_id=1, source_target_pairs={{0,4},{4,0},{8,12},{12,8},{16,20},{20,16},{24,28},{28,24},{1,5},{5... | collective-permute-start | bytes 19464200 | tf_op jit(solution)/shard_map/ppermute | solution.py:79
  433.6 40.2 %all-to-all-start.3 = ((bf16[4,256,1536]{2,1,0:T(8,128)(2,1)}), bf16[4,256,1536]{2,1,0:T(8,128)(2,1)}, u32[]{:S(2)}, u32[]{:S(2)}) async-start(bf16[4,256,1536]{2,1,0:T(8,128)(2,1)} %bitcast.545), calls=%async_computation.3 | async-start | bytes 6291456 | tf_op jit(solution)/shard_map/all_to_all | solution.py:58
  496.1 28.0 %all-to-all-start.6 = ((bf16[4,256,1024]{1,2,0:T(8,128)(2,1)}), bf16[4,256,1024]{1,2,0:T(8,128)(2,1)S(1)}, u32[]{:S(2)}, u32[]{:S(2)}) async-start(bf16[4,256,1024]{1,2,0:T(8,128)(2,1)} %broadcast_in_dim.64), calls=%async_computation.6 | async-start | bytes 4194304 | tf_op jit(solution)/shard_map/all_to_all | solution.py:58
  499.7 190.2 %all-gather.20.cloned.1.call-start = ((), (), s32[]{:S(2)}) async-start(), calls=%async_computation.39 | async-start | bytes 8847360 | tf_op jit(solution)/shard_map/all_gather | solution.py:214
  611.0 54.7 %all-to-all-start.9 = ((bf16[4,256,1536]{2,1,0:T(8,128)(2,1)}), bf16[4,256,1536]{2,1,0:T(8,128)(2,1)}, u32[]{:S(2)}, u32[]{:S(2)}) async-start(bf16[4,256,1536]{2,1,0:T(8,128)(2,1)} %broadcast_in_dim.67), calls=%async_computation.9 | async-start | bytes 6291456 | tf_op jit(solution)/shard_map/all_to_all | solution.py:58
  615.8 906.8 %reduce-scatter.19.cloned.1.call-start = ((), (), s32[]{:S(2)}) async-start(), calls=%async_computation.45 | async-start | bytes 8847360
  765.9 41.4 %all-to-all-start.10 = ((bf16[4,256,1664]{2,1,0:T(8,128)(2,1)}), bf16[4,256,1664]{2,1,0:T(8,128)(2,1)S(1)}, u32[]{:S(2)}, u32[]{:S(2)}) async-start(bf16[4,256,1664]{2,1,0:T(8,128)(2,1)} %bitcast.505), calls=%async_computation.10 | async-start | bytes 6815744 | tf_op jit(solution)/shard_map/all_to_all | solution.py:58
  770.5 753.6 %reduce-scatter.15.cloned.1.call-start = ((), (), s32[]{:S(2)}) async-start(), calls=%async_computation.43 | async-start | bytes 8847360 | tf_op jit(solution)/shard_map/reduce_scatter | solution.py:401
  825.7 89.8 %all-to-all-start.8 = ((bf16[4,256,1536]{2,1,0:T(8,128)(2,1)}), bf16[4,256,1536]{2,1,0:T(8,128)(2,1)}, u32[]{:S(2)}, u32[]{:S(2)}) async-start(bf16[4,256,1536]{2,1,0:T(8,128)(2,1)} %bitcast.544), calls=%async_computation.8 | async-start | bytes 6291456 | tf_op jit(solution)/shard_map/all_to_all | solution.py:58
  830.5 695.2 %reduce-scatter.11.cloned.1.call-start = ((), (), s32[]{:S(2)}) async-start(), calls=%async_computation.41 | async-start | bytes 8847360 | tf_op jit(solution)/shard_map/reduce_scatter | solution.py:400
  915.4 29.4 %all-to-all-start.11 = ((bf16[4,256,1024]{1,2,0:T(8,128)(2,1)}), bf16[4,256,1024]{1,2,0:T(8,128)(2,1)}, u32[]{:S(2)}, u32[]{:S(2)}) async-start(bf16[4,256,1024]{1,2,0:T(8,128)(2,1)} %pad_maximum_fusion.3), calls=%async_computation.11 | async-start | bytes 4194304 | tf_op jit(solution)/shard_map/all_to_all | solution.py:58
  920.0 608.1 %reduce-scatter.17.cloned.1.call-start = ((), (), s32[]{:S(2)}) async-start(), calls=%async_computation.44 | async-start | bytes 8847360 | tf_op jit(solution)/shard_map/reduce_scatter | solution.py:363
  1085.3 40.5 %all-to-all-start.13 = ((bf16[4,256,1664]{2,1,0:T(8,128)(2,1)}), bf16[4,256,1664]{2,1,0:T(8,128)(2,1)S(1)}, u32[]{:S(2)}, u32[]{:S(2)}) async-start(bf16[4,256,1664]{2,1,0:T(8,128)(2,1)} %bitcast.506), calls=%async_computation.13 | async-start | bytes 6815744 | tf_op jit(solution)/shard_map/all_to_all | solution.py:58
  1089.2 451.1 %reduce-scatter.9.cloned.1.call-start = ((), (), s32[]{:S(2)}) async-start(), calls=%async_computation.40 | async-start | bytes 8847360 | tf_op jit(solution)/shard_map/reduce_scatter | solution.py:400
  1134.8 31.9 %all-to-all-start.25 = ((bf16[4,192,1536]{2,1,0:T(8,128)(2,1)}), bf16[4,192,1536]{2,1,0:T(8,128)(2,1)S(1)}, u32[]{:S(2)}, u32[]{:S(2)}) async-start(bf16[4,192,1536]{2,1,0:T(8,128)(2,1)} %bitcast.561), calls=%async_computation.25 | async-start | bytes 4718592 | tf_op jit(solution)/shard_map/all_to_all | solution.py:58
  1166.6 32.5 %all-to-all-start.17 = ((bf16[4,192,1536]{2,1,0:T(8,128)(2,1)}), bf16[4,192,1536]{2,1,0:T(8,128)(2,1)}, u32[]{:S(2)}, u32[]{:S(2)}) async-start(bf16[4,192,1536]{2,1,0:T(8,128)(2,1)} %bitcast.562), calls=%async_computation.17 | async-start | bytes 4718592 | tf_op jit(solution)/shard_map/all_to_all | solution.py:58
  1199.2 77.5 %all-to-all-start.26 = ((bf16[4,48,1536]{2,1,0:T(8,128)(2,1)}), bf16[4,48,1536]{2,1,0:T(8,128)(2,1)}, u32[]{:S(2)}, u32[]{:S(2)}) async-start(bf16[4,48,1536]{2,1,0:T(8,128)(2,1)} %bitcast.564), calls=%async_computation.26 | async-start | bytes 1179648 | tf_op jit(solution)/shard_map/all_to_all | solution.py:83
  1203.3 349.3 %reduce-scatter.13.cloned.1.call-start = ((), (), s32[]{:S(2)}) async-start(), calls=%async_computation.42 | async-start | bytes 8847360 | tf_op jit(solution)/shard_map/reduce_scatter | solution.py:401
  1276.7 30.6 %all-to-all-start.18 = ((bf16[4,48,1536]{2,1,0:T(8,128)(2,1)}), bf16[4,48,1536]{2,1,0:T(8,128)(2,1)}, u32[]{:S(2)}, u32[]{:S(2)}) async-start(bf16[4,48,1536]{2,1,0:T(8,128)(2,1)} %bitcast.563), calls=%async_computation.18 | async-start | bytes 1179648 | tf_op jit(solution)/shard_map/all_to_all | solution.py:83
  1335.2 31.8 %all-to-all-start.23 = ((bf16[4,192,1536]{2,1,0:T(8,128)(2,1)}), bf16[4,192,1536]{2,1,0:T(8,128)(2,1)}, u32[]{:S(2)}, u32[]{:S(2)}) async-start(bf16[4,192,1536]{2,1,0:T(8,128)(2,1)} %bitcast.559), calls=%async_computation.23 | async-start | bytes 4718592 | tf_op jit(solution)/shard_map/all_to_all | solution.py:58
  1352.4 53.1 %collective-permute-start.7 = (bf16[256,1024]{0,1:T(8,128)(2,1)}, bf16[256,1024]{0,1:T(8,128)(2,1)}, u32[]{:S(2)}, u32[]{:S(2)}) collective-permute-start(bf16[256,1024]{0,1:T(8,128)(2,1)} %pad_maximum_fusion.16), channel_id=1, source_target_pairs={{0,4},{4,0},{8,12},{12,8},{16,20},{20,16},{24,28},{28,24},{1,5},{5... | collective-permute-start | bytes 1572872 | tf_op jit(solution)/shard_map/ppermute | solution.py:79
  1367.0 31.0 %all-to-all-start.15 = ((bf16[4,192,1536]{2,1,0:T(8,128)(2,1)}), bf16[4,192,1536]{2,1,0:T(8,128)(2,1)S(1)}, u32[]{:S(2)}, u32[]{:S(2)}) async-start(bf16[4,192,1536]{2,1,0:T(8,128)(2,1)} %bitcast.560), calls=%async_computation.15 | async-start | bytes 4718592 | tf_op jit(solution)/shard_map/all_to_all | solution.py:58
  (139 other events, 2769.8 us)
Sparse Core Ops, SparseCore 0:
  15.0 99.8 all-gather.7
  117.1 92.1 all-gather.9
  211.0 80.7 all-gather.11
  293.3 76.0 all-gather.13
  370.9 76.2 all-gather.15
  448.6 76.2 all-gather.17
  526.5 76.2 all-gather.19
  690.0 83.1 reduce-scatter.18
  809.1 81.7 reduce-scatter.14
  893.1 83.0 reduce-scatter.10
  1007.5 81.2 reduce-scatter.16
  1127.6 82.2 reduce-scatter.8
  1216.1 94.4 reduce-scatter.12

commit v3 on v2

--- a/solution.py
+++ b/solution.py
@@ -3,6 +3,8 @@
 import jax
 import jax.numpy as jnp
 from jax import lax
+from jax.experimental import pallas as pl
+from jax.experimental.pallas import tpu as pltpu
 from jax.sharding import PartitionSpec as P
 
 QUERY_HEADS = 24
@@ -90,7 +92,11 @@
     groups = lax.axis_size("expert")
     rows, width = shard.shape
     chip_rows = exchange_chips(jnp.broadcast_to(shard[None], (chips, rows, width)))
-    own = exchange(jnp.broadcast_to(chip_rows[None], (groups, chips, rows, width)))
+    return exchange(jnp.broadcast_to(chip_rows[None], (groups, chips, rows, width)))
+
+
+def join_cores(own):
+    width = own.shape[-1]
     other = swap_cores(own)
     first = lax.axis_index("dp") % 2 == 0
     both = jnp.stack([jnp.where(first, own, other), jnp.where(first, other, own)])
@@ -112,20 +118,324 @@
     return jnp.concatenate([rows, swap_cores(rows)], axis=0)
 
 
-def scatter_staged(partial):
-    chips = lax.axis_size("dp") // 2
-    groups = lax.axis_size("expert")
-    width = partial.shape[1]
-    blocks = exchange(partial.reshape(groups, -1, width))
-    chip_blocks = jnp.sum(blocks.astype(jnp.float32), axis=0).astype(jnp.bfloat16)
-    arrived = exchange_chips(chip_blocks.reshape(chips, -1, width))
-    return jnp.sum(arrived.astype(jnp.float32), axis=0)
+def sum_groups(partial):
+    blocks = exchange(partial.reshape(lax.axis_size("expert"), -1, partial.shape[1]))
+    return jnp.sum(blocks.astype(jnp.float32), axis=0).astype(jnp.bfloat16)
+
+
+def sum_chips(partial):
+    blocks = exchange_chips(
+        partial.reshape(lax.axis_size("dp") // 2, -1, partial.shape[1])
+    )
+    return jnp.sum(blocks.astype(jnp.float32), axis=0)
 
 
 def dot_f32(left, right, left_dims, right_dims):
     return lax.dot_general(
         left, right, ((left_dims, right_dims), ((), ())), preferred_element_type=jnp.float32
     )
+
+
+def contract(left, right, left_dim, right_dim):
+    return lax.dot_general(
+        left,
+        right,
+        (((left_dim,), (right_dim,)), ((), ())),
+        preferred_element_type=jnp.float32,
+    )
+
+
+def pick_column(table, column):
+    lanes = lax.broadcasted_iota(jnp.int32, table.shape, 1)
+    return jnp.sum(jnp.where(lanes == column, table, 0.0), axis=1, keepdims=True)
+
+
+def expert_forward_kernel(rows_ref, gate_ref, up_ref, share_ref, gate_out, up_out, act_out):
+    rows = rows_ref[...]
+    gate_val = contract(rows, gate_ref[...], 1, 0)
+    up_val = contract(rows, up_ref[...], 1, 0)
+    share = pick_column(share_ref[...], pl.program_id(0))
+    gate_out[...] = gate_val.astype(jnp.bfloat16)
+    up_out[...] = up_val.astype(jnp.bfloat16)
+    act_out[...] = (gate_val * jax.nn.sigmoid(gate_val) * up_val * share).astype(jnp.bfloat16)
+
+
+def expert_forward(rows, gate, up, share):
+    row_total, width = rows.shape
+    experts = share.shape[1]
+    hidden = gate.shape[1] // experts
+    tile = row_total // 2
+    row_block = pl.BlockSpec((tile, width), lambda e, r: (r, 0))
+    weight_block = pl.BlockSpec((width, hidden), lambda e, r: (0, e))
+    hidden_block = pl.BlockSpec((tile, hidden), lambda e, r: (r, e))
+    return pl.pallas_call(
+        expert_forward_kernel,
+        grid=(experts, 2),
+        in_specs=[
+            row_block,
+            weight_block,
+            weight_block,
+            pl.BlockSpec((tile, experts), lambda e, r: (r, 0)),
+        ],
+        out_specs=[hidden_block] * 3,
+        out_shape=[jax.ShapeDtypeStruct((row_total, gate.shape[1]), jnp.bfloat16)] * 3,
+        cost_estimate=pl.CostEstimate(
+            flops=4 * row_total * width * gate.shape[1],
+            transcendentals=row_total * gate.shape[1],
+            bytes_accessed=4 * width * gate.shape[1] + 6 * row_total * gate.shape[1],
+        ),
+    )(rows, gate, up, share)
+
+
+def expert_backward_kernel(
+    grad_ref,
+    down_ref,
+    gate_ref,
+    up_ref,
+    gate_val_ref,
+    up_val_ref,
+    share_ref,
+    grad_gate_out,
+    grad_up_out,
+    rows_out,
+    sums_out,
+    rows_acc,
+    sums_acc,
+):
+    expert = pl.program_id(0)
+    tile = grad_ref.shape[0]
+    window = pl.ds(pl.multiple_of(pl.program_id(1) * tile, tile), tile)
+    grad_scaled = contract(grad_ref[...], down_ref[...], 1, 0)
+    gate_val = gate_val_ref[...].astype(jnp.float32)
+    up_val = up_val_ref[...].astype(jnp.float32)
+    sigmoid_val = jax.nn.sigmoid(gate_val)
+    silu_val = gate_val * sigmoid_val
+    grad_sum = jnp.sum(grad_scaled * silu_val * up_val, axis=1, keepdims=True)
+    grad_inner = grad_scaled * pick_column(share_ref[...], expert)
+    grad_gate = (
+        grad_inner * up_val * sigmoid_val * (1.0 + gate_val * (1.0 - sigmoid_val))
+    ).astype(jnp.bfloat16)
+    grad_up = (grad_inner * silu_val).astype(jnp.bfloat16)
+    grad_gate_out[...] = grad_gate
+    grad_up_out[...] = grad_up
+    grad_rows = contract(grad_gate, gate_ref[...], 1, 1) + contract(
+        grad_up, up_ref[...], 1, 1
+    )
+    lanes = lax.broadcasted_iota(jnp.int32, (tile, sums_acc.shape[1]), 1)
+    grad_sums = jnp.where(lanes == expert, grad_sum, 0.0)
+
+    @pl.when(expert == 0)
+    def _():
+        rows_acc[window, :] = grad_rows
+        sums_acc[window, :] = grad_sums
+
+    @pl.when(expert > 0)
+    def _():
+        rows_acc[window, :] += grad_rows
+        sums_acc[window, :] += grad_sums
+
+    @pl.when(expert == pl.num_programs(0) - 1)
+    def _():
+        rows_out[...] = rows_acc[window, :].astype(jnp.bfloat16)
+        sums_out[...] = sums_acc[window, :]
+
+
+def expert_backward(grad, down, gate, up, gate_val, up_val, share):
+    row_total, width = grad.shape
+    experts = share.shape[1]
+    hidden = gate.shape[1] // experts
+    tile = row_total // 2
+    row_block = pl.BlockSpec((tile, width), lambda e, r: (r, 0))
+    weight_block = pl.BlockSpec((width, hidden), lambda e, r: (0, e))
+    hidden_block = pl.BlockSpec((tile, hidden), lambda e, r: (r, e))
+    hidden_shape = jax.ShapeDtypeStruct((row_total, gate.shape[1]), jnp.bfloat16)
+
+    def last_block(e, r):
+        return (jnp.where(e == experts - 1, r, 0), 0)
+
+    return pl.pallas_call(
+        expert_backward_kernel,
+        grid=(experts, 2),
+        in_specs=[
+            row_block,
+            weight_block,
+            weight_block,
+            weight_block,
+            hidden_block,
+            hidden_block,
+            pl.BlockSpec((tile, experts), lambda e, r: (r, 0)),
+        ],
+        out_specs=[
+            hidden_block,
+            hidden_block,
+            pl.BlockSpec((tile, width), last_block),
+            pl.BlockSpec((tile, 128), last_block),
+        ],
+        out_shape=[
+            hidden_shape,
+            hidden_shape,
+            jax.ShapeDtypeStruct((row_total, width), jnp.bfloat16),
+            jax.ShapeDtypeStruct((row_total, 128), jnp.float32),
+        ],
+        scratch_shapes=[
+            pltpu.VMEM((row_total, width), jnp.float32),
+            pltpu.VMEM((row_total, 128), jnp.float32),
+        ],
+        cost_estimate=pl.CostEstimate(
+            flops=6 * row_total * width * gate.shape[1],
+            transcendentals=row_total * gate.shape[1],
+            bytes_accessed=6 * width * gate.shape[1] + 8 * row_total * gate.shape[1],
+        ),
+    )(grad, down, gate, up, gate_val, up_val, share)
+
+
+def attention_probs(block_ref, query, key):
+    scores = contract(key, query, 1, 1) * HEAD_SIZE ** (-0.5)
+    key_at = lax.broadcasted_iota(jnp.int32, scores.shape, 0)
+    query_at = lax.broadcasted_iota(jnp.int32, scores.shape, 1)
+    offset = block_ref[0] * query.shape[0]
+    masked = jnp.where(key_at <= query_at + offset, scores, -1e30)
+    exp_scores = jnp.exp(masked - jnp.max(masked, axis=0, keepdims=True))
+    return exp_scores / jnp.sum(exp_scores, axis=0, keepdims=True)
+
+
+def head(values, index):
+    return values[:, index * HEAD_SIZE : (index + 1) * HEAD_SIZE]
+
+
+def attention_forward_kernel(block_ref, query_ref, key_ref, value_ref, out_ref):
+    query, key, value = query_ref[...], key_ref[...], value_ref[...]
+    group = QUERY_HEADS // KEY_VALUE_HEADS
+    outs = []
+    for index in range(2 * group):
+        shared = index // group
+        probs = attention_probs(block_ref, head(query, index), head(key, shared))
+        outs.append(contract(head(value, shared), probs.astype(jnp.bfloat16), 0, 0))
+    out_ref[...] = jnp.concatenate(outs, axis=0).T.astype(jnp.bfloat16)
+
+
+def attention_specs(tokens, keys):
+    pairs = KEY_VALUE_HEADS // 2
+    query_block = pl.BlockSpec((tokens, QUERY_HEADS // pairs * HEAD_SIZE), lambda i, b: (0, i))
+    key_block = pl.BlockSpec((keys, 2 * HEAD_SIZE), lambda i, b: (0, i))
+    value_block = pl.BlockSpec((keys, 2 * HEAD_SIZE), lambda i, b: (0, i + pairs))
+    return (pairs, query_block, key_block, value_block)
+
+
+def attention_forward(block, query, key_value):
+    tokens, width = query.shape
+    keys = key_value.shape[0]
+    pairs, query_block, key_block, value_block = attention_specs(tokens, keys)
+    return pl.pallas_call(
+        attention_forward_kernel,
+        grid_spec=pltpu.PrefetchScalarGridSpec(
+            num_scalar_prefetch=1,
+            grid=(pairs,),
+            in_specs=[query_block, key_block, value_block],
+            out_specs=query_block,
+        ),
+        out_shape=jax.ShapeDtypeStruct((tokens, width), jnp.bfloat16),
+        cost_estimate=pl.CostEstimate(
+            flops=16 * tokens * width * keys,
+            transcendentals=QUERY_HEADS * tokens * keys,
+            bytes_accessed=4 * tokens * width + 2 * key_value.size,
+        ),
+    )(block, query, key_value, key_value)
+
+
+def attention_backward_kernel(
+    block_ref, query_ref, grad_ref, key_ref, value_ref, grad_query_out, grad_key_value_out
+):
+    query, grad, key, value = query_ref[...], grad_ref[...], key_ref[...], value_ref[...]
+    group = QUERY_HEADS // KEY_VALUE_HEADS
+    scale = HEAD_SIZE ** (-0.5)
+    grad_queries, grad_keys, grad_values = [], [], []
+    for shared in range(2):
+        grad_key, grad_value = 0.0, 0.0
+        for index in range(shared * group, (shared + 1) * group):
+            query_one, grad_one = head(query, index), head(grad, index)
+            probs = attention_probs(block_ref, query_one, head(key, shared))
+            grad_probs = contract(head(value, shared), grad_one, 1, 1)
+            centre = jnp.sum(probs * grad_probs, axis=0, keepdims=True)
+            grad_scores = (probs * (grad_probs - centre)).astype(jnp.bfloat16)
+            grad_queries.append(contract(head(key, shared), grad_scores, 0, 0) * scale)
+            grad_key += contract(grad_scores, query_one, 1, 0)
+            grad_value += contract(probs.astype(jnp.bfloat16), grad_one, 1, 0)
+        grad_keys.append(grad_key * scale)
+        grad_values.append(grad_value)
+    grad_query_out[...] = jnp.concatenate(grad_queries, axis=0).T
+    grad_key_value_out[...] = jnp.concatenate(grad_keys + grad_values, axis=1).astype(
+        jnp.bfloat16
+    )
+
+
+def attention_backward(block, query, grad, key_value):
+    tokens, width = query.shape
+    keys = key_value.shape[0]
+    pairs, query_block, key_block, value_block = attention_specs(tokens, keys)
+    return pl.pallas_call(
+        attention_backward_kernel,
+        grid_spec=pltpu.PrefetchScalarGridSpec(
+            num_scalar_prefetch=1,
+            grid=(pairs,),
+            in_specs=[query_block, query_block, key_block, value_block],
+            out_specs=[
+                query_block,
+                pl.BlockSpec((keys, 4 * HEAD_SIZE), lambda i, b: (0, i)),
+            ],
+        ),
+        out_shape=[
+            jax.ShapeDtypeStruct((tokens, width), jnp.float32),
+            jax.ShapeDtypeStruct(key_value.shape, jnp.bfloat16),
+        ],
+        cost_estimate=pl.CostEstimate(
+            flops=40 * tokens * width * keys,
+            transcendentals=QUERY_HEADS * tokens * keys,
+            bytes_accessed=8 * tokens * width + 4 * key_value.size,
+        ),
+    )(block, query, grad, key_value, key_value)
+
+
+def place_kernel(part_ref, held_ref, out_ref):
+    del held_ref
+    out_ref[0, 0] = part_ref[...].astype(jnp.float32)
+
+
+def place_first_kernel(part_ref, out_ref):
+    out_ref[0, 0] = part_ref[...].astype(jnp.float32)
+
+
+def place_turned_kernel(part_ref, held_ref, out_ref):
+    del held_ref
+    out_ref[0, 0] = part_ref[...].astype(jnp.float32).T
+
+
+def place_turned_first_kernel(part_ref, out_ref):
+    out_ref[0, 0] = part_ref[...].astype(jnp.float32).T
+
+
+def place(part, held, layer, experts, turned):
+    rows = part.shape[0]
+    hidden = part.shape[1] // experts
+    block = (hidden, rows) if turned else (rows, hidden)
+    kernels = (
+        (place_turned_first_kernel, place_turned_kernel)
+        if turned
+        else (place_first_kernel, place_kernel)
+    )
+    in_specs = [pl.BlockSpec((rows, hidden), lambda e: (0, e))]
+    operands = [part]
+    if held is not None:
+        in_specs.append(pl.BlockSpec(memory_space=pl.ANY))
+        operands.append(held)
+    return pl.pallas_call(
+        kernels[held is not None],
+        grid=(experts,),
+        in_specs=in_specs,
+        out_specs=pl.BlockSpec((1, 1) + block, lambda e: (layer, e, 0, 0)),
+        out_shape=jax.ShapeDtypeStruct((LAYER_COUNT, experts) + block, jnp.float32),
+        input_output_aliases={} if held is None else {1: 0},
+    )(*operands)
 
 
 def body(
@@ -151,12 +461,10 @@
     all_rows = token_total * groups
     query_width = query_weight.shape[2]
     key_width = key_projection_weight.shape[2]
-    query_head_group = QUERY_HEADS // KEY_VALUE_HEADS
-    score_scale = HEAD_SIZE ** (-0.5)
     my_group = lax.axis_index("expert")
     positions = my_group * block_length + jnp.arange(block_length, dtype=jnp.int32)
     cosine_table, sine_table = rotary_tables(positions, HEAD_SIZE // 2)
-    causal = positions[:, None] >= jnp.arange(block_length * groups, dtype=jnp.int32)[None, :]
+    block_at = my_group.astype(jnp.int32).reshape(1)
     expert_ids = jnp.arange(expert_total, dtype=jnp.int32)
     small_width = -(-(expert_total + 2) // 128) * 128
     gate_width = -(-(2 * expert_total) // 128) * 128
@@ -206,7 +514,9 @@
         for layer in range(LAYER_COUNT)
     ]
     packed = [lax.all_gather(shards[0], ("dp", "expert"), axis=0, tiled=True)]
-    packed += [gather_staged(shard) for shard in shards[1:]]
+    staged = [gather_staged(shard) for shard in shards[1:]]
+    inputs, staged = lax.optimization_barrier((inputs, staged))
+    packed += [join_cores(own) for own in staged]
     ff_width = gate_weight.shape[3]
     hidden_width = exp_dev * ff_width
     gathered = [
@@ -220,11 +530,6 @@
         )
         for layer in range(LAYER_COUNT)
     ]
-
-    def spread(columns):
-        return jnp.broadcast_to(
-            columns[:, :, None], columns.shape + (ff_width,)
-        ).reshape(columns.shape[0], hidden_width)
 
     def shares_of(rows, router_full, hot):
         logits = jnp.dot(rows, router_full, preferred_element_type=jnp.float32)
@@ -248,9 +553,7 @@
             cosine_table,
             sine_table,
         ).astype(jnp.bfloat16)
-        query_grouped = query_rotated.reshape(
-            token_total, KEY_VALUE_HEADS, query_head_group, HEAD_SIZE
-        )
+        query_rotated = query_rotated.reshape(token_total, query_width)
         key_rot = rotate_features(
             linear[:, edges[0] : edges[1]].reshape(token_total, KEY_VALUE_HEADS, HEAD_SIZE),
             cosine_table,
@@ -263,22 +566,8 @@
             ],
             axis=1,
         )
-        key_value_all = gather_rows(key_value).reshape(all_rows, 2, KEY_VALUE_HEADS, HEAD_SIZE)
-        key_all, value_all = key_value_all[:, 0], key_value_all[:, 1]
-        scores = (
-            jnp.einsum("qhgd,khd->hgqk", query_grouped, key_all, preferred_element_type=jnp.float32)
-            * score_scale
-        )
-        masked = jnp.where(causal, scores, -1e30)
-        row_max = jnp.max(masked, axis=-1, keepdims=True)
-        exp_scores = jnp.exp(masked - row_max)
-        row_total = jnp.sum(exp_scores, axis=-1, keepdims=True)
-        log_total = row_max + jnp.log(row_total)
-        prob_low = (exp_scores / row_total).astype(jnp.bfloat16)
-        attended = jnp.einsum(
-            "hgqk,khd->qhgd", prob_low, value_all, preferred_element_type=jnp.float32
-        )
-        attended = attended.reshape(token_total, query_width).astype(jnp.bfloat16)
+        key_value_all = gather_rows(key_value)
+        attended = attention_forward(block_at, query_rotated, key_value_all)
         middle = hidden + dot_f32(attended, output_full, (1,), (1,))
         normed_two, inv_two = norm_forward(middle, gain_two)
         normed_two = normed_two.astype(jnp.bfloat16)
@@ -286,19 +575,17 @@
         share_all = shares_of(arrived, router_full, chosen_all[:, layer] > 0)
         share_own = shares_of(normed_two, router_full, chosen_hot[layer])
         share_local = lax.dynamic_slice_in_dim(share_all, my_group * exp_dev, exp_dev, axis=1)
-        gate_val = jnp.dot(arrived, gate_full, preferred_element_type=jnp.float32)
-        up_val = jnp.dot(arrived, up_full, preferred_element_type=jnp.float32)
-        scaled_act = (jax.nn.silu(gate_val) * up_val * spread(share_local)).astype(jnp.bfloat16)
+        gate_low, up_low, scaled_act = expert_forward(
+            arrived, gate_full, up_full, share_local
+        )
         out_rows = dot_f32(scaled_act, down_full, (1,), (1,)).astype(jnp.bfloat16)
         output = middle + sum_rows(out_rows)
         kept_state = (
             hidden,
             inv_one,
             first_normalized,
-            query_grouped,
-            key_all,
-            value_all,
-            log_total,
+            query_rotated,
+            key_value_all,
             attended,
             middle,
             inv_two,
@@ -306,8 +593,8 @@
             share_own,
             share_local,
             arrived,
-            gate_val.astype(jnp.bfloat16),
-            up_val.astype(jnp.bfloat16),
+            gate_low,
+            up_low,
             scaled_act,
             qkv_full,
             output_full,
@@ -328,16 +615,15 @@
     output = hidden.astype(jnp.bfloat16).reshape(sequences_per_device, block_length, model_width)
     grad_hidden = cotangent.astype(jnp.float32).reshape(token_total, model_width)
     attention_list = [None] * LAYER_COUNT
-    expert_list = [None] * LAYER_COUNT
+    expert_held = [None] * 3
+    waiting = None
     for layer in range(LAYER_COUNT - 1, -1, -1):
         (
             layer_hidden,
             inv_one,
             first_normalized,
-            query_grouped,
-            key_all,
-            value_all,
-            log_total,
+            query_rotated,
+            key_value_all,
             attended,
             middle,
             inv_two,
@@ -358,29 +644,19 @@
             down_full,
         ) = kept_states[layer]
         grad_all = gather_rows(grad_hidden.astype(jnp.bfloat16))
+        if waiting is not None:
+            grad_all, waiting = lax.optimization_barrier((grad_all, waiting))
+            waiting = [sum_groups(part) for part in waiting]
         grad_down = dot_f32(grad_all, scaled_act, (0,), (0,)).astype(jnp.bfloat16)
         grad_all, grad_down = lax.optimization_barrier((grad_all, grad_down))
         expert_parts = [lax.psum_scatter(grad_down, "dp", scatter_dimension=0, tiled=True)]
-        grad_scaled = jnp.dot(grad_all, down_full, preferred_element_type=jnp.float32)
-        gate_val = gate_low.astype(jnp.float32)
-        up_val = up_low.astype(jnp.float32)
-        sigmoid_val = jax.nn.sigmoid(gate_val)
-        silu_val = gate_val * sigmoid_val
-        grad_gates = jnp.sum(
-            (grad_scaled * silu_val * up_val).reshape(all_rows, exp_dev, ff_width), axis=2
-        )
-        grad_inner = grad_scaled * spread(share_local)
-        grad_gate_val = (
-            grad_inner * up_val * sigmoid_val * (1.0 + gate_val * (1.0 - sigmoid_val))
-        ).astype(jnp.bfloat16)
-        grad_up_val = (grad_inner * silu_val).astype(jnp.bfloat16)
-        grad_rows = (
-            dot_f32(grad_gate_val, gate_full, (1,), (1,))
-            + dot_f32(grad_up_val, up_full, (1,), (1,))
-        ).astype(jnp.bfloat16)
-        grad_rows, grad_gate_val, grad_up_val = lax.optimization_barrier(
-            (grad_rows, grad_gate_val, grad_up_val)
-        )
+        grad_gate_val, grad_up_val, grad_rows, grad_sums = expert_backward(
+            grad_all, down_full, gate_full, up_full, gate_low, up_low, share_local
+        )
+        grad_gates = grad_sums[:, :exp_dev]
+        if waiting is not None:
+            grad_rows, waiting = lax.optimization_barrier((grad_rows, waiting))
+            attention_list[layer + 1] = sum_chips(jnp.concatenate(waiting, axis=1))
         grad_gate_w = dot_f32(arrived, grad_gate_val, (0,), (0,)).astype(jnp.bfloat16)
         grad_up_w = dot_f32(arrived, grad_up_val, (0,), (0,)).astype(jnp.bfloat16)
         gates_high = grad_gates.astype(jnp.bfloat16)
@@ -395,6 +671,10 @@
         back = sum_rows(
             jnp.concatenate([grad_rows, gate_columns], axis=1)
         )
+        if waiting is not None:
+            back, attention_list[layer + 1] = lax.optimization_barrier(
+                (back, attention_list[layer + 1])
+            )
         back, grad_gate_w, grad_up_w = lax.optimization_barrier((back, grad_gate_w, grad_up_w))
         expert_parts += [
             lax.psum_scatter(grad_gate_w, "dp", scatter_dimension=0, tiled=True),
@@ -414,48 +694,12 @@
         grad_middle = grad_hidden + grad_norm_mid
         grad_branch = grad_middle.astype(jnp.bfloat16)
         grad_output_w = dot_f32(core_major(grad_branch), both_cores(attended), (0,), (0,))
-        grad_attended = (
-            dot_f32(grad_branch, output_full, (1,), (0,))
-            .astype(jnp.bfloat16)
-            .reshape(token_total, KEY_VALUE_HEADS, query_head_group, HEAD_SIZE)
-        )
-        layer_scores = (
-            jnp.einsum("qhgd,khd->hgqk", query_grouped, key_all, preferred_element_type=jnp.float32)
-            * score_scale
-        )
-        softmax_probs = jnp.exp(jnp.where(causal, layer_scores, -1e30) - log_total)
-        grad_probs = jnp.einsum(
-            "qhgd,khd->hgqk", grad_attended, value_all, preferred_element_type=jnp.float32
-        )
-        grad_scores = (
-            softmax_probs
-            * (grad_probs - jnp.sum(softmax_probs * grad_probs, axis=-1, keepdims=True))
-        ).astype(jnp.bfloat16)
-        grad_query = (
-            jnp.einsum("hgqk,khd->qhgd", grad_scores, key_all, preferred_element_type=jnp.float32)
-            * score_scale
-        )
-        grad_key_all = (
-            jnp.einsum(
-                "hgqk,qhgd->khd", grad_scores, query_grouped, preferred_element_type=jnp.float32
-            )
-            * score_scale
-        )
-        grad_value_all = jnp.einsum(
-            "hgqk,qhgd->khd",
-            softmax_probs.astype(jnp.bfloat16),
-            grad_attended,
-            preferred_element_type=jnp.float32,
-        )
-        grad_kv = sum_rows(
-            jnp.concatenate(
-                [
-                    grad_key_all.reshape(all_rows, key_width).astype(jnp.bfloat16),
-                    grad_value_all.reshape(all_rows, key_width).astype(jnp.bfloat16),
-                ],
-                axis=1,
-            )
-        )
+        grad_attended = dot_f32(grad_branch, output_full, (1,), (0,)).astype(jnp.bfloat16)
+        grad_query, grad_key_value_all = attention_backward(
+            block_at, query_rotated, grad_attended, key_value_all
+        )
+        grad_kv = sum_rows(grad_key_value_all).reshape(token_total, -1, 2, 2 * HEAD_SIZE)
+        grad_kv = grad_kv.transpose(0, 2, 1, 3).reshape(token_total, 2 * key_width)
         grad_query_lin = (
             rotate_features(
                 grad_query.reshape(token_total, QUERY_HEADS, HEAD_SIZE), cosine_table, -sine_table
@@ -496,37 +740,42 @@
         )
         small_split = core_major(small_part.T).reshape(2, small_width, -1)
         small_half = jnp.sum(small_split.astype(jnp.float32), axis=0).T
-        attention_list[layer] = (
-            scatter_staged(grad_query_w.astype(jnp.bfloat16)),
-            scatter_staged(grad_output_w.astype(jnp.bfloat16)),
-            scatter_staged(
-                jnp.concatenate([grad_kv_w, small_half], axis=1).astype(jnp.bfloat16)
-            ),
-        )
-        expert_list[layer] = [
-            part.reshape(-1, exp_dev, ff_width) for part in expert_parts
+        grad_kv_w = jnp.concatenate([grad_kv_w, small_half], axis=1)
+        partials = [grad_output_w, grad_query_w, grad_kv_w]
+        partials = [partial.astype(jnp.bfloat16) for partial in partials]
+        if layer > 0:
+            waiting = partials
+        else:
+            early = [sum_groups(part) for part in partials[:2]]
+            attention_list[layer] = jnp.concatenate(
+                [sum_chips(jnp.concatenate(early, axis=1)), sum_chips(sum_groups(partials[2]))],
+                axis=1,
+            )
+        expert_held = [
+            place(part, held, layer, exp_dev, turned)
+            for part, held, turned in zip(expert_parts, expert_held, (True, False, False))
         ]
         grad_hidden = grad_middle + grad_norm_in
-    query_grads, output_grads, other_grads = (
-        stack_member(attention_list, member) for member in range(3)
-    )
-    down_grads, gate_grads, up_grads = (
-        stack_member(expert_list, member).astype(jnp.float32) for member in range(3)
-    )
-    small_grads = other_grads[:, :, 2 * key_width :]
+    stacked = jnp.stack(attention_list)
+    cuts = [query_width, query_width, key_width, key_width, expert_total, 1, 1]
+    cuts = [sum(cuts[:index]) for index in range(len(cuts) + 1)]
+    output_grads, query_grads, key_grads, value_grads, router_grads, one, two = (
+        stacked[:, :, start:stop] for start, stop in zip(cuts[:-1], cuts[1:])
+    )
+    down_grads, gate_grads, up_grads = expert_held
     return (
         output,
         grad_hidden.reshape(sequences_per_device, block_length, model_width),
         query_grads,
-        other_grads[:, :, :key_width],
-        other_grads[:, :, key_width : 2 * key_width],
+        key_grads,
+        value_grads,
         jnp.swapaxes(output_grads, 1, 2),
-        small_grads[:, :, expert_total],
-        small_grads[:, :, expert_total + 1],
-        small_grads[:, :, :expert_total],
-        gate_grads.transpose(0, 2, 1, 3),
-        up_grads.transpose(0, 2, 1, 3),
-        down_grads.transpose(0, 2, 3, 1),
+        one[:, :, 0],
+        two[:, :, 0],
+        router_grads,
+        gate_grads,
+        up_grads,
+        down_grads,
     )
 
 

time: 1580 us -> 1390 us (0.88)
  matrix products: 490 us -> 190 us
  Pallas kernels: 0 us -> 270 us
  local copies, waits for them, and re-layouts: 251 us -> 122 us
  other arithmetic: 181 us -> 92.6 us
  waiting for transfers between devices: 439 us -> 494 us
  blocking collectives: 78 us -> 94.3 us
    pallas_call x0 -> x14, Pallas kernels: none -> 270 us  [the longest x2 80.2 us: expert_backward(): pl.pallas_call(expert_backward_kernel, grid=(experts, 2), in_specs=[row_b...]
    dot_general x18 -> x0, matrix products: 258 us -> none  [the longest x2 51.9 us: body(): jnp.dot(grad_all, down_full, preferred_element_type=jnp.float32)]
    all_gather x6, waiting for transfers between devices: 0.03 us -> 98.7 us  [body(): lax.all_gather(rows.reshape(-1, hidden_width), 'dp', axis=0, tiled=True)]
    all_gather x1, waiting for transfers between devices: 83.7 us -> 2.23 us  [body(): packed = [lax.all_gather(shards[0], ('dp', 'expert'), axis=0, tiled=True)]]
    dot_general x30 -> x26, matrix products: 214 us -> 170 us  [dot_f32(): lax.dot_general(left, right, ((left_dims, right_dims), ((), ())), preferr...]
    convert_element_type x2 -> x0, other arithmetic: 40.5 us -> none  [body(): grad_scores = (softmax_probs * (grad_probs - jnp.sum(softmax_probs * grad...]
    reduce_sum x16 -> x9, other arithmetic: 53.1 us -> 15.9 us  [the longest x6 13.1 us: sum_groups(): return jnp.sum(blocks.astype(jnp.float32), axis=0).astype(jnp.bfloat16)]
    unnamed x248 -> x134, local copies, waits for them, and re-layouts: 52.1 us -> 22.1 us
  transfers between devices with their start and end apart: 51 -> 47, of which waited for: 27 -> 25; matrix products, arithmetic and copies ran while one was open for 56% -> 28% of each run, Pallas kernels for 0% -> 19%
where the time goes in v3:
time: 1390 us; the launch traced here: 1380 us
  waiting for transfers between devices  494 us (36%)
  Pallas kernels  270 us (19%)
  matrix products  190 us (14%)
  local copies, waits for them, and re-layouts  122 us (9%)
  starting transfers between devices  99.4 us (7%)
  blocking collectives  94.3 us (7%)
  other arithmetic  92.6 us (7%)
  between operations  16 us (1%)
    all_to_all x17, waiting for transfers between devices, exchange(): lax.all_to_all(blocks, 'expert', split_axis=0, concat_axis=0, tiled=True)  277 us
    dot_general x26, matrix products, dot_f32(): lax.dot_general(left, right, ((left_dims, right_dims), ((), ())), preferr...  170 us
    all_to_all x4, waiting for transfers between devices, exchange_chips(): lax.all_to_all(blocks, 'dp', split_axis=0, concat_axis=0, axis_index_grou...  110 us
    all_gather x6, waiting for transfers between devices, body(): lax.all_gather(rows.reshape(-1, hidden_width), 'dp', axis=0, tiled=True)  98.7 us
    all_to_all x3, blocking collectives, exchange(): lax.all_to_all(blocks, 'expert', split_axis=0, concat_axis=0, tiled=True)  94.3 us
    pallas_call x2, Pallas kernels, expert_backward(): pl.pallas_call(expert_backward_kernel, grid=(experts, 2), in_specs=[row_b...  80.2 us
    all_to_all x17, starting transfers between devices, exchange(): lax.all_to_all(blocks, 'expert', split_axis=0, concat_axis=0, tiled=True)  76.3 us
    pallas_call x2, Pallas kernels, attention_backward(): pl.pallas_call(attention_backward_kernel, grid_spec=pltpu.PrefetchScalarG...  62.3 us
  transfers between devices with their start and end apart: 47, of which 25 were waited for; matrix products, arithmetic and copies ran while one was open for 28% of the time, Pallas kernels for 19%

profile of v3, /device:TPU:0, one launch (start us, length us, event | category | flops | bytes accessed | tf_op | source)
XLA Modules:
  0.0 1378.8 jit_solution(7944490417298694205)
XLA Ops:
  40.6 52.5 %all-to-all-done = bf16[4,48,4224]{2,1,0:T(8,128)(2,1)S(1)} async-done(((bf16[4,48,4224]{2,1,0:T(8,128)(2,1)}), bf16[4,48,4224]{2,1,0:T(8,128)(2,1)S(1)}, u32[]{:S(2)}, u32[]{:S(2)}) %all-to-all-start) | async-done | bytes 1622048 | tf_op jit(solution)/shard_map/all_to_all | solution.py:85
  102.5 88.8 %all-to-all-done.1 = bf16[4,4,48,4224]{3,2,1,0:T(8,128)(2,1)} async-done(((bf16[4,4,48,4224]{3,2,1,0:T(8,128)(2,1)}), bf16[4,4,48,4224]{3,2,1,0:T(8,128)(2,1)}, u32[]{:S(2)}, u32[]{:S(2)}) %all-to-all-start.1) | async-done | bytes 6488096 | tf_op jit(solution)/shard_map/all_to_all | solution.py:60
  215.4 19.4 %all-to-all-done.2 = bf16[4,256,1024]{2,1,0:T(8,128)(2,1)} async-done(((bf16[4,256,1024]{2,1,0:T(8,128)(2,1)}), bf16[4,256,1024]{2,1,0:T(8,128)(2,1)}, u32[]{:S(2)}, u32[]{:S(2)}) %all-to-all-start.2) | async-done | bytes 2097184 | tf_op jit(solution)/shard_map/all_to_all | solution.py:60
  238.9 23.4 %shard_map.220 = bf16[256,1536]{1,0:T(8,128)(2,1)} custom-call(s32[1]{0:T(128)} %bitcast.9.block_ref, bf16[256,1536]{1,0:T(8,128)(2,1)} %copy.394.query_ref, bf16[1024,1024]{1,0:T(8,128)(2,1)} %bitcast.22.key_ref.value_ref, bf16[1024,1024]{1,0:T(8,128)(2,1)} %bitcast.22.key_ref.value_ref), custom_call_target="tpu_custom_call" | custom-call | flops 6442450944 | bytes 3670016 | tf_op jit(solution)/shard_map/pallas_call | solution.py:329
  283.0 26.5 %all-to-all-done.3 = bf16[4,256,1536]{2,1,0:T(8,128)(2,1)} async-done(((bf16[4,256,1536]{2,1,0:T(8,128)(2,1)}), bf16[4,256,1536]{2,1,0:T(8,128)(2,1)}, u32[]{:S(2)}, u32[]{:S(2)}) %all-to-all-start.3) | async-done | bytes 3145760 | tf_op jit(solution)/shard_map/all_to_all | solution.py:60
  314.0 35.3 %all-gather.12.cloned.1.call-done.up_ref = bf16[1536,2560]{1,0:T(8,128)(2,1)} async-done(((bf16[192,2560]{1,0:T(8,128)(2,1)}), bf16[1536,2560]{1,0:T(8,128)(2,1)}) %all-gather.12.cloned.1.call-update) | async-done | bytes 7864336 | tf_op jit(solution)/shard_map/all_gather | solution.py:524
  349.2 28.3 %shard_map.221 = (bf16[1024,2560]{1,0:T(8,128)(2,1)}, bf16[1024,2560]{1,0:T(8,128)(2,1)}, bf16[1024,2560]{1,0:T(8,128)(2,1)}) custom-call(bf16[1024,1536]{1,0:T(8,128)(2,1)} %bitcast.23.rows_ref, bf16[1536,2560]{1,0:T(8,128)(2,1)} %all-gather.10.cloned.1.call-done.gate_ref, bf16[1536,2560]{1,0:T(8,128)(2,1)} %all-gather.12.cloned.1.call-done.up_ref, ...), custom_call_target="tpu_custom_call" | custom-call | flops 16106127360 | bytes 31457280 | tf_op jit(solution)/shard_map/pallas_call | solution.py:171
  377.5 49.5 %all-gather.14.cloned.1.call-done.down_ref = bf16[1536,2560]{1,0:T(8,128)(2,1)} async-done(((bf16[192,2560]{1,0:T(8,128)(2,1)}), bf16[1536,2560]{1,0:T(8,128)(2,1)}) %all-gather.14.cloned.1.call-update) | async-done | bytes 7864336 | tf_op jit(solution)/shard_map/all_gather | solution.py:524
  457.5 24.5 %all-to-all-done.5 = bf16[4,256,1536]{2,1,0:T(8,128)(2,1)} async-done(((bf16[4,256,1536]{2,1,0:T(8,128)(2,1)}), bf16[4,256,1536]{2,1,0:T(8,128)(2,1)}, u32[]{:S(2)}, u32[]{:S(2)}) %all-to-all-start.5) | async-done | bytes 3145760 | tf_op jit(solution)/shard_map/all_to_all | solution.py:60
  505.2 18.7 %all-to-all-done.6 = bf16[4,256,1024]{2,1,0:T(8,128)(2,1)} async-done(((bf16[4,256,1024]{2,1,0:T(8,128)(2,1)}), bf16[4,256,1024]{2,1,0:T(8,128)(2,1)}, u32[]{:S(2)}, u32[]{:S(2)}) %all-to-all-start.6) | async-done | bytes 2097184 | tf_op jit(solution)/shard_map/all_to_all | solution.py:60
  523.9 23.3 %shard_map.222 = bf16[256,1536]{1,0:T(8,128)(2,1)} custom-call(s32[1]{0:T(128)} %bitcast.9.block_ref, bf16[256,1536]{1,0:T(8,128)(2,1)} %copy.411.query_ref, bf16[1024,1024]{1,0:T(8,128)(2,1)} %bitcast.47.key_ref.value_ref, bf16[1024,1024]{1,0:T(8,128)(2,1)} %bitcast.47.key_ref.value_ref), custom_call_target="tpu_custom_call" | custom-call | flops 6442450944 | bytes 3670016 | tf_op jit(solution)/shard_map/pallas_call | solution.py:329
  552.4 39.6 %all_to_all.120 = bf16[4,256,1536]{2,1,0:T(8,128)(2,1)} all-to-all(bf16[4,256,1536]{2,1,0:T(8,128)(2,1)S(1)} %broadcast_in_dim.44), channel_id=1, replica_groups=mesh['dp'=8,'expert'=4] {'expert'}, dimensions={0} | all-to-all | bytes 6291456 | tf_op jit(solution)/shard_map/all_to_all | solution.py:60
  604.5 28.0 %shard_map.223 = (bf16[1024,2560]{1,0:T(8,128)(2,1)}, bf16[1024,2560]{1,0:T(8,128)(2,1)}, bf16[1024,2560]{1,0:T(8,128)(2,1)}) custom-call(bf16[1024,1536]{1,0:T(8,128)(2,1)} %bitcast.332, bf16[1536,2560]{1,0:T(8,128)(2,1)} %all-gather.16.cloned.1.call-done.gate_ref, bf16[1536,2560]{1,0:T(8,128)(2,1)} %all-gather.18.cloned.1.call-done.up_ref, ...), custom_call_target="tpu_custom_call" | custom-call | flops 16106127360 | bytes 31457280 | tf_op jit(solution)/shard_map/pallas_call | solution.py:171
  632.9 13.6 fusion
  646.4 14.0 %all-gather.20.cloned.1.call-done.down_ref = bf16[1536,2560]{1,0:T(8,128)(2,1)} async-done(((bf16[192,2560]{1,0:T(8,128)(2,1)}), bf16[1536,2560]{1,0:T(8,128)(2,1)}) %all-gather.20.cloned.1.call-update) | async-done | bytes 7864336 | tf_op jit(solution)/shard_map/all_gather | solution.py:524
  660.4 40.1 %shard_map.224 = (bf16[1024,2560]{1,0:T(8,128)(2,1)}, bf16[1024,2560]{1,0:T(8,128)(2,1)}, bf16[1024,1536]{1,0:T(8,128)(2,1)}, f32[1024,128]{1,0:T(8,128)}) custom-call(bf16[1024,1536]{1,0:T(8,128)(2,1)} %bitcast.62.grad_ref, bf16[1536,2560]{1,0:T(8,128)(2,1)} %all-gather.20.cloned.1.call-done.down_ref, ...), custom_call_target="tpu_custom_call" | custom-call | flops 24159191040 | bytes 44564480 | tf_op jit(solution)/shard_map/pallas_call | solution.py:256
  718.6 13.6 convolution_convert_fusion.4
  732.2 13.4 convolution_convert_fusion.3
  764.7 14.1 %convolution_convert_fusion.6 = bf16[1024,1536]{1,0:T(8,128)(2,1)} fusion(bf16[1024,2560]{1,0:T(8,128)(2,1)} %get-tuple-element.55, bf16[1536,2560]{1,0:T(8,128)(2,1)} %all-gather.20.cloned.1.call-done.down_ref), kind=kOutput, calls=%fused_computation.32 | convolution fusion | flops 8054636544 | bytes 16252928 | tf_op jit(solution)/shard_map/dot_general | solution.py:134
  795.9 31.1 %shard_map.225 = (f32[256,1536]{1,0:T(8,128)}, bf16[1024,1024]{1,0:T(8,128)(2,1)}) custom-call(s32[1]{0:T(128)} %bitcast.9.block_ref, bf16[256,1536]{1,0:T(8,128)(2,1)} %copy.411.query_ref, bf16[256,1536]{1,0:T(8,128)(2,1)} %fusion.36.grad_ref, bf16[1024,1024]{1,0:T(8,128)(2,1)} %bitcast.47.key_ref.value_ref, bf16[1024,1024]{1,0:T(8,128)(2,1)} %bitcast.47.key_ref.value_ref), custom_call_target="tpu_custom_call" | custom-call | flops 16106127360 | bytes 7340032 | tf_op jit(solution)/shard_map/pallas_call | solution.py:376
  841.3 15.4 %all-to-all-done.11 = bf16[4,256,1024]{2,1,0:T(8,128)(2,1)} async-done(((bf16[4,256,1024]{2,1,0:T(8,128)(2,1)}), bf16[4,256,1024]{2,1,0:T(8,128)(2,1)}, u32[]{:S(2)}, u32[]{:S(2)}) %all-to-all-start.11) | async-done | bytes 2097184 | tf_op jit(solution)/shard_map/all_to_all | solution.py:60
  898.9 17.3 %all-to-all-done.12 = bf16[4,256,1536]{2,1,0:T(8,128)(2,1)} async-done(((bf16[4,256,1536]{2,1,0:T(8,128)(2,1)}), bf16[4,256,1536]{2,1,0:T(8,128)(2,1)}, u32[]{:S(2)}, u32[]{:S(2)}) %all-to-all-start.12) | async-done | bytes 3145760 | tf_op jit(solution)/shard_map/all_to_all | solution.py:60
  916.2 13.5 convolution_convert_fusion.2
  929.8 24.9 %all_to_all.121 = bf16[4,192,1152]{2,1,0:T(8,128)(2,1)} all-to-all(bf16[4,192,1152]{2,1,0:T(8,128)(2,1)S(1)} %bitcast.310), channel_id=1, replica_groups=mesh['dp'=8,'expert'=4] {'expert'}, dimensions={0} | all-to-all | bytes 3538944 | tf_op jit(solution)/shard_map/all_to_all | solution.py:60
  954.7 29.9 %all_to_all.122 = bf16[4,192,1536]{2,1,0:T(8,128)(2,1)} all-to-all(bf16[4,192,1536]{2,1,0:T(8,128)(2,1)S(1)} %bitcast.348), channel_id=1, replica_groups=mesh['dp'=8,'expert'=4] {'expert'}, dimensions={0} | all-to-all | bytes 4718592 | tf_op jit(solution)/shard_map/all_to_all | solution.py:60
  988.4 40.1 %shard_map.226 = (bf16[1024,2560]{1,0:T(8,128)(2,1)}, bf16[1024,2560]{1,0:T(8,128)(2,1)}, bf16[1024,1536]{1,0:T(8,128)(2,1)}, f32[1024,128]{1,0:T(8,128)}) custom-call(bf16[1024,1536]{1,0:T(8,128)(2,1)} %bitcast.74.grad_ref, bf16[1536,2560]{1,0:T(8,128)(2,1)} %all-gather.14.cloned.1.call-done.down_ref, ...), custom_call_target="tpu_custom_call" | custom-call | flops 24159191040 | bytes 44564480 | tf_op jit(solution)/shard_map/pallas_call | solution.py:256
  1047.7 28.3 %all-to-all-done.17 = bf16[4,48,4224]{2,1,0:T(8,128)(2,1)S(1)} async-done(((bf16[4,48,4224]{2,1,0:T(8,128)(2,1)}), bf16[4,48,4224]{2,1,0:T(8,128)(2,1)S(1)}, u32[]{:S(2)}, u32[]{:S(2)}) %all-to-all-start.17) | async-done | bytes 1622048 | tf_op jit(solution)/shard_map/all_to_all | solution.py:85
  1094.7 13.5 convolution_convert_fusion
  1139.0 31.1 %shard_map.227 = (f32[256,1536]{1,0:T(8,128)}, bf16[1024,1024]{1,0:T(8,128)(2,1)}) custom-call(s32[1]{0:T(128)} %bitcast.9.block_ref, bf16[256,1536]{1,0:T(8,128)(2,1)} %copy.394.query_ref, bf16[256,1536]{1,0:T(8,128)(2,1)} %fusion.33.grad_ref, bf16[1024,1024]{1,0:T(8,128)(2,1)} %bitcast.22.key_ref.value_ref, bf16[1024,1024]{1,0:T(8,128)(2,1)} %bitcast.22.key_ref.value_ref), custom_call_target="tpu_custom_call" | custom-call | flops 16106127360 | bytes 7340032 | tf_op jit(solution)/shard_map/pallas_call | solution.py:376
  1241.6 14.1 %all-to-all-done.22 = bf16[4,192,1152]{2,1,0:T(8,128)(2,1)} async-done(((bf16[4,192,1152]{2,1,0:T(8,128)(2,1)}), bf16[4,192,1152]{2,1,0:T(8,128)(2,1)}, u32[]{:S(2)}, u32[]{:S(2)}) %all-to-all-start.22) | async-done | bytes 1769504 | tf_op jit(solution)/shard_map/all_to_all | solution.py:60
  1262.8 24.6 %all-to-all-done.20 = bf16[4,192,1536]{2,1,0:T(8,128)(2,1)} async-done(((bf16[4,192,1536]{2,1,0:T(8,128)(2,1)}), bf16[4,192,1536]{2,1,0:T(8,128)(2,1)}, u32[]{:S(2)}, u32[]{:S(2)}) %all-to-all-start.20) | async-done | bytes 2359328 | tf_op jit(solution)/shard_map/all_to_all | solution.py:60
  1312.6 24.0 %all-to-all-done.21 = bf16[4,48,3072]{2,1,0:T(8,128)(2,1)} async-done(((bf16[4,48,3072]{2,1,0:T(8,128)(2,1)}), bf16[4,48,3072]{2,1,0:T(8,128)(2,1)}, u32[]{:S(2)}, u32[]{:S(2)}) %all-to-all-start.21) | async-done | bytes 1179680 | tf_op jit(solution)/shard_map/all_to_all | solution.py:85
  (451 shorter events, 488.6 us)
Async XLA Ops:
  7.2 186.5 %all-gather.8.cloned.1.call-start = ((), (), s32[]{:S(2)}) async-start(), calls=%async_computation.30 | async-start | bytes 13381632 | tf_op jit(solution)/shard_map/all_gather | solution.py:516
  14.3 299.7 %all-gather.10.cloned.1.call-start = ((), (), s32[]{:S(2)}) async-start(), calls=%async_computation.31 | async-start | bytes 8847360 | tf_op jit(solution)/shard_map/all_gather | solution.py:524
  18.0 331.2 %all-gather.12.cloned.1.call-start = ((), (), s32[]{:S(2)}) async-start(), calls=%async_computation.32 | async-start | bytes 8847360 | tf_op jit(solution)/shard_map/all_gather | solution.py:524
  22.7 404.3 %all-gather.14.cloned.1.call-start = ((), (), s32[]{:S(2)}) async-start(), calls=%async_computation.33 | async-start | bytes 8847360 | tf_op jit(solution)/shard_map/all_gather | solution.py:524
  27.4 577.1 %all-gather.16.cloned.1.call-start = ((), (), s32[]{:S(2)}) async-start(), calls=%async_computation.34 | async-start | bytes 8847360 | tf_op jit(solution)/shard_map/all_gather | solution.py:524
  31.2 61.8 %all-to-all-start = ((bf16[4,48,4224]{2,1,0:T(8,128)(2,1)}), bf16[4,48,4224]{2,1,0:T(8,128)(2,1)S(1)}, u32[]{:S(2)}, u32[]{:S(2)}) async-start(bf16[4,48,4224]{2,1,0:T(8,128)(2,1)} %broadcast_in_dim.35), calls=%async_computation | async-start | bytes 3244032 | tf_op jit(solution)/shard_map/all_to_all | solution.py:85
  37.6 566.9 %all-gather.18.cloned.1.call-start = ((), (), s32[]{:S(2)}) async-start(), calls=%async_computation.35 | async-start | bytes 8847360 | tf_op jit(solution)/shard_map/all_gather | solution.py:524
  96.2 95.0 %all-to-all-start.1 = ((bf16[4,4,48,4224]{3,2,1,0:T(8,128)(2,1)}), bf16[4,4,48,4224]{3,2,1,0:T(8,128)(2,1)}, u32[]{:S(2)}, u32[]{:S(2)}) async-start(bf16[4,4,48,4224]{3,2,1,0:T(8,128)(2,1)} %broadcast_in_dim.37), calls=%async_computation.1 | async-start | bytes 12976128 | tf_op jit(solution)/shard_map/all_to_all | solution.py:60
  204.6 30.2 %all-to-all-start.2 = ((bf16[4,256,1024]{2,1,0:T(8,128)(2,1)}), bf16[4,256,1024]{2,1,0:T(8,128)(2,1)}, u32[]{:S(2)}, u32[]{:S(2)}) async-start(bf16[4,256,1024]{2,1,0:T(8,128)(2,1)} %broadcast_in_dim.38), calls=%async_computation.2 | async-start | bytes 4194304 | tf_op jit(solution)/shard_map/all_to_all | solution.py:60
  235.5 31.2 %all-to-all-start.4 = ((bf16[4,256,40]{1,2,0:T(8,128)(2,1)}), bf16[4,256,40]{1,2,0:T(8,128)(2,1)S(1)}, u32[]{:S(2)}, u32[]{:S(2)}) async-start(bf16[4,256,40]{1,2,0:T(8,128)(2,1)} %broadcast_in_dim.40), calls=%async_computation.4 | async-start | bytes 163840 | tf_op jit(solution)/shard_map/all_to_all | solution.py:60
  268.8 40.6 %all-to-all-start.3 = ((bf16[4,256,1536]{2,1,0:T(8,128)(2,1)}), bf16[4,256,1536]{2,1,0:T(8,128)(2,1)}, u32[]{:S(2)}, u32[]{:S(2)}) async-start(bf16[4,256,1536]{2,1,0:T(8,128)(2,1)} %broadcast_in_dim.39), calls=%async_computation.3 | async-start | bytes 6291456 | tf_op jit(solution)/shard_map/all_to_all | solution.py:60
  273.5 386.9 %all-gather.20.cloned.1.call-start = ((), (), s32[]{:S(2)}) async-start(), calls=%async_computation.36 | async-start | bytes 8847360 | tf_op jit(solution)/shard_map/all_gather | solution.py:524
  279.7 165.5 %collective-permute-start = (bf16[4,4,48,4224]{3,2,0,1:T(8,128)(2,1)}, bf16[4,4,48,4224]{3,2,0,1:T(8,128)(2,1)}, u32[]{:S(2)}, u32[]{:S(2)}) collective-permute-start(bf16[4,4,48,4224]{3,2,0,1:T(8,128)(2,1)} %copy.405), channel_id=1, source_target_pairs={{0,4},{4,0},{8,12},{12,8},{16,20},{20,16},{24,28},{28,24},{1,5},{5... | collective-permute-start | bytes 19464200 | tf_op jit(solution)/shard_map/ppermute | solution.py:81
  440.3 41.7 %all-to-all-start.5 = ((bf16[4,256,1536]{2,1,0:T(8,128)(2,1)}), bf16[4,256,1536]{2,1,0:T(8,128)(2,1)}, u32[]{:S(2)}, u32[]{:S(2)}) async-start(bf16[4,256,1536]{2,1,0:T(8,128)(2,1)} %bitcast.336), calls=%async_computation.5 | async-start | bytes 6291456 | tf_op jit(solution)/shard_map/all_to_all | solution.py:60
  593.9 38.9 %all-to-all-start.9 = ((bf16[4,256,1536]{2,1,0:T(8,128)(2,1)}), bf16[4,256,1536]{2,1,0:T(8,128)(2,1)}, u32[]{:S(2)}, u32[]{:S(2)}) async-start(bf16[4,256,1536]{2,1,0:T(8,128)(2,1)} %broadcast_in_dim.45), calls=%async_computation.9 | async-start | bytes 6291456 | tf_op jit(solution)/shard_map/all_to_all | solution.py:60
  598.6 743.0 %reduce-scatter.17.cloned.1.call-start = ((), (), s32[]{:S(2)}) async-start(), calls=%async_computation.42 | async-start | bytes 8847360 | tf_op jit(solution)/shard_map/reduce_scatter | solution.py:652
  713.6 44.6 %all-to-all-start.10 = ((bf16[4,256,1664]{2,1,0:T(8,128)(2,1)}), bf16[4,256,1664]{2,1,0:T(8,128)(2,1)}, u32[]{:S(2)}, u32[]{:S(2)}) async-start(bf16[4,256,1664]{2,1,0:T(8,128)(2,1)} %bitcast.309), calls=%async_computation.10 | async-start | bytes 6815744 | tf_op jit(solution)/shard_map/all_to_all | solution.py:60
  718.4 627.6 %reduce-scatter.13.cloned.1.call-start = ((), (), s32[]{:S(2)}) async-start(), calls=%async_computation.40 | async-start | bytes 8847360 | tf_op jit(solution)/shard_map/reduce_scatter | solution.py:681
  762.1 587.9 %reduce-scatter.9.cloned.1.call-start = ((), (), s32[]{:S(2)}) async-start(), calls=%async_computation.38 | async-start | bytes 8847360 | tf_op jit(solution)/shard_map/reduce_scatter | solution.py:680
  778.8 48.2 %all-to-all-start.8 = ((bf16[4,256,1536]{2,1,0:T(8,128)(2,1)}), bf16[4,256,1536]{2,1,0:T(8,128)(2,1)}, u32[]{:S(2)}, u32[]{:S(2)}) async-start(bf16[4,256,1536]{2,1,0:T(8,128)(2,1)} %bitcast.335), calls=%async_computation.8 | async-start | bytes 6291456 | tf_op jit(solution)/shard_map/all_to_all | solution.py:60
  827.0 29.7 %all-to-all-start.11 = ((bf16[4,256,1024]{2,1,0:T(8,128)(2,1)}), bf16[4,256,1024]{2,1,0:T(8,128)(2,1)}, u32[]{:S(2)}, u32[]{:S(2)}) async-start(bf16[4,256,1024]{2,1,0:T(8,128)(2,1)} %bitcast.351), calls=%async_computation.11 | async-start | bytes 4194304 | tf_op jit(solution)/shard_map/all_to_all | solution.py:60
  875.7 40.6 %all-to-all-start.12 = ((bf16[4,256,1536]{2,1,0:T(8,128)(2,1)}), bf16[4,256,1536]{2,1,0:T(8,128)(2,1)}, u32[]{:S(2)}, u32[]{:S(2)}) async-start(bf16[4,256,1536]{2,1,0:T(8,128)(2,1)} %broadcast_in_dim.48), calls=%async_computation.12 | async-start | bytes 6291456 | tf_op jit(solution)/shard_map/all_to_all | solution.py:60
  880.5 473.5 %reduce-scatter.15.cloned.1.call-start = ((), (), s32[]{:S(2)}) async-start(), calls=%async_computation.41 | async-start | bytes 8847360 | tf_op jit(solution)/shard_map/reduce_scatter | solution.py:652
  984.5 48.8 %all-to-all-start.13 = ((bf16[4,192,1536]{2,1,0:T(8,128)(2,1)}), bf16[4,192,1536]{2,1,0:T(8,128)(2,1)S(1)}, u32[]{:S(2)}, u32[]{:S(2)}) async-start(bf16[4,192,1536]{2,1,0:T(8,128)(2,1)} %bitcast.347), calls=%async_computation.13 | async-start | bytes 4718592 | tf_op jit(solution)/shard_map/all_to_all | solution.py:60
  1037.1 38.9 %all-to-all-start.17 = ((bf16[4,48,4224]{2,1,0:T(8,128)(2,1)}), bf16[4,48,4224]{2,1,0:T(8,128)(2,1)S(1)}, u32[]{:S(2)}, u32[]{:S(2)}) async-start(bf16[4,48,4224]{2,1,0:T(8,128)(2,1)} %bitcast.312), calls=%async_computation.17 | async-start | bytes 3244032 | tf_op jit(solution)/shard_map/all_to_all | solution.py:85
  1076.1 43.3 %all-to-all-start.16 = ((bf16[4,256,1664]{2,1,0:T(8,128)(2,1)}), bf16[4,256,1664]{2,1,0:T(8,128)(2,1)}, u32[]{:S(2)}, u32[]{:S(2)}) async-start(bf16[4,256,1664]{2,1,0:T(8,128)(2,1)} %bitcast.95), calls=%async_computation.16 | async-start | bytes 6815744 | tf_op jit(solution)/shard_map/all_to_all | solution.py:60
  1080.8 283.2 %reduce-scatter.7.cloned.1.call-start = ((), (), s32[]{:S(2)}) async-start(), calls=%async_computation.37 | async-start | bytes 8847360 | tf_op jit(solution)/shard_map/reduce_scatter | solution.py:680
  1122.0 246.0 %reduce-scatter.11.cloned.1.call-start = ((), (), s32[]{:S(2)}) async-start(), calls=%async_computation.39 | async-start | bytes 8847360 | tf_op jit(solution)/shard_map/reduce_scatter | solution.py:681
  1176.1 48.3 %collective-permute-start.9 = (bf16[256,768]{0,1:T(8,128)(2,1)}, bf16[256,768]{0,1:T(8,128)(2,1)}, u32[]{:S(2)}, u32[]{:S(2)}) collective-permute-start(bf16[256,768]{0,1:T(8,128)(2,1)} %get-tuple-element.228), channel_id=1, source_target_pairs={{0,4},{4,0},{8,12},{12,8},{16,20},{20,16},{24,28},{28,24},{1,5},{5... | collective-permute-start | bytes 1179656 | tf_op jit(solution)/shard_map/ppermute | solution.py:81
  1199.2 31.0 %all-to-all-start.19 = ((bf16[4,192,1536]{2,1,0:T(8,128)(2,1)}), bf16[4,192,1536]{2,1,0:T(8,128)(2,1)S(1)}, u32[]{:S(2)}, u32[]{:S(2)}) async-start(bf16[4,192,1536]{2,1,0:T(8,128)(2,1)} %bitcast.346), calls=%async_computation.19 | async-start | bytes 4718592 | tf_op jit(solution)/shard_map/all_to_all | solution.py:60
  1255.7 31.8 %all-to-all-start.20 = ((bf16[4,192,1536]{2,1,0:T(8,128)(2,1)}), bf16[4,192,1536]{2,1,0:T(8,128)(2,1)}, u32[]{:S(2)}, u32[]{:S(2)}) async-start(bf16[4,192,1536]{2,1,0:T(8,128)(2,1)} %bitcast.349), calls=%async_computation.20 | async-start | bytes 4718592 | tf_op jit(solution)/shard_map/all_to_all | solution.py:60
  1304.1 32.4 %all-to-all-start.21 = ((bf16[4,48,3072]{2,1,0:T(8,128)(2,1)}), bf16[4,48,3072]{2,1,0:T(8,128)(2,1)}, u32[]{:S(2)}, u32[]{:S(2)}) async-start(bf16[4,48,3072]{2,1,0:T(8,128)(2,1)} %bitcast.324), calls=%async_computation.21 | async-start | bytes 2359296 | tf_op jit(solution)/shard_map/all_to_all | solution.py:85
  (79 other events, 871.3 us)
Sparse Core Ops, SparseCore 0:
  14.4 179.2 all-gather.7
  195.9 75.3 all-gather.9
  273.0 76.2 all-gather.11
  350.7 76.2 all-gather.13
  428.5 76.2 all-gather.15
  506.3 76.2 all-gather.17
  584.2 76.2 all-gather.19
  662.7 83.0 reduce-scatter.16
  762.2 82.9 reduce-scatter.12
  847.3 83.0 reduce-scatter.8
  932.7 83.0 reduce-scatter.14
  1122.1 81.7 reduce-scatter.6
  1206.3 83.0 reduce-scatter.10

commit v4 on v3

--- a/solution.py
+++ b/solution.py
@@ -87,12 +87,14 @@
     )
 
 
-def gather_staged(shard):
+def gather_chips(shard):
     chips = lax.axis_size("dp") // 2
+    return exchange_chips(jnp.broadcast_to(shard[None], (chips,) + shard.shape))
+
+
+def gather_groups(chip_rows):
     groups = lax.axis_size("expert")
-    rows, width = shard.shape
-    chip_rows = exchange_chips(jnp.broadcast_to(shard[None], (chips, rows, width)))
-    return exchange(jnp.broadcast_to(chip_rows[None], (groups, chips, rows, width)))
+    return exchange(jnp.broadcast_to(chip_rows[None], (groups,) + chip_rows.shape))
 
 
 def join_cores(own):
@@ -118,16 +120,27 @@
     return jnp.concatenate([rows, swap_cores(rows)], axis=0)
 
 
-def sum_groups(partial):
-    blocks = exchange(partial.reshape(lax.axis_size("expert"), -1, partial.shape[1]))
-    return jnp.sum(blocks.astype(jnp.float32), axis=0).astype(jnp.bfloat16)
-
-
-def sum_chips(partial):
-    blocks = exchange_chips(
-        partial.reshape(lax.axis_size("dp") // 2, -1, partial.shape[1])
-    )
-    return jnp.sum(blocks.astype(jnp.float32), axis=0)
+def halve(blocks, axis_name, step):
+    size = lax.axis_size(axis_name)
+    side = (lax.axis_index(axis_name) // step) % 2
+    mine = lax.dynamic_index_in_dim(blocks, side, 0, keepdims=False)
+    theirs = lax.dynamic_index_in_dim(blocks, 1 - side, 0, keepdims=False)
+    arrived = lax.ppermute(theirs, axis_name, [(i, i ^ step) for i in range(size)])
+    return (mine.astype(jnp.float32) + arrived.astype(jnp.float32)).astype(jnp.bfloat16)
+
+
+def halvings(axis_name, least):
+    steps = [lax.axis_size(axis_name) // 2]
+    while steps[-1] > least:
+        steps.append(steps[-1] // 2)
+    return [(axis_name, step) for step in steps]
+
+
+def halve_all(partial, steps):
+    width = partial.shape[-1]
+    for axis_name, step in steps:
+        partial = halve(partial.reshape(2, -1, width), axis_name, step)
+    return partial
 
 
 def dot_f32(left, right, left_dims, right_dims):
@@ -405,31 +418,16 @@
     out_ref[0, 0] = part_ref[...].astype(jnp.float32)
 
 
-def place_turned_kernel(part_ref, held_ref, out_ref):
-    del held_ref
-    out_ref[0, 0] = part_ref[...].astype(jnp.float32).T
-
-
-def place_turned_first_kernel(part_ref, out_ref):
-    out_ref[0, 0] = part_ref[...].astype(jnp.float32).T
-
-
-def place(part, held, layer, experts, turned):
+def place(part, held, layer, experts):
     rows = part.shape[0]
-    hidden = part.shape[1] // experts
-    block = (hidden, rows) if turned else (rows, hidden)
-    kernels = (
-        (place_turned_first_kernel, place_turned_kernel)
-        if turned
-        else (place_first_kernel, place_kernel)
-    )
-    in_specs = [pl.BlockSpec((rows, hidden), lambda e: (0, e))]
+    block = (rows, part.shape[1] // experts)
+    in_specs = [pl.BlockSpec(block, lambda e: (0, e))]
     operands = [part]
     if held is not None:
         in_specs.append(pl.BlockSpec(memory_space=pl.ANY))
         operands.append(held)
     return pl.pallas_call(
-        kernels[held is not None],
+        place_first_kernel if held is None else place_kernel,
         grid=(experts,),
         in_specs=in_specs,
         out_specs=pl.BlockSpec((1, 1) + block, lambda e: (layer, e, 0, 0)),
@@ -514,9 +512,6 @@
         for layer in range(LAYER_COUNT)
     ]
     packed = [lax.all_gather(shards[0], ("dp", "expert"), axis=0, tiled=True)]
-    staged = [gather_staged(shard) for shard in shards[1:]]
-    inputs, staged = lax.optimization_barrier((inputs, staged))
-    packed += [join_cores(own) for own in staged]
     ff_width = gate_weight.shape[3]
     hidden_width = exp_dev * ff_width
     gathered = [
@@ -536,6 +531,9 @@
         masked = jnp.where(hot, logits, -1e30)
         exps = jnp.where(hot, jnp.exp(masked - jnp.max(masked, axis=1, keepdims=True)), 0.0)
         return exps / jnp.sum(exps, axis=1, keepdims=True)
+
+    def expert_rows(act, down):
+        return dot_f32(act, down, (1,), (1,)).astype(jnp.bfloat16)
 
     def layer_forward(hidden, layer):
         full = packed[layer]
@@ -567,19 +565,29 @@
             axis=1,
         )
         key_value_all = gather_rows(key_value)
+        ahead = layer + 1 < LAYER_COUNT
+        if ahead:
+            key_value_all, next_shard = lax.optimization_barrier(
+                (key_value_all, shards[layer + 1])
+            )
+            next_rows = gather_chips(next_shard)
         attended = attention_forward(block_at, query_rotated, key_value_all)
         middle = hidden + dot_f32(attended, output_full, (1,), (1,))
         normed_two, inv_two = norm_forward(middle, gain_two)
         normed_two = normed_two.astype(jnp.bfloat16)
         arrived = gather_rows(normed_two)
+        if ahead:
+            arrived, next_rows = lax.optimization_barrier((arrived, next_rows))
+            next_rows = gather_groups(next_rows)
         share_all = shares_of(arrived, router_full, chosen_all[:, layer] > 0)
         share_own = shares_of(normed_two, router_full, chosen_hot[layer])
         share_local = lax.dynamic_slice_in_dim(share_all, my_group * exp_dev, exp_dev, axis=1)
         gate_low, up_low, scaled_act = expert_forward(
             arrived, gate_full, up_full, share_local
         )
-        out_rows = dot_f32(scaled_act, down_full, (1,), (1,)).astype(jnp.bfloat16)
-        output = middle + sum_rows(out_rows)
+        if ahead:
+            scaled_act, next_rows = lax.optimization_barrier((scaled_act, next_rows))
+            packed.append(join_cores(next_rows))
         kept_state = (
             hidden,
             inv_one,
@@ -605,18 +613,23 @@
             up_full,
             down_full,
         )
-        return (output, kept_state)
+        return kept_state
 
     hidden = inputs.astype(jnp.float32).reshape(token_total, model_width)
     kept_states = []
     for layer in range(LAYER_COUNT):
-        hidden, kept_state = layer_forward(hidden, layer)
+        kept_state = layer_forward(hidden, layer)
         kept_states.append(kept_state)
-    output = hidden.astype(jnp.bfloat16).reshape(sequences_per_device, block_length, model_width)
+        last_middle, last_act, last_down = kept_state[6], kept_state[14], kept_state[-1]
+        if layer + 1 < LAYER_COUNT:
+            hidden = last_middle + sum_rows(expert_rows(last_act, last_down))
+    output = None
     grad_hidden = cotangent.astype(jnp.float32).reshape(token_total, model_width)
     attention_list = [None] * LAYER_COUNT
     expert_held = [None] * 3
     waiting = None
+    group_steps = halvings("expert", 1)
+    chip_steps = halvings("dp", 2)
     for layer in range(LAYER_COUNT - 1, -1, -1):
         (
             layer_hidden,
@@ -645,8 +658,12 @@
         ) = kept_states[layer]
         grad_all = gather_rows(grad_hidden.astype(jnp.bfloat16))
         if waiting is not None:
-            grad_all, waiting = lax.optimization_barrier((grad_all, waiting))
-            waiting = [sum_groups(part) for part in waiting]
+            last_act, waiting = lax.optimization_barrier((last_act, waiting))
+            last_rows = expert_rows(last_act, last_down)
+            grad_all, waiting, last_rows = lax.optimization_barrier(
+                (grad_all, waiting, last_rows)
+            )
+            waiting = halve_all(waiting, group_steps[:1])
         grad_down = dot_f32(grad_all, scaled_act, (0,), (0,)).astype(jnp.bfloat16)
         grad_all, grad_down = lax.optimization_barrier((grad_all, grad_down))
         expert_parts = [lax.psum_scatter(grad_down, "dp", scatter_dimension=0, tiled=True)]
@@ -655,8 +672,8 @@
         )
         grad_gates = grad_sums[:, :exp_dev]
         if waiting is not None:
-            grad_rows, waiting = lax.optimization_barrier((grad_rows, waiting))
-            attention_list[layer + 1] = sum_chips(jnp.concatenate(waiting, axis=1))
+            output = last_middle + sum_rows(last_rows)
+            grad_rows, output = lax.optimization_barrier((grad_rows, output))
         grad_gate_w = dot_f32(arrived, grad_gate_val, (0,), (0,)).astype(jnp.bfloat16)
         grad_up_w = dot_f32(arrived, grad_up_val, (0,), (0,)).astype(jnp.bfloat16)
         gates_high = grad_gates.astype(jnp.bfloat16)
@@ -672,9 +689,10 @@
             jnp.concatenate([grad_rows, gate_columns], axis=1)
         )
         if waiting is not None:
-            back, attention_list[layer + 1] = lax.optimization_barrier(
-                (back, attention_list[layer + 1])
+            back, waiting, expert_held = lax.optimization_barrier(
+                (back, waiting, expert_held)
             )
+            waiting = halve_all(waiting, group_steps[1:])
         back, grad_gate_w, grad_up_w = lax.optimization_barrier((back, grad_gate_w, grad_up_w))
         expert_parts += [
             lax.psum_scatter(grad_gate_w, "dp", scatter_dimension=0, tiled=True),
@@ -694,10 +712,19 @@
         grad_middle = grad_hidden + grad_norm_mid
         grad_branch = grad_middle.astype(jnp.bfloat16)
         grad_output_w = dot_f32(core_major(grad_branch), both_cores(attended), (0,), (0,))
+        grad_output_w = grad_output_w.astype(jnp.bfloat16)
+        if layer == 0:
+            grad_output_w = halve_all(grad_output_w, group_steps[:1])
         grad_attended = dot_f32(grad_branch, output_full, (1,), (0,)).astype(jnp.bfloat16)
         grad_query, grad_key_value_all = attention_backward(
             block_at, query_rotated, grad_attended, key_value_all
         )
+        if waiting is not None:
+            grad_query, waiting = lax.optimization_barrier((grad_query, waiting))
+            attention_list[layer + 1] = halve_all(waiting, chip_steps)
+        if layer == 0:
+            grad_query, grad_output_w = lax.optimization_barrier((grad_query, grad_output_w))
+            grad_output_w = halve_all(grad_output_w, group_steps[1:])
         grad_kv = sum_rows(grad_key_value_all).reshape(token_total, -1, 2, 2 * HEAD_SIZE)
         grad_kv = grad_kv.transpose(0, 2, 1, 3).reshape(token_total, 2 * key_width)
         grad_query_lin = (
@@ -740,23 +767,24 @@
         )
         small_split = core_major(small_part.T).reshape(2, small_width, -1)
         small_half = jnp.sum(small_split.astype(jnp.float32), axis=0).T
-        grad_kv_w = jnp.concatenate([grad_kv_w, small_half], axis=1)
-        partials = [grad_output_w, grad_query_w, grad_kv_w]
-        partials = [partial.astype(jnp.bfloat16) for partial in partials]
+        grad_kv_w = jnp.concatenate([grad_kv_w, small_half], axis=1).astype(jnp.bfloat16)
+        grad_query_w = grad_query_w.astype(jnp.bfloat16)
         if layer > 0:
-            waiting = partials
+            waiting = jnp.concatenate([grad_output_w, grad_query_w, grad_kv_w], axis=1)
         else:
-            early = [sum_groups(part) for part in partials[:2]]
             attention_list[layer] = jnp.concatenate(
-                [sum_chips(jnp.concatenate(early, axis=1)), sum_chips(sum_groups(partials[2]))],
+                [
+                    halve_all(grad_output_w, chip_steps),
+                    halve_all(grad_query_w, group_steps + chip_steps),
+                    halve_all(grad_kv_w, group_steps + chip_steps),
+                ],
                 axis=1,
             )
         expert_held = [
-            place(part, held, layer, exp_dev, turned)
-            for part, held, turned in zip(expert_parts, expert_held, (True, False, False))
+            place(part, held, layer, exp_dev) for part, held in zip(expert_parts, expert_held)
         ]
         grad_hidden = grad_middle + grad_norm_in
-    stacked = jnp.stack(attention_list)
+    stacked = jnp.stack(attention_list).astype(jnp.float32)
     cuts = [query_width, query_width, key_width, key_width, expert_total, 1, 1]
     cuts = [sum(cuts[:index]) for index in range(len(cuts) + 1)]
     output_grads, query_grads, key_grads, value_grads, router_grads, one, two = (
@@ -764,7 +792,7 @@
     )
     down_grads, gate_grads, up_grads = expert_held
     return (
-        output,
+        output.astype(jnp.bfloat16).reshape(sequences_per_device, block_length, model_width),
         grad_hidden.reshape(sequences_per_device, block_length, model_width),
         query_grads,
         key_grads,
@@ -775,7 +803,7 @@
         router_grads,
         gate_grads,
         up_grads,
-        down_grads,
+        jnp.swapaxes(down_grads, 2, 3),
     )
 
 

time: 1390 us -> 1350 us (0.971)
  blocking collectives: 94.3 us -> 39.7 us
  waiting for transfers between devices: 494 us -> 541 us
    ppermute x0 -> x16, waiting for transfers between devices: none -> 135 us  [halve(): lax.ppermute(theirs, axis_name, [(i, i ^ step) for i in range(size)])]
    all_gather x6, waiting for transfers between devices: 98.7 us -> 0.03 us  [body(): lax.all_gather(rows.reshape(-1, hidden_width), 'dp', axis=0, tiled=True)]
    all_gather x1, waiting for transfers between devices: 2.23 us -> 83.7 us  [body(): packed = [lax.all_gather(shards[0], ('dp', 'expert'), axis=0, tiled=True)]]
    all_to_all x3 -> x1, blocking collectives: 94.3 us -> 39.7 us  [exchange(): lax.all_to_all(blocks, 'expert', split_axis=0, concat_axis=0, tiled=True)]
    all_to_all x4 -> x1, waiting for transfers between devices: 110 us -> 71.4 us  [exchange_chips(): lax.all_to_all(blocks, 'dp', split_axis=0, concat_axis=0, axis_index_grou...]
    all_to_all x17 -> x13, waiting for transfers between devices: 277 us -> 251 us  [exchange(): lax.all_to_all(blocks, 'expert', split_axis=0, concat_axis=0, tiled=True)]
    ppermute x0 -> x16, starting transfers between devices: none -> 17.3 us  [halve(): lax.ppermute(theirs, axis_name, [(i, i ^ step) for i in range(size)])]
    all_to_all x17 -> x13, starting transfers between devices: 76.3 us -> 60.2 us  [exchange(): lax.all_to_all(blocks, 'expert', split_axis=0, concat_axis=0, tiled=True)]
  transfers between devices with their start and end apart: 47 -> 56, of which waited for: 25 -> 24; matrix products, arithmetic and copies ran while one was open for 28% -> 27% of each run, Pallas kernels for 19% -> 20%
where the time goes in v4:
time: 1350 us; the launch traced here: 1340 us
  waiting for transfers between devices  541 us (40%)
  Pallas kernels  269 us (20%)
  matrix products  179 us (13%)
  local copies, waits for them, and re-layouts  130 us (10%)
  starting transfers between devices  85.9 us (6%)
  other arithmetic  79.4 us (6%)
  blocking collectives  39.7 us (3%)
  between operations  16.5 us (1%)
    all_to_all x13, waiting for transfers between devices, exchange(): lax.all_to_all(blocks, 'expert', split_axis=0, concat_axis=0, tiled=True)  251 us
    dot_general x26, matrix products, dot_f32(): lax.dot_general(left, right, ((left_dims, right_dims), ((), ())), preferr...  162 us
    ppermute x16, waiting for transfers between devices, halve(): lax.ppermute(theirs, axis_name, [(i, i ^ step) for i in range(size)])  135 us
    all_gather x1, waiting for transfers between devices, body(): packed = [lax.all_gather(shards[0], ('dp', 'expert'), axis=0, tiled=True)]  83.7 us
    pallas_call x2, Pallas kernels, expert_backward(): pl.pallas_call(expert_backward_kernel, grid=(experts, 2), in_specs=[row_b...  80 us
    all_to_all x1, waiting for transfers between devices, exchange_chips(): lax.all_to_all(blocks, 'dp', split_axis=0, concat_axis=0, axis_index_grou...  71.4 us
    pallas_call x2, Pallas kernels, attention_backward(): pl.pallas_call(attention_backward_kernel, grid_spec=pltpu.PrefetchScalarG...  62.5 us
    all_to_all x13, starting transfers between devices, exchange(): lax.all_to_all(blocks, 'expert', split_axis=0, concat_axis=0, tiled=True)  60.2 us
  transfers between devices with their start and end apart: 56, of which 24 were waited for; matrix products, arithmetic and copies ran while one was open for 27% of the time, Pallas kernels for 20%

profile of v4, /device:TPU:0, one launch (start us, length us, event | category | flops | bytes accessed | tf_op | source)
XLA Modules:
  0.0 1341.2 jit_solution(3640642827444173305)
XLA Ops:
  32.9 83.7 %all-gather.8.cloned.1.call-done = bf16[1536,4224]{1,0:T(8,128)(2,1)} async-done(((bf16[48,4224]{1,0:T(8,128)(2,1)}), bf16[1536,4224]{1,0:T(8,128)(2,1)}) %all-gather.8.cloned.1.call-update) | async-done | bytes 12976144 | tf_op jit(solution)/shard_map/all_gather | solution.py:514
  138.8 19.1 %all-to-all-done = bf16[4,256,1024]{2,1,0:T(8,128)(2,1)} async-done(((bf16[4,256,1024]{2,1,0:T(8,128)(2,1)}), bf16[4,256,1024]{2,1,0:T(8,128)(2,1)}, u32[]{:S(2)}, u32[]{:S(2)}) %all-to-all-start) | async-done | bytes 2097184 | tf_op jit(solution)/shard_map/all_to_all | solution.py:60
  157.9 23.3 %shard_map.220 = bf16[256,1536]{1,0:T(8,128)(2,1)} custom-call(s32[1]{0:T(128)} %bitcast.2.block_ref, bf16[256,1536]{1,0:T(8,128)(2,1)} %copy.315.query_ref, bf16[1024,1024]{1,0:T(8,128)(2,1)} %bitcast.15.key_ref.value_ref, bf16[1024,1024]{1,0:T(8,128)(2,1)} %bitcast.15.key_ref.value_ref), custom_call_target="tpu_custom_call" | custom-call | flops 6442450944 | bytes 3670016 | tf_op jit(solution)/shard_map/pallas_call | solution.py:342
  196.3 33.0 %all-to-all-done.1 = bf16[4,256,1536]{2,1,0:T(8,128)(2,1)} async-done(((bf16[4,256,1536]{2,1,0:T(8,128)(2,1)}), bf16[4,256,1536]{2,1,0:T(8,128)(2,1)}, u32[]{:S(2)}, u32[]{:S(2)}) %all-to-all-start.1) | async-done | bytes 3145760 | tf_op jit(solution)/shard_map/all_to_all | solution.py:60
  234.5 71.4 %all-to-all-done.2 = bf16[4,48,4224]{2,1,0:T(8,128)(2,1)S(1)} async-done(((bf16[4,48,4224]{2,1,0:T(8,128)(2,1)}), bf16[4,48,4224]{2,1,0:T(8,128)(2,1)S(1)}, u32[]{:S(2)}, u32[]{:S(2)}) %all-to-all-start.2) | async-done | bytes 1622048 | tf_op jit(solution)/shard_map/all_to_all | solution.py:85
  328.3 28.2 %shard_map.221 = (bf16[1024,2560]{1,0:T(8,128)(2,1)}, bf16[1024,2560]{1,0:T(8,128)(2,1)}, bf16[1024,2560]{1,0:T(8,128)(2,1)}) custom-call(bf16[1024,1536]{1,0:T(8,128)(2,1)} %bitcast.24.rows_ref, bf16[1536,2560]{1,0:T(8,128)(2,1)} %all-gather.10.cloned.1.call-done.gate_ref, bf16[1536,2560]{1,0:T(8,128)(2,1)} %all-gather.12.cloned.1.call-done.up_ref, ...), custom_call_target="tpu_custom_call" | custom-call | flops 16106127360 | bytes 31457280 | tf_op jit(solution)/shard_map/pallas_call | solution.py:184
  356.5 38.1 %all-to-all-done.4 = bf16[4,4,48,4224]{3,2,1,0:T(8,128)(2,1)} async-done(((bf16[4,4,48,4224]{3,2,1,0:T(8,128)(2,1)}), bf16[4,4,48,4224]{3,2,1,0:T(8,128)(2,1)}, u32[]{:S(2)}, u32[]{:S(2)}) %all-to-all-start.4) | async-done | bytes 6488096 | tf_op jit(solution)/shard_map/all_to_all | solution.py:60
  400.7 13.4 convolution_convert_fusion.7
  421.7 34.2 %all-to-all-done.5 = bf16[4,256,1536]{2,1,0:T(8,128)(2,1)} async-done(((bf16[4,256,1536]{2,1,0:T(8,128)(2,1)}), bf16[4,256,1536]{2,1,0:T(8,128)(2,1)}, u32[]{:S(2)}, u32[]{:S(2)}) %all-to-all-start.5) | async-done | bytes 3145760 | tf_op jit(solution)/shard_map/all_to_all | solution.py:60
  485.7 18.9 %all-to-all-done.6 = bf16[4,256,1024]{2,1,0:T(8,128)(2,1)} async-done(((bf16[4,256,1024]{2,1,0:T(8,128)(2,1)}), bf16[4,256,1024]{2,1,0:T(8,128)(2,1)}, u32[]{:S(2)}, u32[]{:S(2)}) %all-to-all-start.6) | async-done | bytes 2097184 | tf_op jit(solution)/shard_map/all_to_all | solution.py:60
  504.7 23.3 %shard_map.222 = bf16[256,1536]{1,0:T(8,128)(2,1)} custom-call(s32[1]{0:T(128)} %bitcast.2.block_ref, bf16[256,1536]{1,0:T(8,128)(2,1)} %copy.332.query_ref, bf16[1024,1024]{1,0:T(8,128)(2,1)} %bitcast.48.key_ref.value_ref, bf16[1024,1024]{1,0:T(8,128)(2,1)} %bitcast.48.key_ref.value_ref), custom_call_target="tpu_custom_call" | custom-call | flops 6442450944 | bytes 3670016 | tf_op jit(solution)/shard_map/pallas_call | solution.py:342
  533.4 39.7 %all_to_all.75 = bf16[4,256,1536]{2,1,0:T(8,128)(2,1)} all-to-all(bf16[4,256,1536]{2,1,0:T(8,128)(2,1)S(1)} %broadcast_in_dim.45), channel_id=1, replica_groups=mesh['dp'=8,'expert'=4] {'expert'}, dimensions={0} | all-to-all | bytes 6291456 | tf_op jit(solution)/shard_map/all_to_all | solution.py:60
  584.7 28.0 %shard_map.223 = (bf16[1024,2560]{1,0:T(8,128)(2,1)}, bf16[1024,2560]{1,0:T(8,128)(2,1)}, bf16[1024,2560]{1,0:T(8,128)(2,1)}) custom-call(bf16[1024,1536]{1,0:T(8,128)(2,1)} %bitcast.436, bf16[1536,2560]{1,0:T(8,128)(2,1)} %all-gather.16.cloned.1.call-done.gate_ref, bf16[1536,2560]{1,0:T(8,128)(2,1)} %all-gather.18.cloned.1.call-done.up_ref, ...), custom_call_target="tpu_custom_call" | custom-call | flops 16106127360 | bytes 31457280 | tf_op jit(solution)/shard_map/pallas_call | solution.py:184
  614.2 13.5 %fusion = bf16[1536,2560]{1,0:T(8,128)(2,1)} fusion(bf16[1024,2560]{1,0:T(8,128)(2,1)} %get-tuple-element.81, bf16[1024,1536]{1,0:T(8,128)(2,1)} %bitcast.49.grad_ref), kind=kOutput, calls=%fused_computation.7 | convolution fusion | flops 8056995840 | bytes 16252928 | tf_op jit(solution)/shard_map/dot_general | solution.py:147
  627.7 40.0 %shard_map.224 = (bf16[1024,2560]{1,0:T(8,128)(2,1)}, bf16[1024,2560]{1,0:T(8,128)(2,1)}, bf16[1024,1536]{1,0:T(8,128)(2,1)}, f32[1024,128]{1,0:T(8,128)}) custom-call(bf16[1024,1536]{1,0:T(8,128)(2,1)} %bitcast.49.grad_ref, bf16[1536,2560]{1,0:T(8,128)(2,1)} %all-gather.20.cloned.1.call-done.down_ref, ...), custom_call_target="tpu_custom_call" | custom-call | flops 24159191040 | bytes 44564480 | tf_op jit(solution)/shard_map/pallas_call | solution.py:269
  685.5 13.5 %convolution_convert_fusion.3 = bf16[1536,2560]{1,0:T(8,128)(2,1)} fusion(bf16[1024,1536]{1,0:T(8,128)(2,1)} %bitcast.437, bf16[1024,2560]{1,0:T(8,128)(2,1)} %get-tuple-element.76), kind=kOutput, calls=%fused_computation.4 | convolution fusion | flops 8056995840 | bytes 16252928 | tf_op jit(solution)/shard_map/dot_general | solution.py:147
  699.1 13.6 %convolution_convert_fusion.4 = bf16[1536,2560]{1,0:T(8,128)(2,1)} fusion(bf16[1024,1536]{1,0:T(8,128)(2,1)} %bitcast.438, bf16[1024,2560]{1,0:T(8,128)(2,1)} %get-tuple-element.75), kind=kOutput, calls=%fused_computation.5 | convolution fusion | flops 8056995840 | bytes 16252928 | tf_op jit(solution)/shard_map/dot_general | solution.py:147
  712.7 11.2 all-to-all-done.9
  740.9 31.1 %shard_map.225 = (f32[256,1536]{1,0:T(8,128)}, bf16[1024,1024]{1,0:T(8,128)(2,1)}) custom-call(s32[1]{0:T(128)} %bitcast.2.block_ref, bf16[256,1536]{1,0:T(8,128)(2,1)} %copy.332.query_ref, bf16[256,1536]{1,0:T(8,128)(2,1)} %fusion.38.grad_ref, bf16[1024,1024]{1,0:T(8,128)(2,1)} %bitcast.48.key_ref.value_ref, bf16[1024,1024]{1,0:T(8,128)(2,1)} %bitcast.48.key_ref.value_ref), custom_call_target="tpu_custom_call" | custom-call | flops 16106127360 | bytes 7340032 | tf_op jit(solution)/shard_map/pallas_call | solution.py:389
  840.7 11.4 convolution_convert_fusion.6
  852.1 15.1 %all-to-all-done.11 = bf16[4,256,1536]{2,1,0:T(8,128)(2,1)} async-done(((bf16[4,256,1536]{2,1,0:T(8,128)(2,1)}), bf16[4,256,1536]{2,1,0:T(8,128)(2,1)}, u32[]{:S(2)}, u32[]{:S(2)}) %all-to-all-start.11) | async-done | bytes 3145760 | tf_op jit(solution)/shard_map/all_to_all | solution.py:60
  867.3 13.6 %convolution_convert_fusion.2 = bf16[1536,2560]{1,0:T(8,128)(2,1)} fusion(bf16[1024,1536]{1,0:T(8,128)(2,1)} %bitcast.72.grad_ref, bf16[1024,2560]{1,0:T(8,128)(2,1)} %get-tuple-element.67), kind=kOutput, calls=%fused_computation.3 | convolution fusion | flops 8056995840 | bytes 16252928 | tf_op jit(solution)/shard_map/dot_general | solution.py:147
  891.4 40.0 %shard_map.226 = (bf16[1024,2560]{1,0:T(8,128)(2,1)}, bf16[1024,2560]{1,0:T(8,128)(2,1)}, bf16[1024,1536]{1,0:T(8,128)(2,1)}, f32[1024,128]{1,0:T(8,128)}) custom-call(bf16[1024,1536]{1,0:T(8,128)(2,1)} %bitcast.72.grad_ref, bf16[1536,2560]{1,0:T(8,128)(2,1)} %all-gather.14.cloned.1.call-done.down_ref, ...), custom_call_target="tpu_custom_call" | custom-call | flops 24159191040 | bytes 44564480 | tf_op jit(solution)/shard_map/pallas_call | solution.py:269
  931.4 13.6 %convolution_convert_fusion = bf16[1536,2560]{1,0:T(8,128)(2,1)} fusion(bf16[1024,1536]{1,0:T(8,128)(2,1)} %bitcast.24.rows_ref, bf16[1024,2560]{1,0:T(8,128)(2,1)} %get-tuple-element.97), kind=kOutput, calls=%fused_computation.1 | convolution fusion | flops 8056995840 | bytes 16252928 | tf_op jit(solution)/shard_map/dot_general | solution.py:147
  948.0 42.4 %all-to-all-done.12 = bf16[4,256,1536]{2,1,0:T(8,128)(2,1)} async-done(((bf16[4,256,1536]{2,1,0:T(8,128)(2,1)}), bf16[4,256,1536]{2,1,0:T(8,128)(2,1)}, u32[]{:S(2)}, u32[]{:S(2)}) %all-to-all-start.12) | async-done | bytes 3145760 | tf_op jit(solution)/shard_map/all_to_all | solution.py:60
  1001.2 13.6 %convolution_convert_fusion.1 = bf16[1536,2560]{1,0:T(8,128)(2,1)} fusion(bf16[1024,1536]{1,0:T(8,128)(2,1)} %bitcast.24.rows_ref, bf16[1024,2560]{1,0:T(8,128)(2,1)} %get-tuple-element.96), kind=kOutput, calls=%fused_computation.2 | convolution fusion | flops 8056995840 | bytes 16252928 | tf_op jit(solution)/shard_map/dot_general | solution.py:147
  1020.1 18.9 %all-to-all-done.13 = bf16[4,256,1664]{2,1,0:T(8,128)(2,1)S(1)} async-done(((bf16[4,256,1664]{2,1,0:T(8,128)(2,1)}), bf16[4,256,1664]{2,1,0:T(8,128)(2,1)S(1)}, u32[]{:S(2)}, u32[]{:S(2)}) %all-to-all-start.13) | async-done | bytes 3407904 | tf_op jit(solution)/shard_map/all_to_all | solution.py:60
  1069.6 31.4 %shard_map.230 = (f32[256,1536]{1,0:T(8,128)}, bf16[1024,1024]{1,0:T(8,128)(2,1)}) custom-call(s32[1]{0:T(128)} %bitcast.2.block_ref, bf16[256,1536]{1,0:T(8,128)(2,1)} %copy.315.query_ref, bf16[256,1536]{1,0:T(8,128)(2,1)} %fusion.35.grad_ref, bf16[1024,1024]{1,0:T(8,128)(2,1)} %bitcast.15.key_ref.value_ref, bf16[1024,1024]{1,0:T(8,128)(2,1)} %bitcast.15.key_ref.value_ref), custom_call_target="tpu_custom_call" | custom-call | flops 16106127360 | bytes 7340032 | tf_op jit(solution)/shard_map/pallas_call | solution.py:389
  1118.5 13.6 %all-to-all-done.14 = bf16[4,256,1024]{2,1,0:T(8,128)(2,1)} async-done(((bf16[4,256,1024]{2,1,0:T(8,128)(2,1)}), bf16[4,256,1024]{2,1,0:T(8,128)(2,1)}, u32[]{:S(2)}, u32[]{:S(2)}) %all-to-all-start.14) | async-done | bytes 2097184 | tf_op jit(solution)/shard_map/all_to_all | solution.py:60
  1140.1 16.2 %collective-permute-done.11 = bf16[384,1536]{1,0:T(8,128)(2,1)} collective-permute-done((bf16[384,1536]{1,0:T(8,128)(2,1)}, bf16[384,1536]{1,0:T(8,128)(2,1)}, u32[]{:S(2)}, u32[]{:S(2)}) %collective-permute-start.11) | collective-permute-done | bytes 1179680 | tf_op jit(solution)/shard_map/ppermute | solution.py:128
  1198.8 55.0 %collective-permute-done.27 = bf16[96,4224]{1,0:T(8,128)(2,1)} collective-permute-done((bf16[96,4224]{1,0:T(8,128)(2,1)}, bf16[96,4224]{1,0:T(8,128)(2,1)}, u32[]{:S(2)}, u32[]{:S(2)}) %collective-permute-start.27) | collective-permute-done | bytes 811040 | tf_op jit(solution)/shard_map/ppermute | solution.py:128
  1304.2 12.7 collective-permute-done.19
  (511 shorter events, 450.0 us)
Async XLA Ops:
  7.2 109.4 %all-gather.8.cloned.1.call-start = ((), (), s32[]{:S(2)}) async-start(), calls=%async_computation.21 | async-start | bytes 13381632 | tf_op jit(solution)/shard_map/all_gather | solution.py:514
  16.5 311.8 %all-gather.10.cloned.1.call-start = ((), (), s32[]{:S(2)}) async-start(), calls=%async_computation.22 | async-start | bytes 8847360 | tf_op jit(solution)/shard_map/all_gather | solution.py:519
  20.3 308.0 %all-gather.12.cloned.1.call-start = ((), (), s32[]{:S(2)}) async-start(), calls=%async_computation.23 | async-start | bytes 8847360 | tf_op jit(solution)/shard_map/all_gather | solution.py:519
  25.0 375.7 %all-gather.14.cloned.1.call-start = ((), (), s32[]{:S(2)}) async-start(), calls=%async_computation.24 | async-start | bytes 8847360 | tf_op jit(solution)/shard_map/all_gather | solution.py:519
  29.7 555.0 %all-gather.16.cloned.1.call-start = ((), (), s32[]{:S(2)}) async-start(), calls=%async_computation.25 | async-start | bytes 8847360 | tf_op jit(solution)/shard_map/all_gather | solution.py:519
  193.3 391.4 %all-gather.18.cloned.1.call-start = ((), (), s32[]{:S(2)}) async-start(), calls=%async_computation.26 | async-start | bytes 8847360 | tf_op jit(solution)/shard_map/all_gather | solution.py:519
  230.6 75.3 %all-to-all-start.2 = ((bf16[4,48,4224]{2,1,0:T(8,128)(2,1)}), bf16[4,48,4224]{2,1,0:T(8,128)(2,1)S(1)}, u32[]{:S(2)}, u32[]{:S(2)}) async-start(bf16[4,48,4224]{2,1,0:T(8,128)(2,1)} %broadcast_in_dim.38), calls=%async_computation.2 | async-start | bytes 3244032 | tf_op jit(solution)/shard_map/all_to_all | solution.py:85
  318.0 76.6 %all-to-all-start.4 = ((bf16[4,4,48,4224]{3,2,1,0:T(8,128)(2,1)}), bf16[4,4,48,4224]{3,2,1,0:T(8,128)(2,1)}, u32[]{:S(2)}, u32[]{:S(2)}) async-start(bf16[4,4,48,4224]{3,2,1,0:T(8,128)(2,1)} %broadcast_in_dim.42), calls=%async_computation.4 | async-start | bytes 12976128 | tf_op jit(solution)/shard_map/all_to_all | solution.py:60
  400.7 58.1 %collective-permute-start = (bf16[4,4,48,4224]{3,2,0,1:T(8,128)(2,1)}, bf16[4,4,48,4224]{3,2,0,1:T(8,128)(2,1)}, u32[]{:S(2)}, u32[]{:S(2)}) collective-permute-start(bf16[4,4,48,4224]{3,2,0,1:T(8,128)(2,1)} %copy.326), channel_id=1, source_target_pairs={{0,4},{4,0},{8,12},{12,8},{16,20},{20,16},{24,28},{28,24},{1,5},{5... | collective-permute-start | bytes 19464200 | tf_op jit(solution)/shard_map/ppermute | solution.py:81
  414.1 41.8 %all-to-all-start.5 = ((bf16[4,256,1536]{2,1,0:T(8,128)(2,1)}), bf16[4,256,1536]{2,1,0:T(8,128)(2,1)}, u32[]{:S(2)}, u32[]{:S(2)}) async-start(bf16[4,256,1536]{2,1,0:T(8,128)(2,1)} %bitcast.439), calls=%async_computation.5 | async-start | bytes 6291456 | tf_op jit(solution)/shard_map/all_to_all | solution.py:60
  418.7 209.0 %all-gather.20.cloned.1.call-start = ((), (), s32[]{:S(2)}) async-start(), calls=%async_computation.27 | async-start | bytes 8847360 | tf_op jit(solution)/shard_map/all_gather | solution.py:519
  579.7 460.9 %reduce-scatter.7.cloned.1.call-start = ((), (), s32[]{:S(2)}) async-start(), calls=%async_computation.28 | async-start | bytes 8847360 | tf_op jit(solution)/shard_map/reduce_scatter | solution.py:669
  680.6 43.3 %all-to-all-start.9 = ((bf16[4,256,1664]{2,1,0:T(8,128)(2,1)}), bf16[4,256,1664]{2,1,0:T(8,128)(2,1)}, u32[]{:S(2)}, u32[]{:S(2)}) async-start(bf16[4,256,1664]{2,1,0:T(8,128)(2,1)} %bitcast.401), calls=%async_computation.9 | async-start | bytes 6815744 | tf_op jit(solution)/shard_map/all_to_all | solution.py:60
  685.3 359.4 %reduce-scatter.9.cloned.1.call-start = ((), (), s32[]{:S(2)}) async-start(), calls=%async_computation.29 | async-start | bytes 8847360 | tf_op jit(solution)/shard_map/reduce_scatter | solution.py:698
  727.7 321.0 %reduce-scatter.11.cloned.1.call-start = ((), (), s32[]{:S(2)}) async-start(), calls=%async_computation.30 | async-start | bytes 8847360 | tf_op jit(solution)/shard_map/reduce_scatter | solution.py:699
  825.1 42.2 %all-to-all-start.11 = ((bf16[4,256,1536]{2,1,0:T(8,128)(2,1)}), bf16[4,256,1536]{2,1,0:T(8,128)(2,1)}, u32[]{:S(2)}, u32[]{:S(2)}) async-start(bf16[4,256,1536]{2,1,0:T(8,128)(2,1)} %broadcast_in_dim.48), calls=%async_computation.11 | async-start | bytes 6291456 | tf_op jit(solution)/shard_map/all_to_all | solution.py:60
  829.9 487.2 %reduce-scatter.17.cloned.1.call-start = ((), (), s32[]{:S(2)}) async-start(), calls=%async_computation.33 | async-start | bytes 8847360 | tf_op jit(solution)/shard_map/reduce_scatter | solution.py:669
  884.8 130.0 %collective-permute-start.7 = (bf16[384,4224]{1,0:T(8,128)(2,1)}, bf16[384,4224]{1,0:T(8,128)(2,1)}, u32[]{:S(2)}, u32[]{:S(2)}) collective-permute-start(bf16[384,4224]{1,0:T(8,128)(2,1)} %dynamic-slice_bitcast_fusion), channel_id=1, source_target_pairs={{0,2},{1,3},{2,0},{3,1},{4,6},{5,7},{6,4},{7,5},{8,10},{9,11},{10,... | collective-permute-start | bytes 9732104 | tf_op jit(solution)/shard_map/ppermute | solution.py:128
  886.3 104.2 %all-to-all-start.12 = ((bf16[4,256,1536]{2,1,0:T(8,128)(2,1)}), bf16[4,256,1536]{2,1,0:T(8,128)(2,1)}, u32[]{:S(2)}, u32[]{:S(2)}) async-start(bf16[4,256,1536]{2,1,0:T(8,128)(2,1)} %bitcast.434), calls=%async_computation.12 | async-start | bytes 6291456 | tf_op jit(solution)/shard_map/all_to_all | solution.py:60
  997.2 41.8 %all-to-all-start.13 = ((bf16[4,256,1664]{2,1,0:T(8,128)(2,1)}), bf16[4,256,1664]{2,1,0:T(8,128)(2,1)S(1)}, u32[]{:S(2)}, u32[]{:S(2)}) async-start(bf16[4,256,1664]{2,1,0:T(8,128)(2,1)} %bitcast.400), calls=%async_computation.13 | async-start | bytes 6815744 | tf_op jit(solution)/shard_map/all_to_all | solution.py:60
  1001.0 325.1 %reduce-scatter.15.cloned.1.call-start = ((), (), s32[]{:S(2)}) async-start(), calls=%async_computation.32 | async-start | bytes 8847360 | tf_op jit(solution)/shard_map/reduce_scatter | solution.py:699
  1056.4 52.9 %collective-permute-start.10 = (bf16[256,1536]{1,0:T(8,128)(2,1)}, bf16[256,1536]{1,0:T(8,128)(2,1)}, u32[]{:S(2)}, u32[]{:S(2)}) collective-permute-start(bf16[256,1536]{1,0:T(8,128)(2,1)} %shard_map.220), channel_id=1, source_target_pairs={{0,4},{4,0},{8,12},{12,8},{16,20},{20,16},{24,28},{28,24},{1,5},{5... | collective-permute-start | bytes 2359304 | tf_op jit(solution)/shard_map/ppermute | solution.py:81
  1064.5 44.8 %collective-permute-start.9 = (bf16[256,768]{0,1:T(8,128)(2,1)}, bf16[256,768]{0,1:T(8,128)(2,1)}, u32[]{:S(2)}, u32[]{:S(2)}) collective-permute-start(bf16[256,768]{0,1:T(8,128)(2,1)} %get-tuple-element.235), channel_id=1, source_target_pairs={{0,4},{4,0},{8,12},{12,8},{16,20},{20,16},{24,28},{28,24},{1,5},{5... | collective-permute-start | bytes 1179656 | tf_op jit(solution)/shard_map/ppermute | solution.py:81
  1105.7 224.4 %reduce-scatter.13.cloned.1.call-start = ((), (), s32[]{:S(2)}) async-start(), calls=%async_computation.31 | async-start | bytes 8847360 | tf_op jit(solution)/shard_map/reduce_scatter | solution.py:698
  1107.4 58.5 %collective-permute-start.8 = (bf16[192,4224]{1,0:T(8,128)(2,1)}, bf16[192,4224]{1,0:T(8,128)(2,1)}, u32[]{:S(2)}, u32[]{:S(2)}) collective-permute-start(bf16[192,4224]{1,0:T(8,128)(2,1)} %dynamic-slice_bitcast_fusion.1), channel_id=1, source_target_pairs={{0,1},{1,0},{2,3},{3,2},{4,5},{5,4},{6,7},{7,6},{8,9},{9,8},{10,11... | collective-permute-start | bytes 4866056 | tf_op jit(solution)/shard_map/ppermute | solution.py:128
  1113.1 43.2 %collective-permute-start.11 = (bf16[384,1536]{1,0:T(8,128)(2,1)}, bf16[384,1536]{1,0:T(8,128)(2,1)}, u32[]{:S(2)}, u32[]{:S(2)}) collective-permute-start(bf16[384,1536]{1,0:T(8,128)(2,1)} %dynamic-slice_bitcast_fusion.3), channel_id=1, source_target_pairs={{0,2},{1,3},{2,0},{3,1},{4,6},{5,7},{6,4},{7,5},{8,10},{9,11},{10,... | collective-permute-start | bytes 3538952 | tf_op jit(solution)/shard_map/ppermute | solution.py:128
  1115.9 70.3 %collective-permute-start.15 = (bf16[256,768]{0,1:T(8,128)(2,1)}, bf16[256,768]{0,1:T(8,128)(2,1)}, u32[]{:S(2)}, u32[]{:S(2)}) collective-permute-start(bf16[256,768]{0,1:T(8,128)(2,1)} %get-tuple-element.233), channel_id=1, source_target_pairs={{0,4},{4,0},{8,12},{12,8},{16,20},{20,16},{24,28},{28,24},{1,5},{5... | collective-permute-start | bytes 1179656 | tf_op jit(solution)/shard_map/ppermute | solution.py:81
  1140.1 46.2 %collective-permute-start.21 = (bf16[256,1024]{0,1:T(8,128)(2,1)}, bf16[256,1024]{0,1:T(8,128)(2,1)}, u32[]{:S(2)}, u32[]{:S(2)}) collective-permute-start(bf16[256,1024]{0,1:T(8,128)(2,1)} %pad_maximum_fusion.13), channel_id=1, source_target_pairs={{0,4},{4,0},{8,12},{12,8},{16,20},{20,16},{24,28},{28,24},{1,5},{5... | collective-permute-start | bytes 1572872 | tf_op jit(solution)/shard_map/ppermute | solution.py:81
  1184.9 68.9 %collective-permute-start.27 = (bf16[96,4224]{1,0:T(8,128)(2,1)}, bf16[96,4224]{1,0:T(8,128)(2,1)}, u32[]{:S(2)}, u32[]{:S(2)}) collective-permute-start(bf16[96,4224]{1,0:T(8,128)(2,1)} %dynamic-slice_bitcast_fusion.4), channel_id=1, source_target_pairs={{0,16},{4,20},{8,24},{12,28},{16,0},{20,4},{24,8},{28,12},{1,17},{... | collective-permute-start | bytes 2433032 | tf_op jit(solution)/shard_map/ppermute | solution.py:128
  1188.5 89.4 %collective-permute-start.23 = (bf16[384,1152]{1,0:T(8,128)(2,1)S(1)}, bf16[384,1152]{1,0:T(8,128)(2,1)S(1)}, u32[]{:S(2)}, u32[]{:S(2)}) collective-permute-start(bf16[384,1152]{1,0:T(8,128)(2,1)S(1)} %fusion.82), channel_id=1, source_target_pairs={{0,2},{1,3},{2,0},{3,1},{4,6},{5,7},{6,4},{7,5},{8,10},{9,11},{10,... | collective-permute-start | bytes 2654216 | tf_op jit(solution)/shard_map/ppermute | solution.py:128
  1191.6 71.5 %collective-permute-start.13 = (bf16[96,1536]{1,0:T(8,128)(2,1)S(1)}, bf16[96,1536]{1,0:T(8,128)(2,1)S(1)}, u32[]{:S(2)}, u32[]{:S(2)}) collective-permute-start(bf16[96,1536]{1,0:T(8,128)(2,1)S(1)} %dynamic-slice_bitcast_fusion.18), channel_id=1, source_target_pairs={{0,16},{4,20},{8,24},{12,28},{16,0},{20,4},{24,8},{28,12},{1,17},{... | collective-permute-start | bytes 884744 | tf_op jit(solution)/shard_map/ppermute | solution.py:128
  1197.7 82.2 %collective-permute-start.17 = (bf16[384,1536]{1,0:T(8,128)(2,1)S(1)}, bf16[384,1536]{1,0:T(8,128)(2,1)S(1)}, u32[]{:S(2)}, u32[]{:S(2)}) collective-permute-start(bf16[384,1536]{1,0:T(8,128)(2,1)S(1)} %dynamic-slice_bitcast_fusion.2), channel_id=1, source_target_pairs={{0,2},{1,3},{2,0},{3,1},{4,6},{5,7},{6,4},{7,5},{8,10},{9,11},{10,... | collective-permute-start | bytes 3538952 | tf_op jit(solution)/shard_map/ppermute | solution.py:128
  (99 other events, 1274.0 us)
Sparse Core Ops, SparseCore 0:
  16.7 99.8 all-gather.7
  118.8 76.2 all-gather.9
  196.7 110.7 all-gather.11
  309.0 76.0 all-gather.13
  386.5 76.2 all-gather.15
  464.3 76.2 all-gather.17
  542.8 76.2 all-gather.19
  627.8 82.4 reduce-scatter.6
  727.8 82.7 reduce-scatter.8
  812.8 83.0 reduce-scatter.10
  898.1 83.0 reduce-scatter.16
  1052.9 82.2 reduce-scatter.14
  1137.5 106.7 reduce-scatter.12

commit v5 on v4

--- a/solution.py
+++ b/solution.py
@@ -120,26 +120,30 @@
     return jnp.concatenate([rows, swap_cores(rows)], axis=0)
 
 
-def halve(blocks, axis_name, step):
+def halve(partial, axis_name, step):
     size = lax.axis_size(axis_name)
+    width = partial.shape[-1]
+    blocks = partial.reshape(size // (2 * step), 2, -1, width)
     side = (lax.axis_index(axis_name) // step) % 2
-    mine = lax.dynamic_index_in_dim(blocks, side, 0, keepdims=False)
-    theirs = lax.dynamic_index_in_dim(blocks, 1 - side, 0, keepdims=False)
-    arrived = lax.ppermute(theirs, axis_name, [(i, i ^ step) for i in range(size)])
-    return (mine.astype(jnp.float32) + arrived.astype(jnp.float32)).astype(jnp.bfloat16)
+    mine = lax.dynamic_index_in_dim(blocks, side, 1, keepdims=False)
+    theirs = lax.dynamic_index_in_dim(blocks, 1 - side, 1, keepdims=False)
+    arrived = lax.ppermute(
+        theirs.reshape(-1, width), axis_name, [(i, i ^ step) for i in range(size)]
+    )
+    total = mine.reshape(-1, width).astype(jnp.float32) + arrived.astype(jnp.float32)
+    return total.astype(jnp.bfloat16)
 
 
 def halvings(axis_name, least):
-    steps = [lax.axis_size(axis_name) // 2]
-    while steps[-1] > least:
-        steps.append(steps[-1] // 2)
+    steps = [least]
+    while 2 * steps[-1] < lax.axis_size(axis_name):
+        steps.append(2 * steps[-1])
     return [(axis_name, step) for step in steps]
 
 
 def halve_all(partial, steps):
-    width = partial.shape[-1]
     for axis_name, step in steps:
-        partial = halve(partial.reshape(2, -1, width), axis_name, step)
+        partial = halve(partial, axis_name, step)
     return partial
 
 
@@ -201,6 +205,7 @@
 
 
 def expert_backward_kernel(
+    group_ref,
     grad_ref,
     down_ref,
     gate_ref,
@@ -211,12 +216,12 @@
     grad_gate_out,
     grad_up_out,
     rows_out,
-    sums_out,
     rows_acc,
     sums_acc,
 ):
     expert = pl.program_id(0)
-    tile = grad_ref.shape[0]
+    tile, width = grad_ref.shape
+    experts = pl.num_programs(0)
     window = pl.ds(pl.multiple_of(pl.program_id(1) * tile, tile), tile)
     grad_scaled = contract(grad_ref[...], down_ref[...], 1, 0)
     gate_val = gate_val_ref[...].astype(jnp.float32)
@@ -235,7 +240,11 @@
         grad_up, up_ref[...], 1, 1
     )
     lanes = lax.broadcasted_iota(jnp.int32, (tile, sums_acc.shape[1]), 1)
-    grad_sums = jnp.where(lanes == expert, grad_sum, 0.0)
+    sum_high = grad_sum.astype(jnp.bfloat16).astype(jnp.float32)
+    column = group_ref[0] * experts + expert
+    grad_sums = jnp.where(lanes == column, sum_high, 0.0) + jnp.where(
+        lanes == column + group_ref[1], grad_sum - sum_high, 0.0
+    )
 
     @pl.when(expert == 0)
     def _():
@@ -249,57 +258,57 @@
 
     @pl.when(expert == pl.num_programs(0) - 1)
     def _():
-        rows_out[...] = rows_acc[window, :].astype(jnp.bfloat16)
-        sums_out[...] = sums_acc[window, :]
-
-
-def expert_backward(grad, down, gate, up, gate_val, up_val, share):
+        rows_out[:, :width] = rows_acc[window, :].astype(jnp.bfloat16)
+        rows_out[:, width:] = sums_acc[window, :].astype(jnp.bfloat16)
+
+
+def expert_backward(group, grad, down, gate, up, gate_val, up_val, share, extra):
     row_total, width = grad.shape
     experts = share.shape[1]
     hidden = gate.shape[1] // experts
     tile = row_total // 2
-    row_block = pl.BlockSpec((tile, width), lambda e, r: (r, 0))
-    weight_block = pl.BlockSpec((width, hidden), lambda e, r: (0, e))
-    hidden_block = pl.BlockSpec((tile, hidden), lambda e, r: (r, e))
+    row_block = pl.BlockSpec((tile, width), lambda e, r, g: (r, 0))
+    weight_block = pl.BlockSpec((width, hidden), lambda e, r, g: (0, e))
+    hidden_block = pl.BlockSpec((tile, hidden), lambda e, r, g: (r, e))
     hidden_shape = jax.ShapeDtypeStruct((row_total, gate.shape[1]), jnp.bfloat16)
-
-    def last_block(e, r):
-        return (jnp.where(e == experts - 1, r, 0), 0)
-
     return pl.pallas_call(
         expert_backward_kernel,
-        grid=(experts, 2),
-        in_specs=[
-            row_block,
-            weight_block,
-            weight_block,
-            weight_block,
-            hidden_block,
-            hidden_block,
-            pl.BlockSpec((tile, experts), lambda e, r: (r, 0)),
-        ],
-        out_specs=[
-            hidden_block,
-            hidden_block,
-            pl.BlockSpec((tile, width), last_block),
-            pl.BlockSpec((tile, 128), last_block),
-        ],
+        grid_spec=pltpu.PrefetchScalarGridSpec(
+            num_scalar_prefetch=1,
+            grid=(experts, 2),
+            in_specs=[
+                row_block,
+                weight_block,
+                weight_block,
+                weight_block,
+                hidden_block,
+                hidden_block,
+                pl.BlockSpec((tile, experts), lambda e, r, g: (r, 0)),
+            ],
+            out_specs=[
+                hidden_block,
+                hidden_block,
+                pl.BlockSpec(
+                    (tile, width + extra),
+                    lambda e, r, g: (jnp.where(e == experts - 1, r, 0), 0),
+                ),
+            ],
+            scratch_shapes=[
+                pltpu.VMEM((row_total, width), jnp.float32),
+                pltpu.VMEM((row_total, extra), jnp.float32),
+            ],
+        ),
         out_shape=[
             hidden_shape,
             hidden_shape,
-            jax.ShapeDtypeStruct((row_total, width), jnp.bfloat16),
-            jax.ShapeDtypeStruct((row_total, 128), jnp.float32),
-        ],
-        scratch_shapes=[
-            pltpu.VMEM((row_total, width), jnp.float32),
-            pltpu.VMEM((row_total, 128), jnp.float32),
+            jax.ShapeDtypeStruct((row_total, width + extra), jnp.bfloat16),
         ],
         cost_estimate=pl.CostEstimate(
             flops=6 * row_total * width * gate.shape[1],
             transcendentals=row_total * gate.shape[1],
             bytes_accessed=6 * width * gate.shape[1] + 8 * row_total * gate.shape[1],
         ),
-    )(grad, down, gate, up, gate_val, up_val, share)
+    )(group, grad, down, gate, up, gate_val, up_val, share)
 
 
 def attention_probs(block_ref, query, key):
@@ -463,6 +472,7 @@
     positions = my_group * block_length + jnp.arange(block_length, dtype=jnp.int32)
     cosine_table, sine_table = rotary_tables(positions, HEAD_SIZE // 2)
     block_at = my_group.astype(jnp.int32).reshape(1)
+    group_at = jnp.stack([my_group.astype(jnp.int32), jnp.int32(expert_total)])
     expert_ids = jnp.arange(expert_total, dtype=jnp.int32)
     small_width = -(-(expert_total + 2) // 128) * 128
     gate_width = -(-(2 * expert_total) // 128) * 128
@@ -658,41 +668,43 @@
         ) = kept_states[layer]
         grad_all = gather_rows(grad_hidden.astype(jnp.bfloat16))
         if waiting is not None:
-            last_act, waiting = lax.optimization_barrier((last_act, waiting))
+            out_part, query_part, kv_part = waiting
+            last_act, query_part, kv_part = lax.optimization_barrier(
+                (last_act, query_part, kv_part)
+            )
             last_rows = expert_rows(last_act, last_down)
-            grad_all, waiting, last_rows = lax.optimization_barrier(
-                (grad_all, waiting, last_rows)
-            )
-            waiting = halve_all(waiting, group_steps[:1])
+            grad_all, out_part, query_part, kv_part, last_rows = lax.optimization_barrier(
+                (grad_all, out_part, query_part, kv_part, last_rows)
+            )
+            query_part = halve_all(query_part, group_steps[1:])
+            kv_part = halve_all(kv_part, group_steps[:1])
         grad_down = dot_f32(grad_all, scaled_act, (0,), (0,)).astype(jnp.bfloat16)
         grad_all, grad_down = lax.optimization_barrier((grad_all, grad_down))
         expert_parts = [lax.psum_scatter(grad_down, "dp", scatter_dimension=0, tiled=True)]
-        grad_gate_val, grad_up_val, grad_rows, grad_sums = expert_backward(
-            grad_all, down_full, gate_full, up_full, gate_low, up_low, share_local
-        )
-        grad_gates = grad_sums[:, :exp_dev]
+        grad_gate_val, grad_up_val, grad_rows = expert_backward(
+            group_at,
+            grad_all,
+            down_full,
+            gate_full,
+            up_full,
+            gate_low,
+            up_low,
+            share_local,
+            gate_width,
+        )
         if waiting is not None:
-            output = last_middle + sum_rows(last_rows)
-            grad_rows, output = lax.optimization_barrier((grad_rows, output))
+            grad_rows, query_part, kv_part = lax.optimization_barrier(
+                (grad_rows, query_part, kv_part)
+            )
+            kv_part = halve_all(kv_part, group_steps[1:])
         grad_gate_w = dot_f32(arrived, grad_gate_val, (0,), (0,)).astype(jnp.bfloat16)
         grad_up_w = dot_f32(arrived, grad_up_val, (0,), (0,)).astype(jnp.bfloat16)
-        gates_high = grad_gates.astype(jnp.bfloat16)
-        gates_low = (grad_gates - gates_high.astype(jnp.float32)).astype(jnp.bfloat16)
-        gate_columns = jnp.zeros((all_rows, gate_width), jnp.bfloat16)
-        gate_columns = lax.dynamic_update_slice_in_dim(
-            gate_columns, gates_high, my_group * exp_dev, axis=1
-        )
-        gate_columns = lax.dynamic_update_slice_in_dim(
-            gate_columns, gates_low, expert_total + my_group * exp_dev, axis=1
-        )
-        back = sum_rows(
-            jnp.concatenate([grad_rows, gate_columns], axis=1)
-        )
+        back = sum_rows(grad_rows)
         if waiting is not None:
-            back, waiting, expert_held = lax.optimization_barrier(
-                (back, waiting, expert_held)
-            )
-            waiting = halve_all(waiting, group_steps[1:])
+            back, kv_part, last_rows = lax.optimization_barrier((back, kv_part, last_rows))
+            output = last_middle + sum_rows(last_rows)
+            chip_part = jnp.concatenate([out_part, query_part, kv_part], axis=1)
+            chip_part = halve_all(chip_part, chip_steps[:1])
         back, grad_gate_w, grad_up_w = lax.optimization_barrier((back, grad_gate_w, grad_up_w))
         expert_parts += [
             lax.psum_scatter(grad_gate_w, "dp", scatter_dimension=0, tiled=True),
@@ -712,20 +724,25 @@
         grad_middle = grad_hidden + grad_norm_mid
         grad_branch = grad_middle.astype(jnp.bfloat16)
         grad_output_w = dot_f32(core_major(grad_branch), both_cores(attended), (0,), (0,))
-        grad_output_w = grad_output_w.astype(jnp.bfloat16)
-        if layer == 0:
-            grad_output_w = halve_all(grad_output_w, group_steps[:1])
+        grad_output_w = halve_all(grad_output_w.astype(jnp.bfloat16), group_steps[:1])
         grad_attended = dot_f32(grad_branch, output_full, (1,), (0,)).astype(jnp.bfloat16)
         grad_query, grad_key_value_all = attention_backward(
             block_at, query_rotated, grad_attended, key_value_all
         )
+        grad_query, grad_output_w = lax.optimization_barrier((grad_query, grad_output_w))
+        grad_output_w = halve_all(grad_output_w, group_steps[1:])
         if waiting is not None:
-            grad_query, waiting = lax.optimization_barrier((grad_query, waiting))
-            attention_list[layer + 1] = halve_all(waiting, chip_steps)
-        if layer == 0:
-            grad_query, grad_output_w = lax.optimization_barrier((grad_query, grad_output_w))
-            grad_output_w = halve_all(grad_output_w, group_steps[1:])
-        grad_kv = sum_rows(grad_key_value_all).reshape(token_total, -1, 2, 2 * HEAD_SIZE)
+            grad_query, output, chip_part = lax.optimization_barrier(
+                (grad_query, output, chip_part)
+            )
+            chip_part = halve_all(chip_part, chip_steps[1:])
+        grad_kv = sum_rows(grad_key_value_all)
+        if waiting is not None:
+            grad_kv, expert_held, chip_part = lax.optimization_barrier(
+                (grad_kv, expert_held, chip_part)
+            )
+            attention_list[layer + 1] = chip_part
+        grad_kv = grad_kv.reshape(token_total, -1, 2, 2 * HEAD_SIZE)
         grad_kv = grad_kv.transpose(0, 2, 1, 3).reshape(token_total, 2 * key_width)
         grad_query_lin = (
             rotate_features(
@@ -768,14 +785,15 @@
         small_split = core_major(small_part.T).reshape(2, small_width, -1)
         small_half = jnp.sum(small_split.astype(jnp.float32), axis=0).T
         grad_kv_w = jnp.concatenate([grad_kv_w, small_half], axis=1).astype(jnp.bfloat16)
-        grad_query_w = grad_query_w.astype(jnp.bfloat16)
+        grad_query_w = halve_all(grad_query_w.astype(jnp.bfloat16), group_steps[:1])
         if layer > 0:
-            waiting = jnp.concatenate([grad_output_w, grad_query_w, grad_kv_w], axis=1)
+            waiting = (grad_output_w, grad_query_w, grad_kv_w)
         else:
+            grad_query_w = halve_all(grad_query_w, group_steps[1:])
+            early = jnp.concatenate([grad_output_w, grad_query_w], axis=1)
             attention_list[layer] = jnp.concatenate(
                 [
-                    halve_all(grad_output_w, chip_steps),
-                    halve_all(grad_query_w, group_steps + chip_steps),
+                    halve_all(early, chip_steps),
                     halve_all(grad_kv_w, group_steps + chip_steps),
                 ],
                 axis=1,

time: 1350 us -> 1300 us (0.963)
  waiting for transfers between devices: 541 us -> 475 us
    all_to_all x13, waiting for transfers between devices: 251 us -> 191 us  [exchange(): lax.all_to_all(blocks, 'expert', split_axis=0, concat_axis=0, tiled=True)]
    ppermute x16 -> x18, starting transfers between devices: 17.3 us -> 30.1 us  [halve(): lax.ppermute(theirs.reshape(-1, width), axis_name, [(i, i ^ step) for i i...]
    ppermute x16 -> x18, waiting for transfers between devices: 135 us -> 128 us  [halve(): lax.ppermute(theirs.reshape(-1, width), axis_name, [(i, i ^ step) for i i...]
  transfers between devices with their start and end apart: 56 -> 58, of which waited for: 24 -> 24; matrix products, arithmetic and copies ran while one was open for 27% -> 29% of each run, Pallas kernels for 20% -> 21%
where the time goes in v5:
time: 1300 us; the launch traced here: 1290 us
  waiting for transfers between devices  475 us (37%)
  Pallas kernels  271 us (21%)
  matrix products  180 us (14%)
  local copies, waits for them, and re-layouts  128 us (10%)
  starting transfers between devices  98.1 us (8%)
  other arithmetic  81 us (6%)
  blocking collectives  39.7 us (3%)
  between operations  16.1 us (1%)
    all_to_all x13, waiting for transfers between devices, exchange(): lax.all_to_all(blocks, 'expert', split_axis=0, concat_axis=0, tiled=True)  191 us
    dot_general x26, matrix products, dot_f32(): lax.dot_general(left, right, ((left_dims, right_dims), ((), ())), preferr...  163 us
    ppermute x18, waiting for transfers between devices, halve(): lax.ppermute(theirs.reshape(-1, width), axis_name, [(i, i ^ step) for i i...  128 us
    all_gather x1, waiting for transfers between devices, body(): packed = [lax.all_gather(shards[0], ('dp', 'expert'), axis=0, tiled=True)]  83.6 us
    pallas_call x2, Pallas kernels, expert_backward(): pl.pallas_call(expert_backward_kernel, grid_spec=pltpu.PrefetchScalarGrid...  81.7 us
    all_to_all x1, waiting for transfers between devices, exchange_chips(): lax.all_to_all(blocks, 'dp', split_axis=0, concat_axis=0, axis_index_grou...  71.5 us
    pallas_call x2, Pallas kernels, attention_backward(): pl.pallas_call(attention_backward_kernel, grid_spec=pltpu.PrefetchScalarG...  62.5 us
    all_to_all x13, starting transfers between devices, exchange(): lax.all_to_all(blocks, 'expert', split_axis=0, concat_axis=0, tiled=True)  60.4 us
  transfers between devices with their start and end apart: 58, of which 24 were waited for; matrix products, arithmetic and copies ran while one was open for 29% of the time, Pallas kernels for 21%

profile of v5, /device:TPU:0, one launch (start us, length us, event | category | flops | bytes accessed | tf_op | source)
XLA Modules:
  0.0 1288.6 jit_solution(477497360791218119)
XLA Ops:
  31.3 83.6 %all-gather.8.cloned.1.call-done = bf16[1536,4224]{1,0:T(8,128)(2,1)} async-done(((bf16[48,4224]{1,0:T(8,128)(2,1)}), bf16[1536,4224]{1,0:T(8,128)(2,1)}) %all-gather.8.cloned.1.call-update) | async-done | bytes 12976144 | tf_op jit(solution)/shard_map/all_gather | solution.py:524
  137.1 19.1 %all-to-all-done = bf16[4,256,1024]{2,1,0:T(8,128)(2,1)} async-done(((bf16[4,256,1024]{2,1,0:T(8,128)(2,1)}), bf16[4,256,1024]{2,1,0:T(8,128)(2,1)}, u32[]{:S(2)}, u32[]{:S(2)}) %all-to-all-start) | async-done | bytes 2097184 | tf_op jit(solution)/shard_map/all_to_all | solution.py:60
  156.2 23.3 %shard_map.220 = bf16[256,1536]{1,0:T(8,128)(2,1)} custom-call(s32[1]{0:T(128)} %bitcast.block_ref, bf16[256,1536]{1,0:T(8,128)(2,1)} %copy.291.query_ref, bf16[1024,1024]{1,0:T(8,128)(2,1)} %bitcast.15.key_ref.value_ref, bf16[1024,1024]{1,0:T(8,128)(2,1)} %bitcast.15.key_ref.value_ref), custom_call_target="tpu_custom_call" | custom-call | flops 6442450944 | bytes 3670016 | tf_op jit(solution)/shard_map/pallas_call | solution.py:351
  194.5 33.0 %all-to-all-done.1 = bf16[4,256,1536]{2,1,0:T(8,128)(2,1)} async-done(((bf16[4,256,1536]{2,1,0:T(8,128)(2,1)}), bf16[4,256,1536]{2,1,0:T(8,128)(2,1)}, u32[]{:S(2)}, u32[]{:S(2)}) %all-to-all-start.1) | async-done | bytes 3145760 | tf_op jit(solution)/shard_map/all_to_all | solution.py:60
  232.6 71.5 %all-to-all-done.2 = bf16[4,48,4224]{2,1,0:T(8,128)(2,1)S(1)} async-done(((bf16[4,48,4224]{2,1,0:T(8,128)(2,1)}), bf16[4,48,4224]{2,1,0:T(8,128)(2,1)S(1)}, u32[]{:S(2)}, u32[]{:S(2)}) %all-to-all-start.2) | async-done | bytes 1622048 | tf_op jit(solution)/shard_map/all_to_all | solution.py:85
  326.6 28.2 %shard_map.221 = (bf16[1024,2560]{1,0:T(8,128)(2,1)}, bf16[1024,2560]{1,0:T(8,128)(2,1)}, bf16[1024,2560]{1,0:T(8,128)(2,1)}) custom-call(bf16[1024,1536]{1,0:T(8,128)(2,1)} %bitcast.24.rows_ref, bf16[1536,2560]{1,0:T(8,128)(2,1)} %all-gather.10.cloned.1.call-done.gate_ref, bf16[1536,2560]{1,0:T(8,128)(2,1)} %all-gather.12.cloned.1.call-done.up_ref, ...), custom_call_target="tpu_custom_call" | custom-call | flops 16106127360 | bytes 31457280 | tf_op jit(solution)/shard_map/pallas_call | solution.py:188
  354.8 38.1 %all-to-all-done.4 = bf16[4,4,48,4224]{3,2,1,0:T(8,128)(2,1)} async-done(((bf16[4,4,48,4224]{3,2,1,0:T(8,128)(2,1)}), bf16[4,4,48,4224]{3,2,1,0:T(8,128)(2,1)}, u32[]{:S(2)}, u32[]{:S(2)}) %all-to-all-start.4) | async-done | bytes 6488096 | tf_op jit(solution)/shard_map/all_to_all | solution.py:60
  399.0 13.4 %convolution_convert_fusion.7 = bf16[1024,1536]{1,0:T(8,128)(2,1)} fusion(bf16[1024,2560]{1,0:T(8,128)(2,1)} %get-tuple-element.75, bf16[1536,2560]{1,0:T(8,128)(2,1)} %all-gather.14.cloned.1.call-done.down_ref), kind=kOutput, calls=%fused_computation.33 | convolution fusion | flops 8054636544 | bytes 16252928 | tf_op jit(solution)/shard_map/dot_general | solution.py:151
  420.0 34.2 %all-to-all-done.5 = bf16[4,256,1536]{2,1,0:T(8,128)(2,1)} async-done(((bf16[4,256,1536]{2,1,0:T(8,128)(2,1)}), bf16[4,256,1536]{2,1,0:T(8,128)(2,1)}, u32[]{:S(2)}, u32[]{:S(2)}) %all-to-all-start.5) | async-done | bytes 3145760 | tf_op jit(solution)/shard_map/all_to_all | solution.py:60
  484.0 18.9 %all-to-all-done.6 = bf16[4,256,1024]{2,1,0:T(8,128)(2,1)} async-done(((bf16[4,256,1024]{2,1,0:T(8,128)(2,1)}), bf16[4,256,1024]{2,1,0:T(8,128)(2,1)}, u32[]{:S(2)}, u32[]{:S(2)}) %all-to-all-start.6) | async-done | bytes 2097184 | tf_op jit(solution)/shard_map/all_to_all | solution.py:60
  503.0 23.3 %shard_map.222 = bf16[256,1536]{1,0:T(8,128)(2,1)} custom-call(s32[1]{0:T(128)} %bitcast.block_ref, bf16[256,1536]{1,0:T(8,128)(2,1)} %copy.265.query_ref, bf16[1024,1024]{1,0:T(8,128)(2,1)} %bitcast.48.key_ref.value_ref, bf16[1024,1024]{1,0:T(8,128)(2,1)} %bitcast.48.key_ref.value_ref), custom_call_target="tpu_custom_call" | custom-call | flops 6442450944 | bytes 3670016 | tf_op jit(solution)/shard_map/pallas_call | solution.py:351
  531.8 39.7 %all_to_all.75 = bf16[4,256,1536]{2,1,0:T(8,128)(2,1)} all-to-all(bf16[4,256,1536]{2,1,0:T(8,128)(2,1)S(1)} %broadcast_in_dim.45), channel_id=1, replica_groups=mesh['dp'=8,'expert'=4] {'expert'}, dimensions={0} | all-to-all | bytes 6291456 | tf_op jit(solution)/shard_map/all_to_all | solution.py:60
  583.8 28.0 %shard_map.223 = (bf16[1024,2560]{1,0:T(8,128)(2,1)}, bf16[1024,2560]{1,0:T(8,128)(2,1)}, bf16[1024,2560]{1,0:T(8,128)(2,1)}) custom-call(bf16[1024,1536]{1,0:T(8,128)(2,1)} %bitcast.441, bf16[1536,2560]{1,0:T(8,128)(2,1)} %all-gather.16.cloned.1.call-done.gate_ref, bf16[1536,2560]{1,0:T(8,128)(2,1)} %all-gather.18.cloned.1.call-done.up_ref, ...), custom_call_target="tpu_custom_call" | custom-call | flops 16106127360 | bytes 31457280 | tf_op jit(solution)/shard_map/pallas_call | solution.py:188
  612.5 13.4 %fusion = bf16[1536,2560]{1,0:T(8,128)(2,1)} fusion(bf16[1024,2560]{1,0:T(8,128)(2,1)} %get-tuple-element.91, bf16[1024,1536]{1,0:T(8,128)(2,1)} %bitcast.49.grad_ref), kind=kOutput, calls=%fused_computation.7 | convolution fusion | flops 8056995840 | bytes 16252928 | tf_op jit(solution)/shard_map/dot_general | solution.py:151
  626.5 40.9 %shard_map.224 = (bf16[1024,2560]{1,0:T(8,128)(2,1)}, bf16[1024,2560]{1,0:T(8,128)(2,1)}, bf16[1024,1664]{1,0:T(8,128)(2,1)}) custom-call(s32[2]{0:T(128)} %pad_add_fusion.group_ref, bf16[1024,1536]{1,0:T(8,128)(2,1)} %bitcast.49.grad_ref, bf16[1536,2560]{1,0:T(8,128)(2,1)} %all-gather.20.cloned.1.call-done.down_ref, ...), custom_call_target="tpu_custom_call" | custom-call | flops 24159191040 | bytes 44564480 | tf_op jit(solution)/shard_map/pallas_call | solution.py:274
  672.4 13.5 %convolution_convert_fusion.4 = bf16[1536,2560]{1,0:T(8,128)(2,1)} fusion(bf16[1024,1536]{1,0:T(8,128)(2,1)} %bitcast.442, bf16[1024,2560]{1,0:T(8,128)(2,1)} %get-tuple-element.82), kind=kOutput, calls=%fused_computation.5 | convolution fusion | flops 8056995840 | bytes 16252928 | tf_op jit(solution)/shard_map/dot_general | solution.py:151
  685.9 13.5 %convolution_convert_fusion.3 = bf16[1536,2560]{1,0:T(8,128)(2,1)} fusion(bf16[1024,1536]{1,0:T(8,128)(2,1)} %bitcast.443, bf16[1024,2560]{1,0:T(8,128)(2,1)} %get-tuple-element.83), kind=kOutput, calls=%fused_computation.4 | convolution fusion | flops 8056995840 | bytes 16252928 | tf_op jit(solution)/shard_map/dot_general | solution.py:151
  699.4 11.3 all-to-all-done.9
  741.3 31.2 %shard_map.225 = (f32[256,1536]{1,0:T(8,128)}, bf16[1024,1024]{1,0:T(8,128)(2,1)}) custom-call(s32[1]{0:T(128)} %bitcast.block_ref, bf16[256,1536]{1,0:T(8,128)(2,1)} %copy.265.query_ref, bf16[256,1536]{1,0:T(8,128)(2,1)} %fusion.36.grad_ref, bf16[1024,1024]{1,0:T(8,128)(2,1)} %bitcast.48.key_ref.value_ref, bf16[1024,1024]{1,0:T(8,128)(2,1)} %bitcast.48.key_ref.value_ref), custom_call_target="tpu_custom_call" | custom-call | flops 16106127360 | bytes 7340032 | tf_op jit(solution)/shard_map/pallas_call | solution.py:398
  843.9 10.9 collective-permute-done.7
  857.4 13.4 %convolution_convert_fusion.6 = bf16[1024,1536]{1,0:T(8,128)(2,1)} fusion(bf16[1024,2560]{1,0:T(8,128)(2,1)} %get-tuple-element.91, bf16[1536,2560]{1,0:T(8,128)(2,1)} %all-gather.20.cloned.1.call-done.down_ref), kind=kOutput, calls=%fused_computation.32 | convolution fusion | flops 8054636544 | bytes 16252928 | tf_op jit(solution)/shard_map/dot_general | solution.py:151
  870.8 16.7 %all-to-all-done.11 = bf16[4,256,1536]{2,1,0:T(8,128)(2,1)} async-done(((bf16[4,256,1536]{2,1,0:T(8,128)(2,1)}), bf16[4,256,1536]{2,1,0:T(8,128)(2,1)}, u32[]{:S(2)}, u32[]{:S(2)}) %all-to-all-start.11) | async-done | bytes 3145760 | tf_op jit(solution)/shard_map/all_to_all | solution.py:60
  887.5 13.5 %convolution_convert_fusion.2 = bf16[1536,2560]{1,0:T(8,128)(2,1)} fusion(bf16[1024,1536]{1,0:T(8,128)(2,1)} %bitcast.80.grad_ref, bf16[1024,2560]{1,0:T(8,128)(2,1)} %get-tuple-element.75), kind=kOutput, calls=%fused_computation.3 | convolution fusion | flops 8056995840 | bytes 16252928 | tf_op jit(solution)/shard_map/dot_general | solution.py:151
  906.4 40.9 %shard_map.226 = (bf16[1024,2560]{1,0:T(8,128)(2,1)}, bf16[1024,2560]{1,0:T(8,128)(2,1)}, bf16[1024,1664]{1,0:T(8,128)(2,1)}) custom-call(s32[2]{0:T(128)} %pad_add_fusion.group_ref, bf16[1024,1536]{1,0:T(8,128)(2,1)} %bitcast.80.grad_ref, bf16[1536,2560]{1,0:T(8,128)(2,1)} %all-gather.14.cloned.1.call-done.down_ref, ...), custom_call_target="tpu_custom_call" | custom-call | flops 24159191040 | bytes 44564480 | tf_op jit(solution)/shard_map/pallas_call | solution.py:274
  947.3 14.0 %convolution_convert_fusion.1 = bf16[1536,2560]{1,0:T(8,128)(2,1)} fusion(bf16[1024,1536]{1,0:T(8,128)(2,1)} %bitcast.24.rows_ref, bf16[1024,2560]{1,0:T(8,128)(2,1)} %get-tuple-element.103), kind=kOutput, calls=%fused_computation.2 | convolution fusion | flops 8056995840 | bytes 16252928 | tf_op jit(solution)/shard_map/dot_general | solution.py:151
  971.5 13.4 %convolution_convert_fusion = bf16[1536,2560]{1,0:T(8,128)(2,1)} fusion(bf16[1024,1536]{1,0:T(8,128)(2,1)} %bitcast.24.rows_ref, bf16[1024,2560]{1,0:T(8,128)(2,1)} %get-tuple-element.104), kind=kOutput, calls=%fused_computation.1 | convolution fusion | flops 8056995840 | bytes 16252928 | tf_op jit(solution)/shard_map/dot_general | solution.py:151
  985.0 31.9 %collective-permute-done.12 = bf16[192,1152]{1,0:T(8,128)(2,1)S(1)} collective-permute-done((bf16[192,1152]{1,0:T(8,128)(2,1)S(1)}, bf16[192,1152]{1,0:T(8,128)(2,1)S(1)}, u32[]{:S(2)}, u32[]{:S(2)}) %collective-permute-start.12) | collective-permute-done | bytes 442400 | tf_op jit(solution)/shard_map/ppermute | solution.py:130
  1048.5 31.3 %shard_map.227 = (f32[256,1536]{1,0:T(8,128)}, bf16[1024,1024]{1,0:T(8,128)(2,1)}) custom-call(s32[1]{0:T(128)} %bitcast.block_ref, bf16[256,1536]{1,0:T(8,128)(2,1)} %copy.291.query_ref, bf16[256,1536]{1,0:T(8,128)(2,1)} %fusion.33.grad_ref, bf16[1024,1024]{1,0:T(8,128)(2,1)} %bitcast.15.key_ref.value_ref, bf16[1024,1024]{1,0:T(8,128)(2,1)} %bitcast.15.key_ref.value_ref), custom_call_target="tpu_custom_call" | custom-call | flops 16106127360 | bytes 7340032 | tf_op jit(solution)/shard_map/pallas_call | solution.py:398
  1093.4 20.2 %collective-permute-done.15 = bf16[384,1536]{1,0:T(8,128)(2,1)} collective-permute-done((bf16[384,1536]{1,0:T(8,128)(2,1)}, bf16[384,1536]{1,0:T(8,128)(2,1)}, u32[]{:S(2)}, u32[]{:S(2)}) %collective-permute-start.15) | collective-permute-done | bytes 1179680 | tf_op jit(solution)/shard_map/ppermute | solution.py:130
  1153.0 16.3 %collective-permute-done.21 = bf16[384,1536]{1,0:T(8,128)(2,1)S(1)} collective-permute-done((bf16[384,1536]{1,0:T(8,128)(2,1)S(1)}, bf16[384,1536]{1,0:T(8,128)(2,1)S(1)}, u32[]{:S(2)}, u32[]{:S(2)}) %collective-permute-start.21) | collective-permute-done | bytes 1179680 | tf_op jit(solution)/shard_map/ppermute | solution.py:130
  1170.5 13.2 %collective-permute-done.17 = bf16[48,4224]{1,0:T(8,128)(2,1)S(1)} collective-permute-done((bf16[48,4224]{1,0:T(8,128)(2,1)S(1)}, bf16[48,4224]{1,0:T(8,128)(2,1)S(1)}, u32[]{:S(2)}, u32[]{:S(2)}) %collective-permute-start.17) | collective-permute-done | bytes 405536 | tf_op jit(solution)/shard_map/ppermute | solution.py:130
  1229.3 12.0 collective-permute-done.27
  (501 shorter events, 447.0 us)
Async XLA Ops:
  7.2 107.7 %all-gather.8.cloned.1.call-start = ((), (), s32[]{:S(2)}) async-start(), calls=%async_computation.21 | async-start | bytes 13381632 | tf_op jit(solution)/shard_map/all_gather | solution.py:524
  14.9 311.7 %all-gather.10.cloned.1.call-start = ((), (), s32[]{:S(2)}) async-start(), calls=%async_computation.22 | async-start | bytes 8847360 | tf_op jit(solution)/shard_map/all_gather | solution.py:529
  18.6 308.0 %all-gather.12.cloned.1.call-start = ((), (), s32[]{:S(2)}) async-start(), calls=%async_computation.23 | async-start | bytes 8847360 | tf_op jit(solution)/shard_map/all_gather | solution.py:529
  23.4 375.6 %all-gather.14.cloned.1.call-start = ((), (), s32[]{:S(2)}) async-start(), calls=%async_computation.24 | async-start | bytes 8847360 | tf_op jit(solution)/shard_map/all_gather | solution.py:529
  28.1 555.7 %all-gather.16.cloned.1.call-start = ((), (), s32[]{:S(2)}) async-start(), calls=%async_computation.25 | async-start | bytes 8847360 | tf_op jit(solution)/shard_map/all_gather | solution.py:529
  186.8 40.7 %all-to-all-start.1 = ((bf16[4,256,1536]{2,1,0:T(8,128)(2,1)}), bf16[4,256,1536]{2,1,0:T(8,128)(2,1)}, u32[]{:S(2)}, u32[]{:S(2)}) async-start(bf16[4,256,1536]{2,1,0:T(8,128)(2,1)} %broadcast_in_dim.37), calls=%async_computation.1 | async-start | bytes 6291456 | tf_op jit(solution)/shard_map/all_to_all | solution.py:60
  191.5 392.3 %all-gather.18.cloned.1.call-start = ((), (), s32[]{:S(2)}) async-start(), calls=%async_computation.26 | async-start | bytes 8847360 | tf_op jit(solution)/shard_map/all_gather | solution.py:529
  228.7 75.4 %all-to-all-start.2 = ((bf16[4,48,4224]{2,1,0:T(8,128)(2,1)}), bf16[4,48,4224]{2,1,0:T(8,128)(2,1)S(1)}, u32[]{:S(2)}, u32[]{:S(2)}) async-start(bf16[4,48,4224]{2,1,0:T(8,128)(2,1)} %broadcast_in_dim.38), calls=%async_computation.2 | async-start | bytes 3244032 | tf_op jit(solution)/shard_map/all_to_all | solution.py:85
  316.3 76.6 %all-to-all-start.4 = ((bf16[4,4,48,4224]{3,2,1,0:T(8,128)(2,1)}), bf16[4,4,48,4224]{3,2,1,0:T(8,128)(2,1)}, u32[]{:S(2)}, u32[]{:S(2)}) async-start(bf16[4,4,48,4224]{3,2,1,0:T(8,128)(2,1)} %broadcast_in_dim.42), calls=%async_computation.4 | async-start | bytes 12976128 | tf_op jit(solution)/shard_map/all_to_all | solution.py:60
  399.0 58.1 %collective-permute-start = (bf16[4,4,48,4224]{3,2,0,1:T(8,128)(2,1)}, bf16[4,4,48,4224]{3,2,0,1:T(8,128)(2,1)}, u32[]{:S(2)}, u32[]{:S(2)}) collective-permute-start(bf16[4,4,48,4224]{3,2,0,1:T(8,128)(2,1)} %copy.259), channel_id=1, source_target_pairs={{0,4},{4,0},{8,12},{12,8},{16,20},{20,16},{24,28},{28,24},{1,5},{5... | collective-permute-start | bytes 19464200 | tf_op jit(solution)/shard_map/ppermute | solution.py:81
  412.4 41.8 %all-to-all-start.5 = ((bf16[4,256,1536]{2,1,0:T(8,128)(2,1)}), bf16[4,256,1536]{2,1,0:T(8,128)(2,1)}, u32[]{:S(2)}, u32[]{:S(2)}) async-start(bf16[4,256,1536]{2,1,0:T(8,128)(2,1)} %bitcast.444), calls=%async_computation.5 | async-start | bytes 6291456 | tf_op jit(solution)/shard_map/all_to_all | solution.py:60
  417.1 209.5 %all-gather.20.cloned.1.call-start = ((), (), s32[]{:S(2)}) async-start(), calls=%async_computation.27 | async-start | bytes 8847360 | tf_op jit(solution)/shard_map/all_gather | solution.py:529
  578.0 607.1 %reduce-scatter.7.cloned.1.call-start = ((), (), s32[]{:S(2)}) async-start(), calls=%async_computation.28 | async-start | bytes 8847360 | tf_op jit(solution)/shard_map/reduce_scatter | solution.py:683
  667.4 43.3 %all-to-all-start.9 = ((bf16[4,256,1664]{2,1,0:T(8,128)(2,1)}), bf16[4,256,1664]{2,1,0:T(8,128)(2,1)}, u32[]{:S(2)}, u32[]{:S(2)}) async-start(bf16[4,256,1664]{2,1,0:T(8,128)(2,1)} %bitcast.432), calls=%async_computation.9 | async-start | bytes 6815744 | tf_op jit(solution)/shard_map/all_to_all | solution.py:60
  672.1 517.0 %reduce-scatter.9.cloned.1.call-start = ((), (), s32[]{:S(2)}) async-start(), calls=%async_computation.29 | async-start | bytes 8847360 | tf_op jit(solution)/shard_map/reduce_scatter | solution.py:710
  714.5 478.7 %reduce-scatter.11.cloned.1.call-start = ((), (), s32[]{:S(2)}) async-start(), calls=%async_computation.30 | async-start | bytes 8847360 | tf_op jit(solution)/shard_map/reduce_scatter | solution.py:711
  739.8 41.7 %collective-permute-start.3 = (bf16[384,1536]{1,0:T(8,128)(2,1)}, bf16[384,1536]{1,0:T(8,128)(2,1)}, u32[]{:S(2)}, u32[]{:S(2)}) collective-permute-start(bf16[384,1536]{1,0:T(8,128)(2,1)} %bitcast.71), channel_id=1, source_target_pairs={{0,1},{1,0},{2,3},{3,2},{4,5},{5,4},{6,7},{7,6},{8,9},{9,8},{10,11... | collective-permute-start | bytes 3538952 | tf_op jit(solution)/shard_map/ppermute | solution.py:130
  779.3 41.7 %collective-permute-start.5 = (bf16[256,768]{0,1:T(8,128)(2,1)}, bf16[256,768]{0,1:T(8,128)(2,1)}, u32[]{:S(2)}, u32[]{:S(2)}) collective-permute-start(bf16[256,768]{0,1:T(8,128)(2,1)} %get-tuple-element.253), channel_id=1, source_target_pairs={{0,4},{4,0},{8,12},{12,8},{16,20},{20,16},{24,28},{28,24},{1,5},{5... | collective-permute-start | bytes 1179656 | tf_op jit(solution)/shard_map/ppermute | solution.py:81
  789.4 51.4 %collective-permute-start.4 = (bf16[192,1536]{1,0:T(8,128)(2,1)}, bf16[192,1536]{1,0:T(8,128)(2,1)}, u32[]{:S(2)}, u32[]{:S(2)}) collective-permute-start(bf16[192,1536]{1,0:T(8,128)(2,1)} %dynamic-slice_bitcast_fusion.3), channel_id=1, source_target_pairs={{0,2},{1,3},{2,0},{3,1},{4,6},{5,7},{6,4},{7,5},{8,10},{9,11},{10,... | collective-permute-start | bytes 1769480 | tf_op jit(solution)/shard_map/ppermute | solution.py:130
  830.5 57.0 %all-to-all-start.11 = ((bf16[4,256,1536]{2,1,0:T(8,128)(2,1)}), bf16[4,256,1536]{2,1,0:T(8,128)(2,1)}, u32[]{:S(2)}, u32[]{:S(2)}) async-start(bf16[4,256,1536]{2,1,0:T(8,128)(2,1)} %broadcast_in_dim.48), calls=%async_computation.11 | async-start | bytes 6291456 | tf_op jit(solution)/shard_map/all_to_all | solution.py:60
  835.2 434.6 %reduce-scatter.17.cloned.1.call-start = ((), (), s32[]{:S(2)}) async-start(), calls=%async_computation.33 | async-start | bytes 8847360 | tf_op jit(solution)/shard_map/reduce_scatter | solution.py:683
  902.9 58.3 %collective-permute-start.10 = (bf16[192,1536]{1,0:T(8,128)(2,1)}, bf16[192,1536]{1,0:T(8,128)(2,1)}, u32[]{:S(2)}, u32[]{:S(2)}) collective-permute-start(bf16[192,1536]{1,0:T(8,128)(2,1)} %dynamic-slice_bitcast_fusion.2), channel_id=1, source_target_pairs={{0,2},{1,3},{2,0},{3,1},{4,6},{5,7},{6,4},{7,5},{8,10},{9,11},{10,... | collective-permute-start | bytes 1769480 | tf_op jit(solution)/shard_map/ppermute | solution.py:130
  904.9 58.5 %collective-permute-start.11 = (bf16[384,1152]{1,0:T(8,128)(2,1)}, bf16[384,1152]{1,0:T(8,128)(2,1)}, u32[]{:S(2)}, u32[]{:S(2)}) collective-permute-start(bf16[384,1152]{1,0:T(8,128)(2,1)} %bitcast.104), channel_id=1, source_target_pairs={{0,1},{1,0},{2,3},{3,2},{4,5},{5,4},{6,7},{7,6},{8,9},{9,8},{10,11... | collective-permute-start | bytes 2654216 | tf_op jit(solution)/shard_map/ppermute | solution.py:130
  964.7 53.0 %all-to-all-start.12 = ((bf16[4,256,1664]{2,1,0:T(8,128)(2,1)}), bf16[4,256,1664]{2,1,0:T(8,128)(2,1)}, u32[]{:S(2)}, u32[]{:S(2)}) async-start(bf16[4,256,1664]{2,1,0:T(8,128)(2,1)} %bitcast.431), calls=%async_computation.12 | async-start | bytes 6815744 | tf_op jit(solution)/shard_map/all_to_all | solution.py:60
  969.5 304.4 %reduce-scatter.13.cloned.1.call-start = ((), (), s32[]{:S(2)}) async-start(), calls=%async_computation.31 | async-start | bytes 8847360 | tf_op jit(solution)/shard_map/reduce_scatter | solution.py:710
  969.6 47.3 %collective-permute-start.12 = (bf16[192,1152]{1,0:T(8,128)(2,1)S(1)}, bf16[192,1152]{1,0:T(8,128)(2,1)S(1)}, u32[]{:S(2)}, u32[]{:S(2)}) collective-permute-start(bf16[192,1152]{1,0:T(8,128)(2,1)S(1)} %dynamic-slice_bitcast_fusion.5), channel_id=1, source_target_pairs={{0,2},{1,3},{2,0},{3,1},{4,6},{5,7},{6,4},{7,5},{8,10},{9,11},{10,... | collective-permute-start | bytes 1327112 | tf_op jit(solution)/shard_map/ppermute | solution.py:130
  1025.9 53.8 %collective-permute-start.14 = (bf16[256,1536]{1,0:T(8,128)(2,1)}, bf16[256,1536]{1,0:T(8,128)(2,1)}, u32[]{:S(2)}, u32[]{:S(2)}) collective-permute-start(bf16[256,1536]{1,0:T(8,128)(2,1)} %shard_map.220), channel_id=1, source_target_pairs={{0,4},{4,0},{8,12},{12,8},{16,20},{20,16},{24,28},{28,24},{1,5},{5... | collective-permute-start | bytes 2359304 | tf_op jit(solution)/shard_map/ppermute | solution.py:81
  1035.9 43.9 %collective-permute-start.13 = (bf16[256,768]{0,1:T(8,128)(2,1)}, bf16[256,768]{0,1:T(8,128)(2,1)}, u32[]{:S(2)}, u32[]{:S(2)}) collective-permute-start(bf16[256,768]{0,1:T(8,128)(2,1)} %get-tuple-element.251), channel_id=1, source_target_pairs={{0,4},{4,0},{8,12},{12,8},{16,20},{20,16},{24,28},{28,24},{1,5},{5... | collective-permute-start | bytes 1179656 | tf_op jit(solution)/shard_map/ppermute | solution.py:81
  1036.2 52.5 %all-to-all-start.13 = ((bf16[4,256,1536]{2,1,0:T(8,128)(2,1)}), bf16[4,256,1536]{2,1,0:T(8,128)(2,1)}, u32[]{:S(2)}, u32[]{:S(2)}) async-start(bf16[4,256,1536]{2,1,0:T(8,128)(2,1)} %bitcast.439), calls=%async_computation.13 | async-start | bytes 6291456 | tf_op jit(solution)/shard_map/all_to_all | solution.py:60
  1040.9 236.9 %reduce-scatter.15.cloned.1.call-start = ((), (), s32[]{:S(2)}) async-start(), calls=%async_computation.32 | async-start | bytes 8847360 | tf_op jit(solution)/shard_map/reduce_scatter | solution.py:711
  1043.8 42.6 %collective-permute-start.16 = (bf16[96,4224]{1,0:T(8,128)(2,1)}, bf16[96,4224]{1,0:T(8,128)(2,1)}, u32[]{:S(2)}, u32[]{:S(2)}) collective-permute-start(bf16[96,4224]{1,0:T(8,128)(2,1)} %bitcast.121), channel_id=1, source_target_pairs={{0,8},{4,12},{8,0},{12,4},{16,24},{20,28},{24,16},{28,20},{1,9},{5... | collective-permute-start | bytes 2433032 | tf_op jit(solution)/shard_map/ppermute | solution.py:130
  1088.7 46.6 %all-to-all-start.14 = ((bf16[4,256,1024]{2,1,0:T(8,128)(2,1)}), bf16[4,256,1024]{2,1,0:T(8,128)(2,1)}, u32[]{:S(2)}, u32[]{:S(2)}) async-start(bf16[4,256,1024]{2,1,0:T(8,128)(2,1)} %bitcast.460), calls=%async_computation.14 | async-start | bytes 4194304 | tf_op jit(solution)/shard_map/all_to_all | solution.py:60
  (96 other events, 1436.5 us)
Sparse Core Ops, SparseCore 0:
  15.0 99.8 all-gather.7
  117.1 76.2 all-gather.9
  195.1 110.7 all-gather.11
  307.3 76.0 all-gather.13
  384.9 76.2 all-gather.15
  462.7 76.2 all-gather.17
  541.2 76.2 all-gather.19
  626.1 83.1 reduce-scatter.6
  714.6 82.2 reduce-scatter.8
  799.1 83.0 reduce-scatter.10
  901.1 82.4 reduce-scatter.16
  1020.5 100.5 reduce-scatter.12
  1123.3 91.9 reduce-scatter.14

commit v6 on v5

--- a/solution.py
+++ b/solution.py
@@ -636,7 +636,7 @@
     output = None
     grad_hidden = cotangent.astype(jnp.float32).reshape(token_total, model_width)
     attention_list = [None] * LAYER_COUNT
-    expert_held = [None] * 3
+    placed = []
     waiting = None
     group_steps = halvings("expert", 1)
     chip_steps = halvings("dp", 2)
@@ -668,15 +668,10 @@
         ) = kept_states[layer]
         grad_all = gather_rows(grad_hidden.astype(jnp.bfloat16))
         if waiting is not None:
+            grad_all, waiting = lax.optimization_barrier((grad_all, waiting))
             out_part, query_part, kv_part = waiting
-            last_act, query_part, kv_part = lax.optimization_barrier(
-                (last_act, query_part, kv_part)
-            )
-            last_rows = expert_rows(last_act, last_down)
-            grad_all, out_part, query_part, kv_part, last_rows = lax.optimization_barrier(
-                (grad_all, out_part, query_part, kv_part, last_rows)
-            )
-            query_part = halve_all(query_part, group_steps[1:])
+            out_part = halve_all(out_part, group_steps[1:])
+            query_part = halve_all(query_part, group_steps[:1])
             kv_part = halve_all(kv_part, group_steps[:1])
         grad_down = dot_f32(grad_all, scaled_act, (0,), (0,)).astype(jnp.bfloat16)
         grad_all, grad_down = lax.optimization_barrier((grad_all, grad_down))
@@ -692,19 +687,19 @@
             share_local,
             gate_width,
         )
-        if waiting is not None:
-            grad_rows, query_part, kv_part = lax.optimization_barrier(
-                (grad_rows, query_part, kv_part)
-            )
-            kv_part = halve_all(kv_part, group_steps[1:])
         grad_gate_w = dot_f32(arrived, grad_gate_val, (0,), (0,)).astype(jnp.bfloat16)
         grad_up_w = dot_f32(arrived, grad_up_val, (0,), (0,)).astype(jnp.bfloat16)
         back = sum_rows(grad_rows)
-        if waiting is not None:
-            back, kv_part, last_rows = lax.optimization_barrier((back, kv_part, last_rows))
+        if waiting is None:
+            last_rows = expert_rows(last_act, last_down)
+            back, last_rows = lax.optimization_barrier((back, last_rows))
             output = last_middle + sum_rows(last_rows)
-            chip_part = jnp.concatenate([out_part, query_part, kv_part], axis=1)
-            chip_part = halve_all(chip_part, chip_steps[:1])
+        else:
+            back, out_part, query_part, kv_part = lax.optimization_barrier(
+                (back, out_part, query_part, kv_part)
+            )
+            late_part = jnp.concatenate([query_part, kv_part], axis=1)
+            late_part = halve_all(late_part, group_steps[1:])
         back, grad_gate_w, grad_up_w = lax.optimization_barrier((back, grad_gate_w, grad_up_w))
         expert_parts += [
             lax.psum_scatter(grad_gate_w, "dp", scatter_dimension=0, tiled=True),
@@ -729,21 +724,19 @@
         grad_query, grad_key_value_all = attention_backward(
             block_at, query_rotated, grad_attended, key_value_all
         )
-        grad_query, grad_output_w = lax.optimization_barrier((grad_query, grad_output_w))
-        grad_output_w = halve_all(grad_output_w, group_steps[1:])
-        if waiting is not None:
-            grad_query, output, chip_part = lax.optimization_barrier(
-                (grad_query, output, chip_part)
+        if waiting is None:
+            grad_query, grad_key_value_all, output = lax.optimization_barrier(
+                (grad_query, grad_key_value_all, output)
             )
-            chip_part = halve_all(chip_part, chip_steps[1:])
+        else:
+            grad_query, grad_output_w, late_part = lax.optimization_barrier(
+                (grad_query, grad_output_w, late_part)
+            )
+            grad_output_w = halve_all(grad_output_w, group_steps[1:])
+            chip_part = jnp.concatenate([out_part, late_part], axis=1)
+            attention_list[layer + 1] = halve_all(chip_part, chip_steps)
         grad_kv = sum_rows(grad_key_value_all)
-        if waiting is not None:
-            grad_kv, expert_held, chip_part = lax.optimization_barrier(
-                (grad_kv, expert_held, chip_part)
-            )
-            attention_list[layer + 1] = chip_part
-        grad_kv = grad_kv.reshape(token_total, -1, 2, 2 * HEAD_SIZE)
-        grad_kv = grad_kv.transpose(0, 2, 1, 3).reshape(token_total, 2 * key_width)
+        normed_split = core_major(first_normalized)
         grad_query_lin = (
             rotate_features(
                 grad_query.reshape(token_total, QUERY_HEADS, HEAD_SIZE), cosine_table, -sine_table
@@ -751,6 +744,12 @@
             .astype(jnp.bfloat16)
             .reshape(token_total, query_width)
         )
+        grad_query_w = dot_f32(normed_split, both_cores(grad_query_lin), (0,), (0,))
+        grad_query_w = grad_query_w.astype(jnp.bfloat16)
+        if layer == 0:
+            grad_kv, grad_query_w = lax.optimization_barrier((grad_kv, grad_query_w))
+        grad_kv = grad_kv.reshape(token_total, -1, 2, 2 * HEAD_SIZE)
+        grad_kv = grad_kv.transpose(0, 2, 1, 3).reshape(token_total, 2 * key_width)
         grad_key_lin = (
             rotate_features(
                 grad_kv[:, :key_width].reshape(token_total, KEY_VALUE_HEADS, HEAD_SIZE),
@@ -763,8 +762,6 @@
         grad_kv_lin = jnp.concatenate(
             [grad_key_lin, grad_kv[:, key_width:].astype(jnp.bfloat16)], axis=1
         )
-        normed_split = core_major(first_normalized)
-        grad_query_w = dot_f32(normed_split, both_cores(grad_query_lin), (0,), (0,))
         grad_kv_w = dot_f32(normed_split, both_cores(grad_kv_lin), (0,), (0,))
         grad_normed_one = dot_f32(grad_query_lin, qkv_full[:, : edges[0]], (1,), (1,)) + dot_f32(
             grad_kv_lin, qkv_full[:, edges[0] :], (1,), (1,)
@@ -785,11 +782,10 @@
         small_split = core_major(small_part.T).reshape(2, small_width, -1)
         small_half = jnp.sum(small_split.astype(jnp.float32), axis=0).T
         grad_kv_w = jnp.concatenate([grad_kv_w, small_half], axis=1).astype(jnp.bfloat16)
-        grad_query_w = halve_all(grad_query_w.astype(jnp.bfloat16), group_steps[:1])
         if layer > 0:
             waiting = (grad_output_w, grad_query_w, grad_kv_w)
         else:
-            grad_query_w = halve_all(grad_query_w, group_steps[1:])
+            grad_query_w = halve_all(grad_query_w, group_steps)
             early = jnp.concatenate([grad_output_w, grad_query_w], axis=1)
             attention_list[layer] = jnp.concatenate(
                 [
@@ -798,9 +794,7 @@
                 ],
                 axis=1,
             )
-        expert_held = [
-            place(part, held, layer, exp_dev) for part, held in zip(expert_parts, expert_held)
-        ]
+        placed = placed + [(layer, expert_parts)]
         grad_hidden = grad_middle + grad_norm_in
     stacked = jnp.stack(attention_list).astype(jnp.float32)
     cuts = [query_width, query_width, key_width, key_width, expert_total, 1, 1]
@@ -808,6 +802,13 @@
     output_grads, query_grads, key_grads, value_grads, router_grads, one, two = (
         stacked[:, :, start:stop] for start, stop in zip(cuts[:-1], cuts[1:])
     )
+    expert_held = [None] * 3
+    for layer, expert_parts in placed:
+        if layer > 0:
+            grad_kv_w, expert_parts = lax.optimization_barrier((grad_kv_w, expert_parts))
+        expert_held = [
+            place(part, held, layer, exp_dev) for part, held in zip(expert_parts, expert_held)
+        ]
     down_grads, gate_grads, up_grads = expert_held
     return (
         output.astype(jnp.bfloat16).reshape(sequences_per_device, block_length, model_width),

time: 1300 us -> 1240 us (0.954)
  waiting for transfers between devices: 475 us -> 434 us
  starting transfers between devices: 98.1 us -> 85 us
    ppermute x18 -> x17, waiting for transfers between devices: 128 us -> 105 us  [halve(): lax.ppermute(theirs.reshape(-1, width), axis_name, [(i, i ^ step) for i i...]
    all_to_all x13, waiting for transfers between devices: 191 us -> 178 us  [exchange(): lax.all_to_all(blocks, 'expert', split_axis=0, concat_axis=0, tiled=True)]
    ppermute x18 -> x17, starting transfers between devices: 30.1 us -> 17.1 us  [halve(): lax.ppermute(theirs.reshape(-1, width), axis_name, [(i, i ^ step) for i i...]
  transfers between devices with their start and end apart: 58 -> 57, of which waited for: 24 -> 20; matrix products, arithmetic and copies ran while one was open for 29% -> 29% of each run, Pallas kernels for 21% -> 22%
where the time goes in v6:
time: 1240 us; the launch traced here: 1230 us
  waiting for transfers between devices  434 us (35%)
  Pallas kernels  272 us (22%)
  matrix products  184 us (15%)
  local copies, waits for them, and re-layouts  125 us (10%)
  starting transfers between devices  85 us (7%)
  other arithmetic  74.9 us (6%)
  blocking collectives  39.6 us (3%)
  between operations  16.2 us (1%)
    all_to_all x13, waiting for transfers between devices, exchange(): lax.all_to_all(blocks, 'expert', split_axis=0, concat_axis=0, tiled=True)  178 us
    dot_general x26, matrix products, dot_f32(): lax.dot_general(left, right, ((left_dims, right_dims), ((), ())), preferr...  168 us
    ppermute x17, waiting for transfers between devices, halve(): lax.ppermute(theirs.reshape(-1, width), axis_name, [(i, i ^ step) for i i...  105 us
    pallas_call x2, Pallas kernels, expert_backward(): pl.pallas_call(expert_backward_kernel, grid_spec=pltpu.PrefetchScalarGrid...  82.5 us
    all_gather x1, waiting for transfers between devices, body(): packed = [lax.all_gather(shards[0], ('dp', 'expert'), axis=0, tiled=True)]  80.8 us
    all_to_all x1, waiting for transfers between devices, exchange_chips(): lax.all_to_all(blocks, 'dp', split_axis=0, concat_axis=0, axis_index_grou...  68.7 us
    pallas_call x2, Pallas kernels, attention_backward(): pl.pallas_call(attention_backward_kernel, grid_spec=pltpu.PrefetchScalarG...  62.4 us
    all_to_all x13, starting transfers between devices, exchange(): lax.all_to_all(blocks, 'expert', split_axis=0, concat_axis=0, tiled=True)  59.3 us
  transfers between devices with their start and end apart: 57, of which 20 were waited for; matrix products, arithmetic and copies ran while one was open for 29% of the time, Pallas kernels for 22%

profile of v6, /device:TPU:0, one launch (start us, length us, event | category | flops | bytes accessed | tf_op | source)
XLA Modules:
  0.0 1231.0 jit_solution(15864002929409931790)
XLA Ops:
  34.6 80.8 %all-gather.8.cloned.1.call-done = bf16[1536,4224]{1,0:T(8,128)(2,1)} async-done(((bf16[48,4224]{1,0:T(8,128)(2,1)}), bf16[1536,4224]{1,0:T(8,128)(2,1)}) %all-gather.8.cloned.1.call-update) | async-done | bytes 12976144 | tf_op jit(solution)/shard_map/all_gather | solution.py:524
  138.9 18.4 %all-to-all-done = bf16[4,256,1024]{2,1,0:T(8,128)(2,1)} async-done(((bf16[4,256,1024]{2,1,0:T(8,128)(2,1)}), bf16[4,256,1024]{2,1,0:T(8,128)(2,1)}, u32[]{:S(2)}, u32[]{:S(2)}) %all-to-all-start) | async-done | bytes 2097184 | tf_op jit(solution)/shard_map/all_to_all | solution.py:60
  157.3 23.3 %shard_map.220 = bf16[256,1536]{1,0:T(8,128)(2,1)} custom-call(s32[1]{0:T(128)} %bitcast.block_ref, bf16[256,1536]{1,0:T(8,128)(2,1)} %copy.248.query_ref, bf16[1024,1024]{1,0:T(8,128)(2,1)} %bitcast.14.key_ref.value_ref, bf16[1024,1024]{1,0:T(8,128)(2,1)} %bitcast.14.key_ref.value_ref), custom_call_target="tpu_custom_call" | custom-call | flops 6442450944 | bytes 3670016 | tf_op jit(solution)/shard_map/pallas_call | solution.py:351
  195.6 33.0 %all-to-all-done.1 = bf16[4,256,1536]{2,1,0:T(8,128)(2,1)} async-done(((bf16[4,256,1536]{2,1,0:T(8,128)(2,1)}), bf16[4,256,1536]{2,1,0:T(8,128)(2,1)}, u32[]{:S(2)}, u32[]{:S(2)}) %all-to-all-start.1) | async-done | bytes 3145760 | tf_op jit(solution)/shard_map/all_to_all | solution.py:60
  236.1 68.7 %all-to-all-done.2 = bf16[4,48,4224]{2,1,0:T(8,128)(2,1)} async-done(((bf16[4,48,4224]{2,1,0:T(8,128)(2,1)}), bf16[4,48,4224]{2,1,0:T(8,128)(2,1)}, u32[]{:S(2)}, u32[]{:S(2)}) %all-to-all-start.2) | async-done | bytes 1622048 | tf_op jit(solution)/shard_map/all_to_all | solution.py:85
  329.3 28.4 %shard_map.221 = (bf16[1024,2560]{1,0:T(8,128)(2,1)}, bf16[1024,2560]{1,0:T(8,128)(2,1)}, bf16[1024,2560]{1,0:T(8,128)(2,1)}) custom-call(bf16[1024,1536]{1,0:T(8,128)(2,1)} %bitcast.23.rows_ref, bf16[1536,2560]{1,0:T(8,128)(2,1)} %all-gather.10.cloned.1.call-done.gate_ref, bf16[1536,2560]{1,0:T(8,128)(2,1)} %all-gather.12.cloned.1.call-done.up_ref, ...), custom_call_target="tpu_custom_call" | custom-call | flops 16106127360 | bytes 31457280 | tf_op jit(solution)/shard_map/pallas_call | solution.py:188
  357.7 37.4 %all-to-all-done.4 = bf16[4,4,48,4224]{3,2,1,0:T(8,128)(2,1)} async-done(((bf16[4,4,48,4224]{3,2,1,0:T(8,128)(2,1)}), bf16[4,4,48,4224]{3,2,1,0:T(8,128)(2,1)}, u32[]{:S(2)}, u32[]{:S(2)}) %all-to-all-start.4) | async-done | bytes 6488096 | tf_op jit(solution)/shard_map/all_to_all | solution.py:60
  401.0 13.5 %convolution_convert_fusion.7 = bf16[1024,1536]{1,0:T(8,128)(2,1)} fusion(bf16[1024,2560]{1,0:T(8,128)(2,1)} %get-tuple-element.70, bf16[1536,2560]{1,0:T(8,128)(2,1)} %all-gather.14.cloned.1.call-done.down_ref), kind=kOutput, calls=%fused_computation.33 | convolution fusion | flops 8054636544 | bytes 16252928 | tf_op jit(solution)/shard_map/dot_general | solution.py:151
  422.2 34.1 %all-to-all-done.5 = bf16[4,256,1536]{2,1,0:T(8,128)(2,1)} async-done(((bf16[4,256,1536]{2,1,0:T(8,128)(2,1)}), bf16[4,256,1536]{2,1,0:T(8,128)(2,1)}, u32[]{:S(2)}, u32[]{:S(2)}) %all-to-all-start.5) | async-done | bytes 3145760 | tf_op jit(solution)/shard_map/all_to_all | solution.py:60
  486.7 18.9 %all-to-all-done.6 = bf16[4,256,1024]{2,1,0:T(8,128)(2,1)} async-done(((bf16[4,256,1024]{2,1,0:T(8,128)(2,1)}), bf16[4,256,1024]{2,1,0:T(8,128)(2,1)}, u32[]{:S(2)}, u32[]{:S(2)}) %all-to-all-start.6) | async-done | bytes 2097184 | tf_op jit(solution)/shard_map/all_to_all | solution.py:60
  505.6 23.2 %shard_map.222 = bf16[256,1536]{1,0:T(8,128)(2,1)} custom-call(s32[1]{0:T(128)} %bitcast.block_ref, bf16[256,1536]{1,0:T(8,128)(2,1)} %copy.277.query_ref, bf16[1024,1024]{1,0:T(8,128)(2,1)} %bitcast.48.key_ref.value_ref, bf16[1024,1024]{1,0:T(8,128)(2,1)} %bitcast.48.key_ref.value_ref), custom_call_target="tpu_custom_call" | custom-call | flops 6442450944 | bytes 3670016 | tf_op jit(solution)/shard_map/pallas_call | solution.py:351
  534.3 39.6 %all_to_all.75 = bf16[4,256,1536]{2,1,0:T(8,128)(2,1)} all-to-all(bf16[4,256,1536]{2,1,0:T(8,128)(2,1)S(1)} %broadcast_in_dim.45), channel_id=1, replica_groups=mesh['dp'=8,'expert'=4] {'expert'}, dimensions={0} | all-to-all | bytes 6291456 | tf_op jit(solution)/shard_map/all_to_all | solution.py:60
  585.5 28.3 %shard_map.223 = (bf16[1024,2560]{1,0:T(8,128)(2,1)}, bf16[1024,2560]{1,0:T(8,128)(2,1)}, bf16[1024,2560]{1,0:T(8,128)(2,1)}) custom-call(bf16[1024,1536]{1,0:T(8,128)(2,1)} %bitcast.429, bf16[1536,2560]{1,0:T(8,128)(2,1)} %all-gather.16.cloned.1.call-done.gate_ref, bf16[1536,2560]{1,0:T(8,128)(2,1)} %all-gather.18.cloned.1.call-done.up_ref, ...), custom_call_target="tpu_custom_call" | custom-call | flops 16106127360 | bytes 31457280 | tf_op jit(solution)/shard_map/pallas_call | solution.py:188
  615.1 13.5 %fusion = bf16[1536,2560]{1,0:T(8,128)(2,1)} fusion(bf16[1024,2560]{1,0:T(8,128)(2,1)} %get-tuple-element.72, bf16[1024,1536]{1,0:T(8,128)(2,1)} %bitcast.49.grad_ref), kind=kOutput, calls=%fused_computation.7 | convolution fusion | flops 8056995840 | bytes 16252928 | tf_op jit(solution)/shard_map/dot_general | solution.py:151
  629.3 41.6 %shard_map.224 = (bf16[1024,2560]{1,0:T(8,128)(2,1)}, bf16[1024,2560]{1,0:T(8,128)(2,1)}, bf16[1024,1664]{1,0:T(8,128)(2,1)}) custom-call(s32[2]{0:T(128)} %pad_add_fusion.group_ref, bf16[1024,1536]{1,0:T(8,128)(2,1)} %bitcast.49.grad_ref, bf16[1536,2560]{1,0:T(8,128)(2,1)} %all-gather.20.cloned.1.call-done.down_ref, ...), custom_call_target="tpu_custom_call" | custom-call | flops 24159191040 | bytes 44564480 | tf_op jit(solution)/shard_map/pallas_call | solution.py:274
  675.8 13.5 %convolution_convert_fusion.3 = bf16[1536,2560]{1,0:T(8,128)(2,1)} fusion(bf16[1024,1536]{1,0:T(8,128)(2,1)} %bitcast.430, bf16[1024,2560]{1,0:T(8,128)(2,1)} %get-tuple-element.79), kind=kOutput, calls=%fused_computation.4 | convolution fusion | flops 8056995840 | bytes 16252928 | tf_op jit(solution)/shard_map/dot_general | solution.py:151
  689.4 13.6 %convolution_convert_fusion.6 = bf16[1024,1536]{1,0:T(8,128)(2,1)} fusion(bf16[1024,2560]{1,0:T(8,128)(2,1)} %get-tuple-element.72, bf16[1536,2560]{1,0:T(8,128)(2,1)} %all-gather.20.cloned.1.call-done.down_ref), kind=kOutput, calls=%fused_computation.32 | convolution fusion | flops 8054636544 | bytes 16252928 | tf_op jit(solution)/shard_map/dot_general | solution.py:151
  702.9 12.7 %convolution_convert_fusion.4 = bf16[1536,2560]{1,0:T(8,128)(2,1)} fusion(bf16[1024,1536]{1,0:T(8,128)(2,1)S(1)} %bitcast.431, bf16[1024,2560]{1,0:T(8,128)(2,1)} %get-tuple-element.78), kind=kOutput, calls=%fused_computation.5 | convolution fusion | flops 8056995840 | bytes 16252928 | tf_op jit(solution)/shard_map/dot_general | solution.py:151
  740.0 31.1 %shard_map.225 = (f32[256,1536]{1,0:T(8,128)}, bf16[1024,1024]{1,0:T(8,128)(2,1)}) custom-call(s32[1]{0:T(128)} %bitcast.block_ref, bf16[256,1536]{1,0:T(8,128)(2,1)} %copy.277.query_ref, bf16[256,1536]{1,0:T(8,128)(2,1)} %fusion.36.grad_ref, bf16[1024,1024]{1,0:T(8,128)(2,1)} %bitcast.48.key_ref.value_ref, bf16[1024,1024]{1,0:T(8,128)(2,1)} %bitcast.48.key_ref.value_ref), custom_call_target="tpu_custom_call" | custom-call | flops 16106127360 | bytes 7340032 | tf_op jit(solution)/shard_map/pallas_call | solution.py:398
  844.6 21.6 %all-to-all-done.12 = bf16[4,256,1536]{2,1,0:T(8,128)(2,1)} async-done(((bf16[4,256,1536]{2,1,0:T(8,128)(2,1)}), bf16[4,256,1536]{2,1,0:T(8,128)(2,1)}, u32[]{:S(2)}, u32[]{:S(2)}) %all-to-all-start.12) | async-done | bytes 3145760 | tf_op jit(solution)/shard_map/all_to_all | solution.py:60
  866.3 13.7 %convolution_convert_fusion.2 = bf16[1536,2560]{1,0:T(8,128)(2,1)} fusion(bf16[1024,1536]{1,0:T(8,128)(2,1)} %bitcast.74.grad_ref, bf16[1024,2560]{1,0:T(8,128)(2,1)} %get-tuple-element.70), kind=kOutput, calls=%fused_computation.3 | convolution fusion | flops 8056995840 | bytes 16252928 | tf_op jit(solution)/shard_map/dot_general | solution.py:151
  887.3 40.9 %shard_map.226 = (bf16[1024,2560]{1,0:T(8,128)(2,1)}, bf16[1024,2560]{1,0:T(8,128)(2,1)}, bf16[1024,1664]{1,0:T(8,128)(2,1)}) custom-call(s32[2]{0:T(128)} %pad_add_fusion.group_ref, bf16[1024,1536]{1,0:T(8,128)(2,1)} %bitcast.74.grad_ref, bf16[1536,2560]{1,0:T(8,128)(2,1)} %all-gather.14.cloned.1.call-done.down_ref, ...), custom_call_target="tpu_custom_call" | custom-call | flops 24159191040 | bytes 44564480 | tf_op jit(solution)/shard_map/pallas_call | solution.py:274
  932.0 13.8 %convolution_convert_fusion = bf16[1536,2560]{1,0:T(8,128)(2,1)} fusion(bf16[1024,1536]{1,0:T(8,128)(2,1)} %bitcast.23.rows_ref, bf16[1024,2560]{1,0:T(8,128)(2,1)} %get-tuple-element.97), kind=kOutput, calls=%fused_computation.1 | convolution fusion | flops 8056995840 | bytes 16252928 | tf_op jit(solution)/shard_map/dot_general | solution.py:151
  945.8 14.0 %convolution_convert_fusion.1 = bf16[1536,2560]{1,0:T(8,128)(2,1)} fusion(bf16[1024,1536]{1,0:T(8,128)(2,1)} %bitcast.23.rows_ref, bf16[1024,2560]{1,0:T(8,128)(2,1)} %get-tuple-element.96), kind=kOutput, calls=%fused_computation.2 | convolution fusion | flops 8056995840 | bytes 16252928 | tf_op jit(solution)/shard_map/dot_general | solution.py:151
  994.4 31.3 %shard_map.227 = (f32[256,1536]{1,0:T(8,128)}, bf16[1024,1024]{1,0:T(8,128)(2,1)}) custom-call(s32[1]{0:T(128)} %bitcast.block_ref, bf16[256,1536]{1,0:T(8,128)(2,1)} %copy.248.query_ref, bf16[256,1536]{1,0:T(8,128)(2,1)} %fusion.33.grad_ref, bf16[1024,1024]{1,0:T(8,128)(2,1)} %bitcast.14.key_ref.value_ref, bf16[1024,1024]{1,0:T(8,128)(2,1)} %bitcast.14.key_ref.value_ref), custom_call_target="tpu_custom_call" | custom-call | flops 16106127360 | bytes 7340032 | tf_op jit(solution)/shard_map/pallas_call | solution.py:398
  1056.9 10.6 collective-permute-done.17
  1092.9 33.3 %collective-permute-done.29 = bf16[48,4224]{1,0:T(8,128)(2,1)} collective-permute-done((bf16[48,4224]{1,0:T(8,128)(2,1)}, bf16[48,4224]{1,0:T(8,128)(2,1)}, u32[]{:S(2)}, u32[]{:S(2)}) %collective-permute-start.29) | collective-permute-done | bytes 405536 | tf_op jit(solution)/shard_map/ppermute | solution.py:130
  1131.7 13.8 %collective-permute-done.19 = bf16[192,1536]{1,0:T(8,128)(2,1)S(1)} collective-permute-done((bf16[192,1536]{1,0:T(8,128)(2,1)S(1)}, bf16[192,1536]{1,0:T(8,128)(2,1)S(1)}, u32[]{:S(2)}, u32[]{:S(2)}) %collective-permute-start.19) | collective-permute-done | bytes 589856 | tf_op jit(solution)/shard_map/ppermute | solution.py:130
  1145.7 7.9 collective-permute-done.25
  1156.1 9.9 collective-permute-done.26
  1166.1 14.7 %collective-permute-done.20 = bf16[96,3072]{1,0:T(8,128)(2,1)S(1)} collective-permute-done((bf16[96,3072]{1,0:T(8,128)(2,1)S(1)}, bf16[96,3072]{1,0:T(8,128)(2,1)S(1)}, u32[]{:S(2)}, u32[]{:S(2)}) %collective-permute-start.20) | collective-permute-done | bytes 589856 | tf_op jit(solution)/shard_map/ppermute | solution.py:130
  1181.6 14.8 %collective-permute-done.21 = bf16[48,3072]{1,0:T(8,128)(2,1)S(1)} collective-permute-done((bf16[48,3072]{1,0:T(8,128)(2,1)S(1)}, bf16[48,3072]{1,0:T(8,128)(2,1)S(1)}, u32[]{:S(2)}, u32[]{:S(2)}) %collective-permute-start.21) | collective-permute-done | bytes 294944 | tf_op jit(solution)/shard_map/ppermute | solution.py:130
  (520 shorter events, 400.6 us)
Async XLA Ops:
  7.2 108.2 %all-gather.8.cloned.1.call-start = ((), (), s32[]{:S(2)}) async-start(), calls=%async_computation.21 | async-start | bytes 13381632 | tf_op jit(solution)/shard_map/all_gather | solution.py:524
  15.4 313.9 %all-gather.10.cloned.1.call-start = ((), (), s32[]{:S(2)}) async-start(), calls=%async_computation.22 | async-start | bytes 8847360 | tf_op jit(solution)/shard_map/all_gather | solution.py:529
  19.5 309.8 %all-gather.12.cloned.1.call-start = ((), (), s32[]{:S(2)}) async-start(), calls=%async_computation.23 | async-start | bytes 8847360 | tf_op jit(solution)/shard_map/all_gather | solution.py:529
  25.4 375.7 %all-gather.14.cloned.1.call-start = ((), (), s32[]{:S(2)}) async-start(), calls=%async_computation.24 | async-start | bytes 8847360 | tf_op jit(solution)/shard_map/all_gather | solution.py:529
  31.4 554.1 %all-gather.16.cloned.1.call-start = ((), (), s32[]{:S(2)}) async-start(), calls=%async_computation.25 | async-start | bytes 8847360 | tf_op jit(solution)/shard_map/all_gather | solution.py:529
  187.9 40.7 %all-to-all-start.1 = ((bf16[4,256,1536]{2,1,0:T(8,128)(2,1)}), bf16[4,256,1536]{2,1,0:T(8,128)(2,1)}, u32[]{:S(2)}, u32[]{:S(2)}) async-start(bf16[4,256,1536]{2,1,0:T(8,128)(2,1)} %broadcast_in_dim.37), calls=%async_computation.1 | async-start | bytes 6291456 | tf_op jit(solution)/shard_map/all_to_all | solution.py:60
  192.6 392.9 %all-gather.18.cloned.1.call-start = ((), (), s32[]{:S(2)}) async-start(), calls=%async_computation.26 | async-start | bytes 8847360 | tf_op jit(solution)/shard_map/all_gather | solution.py:529
  230.8 74.0 %all-to-all-start.2 = ((bf16[4,48,4224]{2,1,0:T(8,128)(2,1)}), bf16[4,48,4224]{2,1,0:T(8,128)(2,1)}, u32[]{:S(2)}, u32[]{:S(2)}) async-start(bf16[4,48,4224]{2,1,0:T(8,128)(2,1)} %broadcast_in_dim.38), calls=%async_computation.2 | async-start | bytes 3244032 | tf_op jit(solution)/shard_map/all_to_all | solution.py:85
  318.9 76.2 %all-to-all-start.4 = ((bf16[4,4,48,4224]{3,2,1,0:T(8,128)(2,1)}), bf16[4,4,48,4224]{3,2,1,0:T(8,128)(2,1)}, u32[]{:S(2)}, u32[]{:S(2)}) async-start(bf16[4,4,48,4224]{3,2,1,0:T(8,128)(2,1)} %broadcast_in_dim.42), calls=%async_computation.4 | async-start | bytes 12976128 | tf_op jit(solution)/shard_map/all_to_all | solution.py:60
  401.0 58.2 %collective-permute-start = (bf16[4,4,48,4224]{3,2,0,1:T(8,128)(2,1)}, bf16[4,4,48,4224]{3,2,0,1:T(8,128)(2,1)}, u32[]{:S(2)}, u32[]{:S(2)}) collective-permute-start(bf16[4,4,48,4224]{3,2,0,1:T(8,128)(2,1)} %copy.259), channel_id=1, source_target_pairs={{0,4},{4,0},{8,12},{12,8},{16,20},{20,16},{24,28},{28,24},{1,5},{5... | collective-permute-start | bytes 19464200 | tf_op jit(solution)/shard_map/ppermute | solution.py:81
  414.6 41.8 %all-to-all-start.5 = ((bf16[4,256,1536]{2,1,0:T(8,128)(2,1)}), bf16[4,256,1536]{2,1,0:T(8,128)(2,1)}, u32[]{:S(2)}, u32[]{:S(2)}) async-start(bf16[4,256,1536]{2,1,0:T(8,128)(2,1)} %bitcast.433), calls=%async_computation.5 | async-start | bytes 6291456 | tf_op jit(solution)/shard_map/all_to_all | solution.py:60
  419.2 210.1 %all-gather.20.cloned.1.call-start = ((), (), s32[]{:S(2)}) async-start(), calls=%async_computation.27 | async-start | bytes 8847360 | tf_op jit(solution)/shard_map/all_gather | solution.py:529
  575.9 39.2 %all-to-all-start.7 = ((bf16[4,256,1536]{2,1,0:T(8,128)(2,1)}), bf16[4,256,1536]{2,1,0:T(8,128)(2,1)}, u32[]{:S(2)}, u32[]{:S(2)}) async-start(bf16[4,256,1536]{2,1,0:T(8,128)(2,1)} %broadcast_in_dim.44), calls=%async_computation.7 | async-start | bytes 6291456 | tf_op jit(solution)/shard_map/all_to_all | solution.py:60
  580.6 619.5 %reduce-scatter.9.cloned.1.call-start = ((), (), s32[]{:S(2)}) async-start(), calls=%async_computation.29 | async-start | bytes 8847360 | tf_op jit(solution)/shard_map/reduce_scatter | solution.py:678
  670.9 44.8 %all-to-all-start.9 = ((bf16[4,256,1664]{2,1,0:T(8,128)(2,1)}), bf16[4,256,1664]{2,1,0:T(8,128)(2,1)}, u32[]{:S(2)}, u32[]{:S(2)}) async-start(bf16[4,256,1664]{2,1,0:T(8,128)(2,1)} %bitcast.421), calls=%async_computation.9 | async-start | bytes 6815744 | tf_op jit(solution)/shard_map/all_to_all | solution.py:60
  675.6 524.5 %reduce-scatter.11.cloned.1.call-start = ((), (), s32[]{:S(2)}) async-start(), calls=%async_computation.30 | async-start | bytes 8847360 | tf_op jit(solution)/shard_map/reduce_scatter | solution.py:705
  719.5 480.6 %reduce-scatter.13.cloned.1.call-start = ((), (), s32[]{:S(2)}) async-start(), calls=%async_computation.31 | async-start | bytes 8847360 | tf_op jit(solution)/shard_map/reduce_scatter | solution.py:706
  720.9 68.5 %collective-permute-start.2 = (bf16[256,1536]{1,0:T(8,128)(2,1)}, bf16[256,1536]{1,0:T(8,128)(2,1)}, u32[]{:S(2)}, u32[]{:S(2)}) collective-permute-start(bf16[256,1536]{1,0:T(8,128)(2,1)} %shard_map.222), channel_id=1, source_target_pairs={{0,4},{4,0},{8,12},{12,8},{16,20},{20,16},{24,28},{28,24},{1,5},{5... | collective-permute-start | bytes 2359304 | tf_op jit(solution)/shard_map/ppermute | solution.py:81
  722.9 48.2 %all-to-all-start.10 = ((bf16[4,256,1536]{2,1,0:T(8,128)(2,1)}), bf16[4,256,1536]{2,1,0:T(8,128)(2,1)}, u32[]{:S(2)}, u32[]{:S(2)}) async-start(bf16[4,256,1536]{2,1,0:T(8,128)(2,1)} %bitcast.432), calls=%async_computation.10 | async-start | bytes 6291456 | tf_op jit(solution)/shard_map/all_to_all | solution.py:60
  794.0 40.8 %collective-permute-start.3 = (bf16[384,1536]{1,0:T(8,128)(2,1)}, bf16[384,1536]{1,0:T(8,128)(2,1)}, u32[]{:S(2)}, u32[]{:S(2)}) collective-permute-start(bf16[384,1536]{1,0:T(8,128)(2,1)} %bitcast.82), channel_id=1, source_target_pairs={{0,1},{1,0},{2,3},{3,2},{4,5},{5,4},{6,7},{7,6},{8,9},{9,8},{10,11... | collective-permute-start | bytes 3538952 | tf_op jit(solution)/shard_map/ppermute | solution.py:130
  825.5 40.8 %all-to-all-start.12 = ((bf16[4,256,1536]{2,1,0:T(8,128)(2,1)}), bf16[4,256,1536]{2,1,0:T(8,128)(2,1)}, u32[]{:S(2)}, u32[]{:S(2)}) async-start(bf16[4,256,1536]{2,1,0:T(8,128)(2,1)} %broadcast_in_dim.48), calls=%async_computation.12 | async-start | bytes 6291456 | tf_op jit(solution)/shard_map/all_to_all | solution.py:60
  830.3 381.9 %reduce-scatter.17.cloned.1.call-start = ((), (), s32[]{:S(2)}) async-start(), calls=%async_computation.33 | async-start | bytes 8847360 | tf_op jit(solution)/shard_map/reduce_scatter | solution.py:678
  881.4 80.7 %collective-permute-start.10 = (bf16[384,1152]{1,0:T(8,128)(2,1)}, bf16[384,1152]{1,0:T(8,128)(2,1)}, u32[]{:S(2)}, u32[]{:S(2)}) collective-permute-start(bf16[384,1152]{1,0:T(8,128)(2,1)} %bitcast.104), channel_id=1, source_target_pairs={{0,1},{1,0},{2,3},{3,2},{4,5},{5,4},{6,7},{7,6},{8,9},{9,8},{10,11... | collective-permute-start | bytes 2654216 | tf_op jit(solution)/shard_map/ppermute | solution.py:130
  884.4 80.1 %collective-permute-start.9 = (bf16[384,1536]{1,0:T(8,128)(2,1)}, bf16[384,1536]{1,0:T(8,128)(2,1)}, u32[]{:S(2)}, u32[]{:S(2)}) collective-permute-start(bf16[384,1536]{1,0:T(8,128)(2,1)} %bitcast.101), channel_id=1, source_target_pairs={{0,1},{1,0},{2,3},{3,2},{4,5},{5,4},{6,7},{7,6},{8,9},{9,8},{10,11... | collective-permute-start | bytes 3538952 | tf_op jit(solution)/shard_map/ppermute | solution.py:130
  886.2 73.6 %collective-permute-start.8 = (bf16[192,1536]{1,0:T(8,128)(2,1)}, bf16[192,1536]{1,0:T(8,128)(2,1)}, u32[]{:S(2)}, u32[]{:S(2)}) collective-permute-start(bf16[192,1536]{1,0:T(8,128)(2,1)} %dynamic-slice_bitcast_fusion.3), channel_id=1, source_target_pairs={{0,2},{1,3},{2,0},{3,1},{4,6},{5,7},{6,4},{7,5},{8,10},{9,11},{10,... | collective-permute-start | bytes 1769480 | tf_op jit(solution)/shard_map/ppermute | solution.py:130
  928.2 41.3 %all-to-all-start.13 = ((bf16[4,256,1664]{2,1,0:T(8,128)(2,1)}), bf16[4,256,1664]{2,1,0:T(8,128)(2,1)S(1)}, u32[]{:S(2)}, u32[]{:S(2)}) async-start(bf16[4,256,1664]{2,1,0:T(8,128)(2,1)} %bitcast.420), calls=%async_computation.13 | async-start | bytes 6815744 | tf_op jit(solution)/shard_map/all_to_all | solution.py:60
  932.0 284.2 %reduce-scatter.15.cloned.1.call-start = ((), (), s32[]{:S(2)}) async-start(), calls=%async_computation.32 | async-start | bytes 8847360 | tf_op jit(solution)/shard_map/reduce_scatter | solution.py:706
  974.6 95.0 %collective-permute-start.15 = (bf16[256,768]{0,1:T(8,128)(2,1)}, bf16[256,768]{0,1:T(8,128)(2,1)}, u32[]{:S(2)}, u32[]{:S(2)}) collective-permute-start(bf16[256,768]{0,1:T(8,128)(2,1)} %get-tuple-element.239), channel_id=1, source_target_pairs={{0,4},{4,0},{8,12},{12,8},{16,20},{20,16},{24,28},{28,24},{1,5},{5... | collective-permute-start | bytes 1179656 | tf_op jit(solution)/shard_map/ppermute | solution.py:81
  978.1 55.0 %collective-permute-start.14 = (bf16[192,2688]{1,0:T(8,128)(2,1)}, bf16[192,2688]{1,0:T(8,128)(2,1)}, u32[]{:S(2)}, u32[]{:S(2)}) collective-permute-start(bf16[192,2688]{1,0:T(8,128)(2,1)} %dynamic-slice_bitcast_fusion), channel_id=1, source_target_pairs={{0,2},{1,3},{2,0},{3,1},{4,6},{5,7},{6,4},{7,5},{8,10},{9,11},{10,... | collective-permute-start | bytes 3096584 | tf_op jit(solution)/shard_map/ppermute | solution.py:130
  993.0 42.8 %collective-permute-start.13 = (bf16[384,1536]{1,0:T(8,128)(2,1)}, bf16[384,1536]{1,0:T(8,128)(2,1)}, u32[]{:S(2)}, u32[]{:S(2)}) collective-permute-start(bf16[384,1536]{1,0:T(8,128)(2,1)} %bitcast.113), channel_id=1, source_target_pairs={{0,1},{1,0},{2,3},{3,2},{4,5},{5,4},{6,7},{7,6},{8,9},{9,8},{10,11... | collective-permute-start | bytes 3538952 | tf_op jit(solution)/shard_map/ppermute | solution.py:130
  1029.4 190.8 %reduce-scatter.7.cloned.1.call-start = ((), (), s32[]{:S(2)}) async-start(), calls=%async_computation.28 | async-start | bytes 8847360 | tf_op jit(solution)/shard_map/reduce_scatter | solution.py:705
  1077.3 50.0 %collective-permute-start.18 = (bf16[384,1536]{1,0:T(8,128)(2,1)}, bf16[384,1536]{1,0:T(8,128)(2,1)}, u32[]{:S(2)}, u32[]{:S(2)}) collective-permute-start(bf16[384,1536]{1,0:T(8,128)(2,1)} %bitcast.136), channel_id=1, source_target_pairs={{0,1},{1,0},{2,3},{3,2},{4,5},{5,4},{6,7},{7,6},{8,9},{9,8},{10,11... | collective-permute-start | bytes 3538952 | tf_op jit(solution)/shard_map/ppermute | solution.py:130
  (106 other events, 1664.2 us)
Sparse Core Ops, SparseCore 0:
  15.5 99.8 all-gather.7
  117.6 76.2 all-gather.9
  195.5 109.4 all-gather.11
  306.5 76.6 all-gather.13
  384.7 76.2 all-gather.15
  462.5 76.2 all-gather.17
  541.0 76.2 all-gather.19
  628.7 81.9 reduce-scatter.8
  719.6 83.1 reduce-scatter.10
  805.0 83.0 reduce-scatter.12
  890.4 83.0 reduce-scatter.16
  975.6 89.8 reduce-scatter.14
  1067.8 96.5 reduce-scatter.6

commit v7 on v6

--- a/solution.py
+++ b/solution.py
@@ -120,10 +120,10 @@
     return jnp.concatenate([rows, swap_cores(rows)], axis=0)
 
 
-def halve(partial, axis_name, step):
+def halve(partial, axis_name, step, outer):
     size = lax.axis_size(axis_name)
     width = partial.shape[-1]
-    blocks = partial.reshape(size // (2 * step), 2, -1, width)
+    blocks = partial.reshape(outer, 2, -1, width)
     side = (lax.axis_index(axis_name) // step) % 2
     mine = lax.dynamic_index_in_dim(blocks, side, 1, keepdims=False)
     theirs = lax.dynamic_index_in_dim(blocks, 1 - side, 1, keepdims=False)
@@ -134,16 +134,21 @@
     return total.astype(jnp.bfloat16)
 
 
-def halvings(axis_name, least):
+def near_first(axis_name, least):
+    size = lax.axis_size(axis_name)
     steps = [least]
-    while 2 * steps[-1] < lax.axis_size(axis_name):
+    while 2 * steps[-1] < size:
         steps.append(2 * steps[-1])
-    return [(axis_name, step) for step in steps]
+    return [(axis_name, step, size // (2 * step)) for step in steps]
+
+
+def far_first(axis_name, least):
+    return [(axis_name, step, 1) for _, step, _ in reversed(near_first(axis_name, least))]
 
 
 def halve_all(partial, steps):
-    for axis_name, step in steps:
-        partial = halve(partial, axis_name, step)
+    for step in steps:
+        partial = halve(partial, *step)
     return partial
 
 
@@ -636,10 +641,10 @@
     output = None
     grad_hidden = cotangent.astype(jnp.float32).reshape(token_total, model_width)
     attention_list = [None] * LAYER_COUNT
-    placed = []
     waiting = None
-    group_steps = halvings("expert", 1)
-    chip_steps = halvings("dp", 2)
+    group_steps = near_first("expert", 1)
+    far_steps = far_first("expert", 1)
+    chip_steps = near_first("dp", 2)
     for layer in range(LAYER_COUNT - 1, -1, -1):
         (
             layer_hidden,
@@ -721,6 +726,10 @@
         grad_output_w = dot_f32(core_major(grad_branch), both_cores(attended), (0,), (0,))
         grad_output_w = halve_all(grad_output_w.astype(jnp.bfloat16), group_steps[:1])
         grad_attended = dot_f32(grad_branch, output_full, (1,), (0,)).astype(jnp.bfloat16)
+        if waiting is not None:
+            grad_attended, late_part = lax.optimization_barrier((grad_attended, late_part))
+            chip_part = jnp.concatenate([out_part, late_part], axis=1)
+            chip_part = halve_all(chip_part, chip_steps[:1])
         grad_query, grad_key_value_all = attention_backward(
             block_at, query_rotated, grad_attended, key_value_all
         )
@@ -729,12 +738,11 @@
                 (grad_query, grad_key_value_all, output)
             )
         else:
-            grad_query, grad_output_w, late_part = lax.optimization_barrier(
-                (grad_query, grad_output_w, late_part)
+            grad_query, grad_output_w, chip_part = lax.optimization_barrier(
+                (grad_query, grad_output_w, chip_part)
             )
             grad_output_w = halve_all(grad_output_w, group_steps[1:])
-            chip_part = jnp.concatenate([out_part, late_part], axis=1)
-            attention_list[layer + 1] = halve_all(chip_part, chip_steps)
+            chip_part = halve_all(chip_part, chip_steps[1:])
         grad_kv = sum_rows(grad_key_value_all)
         normed_split = core_major(first_normalized)
         grad_query_lin = (
@@ -747,7 +755,11 @@
         grad_query_w = dot_f32(normed_split, both_cores(grad_query_lin), (0,), (0,))
         grad_query_w = grad_query_w.astype(jnp.bfloat16)
         if layer == 0:
-            grad_kv, grad_query_w = lax.optimization_barrier((grad_kv, grad_query_w))
+            grad_kv, grad_query_w, chip_part = lax.optimization_barrier(
+                (grad_kv, grad_query_w, chip_part)
+            )
+            attention_list[layer + 1] = chip_part
+            grad_query_w = halve_all(grad_query_w, far_steps[:1])
         grad_kv = grad_kv.reshape(token_total, -1, 2, 2 * HEAD_SIZE)
         grad_kv = grad_kv.transpose(0, 2, 1, 3).reshape(token_total, 2 * key_width)
         grad_key_lin = (
@@ -785,16 +797,21 @@
         if layer > 0:
             waiting = (grad_output_w, grad_query_w, grad_kv_w)
         else:
-            grad_query_w = halve_all(grad_query_w, group_steps)
-            early = jnp.concatenate([grad_output_w, grad_query_w], axis=1)
-            attention_list[layer] = jnp.concatenate(
+            grad_kv_w, last_parts = lax.optimization_barrier((grad_kv_w, last_parts))
+            expert_held = [place(part, None, layer + 1, exp_dev) for part in last_parts]
+            grad_kv_w = halve_all(grad_kv_w, group_steps[:1])
+            grad_kv_w, expert_held = lax.optimization_barrier((grad_kv_w, expert_held))
+            late_part = jnp.concatenate(
                 [
-                    halve_all(early, chip_steps),
-                    halve_all(grad_kv_w, group_steps + chip_steps),
+                    halve_all(grad_query_w, far_steps[1:]),
+                    halve_all(grad_kv_w, group_steps[1:]),
                 ],
                 axis=1,
             )
-        placed = placed + [(layer, expert_parts)]
+            attention_list[layer] = jnp.concatenate(
+                [halve_all(grad_output_w, chip_steps), halve_all(late_part, chip_steps)], axis=1
+            )
+        last_parts = expert_parts
         grad_hidden = grad_middle + grad_norm_in
     stacked = jnp.stack(attention_list).astype(jnp.float32)
     cuts = [query_width, query_width, key_width, key_width, expert_total, 1, 1]
@@ -802,13 +819,9 @@
     output_grads, query_grads, key_grads, value_grads, router_grads, one, two = (
         stacked[:, :, start:stop] for start, stop in zip(cuts[:-1], cuts[1:])
     )
-    expert_held = [None] * 3
-    for layer, expert_parts in placed:
-        if layer > 0:
-            grad_kv_w, expert_parts = lax.optimization_barrier((grad_kv_w, expert_parts))
-        expert_held = [
-            place(part, held, layer, exp_dev) for part, held in zip(expert_parts, expert_held)
-        ]
+    expert_held = [
+        place(part, held, 0, exp_dev) for part, held in zip(last_parts, expert_held)
+    ]
     down_grads, gate_grads, up_grads = expert_held
     return (
         output.astype(jnp.bfloat16).reshape(sequences_per_device, block_length, model_width),

time: 1240 us -> 1230 us (level)
  waiting for transfers between devices: 434 us -> 414 us
    ppermute x17, waiting for transfers between devices: 105 us -> 88 us  [halve(): lax.ppermute(theirs.reshape(-1, width), axis_name, [(i, i ^ step) for i i...]
  transfers between devices with their start and end apart: 57 -> 57, of which waited for: 20 -> 19; matrix products, arithmetic and copies ran while one was open for 29% -> 30% of each run, Pallas kernels for 22% -> 22%
where the time goes in v7:
time: 1230 us; the launch traced here: 1220 us
  waiting for transfers between devices  414 us (34%)
  Pallas kernels  273 us (22%)
  matrix products  186 us (15%)
  local copies, waits for them, and re-layouts  128 us (10%)
  starting transfers between devices  86.8 us (7%)
  other arithmetic  76.4 us (6%)
  blocking collectives  39.6 us (3%)
  between operations  16.2 us (1%)
    all_to_all x13, waiting for transfers between devices, exchange(): lax.all_to_all(blocks, 'expert', split_axis=0, concat_axis=0, tiled=True)  176 us
    dot_general x26, matrix products, dot_f32(): lax.dot_general(left, right, ((left_dims, right_dims), ((), ())), preferr...  169 us
    ppermute x17, waiting for transfers between devices, halve(): lax.ppermute(theirs.reshape(-1, width), axis_name, [(i, i ^ step) for i i...  88 us
    pallas_call x2, Pallas kernels, expert_backward(): pl.pallas_call(expert_backward_kernel, grid_spec=pltpu.PrefetchScalarGrid...  82.5 us
    all_gather x1, waiting for transfers between devices, body(): packed = [lax.all_gather(shards[0], ('dp', 'expert'), axis=0, tiled=True)]  80.8 us
    all_to_all x1, waiting for transfers between devices, exchange_chips(): lax.all_to_all(blocks, 'dp', split_axis=0, concat_axis=0, axis_index_grou...  68.6 us
    pallas_call x2, Pallas kernels, attention_backward(): pl.pallas_call(attention_backward_kernel, grid_spec=pltpu.PrefetchScalarG...  62.5 us
    all_to_all x13, starting transfers between devices, exchange(): lax.all_to_all(blocks, 'expert', split_axis=0, concat_axis=0, tiled=True)  59.6 us
  transfers between devices with their start and end apart: 57, of which 19 were waited for; matrix products, arithmetic and copies ran while one was open for 30% of the time, Pallas kernels for 22%

profile of v7, /device:TPU:0, one launch (start us, length us, event | category | flops | bytes accessed | tf_op | source)
XLA Modules:
  0.0 1220.1 jit_solution(7304436455215024530)
XLA Ops:
  34.6 80.8 %all-gather.8.cloned.1.call-done = bf16[1536,4224]{1,0:T(8,128)(2,1)} async-done(((bf16[48,4224]{1,0:T(8,128)(2,1)}), bf16[1536,4224]{1,0:T(8,128)(2,1)}) %all-gather.8.cloned.1.call-update) | async-done | bytes 12976144 | tf_op jit(solution)/shard_map/all_gather | solution.py:529
  138.8 18.4 %all-to-all-done = bf16[4,256,1024]{2,1,0:T(8,128)(2,1)} async-done(((bf16[4,256,1024]{2,1,0:T(8,128)(2,1)}), bf16[4,256,1024]{2,1,0:T(8,128)(2,1)}, u32[]{:S(2)}, u32[]{:S(2)}) %all-to-all-start) | async-done | bytes 2097184 | tf_op jit(solution)/shard_map/all_to_all | solution.py:60
  157.2 23.3 %shard_map.220 = bf16[256,1536]{1,0:T(8,128)(2,1)} custom-call(s32[1]{0:T(128)} %bitcast.block_ref, bf16[256,1536]{1,0:T(8,128)(2,1)} %copy.248.query_ref, bf16[1024,1024]{1,0:T(8,128)(2,1)} %bitcast.14.key_ref.value_ref, bf16[1024,1024]{1,0:T(8,128)(2,1)} %bitcast.14.key_ref.value_ref), custom_call_target="tpu_custom_call" | custom-call | flops 6442450944 | bytes 3670016 | tf_op jit(solution)/shard_map/pallas_call | solution.py:356
  195.7 33.0 %all-to-all-done.1 = bf16[4,256,1536]{2,1,0:T(8,128)(2,1)} async-done(((bf16[4,256,1536]{2,1,0:T(8,128)(2,1)}), bf16[4,256,1536]{2,1,0:T(8,128)(2,1)}, u32[]{:S(2)}, u32[]{:S(2)}) %all-to-all-start.1) | async-done | bytes 3145760 | tf_op jit(solution)/shard_map/all_to_all | solution.py:60
  236.2 68.6 %all-to-all-done.2 = bf16[4,48,4224]{2,1,0:T(8,128)(2,1)} async-done(((bf16[4,48,4224]{2,1,0:T(8,128)(2,1)}), bf16[4,48,4224]{2,1,0:T(8,128)(2,1)}, u32[]{:S(2)}, u32[]{:S(2)}) %all-to-all-start.2) | async-done | bytes 1622048 | tf_op jit(solution)/shard_map/all_to_all | solution.py:85
  329.3 28.4 %shard_map.221 = (bf16[1024,2560]{1,0:T(8,128)(2,1)}, bf16[1024,2560]{1,0:T(8,128)(2,1)}, bf16[1024,2560]{1,0:T(8,128)(2,1)}) custom-call(bf16[1024,1536]{1,0:T(8,128)(2,1)} %bitcast.23.rows_ref, bf16[1536,2560]{1,0:T(8,128)(2,1)} %all-gather.10.cloned.1.call-done.gate_ref, bf16[1536,2560]{1,0:T(8,128)(2,1)} %all-gather.12.cloned.1.call-done.up_ref, ...), custom_call_target="tpu_custom_call" | custom-call | flops 16106127360 | bytes 31457280 | tf_op jit(solution)/shard_map/pallas_call | solution.py:193
  357.7 37.4 %all-to-all-done.4 = bf16[4,4,48,4224]{3,2,1,0:T(8,128)(2,1)} async-done(((bf16[4,4,48,4224]{3,2,1,0:T(8,128)(2,1)}), bf16[4,4,48,4224]{3,2,1,0:T(8,128)(2,1)}, u32[]{:S(2)}, u32[]{:S(2)}) %all-to-all-start.4) | async-done | bytes 6488096 | tf_op jit(solution)/shard_map/all_to_all | solution.py:60
  395.1 6.0 copy.259
  401.1 13.5 %convolution_convert_fusion.7 = bf16[1024,1536]{1,0:T(8,128)(2,1)} fusion(bf16[1024,2560]{1,0:T(8,128)(2,1)} %get-tuple-element.78, bf16[1536,2560]{1,0:T(8,128)(2,1)} %all-gather.14.cloned.1.call-done.down_ref), kind=kOutput, calls=%fused_computation.33 | convolution fusion | flops 8054636544 | bytes 16252928 | tf_op jit(solution)/shard_map/dot_general | solution.py:156
  422.2 34.1 %all-to-all-done.5 = bf16[4,256,1536]{2,1,0:T(8,128)(2,1)} async-done(((bf16[4,256,1536]{2,1,0:T(8,128)(2,1)}), bf16[4,256,1536]{2,1,0:T(8,128)(2,1)}, u32[]{:S(2)}, u32[]{:S(2)}) %all-to-all-start.5) | async-done | bytes 3145760 | tf_op jit(solution)/shard_map/all_to_all | solution.py:60
  459.3 5.6 select_bitcast_fusion.1
  486.7 18.9 %all-to-all-done.6 = bf16[4,256,1024]{2,1,0:T(8,128)(2,1)} async-done(((bf16[4,256,1024]{2,1,0:T(8,128)(2,1)}), bf16[4,256,1024]{2,1,0:T(8,128)(2,1)}, u32[]{:S(2)}, u32[]{:S(2)}) %all-to-all-start.6) | async-done | bytes 2097184 | tf_op jit(solution)/shard_map/all_to_all | solution.py:60
  505.6 23.3 %shard_map.222 = bf16[256,1536]{1,0:T(8,128)(2,1)} custom-call(s32[1]{0:T(128)} %bitcast.block_ref, bf16[256,1536]{1,0:T(8,128)(2,1)} %copy.277.query_ref, bf16[1024,1024]{1,0:T(8,128)(2,1)} %bitcast.48.key_ref.value_ref, bf16[1024,1024]{1,0:T(8,128)(2,1)} %bitcast.48.key_ref.value_ref), custom_call_target="tpu_custom_call" | custom-call | flops 6442450944 | bytes 3670016 | tf_op jit(solution)/shard_map/pallas_call | solution.py:356
  534.4 39.6 %all_to_all.75 = bf16[4,256,1536]{2,1,0:T(8,128)(2,1)} all-to-all(bf16[4,256,1536]{2,1,0:T(8,128)(2,1)S(1)} %broadcast_in_dim.45), channel_id=1, replica_groups=mesh['dp'=8,'expert'=4] {'expert'}, dimensions={0} | all-to-all | bytes 6291456 | tf_op jit(solution)/shard_map/all_to_all | solution.py:60
  585.6 28.4 %shard_map.223 = (bf16[1024,2560]{1,0:T(8,128)(2,1)}, bf16[1024,2560]{1,0:T(8,128)(2,1)}, bf16[1024,2560]{1,0:T(8,128)(2,1)}) custom-call(bf16[1024,1536]{1,0:T(8,128)(2,1)} %bitcast.432, bf16[1536,2560]{1,0:T(8,128)(2,1)} %all-gather.16.cloned.1.call-done.gate_ref, bf16[1536,2560]{1,0:T(8,128)(2,1)} %all-gather.18.cloned.1.call-done.up_ref, ...), custom_call_target="tpu_custom_call" | custom-call | flops 16106127360 | bytes 31457280 | tf_op jit(solution)/shard_map/pallas_call | solution.py:193
  615.2 13.5 %fusion = bf16[1536,2560]{1,0:T(8,128)(2,1)} fusion(bf16[1024,2560]{1,0:T(8,128)(2,1)} %get-tuple-element.80, bf16[1024,1536]{1,0:T(8,128)(2,1)} %bitcast.49.grad_ref), kind=kOutput, calls=%fused_computation.7 | convolution fusion | flops 8056995840 | bytes 16252928 | tf_op jit(solution)/shard_map/dot_general | solution.py:156
  629.3 41.6 %shard_map.224 = (bf16[1024,2560]{1,0:T(8,128)(2,1)}, bf16[1024,2560]{1,0:T(8,128)(2,1)}, bf16[1024,1664]{1,0:T(8,128)(2,1)}) custom-call(s32[2]{0:T(128)} %pad_add_fusion.group_ref, bf16[1024,1536]{1,0:T(8,128)(2,1)} %bitcast.49.grad_ref, bf16[1536,2560]{1,0:T(8,128)(2,1)} %all-gather.20.cloned.1.call-done.down_ref, ...), custom_call_target="tpu_custom_call" | custom-call | flops 24159191040 | bytes 44564480 | tf_op jit(solution)/shard_map/pallas_call | solution.py:279
  675.8 13.5 %convolution_convert_fusion.3 = bf16[1536,2560]{1,0:T(8,128)(2,1)} fusion(bf16[1024,1536]{1,0:T(8,128)(2,1)} %bitcast.433, bf16[1024,2560]{1,0:T(8,128)(2,1)} %get-tuple-element.87), kind=kOutput, calls=%fused_computation.4 | convolution fusion | flops 8056995840 | bytes 16252928 | tf_op jit(solution)/shard_map/dot_general | solution.py:156
  689.3 13.6 %convolution_convert_fusion.6 = bf16[1024,1536]{1,0:T(8,128)(2,1)} fusion(bf16[1024,2560]{1,0:T(8,128)(2,1)} %get-tuple-element.80, bf16[1536,2560]{1,0:T(8,128)(2,1)} %all-gather.20.cloned.1.call-done.down_ref), kind=kOutput, calls=%fused_computation.32 | convolution fusion | flops 8054636544 | bytes 16252928 | tf_op jit(solution)/shard_map/dot_general | solution.py:156
  702.9 12.7 %convolution_convert_fusion.4 = bf16[1536,2560]{1,0:T(8,128)(2,1)} fusion(bf16[1024,1536]{1,0:T(8,128)(2,1)S(1)} %bitcast.434, bf16[1024,2560]{1,0:T(8,128)(2,1)} %get-tuple-element.86), kind=kOutput, calls=%fused_computation.5 | convolution fusion | flops 8056995840 | bytes 16252928 | tf_op jit(solution)/shard_map/dot_general | solution.py:156
  739.9 31.1 %shard_map.225 = (f32[256,1536]{1,0:T(8,128)}, bf16[1024,1024]{1,0:T(8,128)(2,1)}) custom-call(s32[1]{0:T(128)} %bitcast.block_ref, bf16[256,1536]{1,0:T(8,128)(2,1)} %copy.277.query_ref, bf16[256,1536]{1,0:T(8,128)(2,1)} %fusion.36.grad_ref, bf16[1024,1024]{1,0:T(8,128)(2,1)} %bitcast.48.key_ref.value_ref, bf16[1024,1024]{1,0:T(8,128)(2,1)} %bitcast.48.key_ref.value_ref), custom_call_target="tpu_custom_call" | custom-call | flops 16106127360 | bytes 7340032 | tf_op jit(solution)/shard_map/pallas_call | solution.py:403
  844.6 21.5 %all-to-all-done.12 = bf16[4,256,1536]{2,1,0:T(8,128)(2,1)} async-done(((bf16[4,256,1536]{2,1,0:T(8,128)(2,1)}), bf16[4,256,1536]{2,1,0:T(8,128)(2,1)}, u32[]{:S(2)}, u32[]{:S(2)}) %all-to-all-start.12) | async-done | bytes 3145760 | tf_op jit(solution)/shard_map/all_to_all | solution.py:60
  866.1 13.7 %convolution_convert_fusion.2 = bf16[1536,2560]{1,0:T(8,128)(2,1)} fusion(bf16[1024,1536]{1,0:T(8,128)(2,1)} %bitcast.74.grad_ref, bf16[1024,2560]{1,0:T(8,128)(2,1)} %get-tuple-element.78), kind=kOutput, calls=%fused_computation.3 | convolution fusion | flops 8056995840 | bytes 16252928 | tf_op jit(solution)/shard_map/dot_general | solution.py:156
  887.2 40.9 %shard_map.226 = (bf16[1024,2560]{1,0:T(8,128)(2,1)}, bf16[1024,2560]{1,0:T(8,128)(2,1)}, bf16[1024,1664]{1,0:T(8,128)(2,1)}) custom-call(s32[2]{0:T(128)} %pad_add_fusion.group_ref, bf16[1024,1536]{1,0:T(8,128)(2,1)} %bitcast.74.grad_ref, bf16[1536,2560]{1,0:T(8,128)(2,1)} %all-gather.14.cloned.1.call-done.down_ref, ...), custom_call_target="tpu_custom_call" | custom-call | flops 24159191040 | bytes 44564480 | tf_op jit(solution)/shard_map/pallas_call | solution.py:279
  931.9 14.0 %convolution_convert_fusion = bf16[1536,2560]{1,0:T(8,128)(2,1)} fusion(bf16[1024,1536]{1,0:T(8,128)(2,1)} %bitcast.23.rows_ref, bf16[1024,2560]{1,0:T(8,128)(2,1)} %get-tuple-element.105), kind=kOutput, calls=%fused_computation.1 | convolution fusion | flops 8056995840 | bytes 16252928 | tf_op jit(solution)/shard_map/dot_general | solution.py:156
  945.9 13.6 %convolution_convert_fusion.1 = bf16[1536,2560]{1,0:T(8,128)(2,1)} fusion(bf16[1024,1536]{1,0:T(8,128)(2,1)} %bitcast.23.rows_ref, bf16[1024,2560]{1,0:T(8,128)(2,1)} %get-tuple-element.104), kind=kOutput, calls=%fused_computation.2 | convolution fusion | flops 8056995840 | bytes 16252928 | tf_op jit(solution)/shard_map/dot_general | solution.py:156
  1005.2 31.4 %shard_map.227 = (f32[256,1536]{1,0:T(8,128)}, bf16[1024,1024]{1,0:T(8,128)(2,1)}) custom-call(s32[1]{0:T(128)} %bitcast.block_ref, bf16[256,1536]{1,0:T(8,128)(2,1)} %copy.248.query_ref, bf16[256,1536]{1,0:T(8,128)(2,1)} %fusion.33.grad_ref, bf16[1024,1024]{1,0:T(8,128)(2,1)} %bitcast.14.key_ref.value_ref, bf16[1024,1024]{1,0:T(8,128)(2,1)} %bitcast.14.key_ref.value_ref), custom_call_target="tpu_custom_call" | custom-call | flops 16106127360 | bytes 7340032 | tf_op jit(solution)/shard_map/pallas_call | solution.py:403
  1059.9 24.0 %collective-permute-done.18 = bf16[48,4224]{1,0:T(8,128)(2,1)} collective-permute-done((bf16[48,4224]{1,0:T(8,128)(2,1)S(1)}, bf16[48,4224]{1,0:T(8,128)(2,1)}, u32[]{:S(2)}, u32[]{:S(2)}) %collective-permute-start.18) | collective-permute-done | bytes 405536 | tf_op jit(solution)/shard_map/ppermute | solution.py:130
  1111.2 18.4 %collective-permute-done.22 = bf16[384,1536]{1,0:T(8,128)(2,1)} collective-permute-done((bf16[384,1536]{1,0:T(8,128)(2,1)}, bf16[384,1536]{1,0:T(8,128)(2,1)}, u32[]{:S(2)}, u32[]{:S(2)}) %collective-permute-start.22) | collective-permute-done | bytes 1179680 | tf_op jit(solution)/shard_map/ppermute | solution.py:130
  1149.3 8.2 collective-permute-done.27
  1161.8 22.3 %collective-permute-done.28 = bf16[96,2688]{1,0:T(8,128)(2,1)S(1)} collective-permute-done((bf16[96,2688]{1,0:T(8,128)(2,1)S(1)}, bf16[96,2688]{1,0:T(8,128)(2,1)S(1)}, u32[]{:S(2)}, u32[]{:S(2)}) %collective-permute-start.28) | collective-permute-done | bytes 516128 | tf_op jit(solution)/shard_map/ppermute | solution.py:130
  1184.5 13.2 %collective-permute-done.29 = bf16[48,2688]{1,0:T(8,128)(2,1)S(1)} collective-permute-done((bf16[48,2688]{1,0:T(8,128)(2,1)S(1)}, bf16[48,2688]{1,0:T(8,128)(2,1)S(1)}, u32[]{:S(2)}, u32[]{:S(2)}) %collective-permute-start.29) | collective-permute-done | bytes 258080 | tf_op jit(solution)/shard_map/ppermute | solution.py:130
  (525 shorter events, 397.5 us)
Async XLA Ops:
  7.2 108.2 %all-gather.8.cloned.1.call-start = ((), (), s32[]{:S(2)}) async-start(), calls=%async_computation.21 | async-start | bytes 13381632 | tf_op jit(solution)/shard_map/all_gather | solution.py:529
  15.4 313.9 %all-gather.10.cloned.1.call-start = ((), (), s32[]{:S(2)}) async-start(), calls=%async_computation.22 | async-start | bytes 8847360 | tf_op jit(solution)/shard_map/all_gather | solution.py:534
  19.5 309.8 %all-gather.12.cloned.1.call-start = ((), (), s32[]{:S(2)}) async-start(), calls=%async_computation.23 | async-start | bytes 8847360 | tf_op jit(solution)/shard_map/all_gather | solution.py:534
  25.4 375.7 %all-gather.14.cloned.1.call-start = ((), (), s32[]{:S(2)}) async-start(), calls=%async_computation.24 | async-start | bytes 8847360 | tf_op jit(solution)/shard_map/all_gather | solution.py:534
  31.4 554.2 %all-gather.16.cloned.1.call-start = ((), (), s32[]{:S(2)}) async-start(), calls=%async_computation.25 | async-start | bytes 8847360 | tf_op jit(solution)/shard_map/all_gather | solution.py:534
  188.0 40.7 %all-to-all-start.1 = ((bf16[4,256,1536]{2,1,0:T(8,128)(2,1)}), bf16[4,256,1536]{2,1,0:T(8,128)(2,1)}, u32[]{:S(2)}, u32[]{:S(2)}) async-start(bf16[4,256,1536]{2,1,0:T(8,128)(2,1)} %broadcast_in_dim.37), calls=%async_computation.1 | async-start | bytes 6291456 | tf_op jit(solution)/shard_map/all_to_all | solution.py:60
  192.7 392.9 %all-gather.18.cloned.1.call-start = ((), (), s32[]{:S(2)}) async-start(), calls=%async_computation.26 | async-start | bytes 8847360 | tf_op jit(solution)/shard_map/all_gather | solution.py:534
  230.9 73.9 %all-to-all-start.2 = ((bf16[4,48,4224]{2,1,0:T(8,128)(2,1)}), bf16[4,48,4224]{2,1,0:T(8,128)(2,1)}, u32[]{:S(2)}, u32[]{:S(2)}) async-start(bf16[4,48,4224]{2,1,0:T(8,128)(2,1)} %broadcast_in_dim.38), calls=%async_computation.2 | async-start | bytes 3244032 | tf_op jit(solution)/shard_map/all_to_all | solution.py:85
  318.9 76.2 %all-to-all-start.4 = ((bf16[4,4,48,4224]{3,2,1,0:T(8,128)(2,1)}), bf16[4,4,48,4224]{3,2,1,0:T(8,128)(2,1)}, u32[]{:S(2)}, u32[]{:S(2)}) async-start(bf16[4,4,48,4224]{3,2,1,0:T(8,128)(2,1)} %broadcast_in_dim.42), calls=%async_computation.4 | async-start | bytes 12976128 | tf_op jit(solution)/shard_map/all_to_all | solution.py:60
  401.1 58.2 %collective-permute-start = (bf16[4,4,48,4224]{3,2,0,1:T(8,128)(2,1)}, bf16[4,4,48,4224]{3,2,0,1:T(8,128)(2,1)}, u32[]{:S(2)}, u32[]{:S(2)}) collective-permute-start(bf16[4,4,48,4224]{3,2,0,1:T(8,128)(2,1)} %copy.259), channel_id=1, source_target_pairs={{0,4},{4,0},{8,12},{12,8},{16,20},{20,16},{24,28},{28,24},{1,5},{5... | collective-permute-start | bytes 19464200 | tf_op jit(solution)/shard_map/ppermute | solution.py:81
  414.6 41.8 %all-to-all-start.5 = ((bf16[4,256,1536]{2,1,0:T(8,128)(2,1)}), bf16[4,256,1536]{2,1,0:T(8,128)(2,1)}, u32[]{:S(2)}, u32[]{:S(2)}) async-start(bf16[4,256,1536]{2,1,0:T(8,128)(2,1)} %bitcast.436), calls=%async_computation.5 | async-start | bytes 6291456 | tf_op jit(solution)/shard_map/all_to_all | solution.py:60
  419.3 210.0 %all-gather.20.cloned.1.call-start = ((), (), s32[]{:S(2)}) async-start(), calls=%async_computation.27 | async-start | bytes 8847360 | tf_op jit(solution)/shard_map/all_gather | solution.py:534
  575.9 39.2 %all-to-all-start.7 = ((bf16[4,256,1536]{2,1,0:T(8,128)(2,1)}), bf16[4,256,1536]{2,1,0:T(8,128)(2,1)}, u32[]{:S(2)}, u32[]{:S(2)}) async-start(bf16[4,256,1536]{2,1,0:T(8,128)(2,1)} %broadcast_in_dim.44), calls=%async_computation.7 | async-start | bytes 6291456 | tf_op jit(solution)/shard_map/all_to_all | solution.py:60
  580.6 525.9 %reduce-scatter.7.cloned.1.call-start = ((), (), s32[]{:S(2)}) async-start(), calls=%async_computation.28 | async-start | bytes 8847360 | tf_op jit(solution)/shard_map/reduce_scatter | solution.py:683
  670.9 44.8 %all-to-all-start.9 = ((bf16[4,256,1664]{2,1,0:T(8,128)(2,1)}), bf16[4,256,1664]{2,1,0:T(8,128)(2,1)}, u32[]{:S(2)}, u32[]{:S(2)}) async-start(bf16[4,256,1664]{2,1,0:T(8,128)(2,1)} %bitcast.424), calls=%async_computation.9 | async-start | bytes 6815744 | tf_op jit(solution)/shard_map/all_to_all | solution.py:60
  675.6 431.0 %reduce-scatter.11.cloned.1.call-start = ((), (), s32[]{:S(2)}) async-start(), calls=%async_computation.30 | async-start | bytes 8847360 | tf_op jit(solution)/shard_map/reduce_scatter | solution.py:711
  719.5 387.1 %reduce-scatter.9.cloned.1.call-start = ((), (), s32[]{:S(2)}) async-start(), calls=%async_computation.29 | async-start | bytes 8847360 | tf_op jit(solution)/shard_map/reduce_scatter | solution.py:710
  720.9 68.6 %collective-permute-start.2 = (bf16[256,1536]{1,0:T(8,128)(2,1)}, bf16[256,1536]{1,0:T(8,128)(2,1)}, u32[]{:S(2)}, u32[]{:S(2)}) collective-permute-start(bf16[256,1536]{1,0:T(8,128)(2,1)} %shard_map.222), channel_id=1, source_target_pairs={{0,4},{4,0},{8,12},{12,8},{16,20},{20,16},{24,28},{28,24},{1,5},{5... | collective-permute-start | bytes 2359304 | tf_op jit(solution)/shard_map/ppermute | solution.py:81
  722.8 48.3 %all-to-all-start.10 = ((bf16[4,256,1536]{2,1,0:T(8,128)(2,1)}), bf16[4,256,1536]{2,1,0:T(8,128)(2,1)}, u32[]{:S(2)}, u32[]{:S(2)}) async-start(bf16[4,256,1536]{2,1,0:T(8,128)(2,1)} %bitcast.435), calls=%async_computation.10 | async-start | bytes 6291456 | tf_op jit(solution)/shard_map/all_to_all | solution.py:60
  794.1 40.7 %collective-permute-start.3 = (bf16[384,1536]{1,0:T(8,128)(2,1)}, bf16[384,1536]{1,0:T(8,128)(2,1)}, u32[]{:S(2)}, u32[]{:S(2)}) collective-permute-start(bf16[384,1536]{1,0:T(8,128)(2,1)} %bitcast.82), channel_id=1, source_target_pairs={{0,1},{1,0},{2,3},{3,2},{4,5},{5,4},{6,7},{7,6},{8,9},{9,8},{10,11... | collective-permute-start | bytes 3538952 | tf_op jit(solution)/shard_map/ppermute | solution.py:130
  825.4 40.7 %all-to-all-start.12 = ((bf16[4,256,1536]{2,1,0:T(8,128)(2,1)}), bf16[4,256,1536]{2,1,0:T(8,128)(2,1)}, u32[]{:S(2)}, u32[]{:S(2)}) async-start(bf16[4,256,1536]{2,1,0:T(8,128)(2,1)} %broadcast_in_dim.48), calls=%async_computation.12 | async-start | bytes 6291456 | tf_op jit(solution)/shard_map/all_to_all | solution.py:60
  830.3 371.0 %reduce-scatter.17.cloned.1.call-start = ((), (), s32[]{:S(2)}) async-start(), calls=%async_computation.33 | async-start | bytes 8847360 | tf_op jit(solution)/shard_map/reduce_scatter | solution.py:683
  881.3 80.5 %collective-permute-start.10 = (bf16[384,1152]{1,0:T(8,128)(2,1)}, bf16[384,1152]{1,0:T(8,128)(2,1)}, u32[]{:S(2)}, u32[]{:S(2)}) collective-permute-start(bf16[384,1152]{1,0:T(8,128)(2,1)} %bitcast.104), channel_id=1, source_target_pairs={{0,1},{1,0},{2,3},{3,2},{4,5},{5,4},{6,7},{7,6},{8,9},{9,8},{10,11... | collective-permute-start | bytes 2654216 | tf_op jit(solution)/shard_map/ppermute | solution.py:130
  884.3 79.9 %collective-permute-start.9 = (bf16[384,1536]{1,0:T(8,128)(2,1)}, bf16[384,1536]{1,0:T(8,128)(2,1)}, u32[]{:S(2)}, u32[]{:S(2)}) collective-permute-start(bf16[384,1536]{1,0:T(8,128)(2,1)} %bitcast.101), channel_id=1, source_target_pairs={{0,1},{1,0},{2,3},{3,2},{4,5},{5,4},{6,7},{7,6},{8,9},{9,8},{10,11... | collective-permute-start | bytes 3538952 | tf_op jit(solution)/shard_map/ppermute | solution.py:130
  886.1 73.4 %collective-permute-start.8 = (bf16[192,1536]{1,0:T(8,128)(2,1)}, bf16[192,1536]{1,0:T(8,128)(2,1)}, u32[]{:S(2)}, u32[]{:S(2)}) collective-permute-start(bf16[192,1536]{1,0:T(8,128)(2,1)} %dynamic-slice_bitcast_fusion.4), channel_id=1, source_target_pairs={{0,2},{1,3},{2,0},{3,1},{4,6},{5,7},{6,4},{7,5},{8,10},{9,11},{10,... | collective-permute-start | bytes 1769480 | tf_op jit(solution)/shard_map/ppermute | solution.py:130
  928.2 41.1 %all-to-all-start.13 = ((bf16[4,256,1664]{2,1,0:T(8,128)(2,1)}), bf16[4,256,1664]{2,1,0:T(8,128)(2,1)S(1)}, u32[]{:S(2)}, u32[]{:S(2)}) async-start(bf16[4,256,1664]{2,1,0:T(8,128)(2,1)} %bitcast.423), calls=%async_computation.13 | async-start | bytes 6815744 | tf_op jit(solution)/shard_map/all_to_all | solution.py:60
  931.9 273.4 %reduce-scatter.15.cloned.1.call-start = ((), (), s32[]{:S(2)}) async-start(), calls=%async_computation.32 | async-start | bytes 8847360 | tf_op jit(solution)/shard_map/reduce_scatter | solution.py:711
  970.9 238.4 %reduce-scatter.13.cloned.1.call-start = ((), (), s32[]{:S(2)}) async-start(), calls=%async_computation.31 | async-start | bytes 8847360 | tf_op jit(solution)/shard_map/reduce_scatter | solution.py:710
  973.9 113.6 %collective-permute-start.16 = (bf16[256,768]{0,1:T(8,128)(2,1)}, bf16[256,768]{0,1:T(8,128)(2,1)}, u32[]{:S(2)}, u32[]{:S(2)}) collective-permute-start(bf16[256,768]{0,1:T(8,128)(2,1)} %get-tuple-element.253), channel_id=1, source_target_pairs={{0,4},{4,0},{8,12},{12,8},{16,20},{20,16},{24,28},{28,24},{1,5},{5... | collective-permute-start | bytes 1179656 | tf_op jit(solution)/shard_map/ppermute | solution.py:81
  1000.3 40.2 %collective-permute-start.14 = (bf16[384,1536]{1,0:T(8,128)(2,1)}, bf16[384,1536]{1,0:T(8,128)(2,1)}, u32[]{:S(2)}, u32[]{:S(2)}) collective-permute-start(bf16[384,1536]{1,0:T(8,128)(2,1)} %bitcast.116), channel_id=1, source_target_pairs={{0,1},{1,0},{2,3},{3,2},{4,5},{5,4},{6,7},{7,6},{8,9},{9,8},{10,11... | collective-permute-start | bytes 3538952 | tf_op jit(solution)/shard_map/ppermute | solution.py:130
  1036.6 49.5 %all-to-all-start.14 = ((bf16[4,256,1024]{2,1,0:T(8,128)(2,1)}), bf16[4,256,1024]{2,1,0:T(8,128)(2,1)S(1)}, u32[]{:S(2)}, u32[]{:S(2)}) async-start(bf16[4,256,1024]{2,1,0:T(8,128)(2,1)} %bitcast.453), calls=%async_computation.14 | async-start | bytes 4194304 | tf_op jit(solution)/shard_map/all_to_all | solution.py:60
  1086.1 73.4 %collective-permute-start.20 = (bf16[96,1536]{1,0:T(8,128)(2,1)}, bf16[96,1536]{1,0:T(8,128)(2,1)}, u32[]{:S(2)}, u32[]{:S(2)}) collective-permute-start(bf16[96,1536]{1,0:T(8,128)(2,1)} %bitcast.142), channel_id=1, source_target_pairs={{0,8},{4,12},{8,0},{12,4},{16,24},{20,28},{24,16},{28,20},{1,9},{5... | collective-permute-start | bytes 884744 | tf_op jit(solution)/shard_map/ppermute | solution.py:130
  (108 other events, 1719.4 us)
Sparse Core Ops, SparseCore 0:
  15.5 99.8 all-gather.7
  117.6 76.2 all-gather.9
  195.5 109.3 all-gather.11
  306.5 76.7 all-gather.13
  384.7 76.2 all-gather.15
  462.5 76.2 all-gather.17
  541.0 76.2 all-gather.19
  628.8 81.9 reduce-scatter.6
  719.6 83.1 reduce-scatter.10
  805.0 83.0 reduce-scatter.8
  890.3 83.0 reduce-scatter.16
  975.6 109.0 reduce-scatter.14
  1087.0 95.0 reduce-scatter.12

commit v8 on v7

--- a/solution.py
+++ b/solution.py
@@ -182,10 +182,11 @@
     act_out[...] = (gate_val * jax.nn.sigmoid(gate_val) * up_val * share).astype(jnp.bfloat16)
 
 
-def expert_forward(rows, gate, up, share):
+def expert_forward(rows, gate_up, share):
     row_total, width = rows.shape
     experts = share.shape[1]
-    hidden = gate.shape[1] // experts
+    hidden_total = gate_up.shape[1] // 2
+    hidden = hidden_total // experts
     tile = row_total // 2
     row_block = pl.BlockSpec((tile, width), lambda e, r: (r, 0))
     weight_block = pl.BlockSpec((width, hidden), lambda e, r: (0, e))
@@ -196,17 +197,17 @@
         in_specs=[
             row_block,
             weight_block,
-            weight_block,
+            pl.BlockSpec((width, hidden), lambda e, r: (0, experts + e)),
             pl.BlockSpec((tile, experts), lambda e, r: (r, 0)),
         ],
         out_specs=[hidden_block] * 3,
-        out_shape=[jax.ShapeDtypeStruct((row_total, gate.shape[1]), jnp.bfloat16)] * 3,
+        out_shape=[jax.ShapeDtypeStruct((row_total, hidden_total), jnp.bfloat16)] * 3,
         cost_estimate=pl.CostEstimate(
-            flops=4 * row_total * width * gate.shape[1],
-            transcendentals=row_total * gate.shape[1],
-            bytes_accessed=4 * width * gate.shape[1] + 6 * row_total * gate.shape[1],
+            flops=4 * row_total * width * hidden_total,
+            transcendentals=row_total * hidden_total,
+            bytes_accessed=4 * width * hidden_total + 6 * row_total * hidden_total,
         ),
-    )(rows, gate, up, share)
+    )(rows, gate_up, gate_up, share)
 
 
 def expert_backward_kernel(
@@ -267,15 +268,16 @@
         rows_out[:, width:] = sums_acc[window, :].astype(jnp.bfloat16)
 
 
-def expert_backward(group, grad, down, gate, up, gate_val, up_val, share, extra):
+def expert_backward(group, grad, down, gate_up, gate_val, up_val, share, extra):
     row_total, width = grad.shape
     experts = share.shape[1]
-    hidden = gate.shape[1] // experts
+    hidden_total = gate_up.shape[1] // 2
+    hidden = hidden_total // experts
     tile = row_total // 2
     row_block = pl.BlockSpec((tile, width), lambda e, r, g: (r, 0))
     weight_block = pl.BlockSpec((width, hidden), lambda e, r, g: (0, e))
     hidden_block = pl.BlockSpec((tile, hidden), lambda e, r, g: (r, e))
-    hidden_shape = jax.ShapeDtypeStruct((row_total, gate.shape[1]), jnp.bfloat16)
+    hidden_shape = jax.ShapeDtypeStruct((row_total, hidden_total), jnp.bfloat16)
     return pl.pallas_call(
         expert_backward_kernel,
         grid_spec=pltpu.PrefetchScalarGridSpec(
@@ -285,7 +287,7 @@
                 row_block,
                 weight_block,
                 weight_block,
-                weight_block,
+                pl.BlockSpec((width, hidden), lambda e, r, g: (0, experts + e)),
                 hidden_block,
                 hidden_block,
                 pl.BlockSpec((tile, experts), lambda e, r, g: (r, 0)),
@@ -309,11 +311,11 @@
             jax.ShapeDtypeStruct((row_total, width + extra), jnp.bfloat16),
         ],
         cost_estimate=pl.CostEstimate(
-            flops=6 * row_total * width * gate.shape[1],
-            transcendentals=row_total * gate.shape[1],
-            bytes_accessed=6 * width * gate.shape[1] + 8 * row_total * gate.shape[1],
+            flops=6 * row_total * width * hidden_total,
+            transcendentals=row_total * hidden_total,
+            bytes_accessed=6 * width * hidden_total + 8 * row_total * hidden_total,
         ),
-    )(group, grad, down, gate, up, gate_val, up_val, share)
+    )(group, grad, down, gate_up, gate_up, gate_val, up_val, share)
 
 
 def attention_probs(block_ref, query, key):
@@ -527,16 +529,20 @@
         for layer in range(LAYER_COUNT)
     ]
     packed = [lax.all_gather(shards[0], ("dp", "expert"), axis=0, tiled=True)]
+    chip_rows = [None] + [gather_chips(shard) for shard in shards[1:]]
+    inputs, chip_rows = lax.optimization_barrier((inputs, chip_rows))
     ff_width = gate_weight.shape[3]
     hidden_width = exp_dev * ff_width
+    def gather_weights(*weights):
+        rows = [weight.reshape(weight.shape[0], hidden_width) for weight in weights]
+        return lax.all_gather(jnp.concatenate(rows, axis=1), "dp", axis=0, tiled=True)
+
     gathered = [
-        tuple(
-            lax.all_gather(rows.reshape(-1, hidden_width), "dp", axis=0, tiled=True)
-            for rows in (
-                gate_weight[layer].transpose(1, 0, 2),
-                up_weight[layer].transpose(1, 0, 2),
-                down_weight[layer].transpose(2, 0, 1),
-            )
+        (
+            gather_weights(
+                gate_weight[layer].transpose(1, 0, 2), up_weight[layer].transpose(1, 0, 2)
+            ),
+            gather_weights(down_weight[layer].transpose(2, 0, 1)),
         )
         for layer in range(LAYER_COUNT)
     ]
@@ -557,7 +563,7 @@
         router_full = full[:, edges[3] : edges[4]]
         gain_one = full[:, edges[4]].astype(jnp.float32)
         gain_two = full[:, edges[5]].astype(jnp.float32)
-        gate_full, up_full, down_full = gathered[layer]
+        gate_up_full, down_full = gathered[layer]
         first_normalized, inv_one = norm_forward(hidden, gain_one)
         first_normalized = first_normalized.astype(jnp.bfloat16)
         linear = jnp.dot(first_normalized, qkv_full, preferred_element_type=jnp.float32)
@@ -581,24 +587,19 @@
         )
         key_value_all = gather_rows(key_value)
         ahead = layer + 1 < LAYER_COUNT
-        if ahead:
-            key_value_all, next_shard = lax.optimization_barrier(
-                (key_value_all, shards[layer + 1])
-            )
-            next_rows = gather_chips(next_shard)
         attended = attention_forward(block_at, query_rotated, key_value_all)
         middle = hidden + dot_f32(attended, output_full, (1,), (1,))
         normed_two, inv_two = norm_forward(middle, gain_two)
         normed_two = normed_two.astype(jnp.bfloat16)
         arrived = gather_rows(normed_two)
         if ahead:
-            arrived, next_rows = lax.optimization_barrier((arrived, next_rows))
+            arrived, next_rows = lax.optimization_barrier((arrived, chip_rows[layer + 1]))
             next_rows = gather_groups(next_rows)
         share_all = shares_of(arrived, router_full, chosen_all[:, layer] > 0)
         share_own = shares_of(normed_two, router_full, chosen_hot[layer])
         share_local = lax.dynamic_slice_in_dim(share_all, my_group * exp_dev, exp_dev, axis=1)
         gate_low, up_low, scaled_act = expert_forward(
-            arrived, gate_full, up_full, share_local
+            arrived, gate_up_full, share_local
         )
         if ahead:
             scaled_act, next_rows = lax.optimization_barrier((scaled_act, next_rows))
@@ -624,8 +625,7 @@
             gain_one,
             gain_two,
             router_full,
-            gate_full,
-            up_full,
+            gate_up_full,
             down_full,
         )
         return kept_state
@@ -667,8 +667,7 @@
             gain_one,
             gain_two,
             router_full,
-            gate_full,
-            up_full,
+            gate_up_full,
             down_full,
         ) = kept_states[layer]
         grad_all = gather_rows(grad_hidden.astype(jnp.bfloat16))
@@ -685,8 +684,7 @@
             group_at,
             grad_all,
             down_full,
-            gate_full,
-            up_full,
+            gate_up_full,
             gate_low,
             up_low,
             share_local,
@@ -808,8 +806,18 @@
                 ],
                 axis=1,
             )
+            late_part = halve_all(late_part, chip_steps[:1])
+            expert_held = [
+                place(part, held, layer, exp_dev)
+                for part, held in zip(expert_parts[:2], expert_held[:2])
+            ] + expert_held[2:]
+            late_part, expert_held = lax.optimization_barrier((late_part, expert_held))
             attention_list[layer] = jnp.concatenate(
-                [halve_all(grad_output_w, chip_steps), halve_all(late_part, chip_steps)], axis=1
+                [
+                    halve_all(grad_output_w, chip_steps),
+                    halve_all(late_part, chip_steps[1:]),
+                ],
+                axis=1,
             )
         last_parts = expert_parts
         grad_hidden = grad_middle + grad_norm_in
@@ -819,9 +827,7 @@
     output_grads, query_grads, key_grads, value_grads, router_grads, one, two = (
         stacked[:, :, start:stop] for start, stop in zip(cuts[:-1], cuts[1:])
     )
-    expert_held = [
-        place(part, held, 0, exp_dev) for part, held in zip(last_parts, expert_held)
-    ]
+    expert_held[2] = place(last_parts[2], expert_held[2], 0, exp_dev)
     down_grads, gate_grads, up_grads = expert_held
     return (
         output.astype(jnp.bfloat16).reshape(sequences_per_device, block_length, model_width),

time: 1230 us -> 1180 us (0.959)
  waiting for transfers between devices: 414 us -> 365 us
    all_gather x1, waiting for transfers between devices: 80.8 us -> 38.4 us  [body(): packed = [lax.all_gather(shards[0], ('dp', 'expert'), axis=0, tiled=True)]]
    all_gather x6 -> x4, waiting for transfers between devices: 0.01 us -> 17 us  [gather_weights(): lax.all_gather(jnp.concatenate(rows, axis=1), 'dp', axis=0, tiled=True)]
    all_to_all x1, waiting for transfers between devices: 68.6 us -> 54.5 us  [exchange_chips(): lax.all_to_all(blocks, 'dp', split_axis=0, concat_axis=0, axis_index_grou...]
  transfers between devices with their start and end apart: 57 -> 55, of which waited for: 19 -> 20; matrix products, arithmetic and copies ran while one was open for 30% -> 31% of each run, Pallas kernels for 22% -> 23%
where the time goes in v8:
time: 1180 us; the launch traced here: 1170 us
  waiting for transfers between devices  365 us (31%)
  Pallas kernels  273 us (23%)
  matrix products  186 us (16%)
  local copies, waits for them, and re-layouts  122 us (10%)
  starting transfers between devices  91.8 us (8%)
  other arithmetic  80.4 us (7%)
  blocking collectives  39.7 us (3%)
  between operations  16 us (1%)
    all_to_all x13, waiting for transfers between devices, exchange(): lax.all_to_all(blocks, 'expert', split_axis=0, concat_axis=0, tiled=True)  172 us
    dot_general x26, matrix products, dot_f32(): lax.dot_general(left, right, ((left_dims, right_dims), ((), ())), preferr...  169 us
    pallas_call x2, Pallas kernels, expert_backward(): pl.pallas_call(expert_backward_kernel, grid_spec=pltpu.PrefetchScalarGrid...  82.3 us
    ppermute x17, waiting for transfers between devices, halve(): lax.ppermute(theirs.reshape(-1, width), axis_name, [(i, i ^ step) for i i...  82.1 us
    pallas_call x2, Pallas kernels, attention_backward(): pl.pallas_call(attention_backward_kernel, grid_spec=pltpu.PrefetchScalarG...  62.8 us
    all_to_all x13, starting transfers between devices, exchange(): lax.all_to_all(blocks, 'expert', split_axis=0, concat_axis=0, tiled=True)  59.4 us
    pallas_call x2, Pallas kernels, expert_forward(): pl.pallas_call(expert_forward_kernel, grid=(experts, 2), in_specs=[row_bl...  56.8 us
    all_to_all x1, waiting for transfers between devices, exchange_chips(): lax.all_to_all(blocks, 'dp', split_axis=0, concat_axis=0, axis_index_grou...  54.5 us
  transfers between devices with their start and end apart: 55, of which 20 were waited for; matrix products, arithmetic and copies ran while one was open for 31% of the time, Pallas kernels for 23%

profile of v8, /device:TPU:0, one launch (start us, length us, event | category | flops | bytes accessed | tf_op | source)
XLA Modules:
  0.0 1174.0 jit_solution(11666543917926005735)
XLA Ops:
  38.7 6.5 all-to-all-start
  46.0 54.5 %all-to-all-done = bf16[4,48,4224]{2,1,0:T(8,128)(2,1)S(1)} async-done(((bf16[4,48,4224]{2,1,0:T(8,128)(2,1)}), bf16[4,48,4224]{2,1,0:T(8,128)(2,1)S(1)}, u32[]{:S(2)}, u32[]{:S(2)}) %all-to-all-start) | async-done | bytes 1622048 | tf_op jit(solution)/shard_map/all_to_all | solution.py:85
  100.8 38.4 %all-gather.6.cloned.1.call-done = bf16[1536,4224]{1,0:T(8,128)(2,1)} async-done(((bf16[48,4224]{1,0:T(8,128)(2,1)}), bf16[1536,4224]{1,0:T(8,128)(2,1)}) %all-gather.6.cloned.1.call-update) | async-done | bytes 12976144 | tf_op jit(solution)/shard_map/all_gather | solution.py:531
  161.8 19.5 %all-to-all-done.1 = bf16[4,256,1024]{2,1,0:T(8,128)(2,1)} async-done(((bf16[4,256,1024]{2,1,0:T(8,128)(2,1)}), bf16[4,256,1024]{2,1,0:T(8,128)(2,1)}, u32[]{:S(2)}, u32[]{:S(2)}) %all-to-all-start.1) | async-done | bytes 2097184 | tf_op jit(solution)/shard_map/all_to_all | solution.py:60
  181.3 23.3 %shard_map.220 = bf16[256,1536]{1,0:T(8,128)(2,1)} custom-call(s32[1]{0:T(128)} %bitcast.block_ref, bf16[256,1536]{1,0:T(8,128)(2,1)} %copy.248.query_ref, bf16[1024,1024]{1,0:T(8,128)(2,1)} %bitcast.22.key_ref.value_ref, bf16[1024,1024]{1,0:T(8,128)(2,1)} %bitcast.22.key_ref.value_ref), custom_call_target="tpu_custom_call" | custom-call | flops 6442450944 | bytes 3670016 | tf_op jit(solution)/shard_map/pallas_call | solution.py:358
  217.9 35.3 %all-to-all-done.2 = bf16[4,256,1536]{2,1,0:T(8,128)(2,1)} async-done(((bf16[4,256,1536]{2,1,0:T(8,128)(2,1)}), bf16[4,256,1536]{2,1,0:T(8,128)(2,1)}, u32[]{:S(2)}, u32[]{:S(2)}) %all-to-all-start.2) | async-done | bytes 3145760 | tf_op jit(solution)/shard_map/all_to_all | solution.py:60
  282.5 28.3 %shard_map.221 = (bf16[1024,2560]{1,0:T(8,128)(2,1)}, bf16[1024,2560]{1,0:T(8,128)(2,1)}, bf16[1024,2560]{1,0:T(8,128)(2,1)}) custom-call(bf16[1024,1536]{1,0:T(8,128)(2,1)} %bitcast.23.rows_ref, bf16[1536,5120]{1,0:T(8,128)(2,1)} %all-gather.8.cloned.1.call-done.gate_ref.up_ref, bf16[1536,5120]{1,0:T(8,128)(2,1)} %all-gather.8.cloned.1.call-done.gate_ref.up_ref, ...), custom_call_target="tpu_custom_call" | custom-call | flops 16106127360 | bytes 31457280 | tf_op jit(solution)/shard_map/pallas_call | solution.py:194
  310.8 32.0 %all-to-all-done.4 = bf16[4,4,48,4224]{3,2,1,0:T(8,128)(2,1)} async-done(((bf16[4,4,48,4224]{3,2,1,0:T(8,128)(2,1)}), bf16[4,4,48,4224]{3,2,1,0:T(8,128)(2,1)}, u32[]{:S(2)}, u32[]{:S(2)}) %all-to-all-start.4) | async-done | bytes 6488096 | tf_op jit(solution)/shard_map/all_to_all | solution.py:60
  348.9 11.2 all-gather.10.cloned.1.call-done.down_ref
  360.1 13.3 %convolution_convert_fusion.7 = bf16[1024,1536]{1,0:T(8,128)(2,1)} fusion(bf16[1024,2560]{1,0:T(8,128)(2,1)} %get-tuple-element.82, bf16[1536,2560]{1,0:T(8,128)(2,1)} %all-gather.10.cloned.1.call-done.down_ref), kind=kOutput, calls=%fused_computation.33 | convolution fusion | flops 8054636544 | bytes 16252928 | tf_op jit(solution)/shard_map/dot_general | solution.py:156
  381.2 33.8 %all-to-all-done.5 = bf16[4,256,1536]{2,1,0:T(8,128)(2,1)} async-done(((bf16[4,256,1536]{2,1,0:T(8,128)(2,1)}), bf16[4,256,1536]{2,1,0:T(8,128)(2,1)}, u32[]{:S(2)}, u32[]{:S(2)}) %all-to-all-start.5) | async-done | bytes 3145760 | tf_op jit(solution)/shard_map/all_to_all | solution.py:60
  444.6 18.6 %all-to-all-done.6 = bf16[4,256,1024]{2,1,0:T(8,128)(2,1)} async-done(((bf16[4,256,1024]{2,1,0:T(8,128)(2,1)}), bf16[4,256,1024]{2,1,0:T(8,128)(2,1)}, u32[]{:S(2)}, u32[]{:S(2)}) %all-to-all-start.6) | async-done | bytes 2097184 | tf_op jit(solution)/shard_map/all_to_all | solution.py:60
  463.3 23.3 %shard_map.222 = bf16[256,1536]{1,0:T(8,128)(2,1)} custom-call(s32[1]{0:T(128)} %bitcast.block_ref, bf16[256,1536]{1,0:T(8,128)(2,1)} %copy.277.query_ref, bf16[1024,1024]{1,0:T(8,128)(2,1)} %bitcast.48.key_ref.value_ref, bf16[1024,1024]{1,0:T(8,128)(2,1)} %bitcast.48.key_ref.value_ref), custom_call_target="tpu_custom_call" | custom-call | flops 6442450944 | bytes 3670016 | tf_op jit(solution)/shard_map/pallas_call | solution.py:358
  492.0 39.7 %all_to_all.75 = bf16[4,256,1536]{2,1,0:T(8,128)(2,1)} all-to-all(bf16[4,256,1536]{2,1,0:T(8,128)(2,1)S(1)} %broadcast_in_dim.45), channel_id=1, replica_groups=mesh['dp'=8,'expert'=4] {'expert'}, dimensions={0} | all-to-all | bytes 6291456 | tf_op jit(solution)/shard_map/all_to_all | solution.py:60
  543.5 28.5 %shard_map.223 = (bf16[1024,2560]{1,0:T(8,128)(2,1)}, bf16[1024,2560]{1,0:T(8,128)(2,1)}, bf16[1024,2560]{1,0:T(8,128)(2,1)}) custom-call(bf16[1024,1536]{1,0:T(8,128)(2,1)} %bitcast.432, bf16[1536,5120]{1,0:T(8,128)(2,1)} %all-gather.12.cloned.1.call-done.gate_ref.up_ref, bf16[1536,5120]{1,0:T(8,128)(2,1)} %all-gather.12.cloned.1.call-done.gate_ref.up_ref, ...), custom_call_target="tpu_custom_call" | custom-call | flops 16106127360 | bytes 31457280 | tf_op jit(solution)/shard_map/pallas_call | solution.py:194
  572.8 13.4 %fusion = bf16[1536,2560]{1,0:T(8,128)(2,1)} fusion(bf16[1024,2560]{1,0:T(8,128)(2,1)} %get-tuple-element.84, bf16[1024,1536]{1,0:T(8,128)(2,1)} %bitcast.49.grad_ref), kind=kOutput, calls=%fused_computation.7 | convolution fusion | flops 8056995840 | bytes 16252928 | tf_op jit(solution)/shard_map/dot_general | solution.py:156
  586.9 41.1 %shard_map.224 = (bf16[1024,2560]{1,0:T(8,128)(2,1)}, bf16[1024,2560]{1,0:T(8,128)(2,1)}, bf16[1024,1664]{1,0:T(8,128)(2,1)}) custom-call(s32[2]{0:T(128)} %pad_add_fusion.group_ref, bf16[1024,1536]{1,0:T(8,128)(2,1)} %bitcast.49.grad_ref, bf16[1536,2560]{1,0:T(8,128)(2,1)} %all-gather.14.cloned.1.call-done.down_ref, ...), custom_call_target="tpu_custom_call" | custom-call | flops 24159191040 | bytes 44564480 | tf_op jit(solution)/shard_map/pallas_call | solution.py:281
  632.9 13.5 %convolution_convert_fusion.3 = bf16[1536,2560]{1,0:T(8,128)(2,1)} fusion(bf16[1024,1536]{1,0:T(8,128)(2,1)} %bitcast.433, bf16[1024,2560]{1,0:T(8,128)(2,1)} %get-tuple-element.91), kind=kOutput, calls=%fused_computation.4 | convolution fusion | flops 8056995840 | bytes 16252928 | tf_op jit(solution)/shard_map/dot_general | solution.py:156
  646.4 13.6 %convolution_convert_fusion.6 = bf16[1024,1536]{1,0:T(8,128)(2,1)} fusion(bf16[1024,2560]{1,0:T(8,128)(2,1)} %get-tuple-element.84, bf16[1536,2560]{1,0:T(8,128)(2,1)} %all-gather.14.cloned.1.call-done.down_ref), kind=kOutput, calls=%fused_computation.32 | convolution fusion | flops 8054636544 | bytes 16252928 | tf_op jit(solution)/shard_map/dot_general | solution.py:156
  660.0 12.8 %convolution_convert_fusion.4 = bf16[1536,2560]{1,0:T(8,128)(2,1)} fusion(bf16[1024,1536]{1,0:T(8,128)(2,1)S(1)} %bitcast.434, bf16[1024,2560]{1,0:T(8,128)(2,1)} %get-tuple-element.90), kind=kOutput, calls=%fused_computation.5 | convolution fusion | flops 8056995840 | bytes 16252928 | tf_op jit(solution)/shard_map/dot_general | solution.py:156
  696.9 31.2 %shard_map.225 = (f32[256,1536]{1,0:T(8,128)}, bf16[1024,1024]{1,0:T(8,128)(2,1)}) custom-call(s32[1]{0:T(128)} %bitcast.block_ref, bf16[256,1536]{1,0:T(8,128)(2,1)} %copy.277.query_ref, bf16[256,1536]{1,0:T(8,128)(2,1)} %fusion.36.grad_ref, bf16[1024,1024]{1,0:T(8,128)(2,1)} %bitcast.48.key_ref.value_ref, bf16[1024,1024]{1,0:T(8,128)(2,1)} %bitcast.48.key_ref.value_ref), custom_call_target="tpu_custom_call" | custom-call | flops 16106127360 | bytes 7340032 | tf_op jit(solution)/shard_map/pallas_call | solution.py:405
  802.0 21.4 %all-to-all-done.12 = bf16[4,256,1536]{2,1,0:T(8,128)(2,1)} async-done(((bf16[4,256,1536]{2,1,0:T(8,128)(2,1)}), bf16[4,256,1536]{2,1,0:T(8,128)(2,1)}, u32[]{:S(2)}, u32[]{:S(2)}) %all-to-all-start.12) | async-done | bytes 3145760 | tf_op jit(solution)/shard_map/all_to_all | solution.py:60
  823.4 13.7 %convolution_convert_fusion.2 = bf16[1536,2560]{1,0:T(8,128)(2,1)} fusion(bf16[1024,1536]{1,0:T(8,128)(2,1)} %bitcast.74.grad_ref, bf16[1024,2560]{1,0:T(8,128)(2,1)} %get-tuple-element.82), kind=kOutput, calls=%fused_computation.3 | convolution fusion | flops 8056995840 | bytes 16252928 | tf_op jit(solution)/shard_map/dot_general | solution.py:156
  844.4 41.3 %shard_map.226 = (bf16[1024,2560]{1,0:T(8,128)(2,1)}, bf16[1024,2560]{1,0:T(8,128)(2,1)}, bf16[1024,1664]{1,0:T(8,128)(2,1)}) custom-call(s32[2]{0:T(128)} %pad_add_fusion.group_ref, bf16[1024,1536]{1,0:T(8,128)(2,1)} %bitcast.74.grad_ref, bf16[1536,2560]{1,0:T(8,128)(2,1)} %all-gather.10.cloned.1.call-done.down_ref, ...), custom_call_target="tpu_custom_call" | custom-call | flops 24159191040 | bytes 44564480 | tf_op jit(solution)/shard_map/pallas_call | solution.py:281
  889.5 13.8 %convolution_convert_fusion = bf16[1536,2560]{1,0:T(8,128)(2,1)} fusion(bf16[1024,1536]{1,0:T(8,128)(2,1)} %bitcast.23.rows_ref, bf16[1024,2560]{1,0:T(8,128)(2,1)} %get-tuple-element.109), kind=kOutput, calls=%fused_computation.1 | convolution fusion | flops 8056995840 | bytes 16252928 | tf_op jit(solution)/shard_map/dot_general | solution.py:156
  903.3 13.5 %convolution_convert_fusion.1 = bf16[1536,2560]{1,0:T(8,128)(2,1)} fusion(bf16[1024,1536]{1,0:T(8,128)(2,1)} %bitcast.23.rows_ref, bf16[1024,2560]{1,0:T(8,128)(2,1)} %get-tuple-element.108), kind=kOutput, calls=%fused_computation.2 | convolution fusion | flops 8056995840 | bytes 16252928 | tf_op jit(solution)/shard_map/dot_general | solution.py:156
  961.8 31.6 %shard_map.227 = (f32[256,1536]{1,0:T(8,128)}, bf16[1024,1024]{1,0:T(8,128)(2,1)}) custom-call(s32[1]{0:T(128)} %bitcast.block_ref, bf16[256,1536]{1,0:T(8,128)(2,1)} %copy.248.query_ref, bf16[256,1536]{1,0:T(8,128)(2,1)} %fusion.33.grad_ref, bf16[1024,1024]{1,0:T(8,128)(2,1)} %bitcast.22.key_ref.value_ref, bf16[1024,1024]{1,0:T(8,128)(2,1)} %bitcast.22.key_ref.value_ref), custom_call_target="tpu_custom_call" | custom-call | flops 16106127360 | bytes 7340032 | tf_op jit(solution)/shard_map/pallas_call | solution.py:405
  1018.0 22.8 %collective-permute-done.18 = bf16[48,4224]{1,0:T(8,128)(2,1)} collective-permute-done((bf16[48,4224]{1,0:T(8,128)(2,1)S(1)}, bf16[48,4224]{1,0:T(8,128)(2,1)}, u32[]{:S(2)}, u32[]{:S(2)}) %collective-permute-start.18) | collective-permute-done | bytes 405536 | tf_op jit(solution)/shard_map/ppermute | solution.py:130
  1068.6 18.0 %collective-permute-done.22 = bf16[384,1536]{1,0:T(8,128)(2,1)} collective-permute-done((bf16[384,1536]{1,0:T(8,128)(2,1)}, bf16[384,1536]{1,0:T(8,128)(2,1)}, u32[]{:S(2)}, u32[]{:S(2)}) %collective-permute-start.22) | collective-permute-done | bytes 1179680 | tf_op jit(solution)/shard_map/ppermute | solution.py:130
  1106.4 8.1 collective-permute-done.27
  1119.6 22.7 %collective-permute-done.28 = bf16[96,2688]{1,0:T(8,128)(2,1)S(1)} collective-permute-done((bf16[96,2688]{1,0:T(8,128)(2,1)S(1)}, bf16[96,2688]{1,0:T(8,128)(2,1)S(1)}, u32[]{:S(2)}, u32[]{:S(2)}) %collective-permute-start.28) | collective-permute-done | bytes 516128 | tf_op jit(solution)/shard_map/ppermute | solution.py:130
  1154.8 8.8 collective-permute-done.29
  (513 shorter events, 410.5 us)
Async XLA Ops:
  7.2 132.0 %all-gather.6.cloned.1.call-start = ((), (), s32[]{:S(2)}) async-start(), calls=%async_computation.21 | async-start | bytes 13381632 | tf_op jit(solution)/shard_map/all_gather | solution.py:531
  14.3 268.2 %all-gather.8.cloned.1.call-start = ((), (), s32[]{:S(2)}) async-start(), calls=%async_computation.22 | async-start | bytes 17694720 | tf_op jit(solution)/shard_map/all_gather | solution.py:538
  26.5 333.6 %all-gather.10.cloned.1.call-start = ((), (), s32[]{:S(2)}) async-start(), calls=%async_computation.23 | async-start | bytes 8847360 | tf_op jit(solution)/shard_map/all_gather | solution.py:538
  32.4 511.0 %all-gather.12.cloned.1.call-start = ((), (), s32[]{:S(2)}) async-start(), calls=%async_computation.24 | async-start | bytes 17694720 | tf_op jit(solution)/shard_map/all_gather | solution.py:538
  38.7 61.9 %all-to-all-start = ((bf16[4,48,4224]{2,1,0:T(8,128)(2,1)}), bf16[4,48,4224]{2,1,0:T(8,128)(2,1)S(1)}, u32[]{:S(2)}, u32[]{:S(2)}) async-start(bf16[4,48,4224]{2,1,0:T(8,128)(2,1)} %broadcast_in_dim.35), calls=%async_computation | async-start | bytes 3244032 | tf_op jit(solution)/shard_map/all_to_all | solution.py:85
  212.4 40.8 %all-to-all-start.2 = ((bf16[4,256,1536]{2,1,0:T(8,128)(2,1)}), bf16[4,256,1536]{2,1,0:T(8,128)(2,1)}, u32[]{:S(2)}, u32[]{:S(2)}) async-start(bf16[4,256,1536]{2,1,0:T(8,128)(2,1)} %broadcast_in_dim.38), calls=%async_computation.2 | async-start | bytes 6291456 | tf_op jit(solution)/shard_map/all_to_all | solution.py:60
  266.5 76.3 %all-to-all-start.4 = ((bf16[4,4,48,4224]{3,2,1,0:T(8,128)(2,1)}), bf16[4,4,48,4224]{3,2,1,0:T(8,128)(2,1)}, u32[]{:S(2)}, u32[]{:S(2)}) async-start(bf16[4,4,48,4224]{3,2,1,0:T(8,128)(2,1)} %broadcast_in_dim.42), calls=%async_computation.4 | async-start | bytes 12976128 | tf_op jit(solution)/shard_map/all_to_all | solution.py:60
  348.9 69.1 %collective-permute-start = (bf16[4,4,48,4224]{3,2,0,1:T(8,128)(2,1)}, bf16[4,4,48,4224]{3,2,0,1:T(8,128)(2,1)}, u32[]{:S(2)}, u32[]{:S(2)}) collective-permute-start(bf16[4,4,48,4224]{3,2,0,1:T(8,128)(2,1)} %copy.259), channel_id=1, source_target_pairs={{0,4},{4,0},{8,12},{12,8},{16,20},{20,16},{24,28},{28,24},{1,5},{5... | collective-permute-start | bytes 19464200 | tf_op jit(solution)/shard_map/ppermute | solution.py:81
  373.5 41.5 %all-to-all-start.5 = ((bf16[4,256,1536]{2,1,0:T(8,128)(2,1)}), bf16[4,256,1536]{2,1,0:T(8,128)(2,1)}, u32[]{:S(2)}, u32[]{:S(2)}) async-start(bf16[4,256,1536]{2,1,0:T(8,128)(2,1)} %bitcast.436), calls=%async_computation.5 | async-start | bytes 6291456 | tf_op jit(solution)/shard_map/all_to_all | solution.py:60
  378.2 208.7 %all-gather.14.cloned.1.call-start = ((), (), s32[]{:S(2)}) async-start(), calls=%async_computation.25 | async-start | bytes 8847360 | tf_op jit(solution)/shard_map/all_gather | solution.py:538
  533.6 39.2 %all-to-all-start.7 = ((bf16[4,256,1536]{2,1,0:T(8,128)(2,1)}), bf16[4,256,1536]{2,1,0:T(8,128)(2,1)}, u32[]{:S(2)}, u32[]{:S(2)}) async-start(bf16[4,256,1536]{2,1,0:T(8,128)(2,1)} %broadcast_in_dim.44), calls=%async_computation.7 | async-start | bytes 6291456 | tf_op jit(solution)/shard_map/all_to_all | solution.py:60
  538.3 525.8 %reduce-scatter.7.cloned.1.call-start = ((), (), s32[]{:S(2)}) async-start(), calls=%async_computation.26 | async-start | bytes 8847360 | tf_op jit(solution)/shard_map/reduce_scatter | solution.py:682
  627.9 44.9 %all-to-all-start.9 = ((bf16[4,256,1664]{2,1,0:T(8,128)(2,1)}), bf16[4,256,1664]{2,1,0:T(8,128)(2,1)}, u32[]{:S(2)}, u32[]{:S(2)}) async-start(bf16[4,256,1664]{2,1,0:T(8,128)(2,1)} %bitcast.424), calls=%async_computation.9 | async-start | bytes 6815744 | tf_op jit(solution)/shard_map/all_to_all | solution.py:60
  632.7 431.4 %reduce-scatter.11.cloned.1.call-start = ((), (), s32[]{:S(2)}) async-start(), calls=%async_computation.28 | async-start | bytes 8847360 | tf_op jit(solution)/shard_map/reduce_scatter | solution.py:709
  676.7 387.4 %reduce-scatter.9.cloned.1.call-start = ((), (), s32[]{:S(2)}) async-start(), calls=%async_computation.27 | async-start | bytes 8847360 | tf_op jit(solution)/shard_map/reduce_scatter | solution.py:708
  678.1 68.6 %collective-permute-start.2 = (bf16[256,1536]{1,0:T(8,128)(2,1)}, bf16[256,1536]{1,0:T(8,128)(2,1)}, u32[]{:S(2)}, u32[]{:S(2)}) collective-permute-start(bf16[256,1536]{1,0:T(8,128)(2,1)} %shard_map.222), channel_id=1, source_target_pairs={{0,4},{4,0},{8,12},{12,8},{16,20},{20,16},{24,28},{28,24},{1,5},{5... | collective-permute-start | bytes 2359304 | tf_op jit(solution)/shard_map/ppermute | solution.py:81
  680.1 48.0 %all-to-all-start.10 = ((bf16[4,256,1536]{2,1,0:T(8,128)(2,1)}), bf16[4,256,1536]{2,1,0:T(8,128)(2,1)}, u32[]{:S(2)}, u32[]{:S(2)}) async-start(bf16[4,256,1536]{2,1,0:T(8,128)(2,1)} %bitcast.435), calls=%async_computation.10 | async-start | bytes 6291456 | tf_op jit(solution)/shard_map/all_to_all | solution.py:60
  751.3 40.9 %collective-permute-start.3 = (bf16[384,1536]{1,0:T(8,128)(2,1)}, bf16[384,1536]{1,0:T(8,128)(2,1)}, u32[]{:S(2)}, u32[]{:S(2)}) collective-permute-start(bf16[384,1536]{1,0:T(8,128)(2,1)} %bitcast.82), channel_id=1, source_target_pairs={{0,1},{1,0},{2,3},{3,2},{4,5},{5,4},{6,7},{7,6},{8,9},{9,8},{10,11... | collective-permute-start | bytes 3538952 | tf_op jit(solution)/shard_map/ppermute | solution.py:130
  782.8 40.5 %all-to-all-start.12 = ((bf16[4,256,1536]{2,1,0:T(8,128)(2,1)}), bf16[4,256,1536]{2,1,0:T(8,128)(2,1)}, u32[]{:S(2)}, u32[]{:S(2)}) async-start(bf16[4,256,1536]{2,1,0:T(8,128)(2,1)} %broadcast_in_dim.48), calls=%async_computation.12 | async-start | bytes 6291456 | tf_op jit(solution)/shard_map/all_to_all | solution.py:60
  787.7 354.8 %reduce-scatter.13.cloned.1.call-start = ((), (), s32[]{:S(2)}) async-start(), calls=%async_computation.29 | async-start | bytes 8847360 | tf_op jit(solution)/shard_map/reduce_scatter | solution.py:682
  838.5 80.5 %collective-permute-start.10 = (bf16[384,1152]{1,0:T(8,128)(2,1)}, bf16[384,1152]{1,0:T(8,128)(2,1)}, u32[]{:S(2)}, u32[]{:S(2)}) collective-permute-start(bf16[384,1152]{1,0:T(8,128)(2,1)} %bitcast.104), channel_id=1, source_target_pairs={{0,1},{1,0},{2,3},{3,2},{4,5},{5,4},{6,7},{7,6},{8,9},{9,8},{10,11... | collective-permute-start | bytes 2654216 | tf_op jit(solution)/shard_map/ppermute | solution.py:130
  841.5 80.0 %collective-permute-start.9 = (bf16[384,1536]{1,0:T(8,128)(2,1)}, bf16[384,1536]{1,0:T(8,128)(2,1)}, u32[]{:S(2)}, u32[]{:S(2)}) collective-permute-start(bf16[384,1536]{1,0:T(8,128)(2,1)} %bitcast.101), channel_id=1, source_target_pairs={{0,1},{1,0},{2,3},{3,2},{4,5},{5,4},{6,7},{7,6},{8,9},{9,8},{10,11... | collective-permute-start | bytes 3538952 | tf_op jit(solution)/shard_map/ppermute | solution.py:130
  843.3 73.5 %collective-permute-start.8 = (bf16[192,1536]{1,0:T(8,128)(2,1)}, bf16[192,1536]{1,0:T(8,128)(2,1)}, u32[]{:S(2)}, u32[]{:S(2)}) collective-permute-start(bf16[192,1536]{1,0:T(8,128)(2,1)} %dynamic-slice_bitcast_fusion.4), channel_id=1, source_target_pairs={{0,2},{1,3},{2,0},{3,1},{4,6},{5,7},{6,4},{7,5},{8,10},{9,11},{10,... | collective-permute-start | bytes 1769480 | tf_op jit(solution)/shard_map/ppermute | solution.py:130
  885.7 40.2 %all-to-all-start.13 = ((bf16[4,256,1664]{2,1,0:T(8,128)(2,1)}), bf16[4,256,1664]{2,1,0:T(8,128)(2,1)S(1)}, u32[]{:S(2)}, u32[]{:S(2)}) async-start(bf16[4,256,1664]{2,1,0:T(8,128)(2,1)} %bitcast.423), calls=%async_computation.13 | async-start | bytes 6815744 | tf_op jit(solution)/shard_map/all_to_all | solution.py:60
  889.4 257.1 %reduce-scatter.15.cloned.1.call-start = ((), (), s32[]{:S(2)}) async-start(), calls=%async_computation.30 | async-start | bytes 8847360 | tf_op jit(solution)/shard_map/reduce_scatter | solution.py:708
  927.6 223.2 %reduce-scatter.17.cloned.1.call-start = ((), (), s32[]{:S(2)}) async-start(), calls=%async_computation.31 | async-start | bytes 8847360 | tf_op jit(solution)/shard_map/reduce_scatter | solution.py:709
  930.4 114.0 %collective-permute-start.16 = (bf16[256,768]{0,1:T(8,128)(2,1)}, bf16[256,768]{0,1:T(8,128)(2,1)}, u32[]{:S(2)}, u32[]{:S(2)}) collective-permute-start(bf16[256,768]{0,1:T(8,128)(2,1)} %get-tuple-element.261), channel_id=1, source_target_pairs={{0,4},{4,0},{8,12},{12,8},{16,20},{20,16},{24,28},{28,24},{1,5},{5... | collective-permute-start | bytes 1179656 | tf_op jit(solution)/shard_map/ppermute | solution.py:81
  956.7 40.5 %collective-permute-start.14 = (bf16[384,1536]{1,0:T(8,128)(2,1)}, bf16[384,1536]{1,0:T(8,128)(2,1)}, u32[]{:S(2)}, u32[]{:S(2)}) collective-permute-start(bf16[384,1536]{1,0:T(8,128)(2,1)} %bitcast.116), channel_id=1, source_target_pairs={{0,1},{1,0},{2,3},{3,2},{4,5},{5,4},{6,7},{7,6},{8,9},{9,8},{10,11... | collective-permute-start | bytes 3538952 | tf_op jit(solution)/shard_map/ppermute | solution.py:130
  961.8 38.5 %collective-permute-start.15 = (bf16[96,4224]{1,0:T(8,128)(2,1)}, bf16[96,4224]{1,0:T(8,128)(2,1)}, u32[]{:S(2)}, u32[]{:S(2)}) collective-permute-start(bf16[96,4224]{1,0:T(8,128)(2,1)} %bitcast.119), channel_id=1, source_target_pairs={{0,8},{4,12},{8,0},{12,4},{16,24},{20,28},{24,16},{28,20},{1,9},{5... | collective-permute-start | bytes 2433032 | tf_op jit(solution)/shard_map/ppermute | solution.py:130
  993.3 49.7 %all-to-all-start.14 = ((bf16[4,256,1024]{2,1,0:T(8,128)(2,1)}), bf16[4,256,1024]{2,1,0:T(8,128)(2,1)S(1)}, u32[]{:S(2)}, u32[]{:S(2)}) async-start(bf16[4,256,1024]{2,1,0:T(8,128)(2,1)} %bitcast.453), calls=%async_computation.14 | async-start | bytes 4194304 | tf_op jit(solution)/shard_map/all_to_all | solution.py:60
  1002.5 38.3 %collective-permute-start.18 = (bf16[48,4224]{1,0:T(8,128)(2,1)S(1)}, bf16[48,4224]{1,0:T(8,128)(2,1)}, u32[]{:S(2)}, u32[]{:S(2)}) collective-permute-start(bf16[48,4224]{1,0:T(8,128)(2,1)S(1)} %dynamic-slice_bitcast_fusion.6), channel_id=1, source_target_pairs={{0,16},{4,20},{8,24},{12,28},{16,0},{20,4},{24,8},{28,12},{1,17},{... | collective-permute-start | bytes 1216520 | tf_op jit(solution)/shard_map/ppermute | solution.py:130
  1043.0 74.3 %collective-permute-start.20 = (bf16[96,1536]{1,0:T(8,128)(2,1)}, bf16[96,1536]{1,0:T(8,128)(2,1)}, u32[]{:S(2)}, u32[]{:S(2)}) collective-permute-start(bf16[96,1536]{1,0:T(8,128)(2,1)} %bitcast.142), channel_id=1, source_target_pairs={{0,8},{4,12},{8,0},{12,4},{16,24},{20,28},{24,16},{28,20},{1,9},{5... | collective-permute-start | bytes 884744 | tf_op jit(solution)/shard_map/ppermute | solution.py:130
  (102 other events, 1612.3 us)
Sparse Core Ops, SparseCore 0:
  14.4 124.7 all-gather.5
  141.4 141.0 all-gather.7
  284.1 75.9 all-gather.9
  361.6 140.9 all-gather.11
  504.7 75.8 all-gather.13
  586.4 82.7 reduce-scatter.6
  676.8 83.5 reduce-scatter.10
  762.6 83.0 reduce-scatter.8
  848.0 83.0 reduce-scatter.12
  933.3 109.0 reduce-scatter.14
  1044.7 96.0 reduce-scatter.16

commit v9 on v8

--- a/solution.py
+++ b/solution.py
@@ -753,10 +753,7 @@
         grad_query_w = dot_f32(normed_split, both_cores(grad_query_lin), (0,), (0,))
         grad_query_w = grad_query_w.astype(jnp.bfloat16)
         if layer == 0:
-            grad_kv, grad_query_w, chip_part = lax.optimization_barrier(
-                (grad_kv, grad_query_w, chip_part)
-            )
-            attention_list[layer + 1] = chip_part
+            grad_kv, grad_query_w = lax.optimization_barrier((grad_kv, grad_query_w))
             grad_query_w = halve_all(grad_query_w, far_steps[:1])
         grad_kv = grad_kv.reshape(token_total, -1, 2, 2 * HEAD_SIZE)
         grad_kv = grad_kv.transpose(0, 2, 1, 3).reshape(token_total, 2 * key_width)
@@ -798,7 +795,10 @@
             grad_kv_w, last_parts = lax.optimization_barrier((grad_kv_w, last_parts))
             expert_held = [place(part, None, layer + 1, exp_dev) for part in last_parts]
             grad_kv_w = halve_all(grad_kv_w, group_steps[:1])
-            grad_kv_w, expert_held = lax.optimization_barrier((grad_kv_w, expert_held))
+            grad_kv_w, expert_held, chip_part = lax.optimization_barrier(
+                (grad_kv_w, expert_held, chip_part)
+            )
+            attention_list[layer + 1] = (chip_part[:, :query_width], chip_part[:, query_width:])
             late_part = jnp.concatenate(
                 [
                     halve_all(grad_query_w, far_steps[1:]),
@@ -812,20 +812,18 @@
                 for part, held in zip(expert_parts[:2], expert_held[:2])
             ] + expert_held[2:]
             late_part, expert_held = lax.optimization_barrier((late_part, expert_held))
-            attention_list[layer] = jnp.concatenate(
-                [
-                    halve_all(grad_output_w, chip_steps),
-                    halve_all(late_part, chip_steps[1:]),
-                ],
-                axis=1,
+            attention_list[layer] = (
+                halve_all(grad_output_w, chip_steps),
+                halve_all(late_part, chip_steps[1:]),
             )
         last_parts = expert_parts
         grad_hidden = grad_middle + grad_norm_in
-    stacked = jnp.stack(attention_list).astype(jnp.float32)
-    cuts = [query_width, query_width, key_width, key_width, expert_total, 1, 1]
+    output_grads = jnp.stack([parts[0] for parts in attention_list]).astype(jnp.float32)
+    cuts = [query_width, key_width, key_width, expert_total, 1, 1]
     cuts = [sum(cuts[:index]) for index in range(len(cuts) + 1)]
-    output_grads, query_grads, key_grads, value_grads, router_grads, one, two = (
-        stacked[:, :, start:stop] for start, stop in zip(cuts[:-1], cuts[1:])
+    query_grads, key_grads, value_grads, router_grads, one, two = (
+        jnp.stack([parts[1][:, start:stop] for parts in attention_list]).astype(jnp.float32)
+        for start, stop in zip(cuts[:-1], cuts[1:])
     )
     expert_held[2] = place(last_parts[2], expert_held[2], 0, exp_dev)
     down_grads, gate_grads, up_grads = expert_held

time: 1180 us -> 1180 us (level)
  transfers between devices with their start and end apart: 55 -> 55, of which waited for: 20 -> 22; matrix products, arithmetic and copies ran while one was open for 31% -> 31% of each run, Pallas kernels for 23% -> 23%
where the time goes in v9:
time: 1180 us; the launch traced here: 1170 us
  waiting for transfers between devices  358 us (30%)
  Pallas kernels  272 us (23%)
  matrix products  184 us (16%)
  local copies, waits for them, and re-layouts  123 us (10%)
  starting transfers between devices  93.7 us (8%)
  other arithmetic  84.4 us (7%)
  blocking collectives  39.7 us (3%)
  between operations  16.1 us (1%)
    all_to_all x13, waiting for transfers between devices, exchange(): lax.all_to_all(blocks, 'expert', split_axis=0, concat_axis=0, tiled=True)  173 us
    dot_general x26, matrix products, dot_f32(): lax.dot_general(left, right, ((left_dims, right_dims), ((), ())), preferr...  167 us
    pallas_call x2, Pallas kernels, expert_backward(): pl.pallas_call(expert_backward_kernel, grid_spec=pltpu.PrefetchScalarGrid...  82.3 us
    ppermute x17, waiting for transfers between devices, halve(): lax.ppermute(theirs.reshape(-1, width), axis_name, [(i, i ^ step) for i i...  74.6 us
    pallas_call x2, Pallas kernels, attention_backward(): pl.pallas_call(attention_backward_kernel, grid_spec=pltpu.PrefetchScalarG...  62.3 us
    all_to_all x13, starting transfers between devices, exchange(): lax.all_to_all(blocks, 'expert', split_axis=0, concat_axis=0, tiled=True)  59.4 us
    pallas_call x2, Pallas kernels, expert_forward(): pl.pallas_call(expert_forward_kernel, grid=(experts, 2), in_specs=[row_bl...  56.8 us
    all_to_all x1, waiting for transfers between devices, exchange_chips(): lax.all_to_all(blocks, 'dp', split_axis=0, concat_axis=0, axis_index_grou...  54.5 us
  transfers between devices with their start and end apart: 55, of which 22 were waited for; matrix products, arithmetic and copies ran while one was open for 31% of the time, Pallas kernels for 23%

profile of v9, /device:TPU:0, one launch (start us, length us, event | category | flops | bytes accessed | tf_op | source)
XLA Modules:
  0.0 1171.0 jit_solution(1792790912018325148)
XLA Ops:
  38.7 6.5 all-to-all-start
  46.0 54.5 %all-to-all-done = bf16[4,48,4224]{2,1,0:T(8,128)(2,1)S(1)} async-done(((bf16[4,48,4224]{2,1,0:T(8,128)(2,1)}), bf16[4,48,4224]{2,1,0:T(8,128)(2,1)S(1)}, u32[]{:S(2)}, u32[]{:S(2)}) %all-to-all-start) | async-done | bytes 1622048 | tf_op jit(solution)/shard_map/all_to_all | solution.py:85
  100.8 38.4 %all-gather.6.cloned.1.call-done = bf16[1536,4224]{1,0:T(8,128)(2,1)} async-done(((bf16[48,4224]{1,0:T(8,128)(2,1)}), bf16[1536,4224]{1,0:T(8,128)(2,1)}) %all-gather.6.cloned.1.call-update) | async-done | bytes 12976144 | tf_op jit(solution)/shard_map/all_gather | solution.py:531
  161.7 19.5 %all-to-all-done.1 = bf16[4,256,1024]{2,1,0:T(8,128)(2,1)} async-done(((bf16[4,256,1024]{2,1,0:T(8,128)(2,1)}), bf16[4,256,1024]{2,1,0:T(8,128)(2,1)}, u32[]{:S(2)}, u32[]{:S(2)}) %all-to-all-start.1) | async-done | bytes 2097184 | tf_op jit(solution)/shard_map/all_to_all | solution.py:60
  181.2 23.3 %shard_map.220 = bf16[256,1536]{1,0:T(8,128)(2,1)} custom-call(s32[1]{0:T(128)} %bitcast.block_ref, bf16[256,1536]{1,0:T(8,128)(2,1)} %copy.255.query_ref, bf16[1024,1024]{1,0:T(8,128)(2,1)} %bitcast.22.key_ref.value_ref, bf16[1024,1024]{1,0:T(8,128)(2,1)} %bitcast.22.key_ref.value_ref), custom_call_target="tpu_custom_call" | custom-call | flops 6442450944 | bytes 3670016 | tf_op jit(solution)/shard_map/pallas_call | solution.py:358
  217.8 35.3 %all-to-all-done.2 = bf16[4,256,1536]{2,1,0:T(8,128)(2,1)} async-done(((bf16[4,256,1536]{2,1,0:T(8,128)(2,1)}), bf16[4,256,1536]{2,1,0:T(8,128)(2,1)}, u32[]{:S(2)}, u32[]{:S(2)}) %all-to-all-start.2) | async-done | bytes 3145760 | tf_op jit(solution)/shard_map/all_to_all | solution.py:60
  282.5 28.4 %shard_map.221 = (bf16[1024,2560]{1,0:T(8,128)(2,1)}, bf16[1024,2560]{1,0:T(8,128)(2,1)}, bf16[1024,2560]{1,0:T(8,128)(2,1)}) custom-call(bf16[1024,1536]{1,0:T(8,128)(2,1)} %bitcast.23.rows_ref, bf16[1536,5120]{1,0:T(8,128)(2,1)} %all-gather.8.cloned.1.call-done.gate_ref.up_ref, bf16[1536,5120]{1,0:T(8,128)(2,1)} %all-gather.8.cloned.1.call-done.gate_ref.up_ref, ...), custom_call_target="tpu_custom_call" | custom-call | flops 16106127360 | bytes 31457280 | tf_op jit(solution)/shard_map/pallas_call | solution.py:194
  310.9 31.8 %all-to-all-done.4 = bf16[4,4,48,4224]{3,2,1,0:T(8,128)(2,1)} async-done(((bf16[4,4,48,4224]{3,2,1,0:T(8,128)(2,1)}), bf16[4,4,48,4224]{3,2,1,0:T(8,128)(2,1)}, u32[]{:S(2)}, u32[]{:S(2)}) %all-to-all-start.4) | async-done | bytes 6488096 | tf_op jit(solution)/shard_map/all_to_all | solution.py:60
  342.7 6.1 copy.266
  348.8 11.3 all-gather.10.cloned.1.call-done.down_ref
  360.1 13.3 %convolution_convert_fusion.7 = bf16[1024,1536]{1,0:T(8,128)(2,1)} fusion(bf16[1024,2560]{1,0:T(8,128)(2,1)} %get-tuple-element.82, bf16[1536,2560]{1,0:T(8,128)(2,1)} %all-gather.10.cloned.1.call-done.down_ref), kind=kOutput, calls=%fused_computation.33 | convolution fusion | flops 8054636544 | bytes 16252928 | tf_op jit(solution)/shard_map/dot_general | solution.py:156
  381.2 33.8 %all-to-all-done.5 = bf16[4,256,1536]{2,1,0:T(8,128)(2,1)} async-done(((bf16[4,256,1536]{2,1,0:T(8,128)(2,1)}), bf16[4,256,1536]{2,1,0:T(8,128)(2,1)}, u32[]{:S(2)}, u32[]{:S(2)}) %all-to-all-start.5) | async-done | bytes 3145760 | tf_op jit(solution)/shard_map/all_to_all | solution.py:60
  444.6 18.6 %all-to-all-done.6 = bf16[4,256,1024]{2,1,0:T(8,128)(2,1)} async-done(((bf16[4,256,1024]{2,1,0:T(8,128)(2,1)}), bf16[4,256,1024]{2,1,0:T(8,128)(2,1)}, u32[]{:S(2)}, u32[]{:S(2)}) %all-to-all-start.6) | async-done | bytes 2097184 | tf_op jit(solution)/shard_map/all_to_all | solution.py:60
  463.2 23.3 %shard_map.222 = bf16[256,1536]{1,0:T(8,128)(2,1)} custom-call(s32[1]{0:T(128)} %bitcast.block_ref, bf16[256,1536]{1,0:T(8,128)(2,1)} %copy.284.query_ref, bf16[1024,1024]{1,0:T(8,128)(2,1)} %bitcast.48.key_ref.value_ref, bf16[1024,1024]{1,0:T(8,128)(2,1)} %bitcast.48.key_ref.value_ref), custom_call_target="tpu_custom_call" | custom-call | flops 6442450944 | bytes 3670016 | tf_op jit(solution)/shard_map/pallas_call | solution.py:358
  492.0 39.7 %all_to_all.75 = bf16[4,256,1536]{2,1,0:T(8,128)(2,1)} all-to-all(bf16[4,256,1536]{2,1,0:T(8,128)(2,1)S(1)} %broadcast_in_dim.45), channel_id=1, replica_groups=mesh['dp'=8,'expert'=4] {'expert'}, dimensions={0} | all-to-all | bytes 6291456 | tf_op jit(solution)/shard_map/all_to_all | solution.py:60
  543.4 28.4 %shard_map.223 = (bf16[1024,2560]{1,0:T(8,128)(2,1)}, bf16[1024,2560]{1,0:T(8,128)(2,1)}, bf16[1024,2560]{1,0:T(8,128)(2,1)}) custom-call(bf16[1024,1536]{1,0:T(8,128)(2,1)} %bitcast.449, bf16[1536,5120]{1,0:T(8,128)(2,1)} %all-gather.12.cloned.1.call-done.gate_ref.up_ref, bf16[1536,5120]{1,0:T(8,128)(2,1)} %all-gather.12.cloned.1.call-done.gate_ref.up_ref, ...), custom_call_target="tpu_custom_call" | custom-call | flops 16106127360 | bytes 31457280 | tf_op jit(solution)/shard_map/pallas_call | solution.py:194
  572.7 13.4 %fusion = bf16[1536,2560]{1,0:T(8,128)(2,1)} fusion(bf16[1024,2560]{1,0:T(8,128)(2,1)} %get-tuple-element.84, bf16[1024,1536]{1,0:T(8,128)(2,1)} %bitcast.49.grad_ref), kind=kOutput, calls=%fused_computation.7 | convolution fusion | flops 8056995840 | bytes 16252928 | tf_op jit(solution)/shard_map/dot_general | solution.py:156
  586.7 41.0 %shard_map.224 = (bf16[1024,2560]{1,0:T(8,128)(2,1)}, bf16[1024,2560]{1,0:T(8,128)(2,1)}, bf16[1024,1664]{1,0:T(8,128)(2,1)}) custom-call(s32[2]{0:T(128)} %pad_add_fusion.group_ref, bf16[1024,1536]{1,0:T(8,128)(2,1)} %bitcast.49.grad_ref, bf16[1536,2560]{1,0:T(8,128)(2,1)} %all-gather.14.cloned.1.call-done.down_ref, ...), custom_call_target="tpu_custom_call" | custom-call | flops 24159191040 | bytes 44564480 | tf_op jit(solution)/shard_map/pallas_call | solution.py:281
  632.7 13.5 %convolution_convert_fusion.3 = bf16[1536,2560]{1,0:T(8,128)(2,1)} fusion(bf16[1024,1536]{1,0:T(8,128)(2,1)} %bitcast.450, bf16[1024,2560]{1,0:T(8,128)(2,1)} %get-tuple-element.91), kind=kOutput, calls=%fused_computation.4 | convolution fusion | flops 8056995840 | bytes 16252928 | tf_op jit(solution)/shard_map/dot_general | solution.py:156
  646.2 13.6 %convolution_convert_fusion.6 = bf16[1024,1536]{1,0:T(8,128)(2,1)} fusion(bf16[1024,2560]{1,0:T(8,128)(2,1)} %get-tuple-element.84, bf16[1536,2560]{1,0:T(8,128)(2,1)} %all-gather.14.cloned.1.call-done.down_ref), kind=kOutput, calls=%fused_computation.32 | convolution fusion | flops 8054636544 | bytes 16252928 | tf_op jit(solution)/shard_map/dot_general | solution.py:156
  659.7 12.8 %convolution_convert_fusion.4 = bf16[1536,2560]{1,0:T(8,128)(2,1)} fusion(bf16[1024,1536]{1,0:T(8,128)(2,1)S(1)} %bitcast.451, bf16[1024,2560]{1,0:T(8,128)(2,1)} %get-tuple-element.90), kind=kOutput, calls=%fused_computation.5 | convolution fusion | flops 8056995840 | bytes 16252928 | tf_op jit(solution)/shard_map/dot_general | solution.py:156
  696.7 31.1 %shard_map.225 = (f32[256,1536]{1,0:T(8,128)}, bf16[1024,1024]{1,0:T(8,128)(2,1)}) custom-call(s32[1]{0:T(128)} %bitcast.block_ref, bf16[256,1536]{1,0:T(8,128)(2,1)} %copy.284.query_ref, bf16[256,1536]{1,0:T(8,128)(2,1)} %fusion.36.grad_ref, bf16[1024,1024]{1,0:T(8,128)(2,1)} %bitcast.48.key_ref.value_ref, bf16[1024,1024]{1,0:T(8,128)(2,1)} %bitcast.48.key_ref.value_ref), custom_call_target="tpu_custom_call" | custom-call | flops 16106127360 | bytes 7340032 | tf_op jit(solution)/shard_map/pallas_call | solution.py:405
  801.5 21.7 %all-to-all-done.12 = bf16[4,256,1536]{2,1,0:T(8,128)(2,1)} async-done(((bf16[4,256,1536]{2,1,0:T(8,128)(2,1)}), bf16[4,256,1536]{2,1,0:T(8,128)(2,1)}, u32[]{:S(2)}, u32[]{:S(2)}) %all-to-all-start.12) | async-done | bytes 3145760 | tf_op jit(solution)/shard_map/all_to_all | solution.py:60
  823.2 13.7 %convolution_convert_fusion.2 = bf16[1536,2560]{1,0:T(8,128)(2,1)} fusion(bf16[1024,1536]{1,0:T(8,128)(2,1)} %bitcast.74.grad_ref, bf16[1024,2560]{1,0:T(8,128)(2,1)} %get-tuple-element.82), kind=kOutput, calls=%fused_computation.3 | convolution fusion | flops 8056995840 | bytes 16252928 | tf_op jit(solution)/shard_map/dot_general | solution.py:156
  844.3 41.3 %shard_map.226 = (bf16[1024,2560]{1,0:T(8,128)(2,1)}, bf16[1024,2560]{1,0:T(8,128)(2,1)}, bf16[1024,1664]{1,0:T(8,128)(2,1)}) custom-call(s32[2]{0:T(128)} %pad_add_fusion.group_ref, bf16[1024,1536]{1,0:T(8,128)(2,1)} %bitcast.74.grad_ref, bf16[1536,2560]{1,0:T(8,128)(2,1)} %all-gather.10.cloned.1.call-done.down_ref, ...), custom_call_target="tpu_custom_call" | custom-call | flops 24159191040 | bytes 44564480 | tf_op jit(solution)/shard_map/pallas_call | solution.py:281
  889.4 13.8 %convolution_convert_fusion = bf16[1536,2560]{1,0:T(8,128)(2,1)} fusion(bf16[1024,1536]{1,0:T(8,128)(2,1)} %bitcast.23.rows_ref, bf16[1024,2560]{1,0:T(8,128)(2,1)} %get-tuple-element.109), kind=kOutput, calls=%fused_computation.1 | convolution fusion | flops 8056995840 | bytes 16252928 | tf_op jit(solution)/shard_map/dot_general | solution.py:156
  903.2 13.5 %convolution_convert_fusion.1 = bf16[1536,2560]{1,0:T(8,128)(2,1)} fusion(bf16[1024,1536]{1,0:T(8,128)(2,1)} %bitcast.23.rows_ref, bf16[1024,2560]{1,0:T(8,128)(2,1)} %get-tuple-element.108), kind=kOutput, calls=%fused_computation.2 | convolution fusion | flops 8056995840 | bytes 16252928 | tf_op jit(solution)/shard_map/dot_general | solution.py:156
  962.0 31.2 %shard_map.227 = (f32[256,1536]{1,0:T(8,128)}, bf16[1024,1024]{1,0:T(8,128)(2,1)}) custom-call(s32[1]{0:T(128)} %bitcast.block_ref, bf16[256,1536]{1,0:T(8,128)(2,1)} %copy.255.query_ref, bf16[256,1536]{1,0:T(8,128)(2,1)} %fusion.33.grad_ref, bf16[1024,1024]{1,0:T(8,128)(2,1)} %bitcast.22.key_ref.value_ref, bf16[1024,1024]{1,0:T(8,128)(2,1)} %bitcast.22.key_ref.value_ref), custom_call_target="tpu_custom_call" | custom-call | flops 16106127360 | bytes 7340032 | tf_op jit(solution)/shard_map/pallas_call | solution.py:405
  1018.5 22.9 %collective-permute-done.23 = bf16[48,4224]{1,0:T(8,128)(2,1)} collective-permute-done((bf16[48,4224]{1,0:T(8,128)(2,1)}, bf16[48,4224]{1,0:T(8,128)(2,1)}, u32[]{:S(2)}, u32[]{:S(2)}) %collective-permute-start.23) | collective-permute-done | bytes 405536 | tf_op jit(solution)/shard_map/ppermute | solution.py:130
  1072.1 8.1 collective-permute-done.29
  1106.0 8.0 collective-permute-done.24
  1116.1 23.1 %collective-permute-done.25 = bf16[96,2688]{1,0:T(8,128)(2,1)S(1)} collective-permute-done((bf16[96,2688]{1,0:T(8,128)(2,1)S(1)}, bf16[96,2688]{1,0:T(8,128)(2,1)S(1)}, u32[]{:S(2)}, u32[]{:S(2)}) %collective-permute-start.25) | collective-permute-done | bytes 516128 | tf_op jit(solution)/shard_map/ppermute | solution.py:130
  (517 shorter events, 419.9 us)
Async XLA Ops:
  7.2 132.0 %all-gather.6.cloned.1.call-start = ((), (), s32[]{:S(2)}) async-start(), calls=%async_computation.21 | async-start | bytes 13381632 | tf_op jit(solution)/shard_map/all_gather | solution.py:531
  14.3 268.2 %all-gather.8.cloned.1.call-start = ((), (), s32[]{:S(2)}) async-start(), calls=%async_computation.22 | async-start | bytes 17694720 | tf_op jit(solution)/shard_map/all_gather | solution.py:538
  26.5 333.6 %all-gather.10.cloned.1.call-start = ((), (), s32[]{:S(2)}) async-start(), calls=%async_computation.23 | async-start | bytes 8847360 | tf_op jit(solution)/shard_map/all_gather | solution.py:538
  32.4 511.0 %all-gather.12.cloned.1.call-start = ((), (), s32[]{:S(2)}) async-start(), calls=%async_computation.24 | async-start | bytes 17694720 | tf_op jit(solution)/shard_map/all_gather | solution.py:538
  38.7 61.9 %all-to-all-start = ((bf16[4,48,4224]{2,1,0:T(8,128)(2,1)}), bf16[4,48,4224]{2,1,0:T(8,128)(2,1)S(1)}, u32[]{:S(2)}, u32[]{:S(2)}) async-start(bf16[4,48,4224]{2,1,0:T(8,128)(2,1)} %broadcast_in_dim.35), calls=%async_computation | async-start | bytes 3244032 | tf_op jit(solution)/shard_map/all_to_all | solution.py:85
  212.3 40.8 %all-to-all-start.2 = ((bf16[4,256,1536]{2,1,0:T(8,128)(2,1)}), bf16[4,256,1536]{2,1,0:T(8,128)(2,1)}, u32[]{:S(2)}, u32[]{:S(2)}) async-start(bf16[4,256,1536]{2,1,0:T(8,128)(2,1)} %broadcast_in_dim.38), calls=%async_computation.2 | async-start | bytes 6291456 | tf_op jit(solution)/shard_map/all_to_all | solution.py:60
  266.4 76.3 %all-to-all-start.4 = ((bf16[4,4,48,4224]{3,2,1,0:T(8,128)(2,1)}), bf16[4,4,48,4224]{3,2,1,0:T(8,128)(2,1)}, u32[]{:S(2)}, u32[]{:S(2)}) async-start(bf16[4,4,48,4224]{3,2,1,0:T(8,128)(2,1)} %broadcast_in_dim.42), calls=%async_computation.4 | async-start | bytes 12976128 | tf_op jit(solution)/shard_map/all_to_all | solution.py:60
  348.8 69.1 %collective-permute-start = (bf16[4,4,48,4224]{3,2,0,1:T(8,128)(2,1)}, bf16[4,4,48,4224]{3,2,0,1:T(8,128)(2,1)}, u32[]{:S(2)}, u32[]{:S(2)}) collective-permute-start(bf16[4,4,48,4224]{3,2,0,1:T(8,128)(2,1)} %copy.266), channel_id=1, source_target_pairs={{0,4},{4,0},{8,12},{12,8},{16,20},{20,16},{24,28},{28,24},{1,5},{5... | collective-permute-start | bytes 19464200 | tf_op jit(solution)/shard_map/ppermute | solution.py:81
  373.4 41.5 %all-to-all-start.5 = ((bf16[4,256,1536]{2,1,0:T(8,128)(2,1)}), bf16[4,256,1536]{2,1,0:T(8,128)(2,1)}, u32[]{:S(2)}, u32[]{:S(2)}) async-start(bf16[4,256,1536]{2,1,0:T(8,128)(2,1)} %bitcast.453), calls=%async_computation.5 | async-start | bytes 6291456 | tf_op jit(solution)/shard_map/all_to_all | solution.py:60
  378.1 208.6 %all-gather.14.cloned.1.call-start = ((), (), s32[]{:S(2)}) async-start(), calls=%async_computation.25 | async-start | bytes 8847360 | tf_op jit(solution)/shard_map/all_gather | solution.py:538
  533.6 39.2 %all-to-all-start.7 = ((bf16[4,256,1536]{2,1,0:T(8,128)(2,1)}), bf16[4,256,1536]{2,1,0:T(8,128)(2,1)}, u32[]{:S(2)}, u32[]{:S(2)}) async-start(bf16[4,256,1536]{2,1,0:T(8,128)(2,1)} %broadcast_in_dim.44), calls=%async_computation.7 | async-start | bytes 6291456 | tf_op jit(solution)/shard_map/all_to_all | solution.py:60
  538.2 531.2 %reduce-scatter.7.cloned.1.call-start = ((), (), s32[]{:S(2)}) async-start(), calls=%async_computation.26 | async-start | bytes 8847360 | tf_op jit(solution)/shard_map/reduce_scatter | solution.py:682
  627.7 44.9 %all-to-all-start.9 = ((bf16[4,256,1664]{2,1,0:T(8,128)(2,1)}), bf16[4,256,1664]{2,1,0:T(8,128)(2,1)}, u32[]{:S(2)}, u32[]{:S(2)}) async-start(bf16[4,256,1664]{2,1,0:T(8,128)(2,1)} %bitcast.441), calls=%async_computation.9 | async-start | bytes 6815744 | tf_op jit(solution)/shard_map/all_to_all | solution.py:60
  632.4 437.0 %reduce-scatter.11.cloned.1.call-start = ((), (), s32[]{:S(2)}) async-start(), calls=%async_computation.28 | async-start | bytes 8847360 | tf_op jit(solution)/shard_map/reduce_scatter | solution.py:709
  676.4 393.1 %reduce-scatter.9.cloned.1.call-start = ((), (), s32[]{:S(2)}) async-start(), calls=%async_computation.27 | async-start | bytes 8847360 | tf_op jit(solution)/shard_map/reduce_scatter | solution.py:708
  677.9 68.5 %collective-permute-start.2 = (bf16[256,1536]{1,0:T(8,128)(2,1)}, bf16[256,1536]{1,0:T(8,128)(2,1)}, u32[]{:S(2)}, u32[]{:S(2)}) collective-permute-start(bf16[256,1536]{1,0:T(8,128)(2,1)} %shard_map.222), channel_id=1, source_target_pairs={{0,4},{4,0},{8,12},{12,8},{16,20},{20,16},{24,28},{28,24},{1,5},{5... | collective-permute-start | bytes 2359304 | tf_op jit(solution)/shard_map/ppermute | solution.py:81
  679.8 48.0 %all-to-all-start.10 = ((bf16[4,256,1536]{2,1,0:T(8,128)(2,1)}), bf16[4,256,1536]{2,1,0:T(8,128)(2,1)}, u32[]{:S(2)}, u32[]{:S(2)}) async-start(bf16[4,256,1536]{2,1,0:T(8,128)(2,1)} %bitcast.452), calls=%async_computation.10 | async-start | bytes 6291456 | tf_op jit(solution)/shard_map/all_to_all | solution.py:60
  751.1 40.7 %collective-permute-start.3 = (bf16[384,1536]{1,0:T(8,128)(2,1)}, bf16[384,1536]{1,0:T(8,128)(2,1)}, u32[]{:S(2)}, u32[]{:S(2)}) collective-permute-start(bf16[384,1536]{1,0:T(8,128)(2,1)} %bitcast.82), channel_id=1, source_target_pairs={{0,1},{1,0},{2,3},{3,2},{4,5},{5,4},{6,7},{7,6},{8,9},{9,8},{10,11... | collective-permute-start | bytes 3538952 | tf_op jit(solution)/shard_map/ppermute | solution.py:130
  782.4 40.9 %all-to-all-start.12 = ((bf16[4,256,1536]{2,1,0:T(8,128)(2,1)}), bf16[4,256,1536]{2,1,0:T(8,128)(2,1)}, u32[]{:S(2)}, u32[]{:S(2)}) async-start(bf16[4,256,1536]{2,1,0:T(8,128)(2,1)} %broadcast_in_dim.48), calls=%async_computation.12 | async-start | bytes 6291456 | tf_op jit(solution)/shard_map/all_to_all | solution.py:60
  787.2 352.1 %reduce-scatter.13.cloned.1.call-start = ((), (), s32[]{:S(2)}) async-start(), calls=%async_computation.29 | async-start | bytes 8847360 | tf_op jit(solution)/shard_map/reduce_scatter | solution.py:682
  838.4 80.6 %collective-permute-start.10 = (bf16[384,1152]{1,0:T(8,128)(2,1)}, bf16[384,1152]{1,0:T(8,128)(2,1)}, u32[]{:S(2)}, u32[]{:S(2)}) collective-permute-start(bf16[384,1152]{1,0:T(8,128)(2,1)} %bitcast.104), channel_id=1, source_target_pairs={{0,1},{1,0},{2,3},{3,2},{4,5},{5,4},{6,7},{7,6},{8,9},{9,8},{10,11... | collective-permute-start | bytes 2654216 | tf_op jit(solution)/shard_map/ppermute | solution.py:130
  841.3 80.1 %collective-permute-start.9 = (bf16[384,1536]{1,0:T(8,128)(2,1)}, bf16[384,1536]{1,0:T(8,128)(2,1)}, u32[]{:S(2)}, u32[]{:S(2)}) collective-permute-start(bf16[384,1536]{1,0:T(8,128)(2,1)} %bitcast.101), channel_id=1, source_target_pairs={{0,1},{1,0},{2,3},{3,2},{4,5},{5,4},{6,7},{7,6},{8,9},{9,8},{10,11... | collective-permute-start | bytes 3538952 | tf_op jit(solution)/shard_map/ppermute | solution.py:130
  843.2 73.6 %collective-permute-start.8 = (bf16[192,1536]{1,0:T(8,128)(2,1)}, bf16[192,1536]{1,0:T(8,128)(2,1)}, u32[]{:S(2)}, u32[]{:S(2)}) collective-permute-start(bf16[192,1536]{1,0:T(8,128)(2,1)} %dynamic-slice_bitcast_fusion.4), channel_id=1, source_target_pairs={{0,2},{1,3},{2,0},{3,1},{4,6},{5,7},{6,4},{7,5},{8,10},{9,11},{10,... | collective-permute-start | bytes 1769480 | tf_op jit(solution)/shard_map/ppermute | solution.py:130
  885.6 40.5 %all-to-all-start.13 = ((bf16[4,256,1664]{2,1,0:T(8,128)(2,1)}), bf16[4,256,1664]{2,1,0:T(8,128)(2,1)S(1)}, u32[]{:S(2)}, u32[]{:S(2)}) async-start(bf16[4,256,1664]{2,1,0:T(8,128)(2,1)} %bitcast.440), calls=%async_computation.13 | async-start | bytes 6815744 | tf_op jit(solution)/shard_map/all_to_all | solution.py:60
  889.4 254.1 %reduce-scatter.15.cloned.1.call-start = ((), (), s32[]{:S(2)}) async-start(), calls=%async_computation.30 | async-start | bytes 8847360 | tf_op jit(solution)/shard_map/reduce_scatter | solution.py:708
  927.8 222.8 %reduce-scatter.17.cloned.1.call-start = ((), (), s32[]{:S(2)}) async-start(), calls=%async_computation.31 | async-start | bytes 8847360 | tf_op jit(solution)/shard_map/reduce_scatter | solution.py:709
  930.7 115.0 %collective-permute-start.16 = (bf16[256,768]{0,1:T(8,128)(2,1)}, bf16[256,768]{0,1:T(8,128)(2,1)}, u32[]{:S(2)}, u32[]{:S(2)}) collective-permute-start(bf16[256,768]{0,1:T(8,128)(2,1)} %get-tuple-element.235), channel_id=1, source_target_pairs={{0,4},{4,0},{8,12},{12,8},{16,20},{20,16},{24,28},{28,24},{1,5},{5... | collective-permute-start | bytes 1179656 | tf_op jit(solution)/shard_map/ppermute | solution.py:81
  956.9 40.1 %collective-permute-start.14 = (bf16[384,1536]{1,0:T(8,128)(2,1)}, bf16[384,1536]{1,0:T(8,128)(2,1)}, u32[]{:S(2)}, u32[]{:S(2)}) collective-permute-start(bf16[384,1536]{1,0:T(8,128)(2,1)} %bitcast.116), channel_id=1, source_target_pairs={{0,1},{1,0},{2,3},{3,2},{4,5},{5,4},{6,7},{7,6},{8,9},{9,8},{10,11... | collective-permute-start | bytes 3538952 | tf_op jit(solution)/shard_map/ppermute | solution.py:130
  962.0 38.3 %collective-permute-start.15 = (bf16[96,4224]{1,0:T(8,128)(2,1)}, bf16[96,4224]{1,0:T(8,128)(2,1)}, u32[]{:S(2)}, u32[]{:S(2)}) collective-permute-start(bf16[96,4224]{1,0:T(8,128)(2,1)} %bitcast.119), channel_id=1, source_target_pairs={{0,8},{4,12},{8,0},{12,4},{16,24},{20,28},{24,16},{28,20},{1,9},{5... | collective-permute-start | bytes 2433032 | tf_op jit(solution)/shard_map/ppermute | solution.py:130
  993.2 51.2 %all-to-all-start.14 = ((bf16[4,256,1024]{2,1,0:T(8,128)(2,1)}), bf16[4,256,1024]{2,1,0:T(8,128)(2,1)S(1)}, u32[]{:S(2)}, u32[]{:S(2)}) async-start(bf16[4,256,1024]{2,1,0:T(8,128)(2,1)} %bitcast.470), calls=%async_computation.14 | async-start | bytes 4194304 | tf_op jit(solution)/shard_map/all_to_all | solution.py:60
  1003.4 38.0 %collective-permute-start.23 = (bf16[48,4224]{1,0:T(8,128)(2,1)}, bf16[48,4224]{1,0:T(8,128)(2,1)}, u32[]{:S(2)}, u32[]{:S(2)}) collective-permute-start(bf16[48,4224]{1,0:T(8,128)(2,1)} %dynamic-slice_bitcast_fusion.6), channel_id=1, source_target_pairs={{0,16},{4,20},{8,24},{12,28},{16,0},{20,4},{24,8},{28,12},{1,17},{... | collective-permute-start | bytes 1216520 | tf_op jit(solution)/shard_map/ppermute | solution.py:130
  1011.3 34.4 %collective-permute-start.17 = (bf16[256,1536]{0,1:T(8,128)(2,1)}, bf16[256,1536]{0,1:T(8,128)(2,1)}, u32[]{:S(2)}, u32[]{:S(2)}) collective-permute-start(bf16[256,1536]{0,1:T(8,128)(2,1)} %bitcast.121), channel_id=1, source_target_pairs={{0,4},{4,0},{8,12},{12,8},{16,20},{20,16},{24,28},{28,24},{1,5},{5... | collective-permute-start | bytes 2359304 | tf_op jit(solution)/shard_map/ppermute | solution.py:81
  (99 other events, 1566.5 us)
Sparse Core Ops, SparseCore 0:
  14.4 124.7 all-gather.5
  141.4 141.0 all-gather.7
  284.1 75.9 all-gather.9
  361.6 140.9 all-gather.11
  504.7 75.8 all-gather.13
  586.3 82.8 reduce-scatter.6
  676.5 83.7 reduce-scatter.10
  762.7 83.0 reduce-scatter.8
  848.0 83.0 reduce-scatter.12
  933.3 109.0 reduce-scatter.14
  1044.7 100.2 reduce-scatter.16
